TPU v7x, 32 devices: a whole 2x2x4 slice. The times are simulated.
32 devices in a mesh: dp: 8 (over y, x, core), tensor: 4 (over z).
Axes of the slice: x: 2, y: 2, z: 4, core: 2. Of those that a mesh axis runs over, the one named last changes fastest.
Arguments:
- word_in: bfloat16 [16384, 768], P('dp'), may hold values from -6 to 6
- entity_in: bfloat16 [4096, 768], P('dp'), may hold values from -6 to 6
- entity_spans: int32 [32, 128, 2], P('dp'), may hold values from 0 to 512, as said below
- word_mask: int32 [32, 512], P('dp'), may hold values 0 or 1
- entity_mask: int32 [32, 128], P('dp'), may hold values 0 or 1
- pos_table: bfloat16 [512, 768], replicated, may hold values from -6 to 6
- query_w: bfloat16 [4, 768, 768], P(None, None, 'tensor'), may hold values from -0.21875 to 0.21875
- query_b: bfloat16 [4, 768], P(None, 'tensor'), may hold values from -3 to 3
- key_w: bfloat16 [768, 768], P(None, 'tensor'), may hold values from -0.21875 to 0.21875
- value_w: bfloat16 [768, 768], P(None, 'tensor'), may hold values from -0.21875 to 0.21875
- value_b: bfloat16 [768], P('tensor'), may hold values from -0.29882812 to 0.29882812
- out_w: bfloat16 [768, 768], P('tensor'), may hold values from -3.5 to 3.5
- out_b: bfloat16 [768], replicated, may hold values from -3 to 3
- norm1_gain: bfloat16 [768], replicated, may hold values from 0.099609375 to 1.8984375
- norm1_bias: bfloat16 [768], replicated, may hold values from -2 to 2
- up_w: bfloat16 [768, 3072], P(None, 'tensor'), may hold values from -0.21875 to 0.21875
- up_b: bfloat16 [3072], P('tensor'), may hold values from -3 to 3
- down_w: bfloat16 [3072, 768], P('tensor'), may hold values from -0.109375 to 0.109375
- down_b: bfloat16 [768], replicated, may hold values from -3 to 3
- norm2_gain: bfloat16 [768], replicated, may hold values from 0.099609375 to 1.8984375
- norm2_bias: bfloat16 [768], replicated, may hold values from -2 to 2
- cot_words: bfloat16 [16384, 768], P(('dp', 'tensor')), may hold values from -6 to 6
- cot_entities: bfloat16 [4096, 768], P(('dp', 'tensor')), may hold values from -6 to 6
Outputs:
- out_words: bfloat16 [16384, 768], P(('dp', 'tensor'))
- out_entities: bfloat16 [4096, 768], P(('dp', 'tensor'))
- grad_words: float32 [16384, 768], P(('dp', 'tensor'))
- grad_entities: float32 [4096, 768], P(('dp', 'tensor'))
- grad_pos: float32 [512, 768], replicated
- grad_query_w: float32 [4, 768, 768], P(None, None, 'tensor')
- grad_query_b: float32 [4, 768], P(None, 'tensor')
- grad_key_w: float32 [768, 768], P(None, 'tensor')
- grad_value_w: float32 [768, 768], P(None, 'tensor')
- grad_value_b: float32 [768], P('tensor')
- grad_out_w: float32 [768, 768], P('tensor')
- grad_out_b: float32 [768], replicated
- grad_norm1_gain: float32 [768], replicated
- grad_norm1_bias: float32 [768], replicated
- grad_up_w: float32 [768, 3072], P(None, 'tensor')
- grad_up_b: float32 [3072], P('tensor')
- grad_down_w: float32 [3072, 768], P('tensor')
- grad_down_b: float32 [768], replicated
- grad_norm2_gain: float32 [768], replicated
- grad_norm2_bias: float32 [768], replicated
Inputs may be any that keep to these rules, and one draw needn't show every extreme that they name: entity_spans[s, e] = (start, end): entity e of sequence s covers words start to end - 1, 1 to 30 words; in every sequence entity 0 covers words 0 to 29 and entity 1 ends at the last word.
All inputs are finite; a program needn't handle non-finite values. No bound on the sum of `word_mask` or of `entity_mask` on one device may be relied on, other than what follows from the above.
Results may differ from a plain program's by a relative error of at most 0.015.
The roundings to bfloat16 on the way count: a program that leaves them out, or rounds other values in their place, can miss the bound.
Values may be sent and summed in bfloat16 or wider, within the bound.
No kernel may reach another device: no remote copies, remote signals or barrier semaphores. Data moves between devices by JAX's collectives and lax.ppermute only.
A program may use at most 128 MiB of HBM per device.

v0:
```python
from functools import partial

import jax
import jax.numpy as jnp
from jax import lax
from jax.sharding import PartitionSpec as P

HEAD_DIM = 64


norm_epsilon = 1e-12
highest = lax.Precision.HIGHEST


def exact_gelu(values):
    return jax.nn.gelu(values, approximate=False)


def span_weights(entity_spans, word_count):
    word_pos = lax.broadcasted_iota(
        jnp.int32, (entity_spans.shape[0], entity_spans.shape[1], word_count), 2
    )
    span_start = entity_spans[:, :, 0:1]
    span_end = entity_spans[:, :, 1:2]
    inside = jnp.logical_and(word_pos >= span_start, word_pos < span_end)
    return jnp.where(inside, 1.0, 0.0).astype(jnp.float32) / (span_end - span_start).astype(
        jnp.float32
    )


def norm_forward(values, gain_row, shift_row):
    row_mean = jnp.mean(values, axis=-1, keepdims=True)
    centered = values - row_mean
    row_var = jnp.mean(centered * centered, axis=-1, keepdims=True)
    inv_std = lax.rsqrt(row_var + norm_epsilon)
    scaled = centered * inv_std
    return (scaled * gain_row + shift_row, scaled, inv_std)


def norm_backward(grad_in, scaled, inv_std, gain_row):
    grad_gain = jnp.sum(grad_in * scaled, axis=0)
    grad_shift = jnp.sum(grad_in, axis=0)
    grad_scaled = grad_in * gain_row
    mean_first = jnp.mean(grad_scaled, axis=-1, keepdims=True)
    mean_second = jnp.mean(grad_scaled * scaled, axis=-1, keepdims=True)
    return (inv_std * (grad_scaled - mean_first - scaled * mean_second), grad_gain, grad_shift)


def seq_scores(query_words, query_ents, key_rows, word_count, scale_value):
    score_words = jnp.einsum(
        "qhd,khd->hqk", query_words, key_rows[:word_count], preferred_element_type=jnp.float32
    )
    score_ents = jnp.einsum(
        "qhd,khd->hqk", query_ents, key_rows[word_count:], preferred_element_type=jnp.float32
    )
    return jnp.concatenate([score_words, score_ents], axis=2) * scale_value


def attend_forward(seq_block, word_count, scale_value):
    query_words, query_ents, key_rows, value_rows = seq_block
    scores = seq_scores(query_words, query_ents, key_rows, word_count, scale_value)
    row_max = jnp.max(scores, axis=2, keepdims=True)
    exp_scores = jnp.exp(scores - row_max)
    row_total = jnp.sum(exp_scores, axis=2, keepdims=True)
    probs_low = (exp_scores / row_total).astype(jnp.bfloat16)
    context = jnp.einsum("hqk,khd->qhd", probs_low, value_rows, preferred_element_type=jnp.float32)
    return (context.astype(jnp.bfloat16), row_max + jnp.log(row_total))


def attend_backward(seq_block, word_count, scale_value):
    query_words, query_ents, key_rows, value_rows, log_total, grad_context = seq_block
    scores = seq_scores(query_words, query_ents, key_rows, word_count, scale_value)
    probs = jnp.exp(scores - log_total)
    probs_low = probs.astype(jnp.bfloat16)
    grad_probs = jnp.einsum(
        "qhd,khd->hqk", grad_context, value_rows, preferred_element_type=jnp.float32
    )
    grad_values = jnp.einsum(
        "hqk,qhd->khd", probs_low, grad_context, preferred_element_type=jnp.float32
    )
    row_dot = jnp.sum(grad_probs * probs, axis=2, keepdims=True)
    grad_scores = (probs * (grad_probs - row_dot)).astype(jnp.bfloat16)
    grad_on_words = grad_scores[:, :, :word_count]
    grad_on_ents = grad_scores[:, :, word_count:]
    grad_qwords = (
        jnp.einsum(
            "hqk,khd->qhd", grad_on_words, key_rows[:word_count], preferred_element_type=jnp.float32
        )
        * scale_value
    )
    grad_qents = (
        jnp.einsum(
            "hqk,khd->qhd", grad_on_ents, key_rows[word_count:], preferred_element_type=jnp.float32
        )
        * scale_value
    )
    grad_kwords = (
        jnp.einsum("hqk,qhd->khd", grad_on_words, query_words, preferred_element_type=jnp.float32)
        * scale_value
    )
    grad_kents = (
        jnp.einsum("hqk,qhd->khd", grad_on_ents, query_ents, preferred_element_type=jnp.float32)
        * scale_value
    )
    grad_keys = jnp.concatenate([grad_kwords, grad_kents], axis=0)
    return (
        grad_qwords.astype(jnp.bfloat16),
        grad_qents.astype(jnp.bfloat16),
        grad_keys.astype(jnp.bfloat16),
        grad_values.astype(jnp.bfloat16),
    )


def project_rows(rows_low, weight, bias_row):
    return (
        jnp.dot(rows_low, weight, preferred_element_type=jnp.float32) + bias_row.astype(jnp.float32)
    ).astype(jnp.bfloat16)


def rows_times(rows_low, grad_low):
    return jnp.einsum("rd,rh->dh", rows_low, grad_low, preferred_element_type=jnp.float32)


def grad_back(grad_low, weight):
    return jnp.einsum("rh,dh->rd", grad_low, weight, preferred_element_type=jnp.float32)


def column_sum(grad_low):
    return jnp.sum(grad_low.astype(jnp.float32), axis=0)


def shards(
    word_in,
    entity_in,
    entity_spans,
    word_mask,
    entity_mask,
    pos_table,
    query_w,
    query_b,
    key_w,
    value_w,
    value_b,
    out_w,
    out_b,
    norm1_gain,
    norm1_bias,
    up_w,
    up_b,
    down_w,
    down_b,
    norm2_gain,
    norm2_bias,
    cot_words,
    cot_entities,
):
    seq_count = entity_spans.shape[0]
    ent_count = entity_spans.shape[1]
    word_count = word_mask.shape[1]
    width = word_in.shape[1]
    local_width = key_w.shape[1]
    head_count = local_width // HEAD_DIM
    scale_value = HEAD_DIM ** (-0.5)
    tensor_count = lax.axis_size("tensor")
    tensor_index = lax.axis_index("tensor")
    word_total = seq_count * word_count
    ent_total = seq_count * ent_count
    word_share = word_total // tensor_count
    ent_share = ent_total // tensor_count
    member = span_weights(entity_spans, word_count)
    pos_mean = jnp.einsum("sel,ld->sed", member, pos_table.astype(jnp.float32), precision=highest)
    ent_rows = entity_in.astype(jnp.float32) + pos_mean.reshape(ent_total, width)
    ent_low = ent_rows.astype(jnp.bfloat16)
    qw_words = project_rows(word_in, query_w[0], query_b[0])
    qe_words = project_rows(word_in, query_w[1], query_b[1])
    qw_ents = project_rows(ent_low, query_w[2], query_b[2])
    qe_ents = project_rows(ent_low, query_w[3], query_b[3])
    key_words = jnp.dot(word_in, key_w, preferred_element_type=jnp.float32).astype(jnp.bfloat16)
    key_ents = jnp.dot(ent_low, key_w, preferred_element_type=jnp.float32).astype(jnp.bfloat16)
    val_words = project_rows(word_in, value_w, value_b)
    val_ents = project_rows(ent_low, value_w, value_b)

    def by_sequence(word_part, ent_part):
        return jnp.concatenate(
            [
                word_part.reshape(seq_count, word_count, head_count, HEAD_DIM),
                ent_part.reshape(seq_count, ent_count, head_count, HEAD_DIM),
            ],
            axis=1,
        )

    def split_rows(seq_array):
        return (
            seq_array[:, :word_count].reshape(word_total, local_width),
            seq_array[:, word_count:].reshape(ent_total, local_width),
        )

    query_wordkeys = by_sequence(qw_words, qw_ents)
    query_entkeys = by_sequence(qe_words, qe_ents)
    key_seq = by_sequence(key_words, key_ents)
    value_seq = by_sequence(val_words, val_ents)
    context_seq, log_totals = lax.map(
        partial(attend_forward, word_count=word_count, scale_value=scale_value),
        (query_wordkeys, query_entkeys, key_seq, value_seq),
    )
    ctx_words, ctx_ents = split_rows(context_seq)
    attn_words = jnp.dot(ctx_words, out_w, preferred_element_type=jnp.float32)
    attn_ents = jnp.dot(ctx_ents, out_w, preferred_element_type=jnp.float32)
    attn_words, attn_ents = (
        lax.psum_scatter(attn_words, "tensor", scatter_dimension=0, tiled=True),
        lax.psum_scatter(attn_ents, "tensor", scatter_dimension=0, tiled=True),
    )
    word_resid = lax.dynamic_slice_in_dim(word_in, tensor_index * word_share, word_share, 0).astype(
        jnp.float32
    )
    ent_resid = lax.dynamic_slice_in_dim(ent_rows, tensor_index * ent_share, ent_share, 0)
    attended = jnp.concatenate([word_resid + attn_words, ent_resid + attn_ents], 0) + out_b.astype(
        jnp.float32
    )
    gain_one = norm1_gain.astype(jnp.float32)
    normed, scaled_one, inv_one = norm_forward(attended, gain_one, norm1_bias.astype(jnp.float32))
    normed_low = normed.astype(jnp.bfloat16)
    full_words, full_ents = (
        lax.all_gather(normed_low[:word_share], "tensor", axis=0, tiled=True),
        lax.all_gather(normed_low[word_share:], "tensor", axis=0, tiled=True),
    )
    ffn_input = jnp.concatenate([full_words, full_ents], 0)
    up_full, up_bias, down_full = (up_w, up_b, down_w)
    hidden_pre = jnp.dot(ffn_input, up_full, preferred_element_type=jnp.float32) + up_bias.astype(
        jnp.float32
    )
    activ_low = exact_gelu(hidden_pre).astype(jnp.bfloat16)
    ffn_out = jnp.dot(activ_low, down_full, preferred_element_type=jnp.float32)
    ffn_words, ffn_ents = (
        lax.psum_scatter(ffn_out[:word_total], "tensor", scatter_dimension=0, tiled=True),
        lax.psum_scatter(ffn_out[word_total:], "tensor", scatter_dimension=0, tiled=True),
    )
    ffn_share = jnp.concatenate([ffn_words, ffn_ents], 0)
    mixed_rows = normed + ffn_share + down_b.astype(jnp.float32)
    gain_two = norm2_gain.astype(jnp.float32)
    output, scaled_two, inv_two = norm_forward(mixed_rows, gain_two, norm2_bias.astype(jnp.float32))
    out_low = output.astype(jnp.bfloat16)
    mask_words = lax.dynamic_slice_in_dim(
        word_mask.reshape(word_total), tensor_index * word_share, word_share, 0
    )
    mask_ents = lax.dynamic_slice_in_dim(
        entity_mask.reshape(ent_total), tensor_index * ent_share, ent_share, 0
    )
    row_mask = jnp.concatenate([mask_words, mask_ents], 0).astype(jnp.float32)[:, None]
    grad_output = row_mask * jnp.concatenate([cot_words, cot_entities], 0).astype(jnp.float32)
    grad_mixed, grad_gain_two, grad_bias_two = norm_backward(
        grad_output, scaled_two, inv_two, gain_two
    )
    grad_down_b = jnp.sum(grad_mixed, axis=0)
    mixed_low = grad_mixed.astype(jnp.bfloat16)
    back_words, back_ents = (
        lax.all_gather(mixed_low[:word_share], "tensor", axis=0, tiled=True),
        lax.all_gather(mixed_low[word_share:], "tensor", axis=0, tiled=True),
    )
    back_rows = jnp.concatenate([back_words, back_ents], 0)
    grad_activ = jnp.einsum("rd,fd->rf", back_rows, down_full, preferred_element_type=jnp.float32)
    unused_value, gelu_back = jax.vjp(exact_gelu, hidden_pre)
    pre_low = gelu_back(grad_activ)[0].astype(jnp.bfloat16)
    grad_down_w = jnp.einsum("rf,rd->fd", activ_low, back_rows, preferred_element_type=jnp.float32)
    grad_up_w = rows_times(ffn_input, pre_low)
    grad_up_b = column_sum(pre_low)
    normed_part = grad_back(pre_low, up_full)
    part_words, part_ents = (
        lax.psum_scatter(normed_part[:word_total], "tensor", scatter_dimension=0, tiled=True),
        lax.psum_scatter(normed_part[word_total:], "tensor", scatter_dimension=0, tiled=True),
    )
    grad_normed = grad_mixed + jnp.concatenate([part_words, part_ents], 0)
    grad_attended, grad_gain_one, grad_bias_one = norm_backward(
        grad_normed, scaled_one, inv_one, gain_one
    )
    grad_out_b = jnp.sum(grad_attended, axis=0)
    attended_low = grad_attended.astype(jnp.bfloat16)
    upper_words, upper_ents = (
        lax.all_gather(attended_low[:word_share], "tensor", axis=0, tiled=True),
        lax.all_gather(attended_low[word_share:], "tensor", axis=0, tiled=True),
    )
    grad_out_w = jnp.einsum(
        "rh,rd->hd", ctx_words, upper_words, preferred_element_type=jnp.float32
    ) + jnp.einsum("rh,rd->hd", ctx_ents, upper_ents, preferred_element_type=jnp.float32)
    grad_ctx_words = grad_back(upper_words, out_w).astype(jnp.bfloat16)
    grad_ctx_ents = grad_back(upper_ents, out_w).astype(jnp.bfloat16)
    grad_ctx_seq = by_sequence(grad_ctx_words, grad_ctx_ents)
    grad_qw_seq, grad_qe_seq, grad_key_seq, grad_val_seq = lax.map(
        partial(attend_backward, word_count=word_count, scale_value=scale_value),
        (query_wordkeys, query_entkeys, key_seq, value_seq, log_totals, grad_ctx_seq),
    )
    gqw_words, gqw_ents = split_rows(grad_qw_seq)
    gqe_words, gqe_ents = split_rows(grad_qe_seq)
    gkey_words, gkey_ents = split_rows(grad_key_seq)
    gval_words, gval_ents = split_rows(grad_val_seq)
    grad_query_w = jnp.stack(
        [
            rows_times(word_in, gqw_words),
            rows_times(word_in, gqe_words),
            rows_times(ent_low, gqw_ents),
            rows_times(ent_low, gqe_ents),
        ]
    )
    grad_query_b = jnp.stack(
        [column_sum(gqw_words), column_sum(gqe_words), column_sum(gqw_ents), column_sum(gqe_ents)]
    )
    grad_key_w = rows_times(word_in, gkey_words) + rows_times(ent_low, gkey_ents)
    grad_value_w = rows_times(word_in, gval_words) + rows_times(ent_low, gval_ents)
    grad_value_b = column_sum(gval_words) + column_sum(gval_ents)
    input_words = (
        grad_back(gqw_words, query_w[0])
        + grad_back(gqe_words, query_w[1])
        + grad_back(gkey_words, key_w)
        + grad_back(gval_words, value_w)
    )
    input_ents = (
        grad_back(gqw_ents, query_w[2])
        + grad_back(gqe_ents, query_w[3])
        + grad_back(gkey_ents, key_w)
        + grad_back(gval_ents, value_w)
    )
    input_words, input_ents = (
        lax.psum_scatter(input_words, "tensor", scatter_dimension=0, tiled=True),
        lax.psum_scatter(input_ents, "tensor", scatter_dimension=0, tiled=True),
    )
    grad_words = input_words + grad_attended[:word_share]
    grad_ents = input_ents + grad_attended[word_share:]
    member_share = lax.dynamic_slice_in_dim(
        member.reshape(ent_total, word_count), tensor_index * ent_share, ent_share, 0
    )
    grad_pos = jnp.einsum("el,ed->ld", member_share, grad_ents, precision=highest)
    shared_sums = lax.psum(
        (
            grad_gain_one,
            grad_bias_one,
            grad_out_b,
            grad_gain_two,
            grad_bias_two,
            grad_down_b,
            grad_pos,
        ),
        ("dp", "tensor"),
    )
    summed_every = lax.psum(
        (
            grad_query_w,
            grad_query_b,
            grad_key_w,
            grad_value_w,
            grad_value_b,
            grad_out_w,
            grad_up_w,
            grad_up_b,
            grad_down_w,
        ),
        "dp",
    )
    summed_attn = summed_every[:6]
    summed_ffn = summed_every[6:]
    return (
        out_low[:word_share],
        out_low[word_share:],
        grad_words,
        grad_ents,
        shared_sums[6],
        summed_attn[0],
        summed_attn[1],
        summed_attn[2],
        summed_attn[3],
        summed_attn[4],
        summed_attn[5],
        shared_sums[2],
        shared_sums[0],
        shared_sums[1],
        summed_ffn[0],
        summed_ffn[1],
        summed_ffn[2],
        shared_sums[5],
        shared_sums[3],
        shared_sums[4],
    )


def solution(mesh):
    placed = (
        P("dp", None),
        P("dp", None),
        P("dp", None, None),
        P("dp", None),
        P("dp", None),
        P(),
        P(None, None, "tensor"),
        P(None, "tensor"),
        P(None, "tensor"),
        P(None, "tensor"),
        P("tensor"),
        P("tensor", None),
        P(),
        P(),
        P(),
        P(None, "tensor"),
        P("tensor"),
        P("tensor", None),
        P(),
        P(),
        P(),
        P(("dp", "tensor"), None),
        P(("dp", "tensor"), None),
    )
    return jax.shard_map(
        shards,
        mesh=mesh,
        in_specs=placed,
        out_specs=(
            P(("dp", "tensor"), None),
            P(("dp", "tensor"), None),
            P(("dp", "tensor"), None),
            P(("dp", "tensor"), None),
            P(),
            P(None, None, "tensor"),
            P(None, "tensor"),
            P(None, "tensor"),
            P(None, "tensor"),
            P("tensor"),
            P("tensor", None),
            P(),
            P(),
            P(),
            P(None, "tensor"),
            P("tensor"),
            P("tensor", None),
            P(),
            P(),
            P(),
        ),
        check_vma=False,
    )
```

profile of v0, /device:TPU:0, one launch (start us, length us, event | category | flops | bytes accessed | tf_op | source)
XLA Modules:
  0.0 1383.1 jit_solution(4448809317073947691)
XLA Ops:
  8.8 2.8 fusion.135
  22.9 3.9 fusion.125
  26.8 3.1 reshape.253
  31.3 3.0 reshape.250
  39.3 4.0 fusion.126
  46.6 3.0 reshape.255
  54.5 43.1 %while.28 = (s32[]{:T(128)}, bf16[4,640,3,64]{1,3,2,0:T(8,128)(2,1)}, f32[4,3,640,1]{2,1,3,0:T(4,128)}, bf16[4,640,3,64]{1,3,2,0:T(8,128)(2,1)}, bf16[4,640,3,64...) while((s32[]{:T(128)}, ...), condition=%wide.region_3.4_spmd, body=%wide.region_0.3_spmd.sunk | while | flops 329439360 | bytes 36685968 | solution.py:202
  62.5 2.8 fusion.310
  73.3 2.8 fusion.310
  104.5 3.7 fusion.210
  108.9 30.7 %reduce-scatter.11.cloned.1.call-done = f32[128,768]{1,0:T(8,128)} async-done(((f32[512,768]{1,0:T(8,128)}), f32[128,768]{1,0:T(8,128)}) %reduce-scatter.11.cloned.1.call-update) | async-done | bytes 393232 | tf_op jit(solution)/shard_map/reduce_scatter | solution.py:211
  140.7 110.8 %reduce-scatter.9.cloned.1.call-done = f32[512,768]{1,0:T(8,128)} async-done(((f32[2048,768]{1,0:T(8,128)}), f32[512,768]{1,0:T(8,128)}) %reduce-scatter.9.cloned.1.call-update) | async-done | bytes 1572880 | tf_op jit(solution)/shard_map/reduce_scatter | solution.py:210
  257.2 25.2 %all_gather.19 = bf16[512,768]{1,0:T(8,128)(2,1)} all-gather(bf16[128,768]{1,0:T(8,128)(2,1)S(1)} %slice.175), channel_id=1, replica_groups=mesh['dp'=8,'tensor'=4] {'tensor'}, dimensions={0}, use_global_device_ids=true | all-gather | bytes 983040 | tf_op jit(solution)/shard_map/all_gather | solution.py:225
  282.4 43.7 %all-gather.4.cloned.1.call-done = bf16[2048,768]{1,0:T(8,128)(2,1)} async-done(((bf16[512,768]{1,0:T(8,128)(2,1)}), bf16[2048,768]{1,0:T(8,128)(2,1)}) %all-gather.4.cloned.1.call-update) | async-done | bytes 3145744 | tf_op jit(solution)/shard_map/all_gather | solution.py:224
  328.4 22.7 %multiply_convert_fusion.1 = (bf16[2560,768]{1,0:T(8,128)(2,1)S(1)}, f32[2560,768]{1,0:T(8,128)}, f32[2560,768]{1,0:T(8,128)}) fusion(f32[768]{0:T(1024)S(1)} %convert_element_type.189, bf16[2560,768]{1,0:T(8,128)(2,1)S(1)} %constant_dynamic-update-slice_fusion, bf16[768,768]{1,0:T(8,128)(2,1)S(1)} %copy-done), kind=kOutput, calls=%fused_computation.100 | convolution fusion | flops 3149660160 | bytes 24775680 | tf_op jit(solution)/shard_map/dot_general | solution.py:229
  351.1 3.3 fusion.211
  354.4 3.1 copy-done.23
  358.8 5.8 slice.176
  366.1 27.7 %reduce-scatter.15.cloned.1.call-done = f32[128,768]{1,0:T(8,128)} async-done(((f32[512,768]{1,0:T(8,128)}), f32[128,768]{1,0:T(8,128)}) %reduce-scatter.15.cloned.1.call-update) | async-done | bytes 393232 | tf_op jit(solution)/shard_map/reduce_scatter | solution.py:236
  393.9 111.8 %reduce-scatter.13.cloned.1.call-done = f32[512,768]{1,0:T(8,128)} async-done(((f32[2048,768]{1,0:T(8,128)}), f32[512,768]{1,0:T(8,128)}) %reduce-scatter.13.cloned.1.call-update) | async-done | bytes 1572880 | tf_op jit(solution)/shard_map/reduce_scatter | solution.py:235
  517.0 25.3 %all_gather.21 = bf16[512,768]{1,0:T(8,128)(2,1)} all-gather(bf16[128,768]{1,0:T(8,128)(2,1)S(1)} %slice.181), channel_id=1, replica_groups=mesh['dp'=8,'tensor'=4] {'tensor'}, dimensions={0}, use_global_device_ids=true | all-gather | bytes 983040 | tf_op jit(solution)/shard_map/all_gather | solution.py:258
  542.3 43.6 %all-gather.6.cloned.1.call-done = bf16[2048,768]{1,0:T(8,128)(2,1)} async-done(((bf16[512,768]{1,0:T(8,128)(2,1)}), bf16[2048,768]{1,0:T(8,128)(2,1)}) %all-gather.6.cloned.1.call-update) | async-done | bytes 3145744 | tf_op jit(solution)/shard_map/all_gather | solution.py:257
  588.3 10.2 convert_reduce_fusion
  598.6 3.3 fusion.212
  601.9 3.1 copy-done.24
  606.3 5.8 slice.182
  612.2 29.2 %reduce-scatter.19.cloned.1.call-done = f32[128,768]{1,0:T(8,128)} async-done(((f32[512,768]{1,0:T(8,128)}), f32[128,768]{1,0:T(8,128)}) %reduce-scatter.19.cloned.1.call-update) | async-done | bytes 393232 | tf_op jit(solution)/shard_map/reduce_scatter | solution.py:270
  641.4 112.0 %reduce-scatter.17.cloned.1.call-done = f32[512,768]{1,0:T(8,128)} async-done(((f32[2048,768]{1,0:T(8,128)}), f32[512,768]{1,0:T(8,128)}) %reduce-scatter.17.cloned.1.call-update) | async-done | bytes 1572880 | tf_op jit(solution)/shard_map/reduce_scatter | solution.py:269
  753.3 3.2 multiply_reduce_fusion.2
  760.0 24.2 %all_gather.23 = bf16[512,768]{1,0:T(8,128)(2,1)S(1)} all-gather(bf16[128,768]{1,0:T(8,128)(2,1)S(1)} %slice.185), channel_id=1, replica_groups=mesh['dp'=8,'tensor'=4] {'tensor'}, dimensions={0}, use_global_device_ids=true | all-gather | bytes 983040 | tf_op jit(solution)/shard_map/all_gather | solution.py:280
  784.7 44.1 %all-gather.8.cloned.1.call-done = bf16[2048,768]{1,0:T(8,128)(2,1)} async-done(((bf16[512,768]{1,0:T(8,128)(2,1)}), bf16[2048,768]{1,0:T(8,128)(2,1)}) %all-gather.8.cloned.1.call-update) | async-done | bytes 3145744 | tf_op jit(solution)/shard_map/all_gather | solution.py:279
  828.7 3.0 convolution_convert_fusion
  837.9 96.6 %while.29 = (s32[]{:T(128)}, bf16[4,640,3,64]{1,3,2,0:T(8,128)(2,1)}, bf16[4,640,3,64]{1,3,2,0:T(8,128)(2,1)}, bf16[4,640,3,64]{1,3,2,0:T(8,128)(2,1)}, bf16[4,6...) while((s32[]{:T(128)}, ...), condition=%wide.region_20.21_spmd, body=%wide.region_18.20_spmd.sunk | while | flops 962275840 | bytes 46992568 | solution.py:288
  842.6 7.4 multiply_convert_fusion.3
  866.7 7.5 multiply_convert_fusion.3
  890.9 7.5 multiply_convert_fusion.3
  915.1 7.4 multiply_convert_fusion.3
  950.6 3.9 add_add_fusion
  958.7 8.2 fusion.216
  966.9 4.8 fusion.215
  985.4 3.4 pad_maximum_fusion
  988.8 2.9 convolution_bitcast_fusion.1
  996.7 49.9 %all-reduce = (f32[768]{0:T(1024)}, f32[768]{0:T(1024)}, f32[768]{0:T(1024)}, f32[768]{0:T(1024)}, f32[768]{0:T(1024)}, /*index=5*/f32[768]{0:T(1024)}) all-reduce(f32[768]{0:T(1024)S(1)} %get-tuple-element.185, f32[768]{0:T(1024)S(1)} %get-tuple-element.124, ...), channel_id=1, replica_groups=mesh['dp'=8,'tensor'=4] {'dp','tensor'}, use_global_device_ids=true, to_apply=%region_37.38 | all-reduce | flops 4608 | bytes 36864 | tf_op jit(solution)/shard_map/psum | solution.py:332
  1052.1 14.3 %all-reduce.1 = (f32[4,192]{1,0:T(4,128)}, f32[192]{0:T(256)}, f32[768]{0:T(1024)}) all-reduce(f32[4,192]{1,0:T(4,128)S(1)} %pad_maximum_fusion.3, f32[192]{0:T(256)S(1)} %add.306, f32[768]{0:T(1024)S(1)} %get-tuple-element.187), channel_id=1, replica_groups=mesh['dp'=8,'tensor'=4] {'dp'}, use_global_device_ids=true, to_apply=%region_29.30 | all-reduce | flops 1728 | bytes 13824 | tf_op jit(solution)/shard_map/psum | solution.py:344
  1066.4 24.1 %reduce-scatter.21.cloned.1.call-done = f32[512,768]{1,0:T(8,128)} async-done(((f32[2048,768]{1,0:T(8,128)}), f32[512,768]{1,0:T(8,128)}) %reduce-scatter.21.cloned.1.call-update) | async-done | bytes 1572880 | tf_op jit(solution)/shard_map/reduce_scatter | solution.py:323
  1093.3 136.0 %all-reduce.6.cloned.1.call-done = f32[512,768]{1,0:T(8,128)} async-done(((f32[512,768]{1,0:T(8,128)}), f32[512,768]{1,0:T(8,128)}) %all-reduce.6.cloned.1.call-update) | async-done | bytes 1572880 | tf_op jit(solution)/shard_map/psum | solution.py:332
  1229.3 137.3 %all-reduce.8.cloned.1.call-done = (f32[4,768,192]{1,2,0:T(8,128)}, f32[768,192]{0,1:T(8,128)}, f32[768,192]{0,1:T(8,128)}, f32[192,768]{1,0:T(8,128)}, f32[768,768]{1,0:T(8,128)}, /*index=5*/f32[768,768]{1,0:T(8,128)}) async-done(((f32[4,768,192]{1,2,0:T(8,128)}, f32[768,192]{0,1:T(8,128)}, f32[768,192]{0,1:T(8,128)}, f32[192,768]{1,0:T(8,128)}, f32[768,768]{1,0:T(8,128)}, ...) | async-done | bytes 8847376 | tf_op jit(solution)/shard_map/psum | solution.py:344
  1366.6 2.8 copy.193
  (414 shorter events, 229.0 us)
Async XLA Ops:
  7.2 321.2 %copy-start = (bf16[768,768]{1,0:T(8,128)(2,1)S(1)}, bf16[768,768]{1,0:T(8,128)(2,1)}, u32[]{:S(2)}) copy-start(bf16[768,768]{1,0:T(8,128)(2,1)} %param.42) | copy-start | bytes 3538948
  7.2 4.4 copy-start.59
  7.2 132.3 %reduce-scatter.11.cloned.1.call-start = ((), (), s32[]{:S(2)}) async-start(), calls=%async_computation.9 | async-start | bytes 1966080 | tf_op jit(solution)/shard_map/reduce_scatter | solution.py:211
  13.0 23.4 %copy-start.6 = (bf16[512,768]{1,0:T(8,128)(2,1)}, bf16[512,768]{1,0:T(8,128)(2,1)S(1)}, u32[]{:S(2)}) copy-start(bf16[512,768]{1,0:T(8,128)(2,1)S(1)} %get-tuple-element.194) | copy-start | bytes 2359300
  43.2 7.6 copy-start.60
  54.5 45.2 %copy-start.34 = (bf16[192,768]{1,0:T(8,128)(2,1)S(1)}, bf16[192,768]{1,0:T(8,128)(2,1)}, u32[]{:S(2)}) copy-start(bf16[192,768]{1,0:T(8,128)(2,1)} %param.38) | copy-start | bytes 884740
  57.1 3.9 copy-start.2
  67.9 3.9 copy-start.2
  78.7 3.9 copy-start.2
  89.5 3.9 copy-start.2
  97.7 5.7 copy-start.11
  97.7 5.7 copy-start.13
  101.3 150.3 %reduce-scatter.9.cloned.1.call-start = ((), (), s32[]{:S(2)}) async-start(), calls=%async_computation.8 | async-start | bytes 7864320 | tf_op jit(solution)/shard_map/reduce_scatter | solution.py:210
  108.2 217.9 %all-gather.4.cloned.1.call-start = ((), (), s32[]{:S(2)}) async-start(), calls=%async_computation.10 | async-start | bytes 3932160 | tf_op jit(solution)/shard_map/all_gather | solution.py:224
  256.2 137.6 %reduce-scatter.15.cloned.1.call-start = ((), (), s32[]{:S(2)}) async-start(), calls=%async_computation.12 | async-start | bytes 1966080 | tf_op jit(solution)/shard_map/reduce_scatter | solution.py:236
  328.4 22.7 %copy-start.37 = (bf16[2560,768]{1,0:T(8,128)(2,1)}, bf16[2560,768]{1,0:T(8,128)(2,1)S(1)}, u32[]{:S(2)}) copy-start(bf16[2560,768]{1,0:T(8,128)(2,1)S(1)} %constant_dynamic-update-slice_fusion) | copy-start | bytes 11796484
  328.4 22.7 %copy-start.82 = (bf16[768,768]{1,0:T(8,128)(2,1)S(1)}, bf16[768,768]{1,0:T(8,128)(2,1)}, u32[]{:S(2)}) copy-start(bf16[768,768]{1,0:T(8,128)(2,1)} %param.44) | copy-start | bytes 3538948
  358.8 146.9 %reduce-scatter.13.cloned.1.call-start = ((), (), s32[]{:S(2)}) async-start(), calls=%async_computation.11 | async-start | bytes 7864320 | tf_op jit(solution)/shard_map/reduce_scatter | solution.py:235
  364.6 221.2 %all-gather.6.cloned.1.call-start = ((), (), s32[]{:S(2)}) async-start(), calls=%async_computation.13 | async-start | bytes 3932160 | tf_op jit(solution)/shard_map/all_gather | solution.py:257
  516.0 125.3 %reduce-scatter.19.cloned.1.call-start = ((), (), s32[]{:S(2)}) async-start(), calls=%async_computation.15 | async-start | bytes 1966080 | tf_op jit(solution)/shard_map/reduce_scatter | solution.py:270
  588.2 10.4 copy-start.39
  606.2 147.1 %reduce-scatter.17.cloned.1.call-start = ((), (), s32[]{:S(2)}) async-start(), calls=%async_computation.14 | async-start | bytes 7864320 | tf_op jit(solution)/shard_map/reduce_scatter | solution.py:269
  612.1 216.6 %all-gather.8.cloned.1.call-start = ((), (), s32[]{:S(2)}) async-start(), calls=%async_computation.16 | async-start | bytes 3932160 | tf_op jit(solution)/shard_map/all_gather | solution.py:279
  759.9 221.3 %reduce-scatter.23.cloned.1.call-start = ((), (), s32[]{:S(2)}) async-start(), calls=%async_computation.18 | async-start | bytes 1966080 | tf_op jit(solution)/shard_map/reduce_scatter | solution.py:324
  784.2 47.6 %copy-start.25 = (bf16[512,768]{1,0:T(8,128)(2,1)}, bf16[512,768]{1,0:T(8,128)(2,1)S(1)}, u32[]{:S(2)}) copy-start(bf16[512,768]{1,0:T(8,128)(2,1)S(1)} %all_gather.23) | copy-start | bytes 2359300
  832.5 5.4 copy-start.12
  832.5 5.4 copy-start.14
  850.1 9.3 copy-start.3
  874.2 9.3 copy-start.3
  898.4 9.3 copy-start.3
  922.5 9.3 copy-start.3
  934.5 4.7 copy-start.53
  942.1 148.4 %reduce-scatter.21.cloned.1.call-start = ((), (), s32[]{:S(2)}) async-start(), calls=%async_computation.17 | async-start | bytes 7864320 | tf_op jit(solution)/shard_map/reduce_scatter | solution.py:323
  954.6 274.7 %all-reduce.6.cloned.1.call-start = ((), (), s32[]{:S(2)}) async-start(), calls=%async_computation.19 | async-start | bytes 3145728 | tf_op jit(solution)/shard_map/psum | solution.py:332
  958.7 8.2 copy-start.38
  958.7 8.2 copy-start.86
  966.8 4.9 copy-start.7
  966.9 4.9 copy-start.48
  966.9 6.0 copy-start.50
  966.9 7.2 copy-start.30
  982.3 6.5 copy-start.51
  985.0 381.5 %all-reduce.8.cloned.1.call-start = ((), (), s32[]{:S(2)}) async-start(), calls=%async_computation.20 | async-start | bytes 17694720 | tf_op jit(solution)/shard_map/psum | solution.py:344
  992.9 3.8 copy-start.64
  992.9 3.8 copy-start.65
  992.9 3.8 copy-start.66
  992.9 56.2 %copy-start.21 = (bf16[4,640,3,64]{1,3,2,0:T(8,128)(2,1)S(1)}, bf16[4,640,3,64]{1,3,2,0:T(8,128)(2,1)}, u32[]{:S(2)}) copy-start(bf16[4,640,3,64]{1,3,2,0:T(8,128)(2,1)} %get-tuple-element.120) | copy-start | bytes 2949124
  1366.6 4.2 copy-start.63
  1369.4 3.9 copy-start.41
  (58 other events, 117.0 us)
Sparse Core Ops, SparseCore 0:
  101.4 38.1 reduce-scatter.10
  141.9 109.6 reduce-scatter.8
  256.3 69.7 all-gather.3
  358.9 34.9 reduce-scatter.14
  396.0 109.6 reduce-scatter.12
  516.1 69.6 all-gather.5
  606.3 34.9 reduce-scatter.18
  643.7 109.6 reduce-scatter.16
  760.0 68.6 all-gather.7
  942.2 35.2 reduce-scatter.22
  979.8 110.6 reduce-scatter.20
  1096.3 132.9 all-reduce.5
  1235.6 130.8 all-reduce.7
where the time goes:
time: 1390 us; the launch traced here: 1380 us
  waiting for transfers between devices  851 us (61%)
  matrix products  224 us (16%)
  blocking collectives  139 us (10%)
  local copies, waits for them, and re-layouts  101 us (7%)
  other arithmetic  50.2 us (4%)
  between operations  15.6 us (1%)
    psum x1, waiting for transfers between devices, shards(): lax.psum((grad_query_w, grad_query_b, grad_key_w, grad_value_w, grad_valu...  137 us
    psum x1, waiting for transfers between devices, shards(): lax.psum((grad_gain_one, grad_bias_one, grad_out_b, grad_gain_two, grad_b...  136 us
    reduce_scatter x1, waiting for transfers between devices, shards(): lax.psum_scatter(normed_part[:word_total], 'tensor', scatter_dimension=0,...  112 us
    reduce_scatter x1, waiting for transfers between devices, shards(): lax.psum_scatter(ffn_out[:word_total], 'tensor', scatter_dimension=0, til...  112 us
    reduce_scatter x1, waiting for transfers between devices, shards(): lax.psum_scatter(attn_words, 'tensor', scatter_dimension=0, tiled=True)  111 us
    psum x1, blocking collectives, shards(): lax.psum((grad_gain_one, grad_bias_one, grad_out_b, grad_gain_two, grad_b...  49.9 us
    all_gather x1, waiting for transfers between devices, shards(): lax.all_gather(attended_low[:word_share], 'tensor', axis=0, tiled=True)  44.1 us
    all_gather x1, waiting for transfers between devices, shards(): lax.all_gather(normed_low[:word_share], 'tensor', axis=0, tiled=True)  43.7 us
  transfers between devices with their start and end apart: 13, of which 12 were waited for; matrix products, arithmetic and copies ran while one was open for 6% of the time, Pallas kernels for 0%

commit v1 on v0

v1 whole, which is shorter than its diff:
```python
from functools import partial

import jax
import jax.numpy as jnp
from jax import lax
from jax.experimental import pallas as pl
from jax.experimental.pallas import tpu as pltpu
from jax.sharding import PartitionSpec as P

HEAD_DIM = 64
norm_epsilon = 1e-12
F32 = jnp.float32
BF16 = jnp.bfloat16
NT = (((1,), (1,)), ((), ()))
TN = (((0,), (0,)), ((), ()))


def mm(a, b):
    return jnp.dot(a, b, preferred_element_type=F32)


def mm_nt(a, b):
    return lax.dot_general(a, b, NT, preferred_element_type=F32)


def mm_tn(a, b):
    return lax.dot_general(a, b, TN, preferred_element_type=F32)


def attn_forward_kernel(
    words, ents, gw, heads, rows_ref, w_ref, b_ref, pw_ref, pe_ref, ctx_ref, lt_ref, qw_s, qe_s, k_s, v_s
):
    half = 2 * gw
    pw_ref[...] = (mm(rows_ref[:words], w_ref[:, : 4 * gw]) + b_ref[:, : 4 * gw]).astype(BF16)
    pe_ref[...] = (mm(rows_ref[words:], w_ref[:, half:]) + b_ref[:, half:]).astype(BF16)
    for h in range(heads):
        o = h * HEAD_DIM
        e = o + HEAD_DIM
        qw_s[h, :words] = pw_ref[:, o:e]
        qw_s[h, words:] = pe_ref[:, half + o : half + e]
        qe_s[h, :words] = pw_ref[:, gw + o : gw + e]
        qe_s[h, words:] = pe_ref[:, half + gw + o : half + gw + e]
        k_s[h, :words] = pw_ref[:, half + o : half + e]
        k_s[h, words:] = pe_ref[:, o:e]
        v_s[h, :words] = pw_ref[:, half + gw + o : half + gw + e]
        v_s[h, words:] = pe_ref[:, gw + o : gw + e]

    scale = HEAD_DIM**-0.5
    block = 128

    def step(qb, carry):
        rows = pl.ds(pl.multiple_of(qb * block, block), block)
        parts = []
        for h in range(heads):
            sw = mm_nt(qw_s[h, rows], k_s[h, :words])
            se = mm_nt(qe_s[h, rows], k_s[h, words:])
            top = jnp.maximum(jnp.max(sw, 1, keepdims=True), jnp.max(se, 1, keepdims=True))
            ew = jnp.exp((sw - top) * scale)
            ee = jnp.exp((se - top) * scale)
            total = jnp.sum(ew, 1, keepdims=True) + jnp.sum(ee, 1, keepdims=True)
            inv = 1.0 / total
            ctx = mm((ew * inv).astype(BF16), v_s[h, :words]) + mm(
                (ee * inv).astype(BF16), v_s[h, words:]
            )
            parts.append(ctx)
            logt = top * scale + jnp.log(total)
            lt_ref[h : h + 1, rows] = jnp.broadcast_to(logt, (block, block)).T[0:1]
        ctx_ref[rows, :] = jnp.concatenate(parts, 1).astype(BF16)
        return carry

    lax.fori_loop(0, rows_ref.shape[0] // block, step, 0)


def attn_forward(rows_low, weight, bias, words, heads):
    total, width = rows_low.shape
    ents = total - words
    gw = heads * HEAD_DIM
    return pl.pallas_call(
        partial(attn_forward_kernel, words, ents, gw, heads),
        out_shape=(
            jax.ShapeDtypeStruct((words, 4 * gw), BF16),
            jax.ShapeDtypeStruct((ents, 4 * gw), BF16),
            jax.ShapeDtypeStruct((total, gw), BF16),
            jax.ShapeDtypeStruct((8, total), F32),
        ),
        scratch_shapes=[pltpu.VMEM((heads, total, HEAD_DIM), BF16) for _ in range(4)],
        compiler_params=pltpu.CompilerParams(vmem_limit_bytes=24 << 20),
        cost_estimate=pl.CostEstimate(
            flops=2 * total * width * 4 * gw + 4 * total * total * 256 * heads,
            bytes_accessed=6 << 20,
            transcendentals=heads * total * total,
        ),
    )(rows_low, weight, bias)


def attn_backward_kernel(
    words,
    gw,
    heads,
    rt_ref,
    pw_ref,
    pe_ref,
    lt_ref,
    dctx_ref,
    w_ref,
    acc_ref,
    dw_ref,
    out_ref,
    db_ref,
    qw_s,
    qe_s,
    k_s,
    v_s,
    dc_s,
    p_s,
    ds_s,
    dpw_s,
    dpe_s,
):
    half = 2 * gw
    total = rt_ref.shape[1]
    for h in range(heads):
        o = h * HEAD_DIM
        e = o + HEAD_DIM
        qw_s[h, :words] = pw_ref[:, o:e]
        qw_s[h, words:] = pe_ref[:, half + o : half + e]
        qe_s[h, :words] = pw_ref[:, gw + o : gw + e]
        qe_s[h, words:] = pe_ref[:, half + gw + o : half + gw + e]
        k_s[h, :words] = pw_ref[:, half + o : half + e]
        k_s[h, words:] = pe_ref[:, o:e]
        v_s[h, :words] = pw_ref[:, half + gw + o : half + gw + e]
        v_s[h, words:] = pe_ref[:, gw + o : gw + e]
        dc_s[h] = dctx_ref[:, o:e]
    scale = HEAD_DIM**-0.5
    block = 128
    for h in range(heads):
        o = h * HEAD_DIM
        e = o + HEAD_DIM

        def step(qb, carry):
            rows = pl.ds(pl.multiple_of(qb * block, block), block)
            logt = lt_ref[h : h + 1, rows]
            pw = jnp.exp(mm_nt(k_s[h, :words], qw_s[h, rows]) * scale - logt)
            pe = jnp.exp(mm_nt(k_s[h, words:], qe_s[h, rows]) * scale - logt)
            gw_ = mm_nt(v_s[h, :words], dc_s[h, rows])
            ge_ = mm_nt(v_s[h, words:], dc_s[h, rows])
            p_s[:words, rows] = pw.astype(BF16)
            p_s[words:, rows] = pe.astype(BF16)
            dot = jnp.sum(pw * gw_, 0, keepdims=True) + jnp.sum(pe * ge_, 0, keepdims=True)
            ds_s[:words, rows] = (pw * (gw_ - dot)).astype(BF16)
            ds_s[words:, rows] = (pe * (ge_ - dot)).astype(BF16)
            return carry

        lax.fori_loop(0, total // block, step, 0)
        dv = mm(p_s[...], dc_s[h]).astype(BF16)
        dkw = (mm(ds_s[:words], qw_s[h]) * scale).astype(BF16)
        dke = (mm(ds_s[words:], qe_s[h]) * scale).astype(BF16)
        dqw = (mm_tn(ds_s[:words], k_s[h, :words]) * scale).astype(BF16)
        dqe = (mm_tn(ds_s[words:], k_s[h, words:]) * scale).astype(BF16)
        dpw_s[:, o:e] = dqw[:words]
        dpw_s[:, gw + o : gw + e] = dqe[:words]
        dpw_s[:, half + o : half + e] = dkw
        dpw_s[:, half + gw + o : half + gw + e] = dv[:words]
        dpe_s[:, o:e] = dke
        dpe_s[:, gw + o : gw + e] = dv[words:]
        dpe_s[:, half + o : half + e] = dqw[words:]
        dpe_s[:, half + gw + o : half + gw + e] = dqe[words:]
    dpw = dpw_s[...]
    dpe = dpe_s[...]
    dw_ref[:, :half] = mm(rt_ref[:, :words], dpw[:, :half]).astype(BF16)
    dw_ref[:, half : 2 * half] = (
        mm(rt_ref[:, :words], dpw[:, half:]) + mm(rt_ref[:, words:], dpe[:, :half])
    ).astype(BF16)
    dw_ref[:, 2 * half :] = mm(rt_ref[:, words:], dpe[:, half:]).astype(BF16)
    out_ref[:words] = acc_ref[:words] + mm_nt(dpw, w_ref[:, : 2 * half])
    out_ref[words:] = acc_ref[words:] + mm_nt(dpe, w_ref[:, half:])
    sw = jnp.sum(dpw.astype(F32), 0, keepdims=True)
    se = jnp.sum(dpe.astype(F32), 0, keepdims=True)
    db_ref[0:1, :half] = sw[:, :half]
    db_ref[0:1, half : 2 * half] = sw[:, half:] + se[:, :half]
    db_ref[0:1, 2 * half :] = se[:, half:]


def attn_backward(rows_t, proj_w, proj_e, log_total, grad_ctx, weight, acc, heads):
    width, total = rows_t.shape
    words = proj_w.shape[0]
    ents = total - words
    gw = heads * HEAD_DIM
    return pl.pallas_call(
        partial(attn_backward_kernel, words, gw, heads),
        out_shape=(
            jax.ShapeDtypeStruct((width, 6 * gw), BF16),
            jax.ShapeDtypeStruct((total, width), F32),
            jax.ShapeDtypeStruct((8, 6 * gw), F32),
        ),
        scratch_shapes=[pltpu.VMEM((heads, total, HEAD_DIM), BF16) for _ in range(5)]
        + [
            pltpu.VMEM((total, total), BF16),
            pltpu.VMEM((total, total), BF16),
            pltpu.VMEM((words, 4 * gw), BF16),
            pltpu.VMEM((ents, 4 * gw), BF16),
        ],
        input_output_aliases={6: 1},
        compiler_params=pltpu.CompilerParams(vmem_limit_bytes=40 << 20),
        cost_estimate=pl.CostEstimate(
            flops=4 * total * width * 4 * gw + 10 * total * total * 256 * heads,
            bytes_accessed=12 << 20,
            transcendentals=heads * total * total,
        ),
    )(rows_t, proj_w, proj_e, log_total, grad_ctx, weight, acc)


def norm_forward(values, gain_row, shift_row):
    row_mean = jnp.mean(values, axis=-1, keepdims=True)
    centered = values - row_mean
    row_var = jnp.mean(centered * centered, axis=-1, keepdims=True)
    inv_std = lax.rsqrt(row_var + norm_epsilon)
    scaled = centered * inv_std
    return (scaled * gain_row + shift_row, scaled, inv_std)


def norm_backward(grad_in, scaled, inv_std, gain_row):
    grad_gain = jnp.sum(grad_in * scaled, axis=0)
    grad_shift = jnp.sum(grad_in, axis=0)
    grad_scaled = grad_in * gain_row
    mean_first = jnp.mean(grad_scaled, axis=-1, keepdims=True)
    mean_second = jnp.mean(grad_scaled * scaled, axis=-1, keepdims=True)
    return (inv_std * (grad_scaled - mean_first - scaled * mean_second), grad_gain, grad_shift)


def exact_gelu(values):
    return jax.nn.gelu(values, approximate=False)


class Links:
    def __init__(self):
        self.dp = lax.axis_size("dp")
        self.ring = lax.axis_size("tensor")
        dp_index = lax.axis_index("dp")
        self.z = lax.axis_index("tensor")
        self.core = dp_index % 2
        self.bits = (self.dp // 2).bit_length() - 1
        self.bit = [(dp_index // (2 << k)) % 2 for k in range(self.bits)]

    def next_z(self, v):
        n = self.ring
        return lax.ppermute(v, "tensor", [(i, (i + 1) % n) for i in range(n)])

    def shift_z(self, v, by):
        n = self.ring
        return lax.ppermute(v, "tensor", [(i, (i + by) % n) for i in range(n)])

    def swap_z(self, v, mask):
        return lax.ppermute(v, "tensor", [(i, i ^ mask) for i in range(self.ring)])

    def swap_core(self, v):
        return lax.ppermute(v, "dp", [(i, i ^ 1) for i in range(self.dp)])

    def swap_bit(self, v, k):
        return lax.ppermute(v, "dp", [(i, i ^ (2 << k)) for i in range(self.dp)])


def take_rows(v, start, size):
    return lax.dynamic_slice_in_dim(v, start, size, 0)


def gather_stage(links, own, k):
    quarter = own.shape[0] // 4
    part = 2 * links.core + links.bit[k]
    cur = take_rows(own, part * quarter, quarter)
    groups = []
    for _ in range(links.ring - 1):
        cur = links.next_z(cur)
        other = links.swap_bit(cur, k)
        groups.append((cur, other, links.swap_core(cur), links.swap_core(other)))
    return groups


def assemble(links, pieces, k):
    part = 2 * links.core + links.bit[k]
    quarter = pieces[0].shape[0]
    buf = jnp.zeros((4 * quarter,) + pieces[0].shape[1:], pieces[0].dtype)
    for i, piece in enumerate(pieces):
        buf = lax.dynamic_update_slice_in_dim(buf, piece, (part ^ i) * quarter, 0)
    return buf


def add_low(a, b):
    return (a.astype(F32) + b.astype(F32)).astype(BF16)


def join_rows(mine, other, flag):
    return jnp.where(flag == 0, jnp.concatenate([mine, other], 0), jnp.concatenate([other, mine], 0))


def reduce_group(links, grad, k):
    half = grad.shape[0] // 2
    c = links.core
    kept = add_low(take_rows(grad, c * half, half), links.swap_core(take_rows(grad, (1 - c) * half, half)))
    b = links.bit[k]
    quarter = half // 2
    return add_low(
        take_rows(kept, b * quarter, quarter),
        links.swap_bit(take_rows(kept, (1 - b) * quarter, quarter), k),
    )


def reduce_stage(links, grads, k):
    n = links.ring
    order = list(range(1, n)) + [0]
    acc = None
    for r in order:
        quarter = reduce_group(links, grads[r], k)
        acc = quarter if acc is None else add_low(quarter, links.next_z(acc))
    for j in range(links.bits):
        if j != k:
            acc = add_low(acc, links.swap_bit(acc, j))
    other = links.swap_bit(acc, k)
    return assemble(links, (acc, other, links.swap_core(acc), links.swap_core(other)), k)


def reduce_everywhere(links, v):
    v = v + links.swap_core(v)
    for j in range(links.bits):
        v = v + links.swap_bit(v, j)
    mask = 1
    while mask < links.ring:
        v = v + links.swap_z(v, mask)
        mask *= 2
    return v


def reduce_pos(links, v):
    flags = [(links.core, links.swap_core)] + [
        (links.bit[j], partial(links.swap_bit, k=j)) for j in range(min(2, links.bits))
    ]
    for flag, swap in flags:
        half = v.shape[0] // 2
        v = add_low(take_rows(v, flag * half, half), swap(take_rows(v, (1 - flag) * half, half)))
    for j in range(2, links.bits):
        v = add_low(v, links.swap_bit(v, j))
    mask = 1
    while mask < links.ring:
        v = add_low(v, links.swap_z(v, mask))
        mask *= 2
    for flag, swap in reversed(flags):
        v = join_rows(v, swap(v), flag)
    return v


def shards(
    word_in,
    entity_in,
    entity_spans,
    word_mask,
    entity_mask,
    pos_table,
    query_w,
    query_b,
    key_w,
    value_w,
    value_b,
    out_w,
    out_b,
    norm1_gain,
    norm1_bias,
    up_w,
    up_b,
    down_w,
    down_b,
    norm2_gain,
    norm2_bias,
    cot_words,
    cot_entities,
):
    links = Links()
    n = links.ring
    z = links.z
    words = cot_words.shape[0]
    ents = cot_entities.shape[0]
    width = word_in.shape[1]
    gw = key_w.shape[1]
    heads = gw // HEAD_DIM
    ff = up_w.shape[1]

    qkv_own = jnp.concatenate([query_w[0], query_w[1], key_w, value_w, query_w[2], query_w[3]], 1)
    ffn_own = jnp.concatenate([out_w, up_w, down_w], 0)
    bias_own = jnp.concatenate(
        [query_b[0], query_b[1], jnp.zeros((gw,), BF16), value_b, query_b[2], query_b[3], up_b]
    )[None]
    biases = [bias_own] + [links.shift_z(bias_own, r) for r in range(1, n)]
    qkv_parts = gather_stage(links, qkv_own, 0)
    ffn_start, _ = lax.optimization_barrier((ffn_own, qkv_parts[-1][0]))
    ffn_parts = gather_stage(links, ffn_start, 1)
    qkv = [qkv_own] + [assemble(links, p, 0) for p in qkv_parts]
    ffn = [ffn_own] + [assemble(links, p, 1) for p in ffn_parts]

    words_own = take_rows(word_in, z * words, words)
    ents_own = take_rows(entity_in, z * ents, ents)
    spans = lax.dynamic_index_in_dim(entity_spans, z, 0, keepdims=False)
    position = lax.broadcasted_iota(jnp.int32, (ents, words), 1)
    inside = jnp.logical_and(position >= spans[:, 0:1], position < spans[:, 1:2])
    inside_low = jnp.where(inside, 1.0, 0.0).astype(BF16)
    share = 1.0 / (spans[:, 1:2] - spans[:, 0:1]).astype(F32)
    ent_rows = ents_own.astype(F32) + mm(inside_low, pos_table) * share
    rows_low = jnp.concatenate([words_own, ent_rows.astype(BF16)], 0)
    rows_t = rows_low.T

    saved = []
    for r in range(n):
        saved.append(attn_forward(rows_low, qkv[r], biases[r][:, : 6 * gw].astype(F32), words, heads))

    out_parts = [g[:gw] for g in ffn]
    up_parts = [g[gw : gw + width] for g in ffn]
    down_parts = [g[gw + width :] for g in ffn]
    attn = sum(mm(saved[r][2], out_parts[r]) for r in range(n))
    resid = jnp.concatenate([words_own.astype(F32), ent_rows], 0)
    attended = resid + attn + out_b.astype(F32)
    gain_one = norm1_gain.astype(F32)
    normed, scaled_one, inv_one = norm_forward(attended, gain_one, norm1_bias.astype(F32))
    normed_low = normed.astype(BF16)
    hidden = [mm(normed_low, up_parts[r]) + biases[r][:, 6 * gw :].astype(F32) for r in range(n)]
    activ = [exact_gelu(v).astype(BF16) for v in hidden]
    ffn_out = sum(mm(activ[r], down_parts[r]) for r in range(n))
    mixed = normed + ffn_out + down_b.astype(F32)
    gain_two = norm2_gain.astype(F32)
    output, scaled_two, inv_two = norm_forward(mixed, gain_two, norm2_bias.astype(F32))
    out_low = output.astype(BF16)
    mask_row = jnp.concatenate(
        [
            lax.dynamic_index_in_dim(word_mask, z, 0, keepdims=False),
            lax.dynamic_index_in_dim(entity_mask, z, 0, keepdims=False),
        ]
    ).astype(F32)[:, None]
    grad_output = mask_row * jnp.concatenate([cot_words, cot_entities], 0).astype(F32)
    grad_mixed, grad_gain_two, grad_bias_two = norm_backward(grad_output, scaled_two, inv_two, gain_two)
    grad_down_b = jnp.sum(grad_mixed, axis=0)
    mixed_low = grad_mixed.astype(BF16)
    grad_normed = grad_mixed
    grad_up_b = []
    up_grads = []
    down_grads = []
    for r in range(n):
        grad_activ = mm_nt(mixed_low, down_parts[r])
        _, gelu_back = jax.vjp(exact_gelu, hidden[r])
        pre_low = gelu_back(grad_activ)[0].astype(BF16)
        down_grads.append(mm_tn(activ[r], mixed_low).astype(BF16))
        up_grads.append(mm_tn(normed_low, pre_low).astype(BF16))
        grad_up_b.append(jnp.sum(pre_low.astype(F32), 0))
        grad_normed = grad_normed + mm_nt(pre_low, up_parts[r])
    grad_attended, grad_gain_one, grad_bias_one = norm_backward(grad_normed, scaled_one, inv_one, gain_one)
    grad_out_b = jnp.sum(grad_attended, axis=0)
    attended_low = grad_attended.astype(BF16)
    out_grads = [mm_tn(saved[r][2], attended_low).astype(BF16) for r in range(n)]
    ffn_grads = [jnp.concatenate([out_grads[r], up_grads[r], down_grads[r]], 0) for r in range(n)]
    ffn_sum = reduce_stage(links, ffn_grads, 1).astype(F32)

    acc = grad_attended
    qkv_grads = [None] * n
    qkv_bias = [None] * n
    for r in list(range(1, n)) + [0]:
        grad_ctx = mm_nt(attended_low, out_parts[r]).astype(BF16)
        proj_w, proj_e, _, log_total = saved[r]
        qkv_grads[r], acc, bias_sum = attn_backward(
            rows_t, proj_w, proj_e, log_total, grad_ctx, qkv[r], acc, heads
        )
        qkv_bias[r] = bias_sum[0]
    qkv_sum = reduce_stage(links, qkv_grads, 0).astype(F32)
    grad_ents = acc[words:]
    scaled_ents = grad_ents * share
    ents_high = scaled_ents.astype(BF16)
    ents_rest = (scaled_ents - ents_high.astype(F32)).astype(BF16)
    grad_pos = mm_tn(inside_low, ents_high) + mm_tn(inside_low, ents_rest)
    pos_sum = reduce_pos(links, grad_pos.astype(BF16)).astype(F32)

    group_vec = jnp.stack([jnp.concatenate([qkv_bias[r], grad_up_b[r]]) for r in range(n)])
    group_abs = jnp.take(group_vec, (z - jnp.arange(n)) % n, axis=0)
    flat = jnp.concatenate(
        [
            grad_gain_one,
            grad_bias_one,
            grad_out_b,
            grad_gain_two,
            grad_bias_two,
            grad_down_b,
            group_abs.reshape(-1),
        ]
    )
    vec = reduce_everywhere(links, flat.reshape(-1, width))
    own_vec = lax.dynamic_index_in_dim(
        vec[6:].reshape(n, 6 * gw + ff), z, 0, keepdims=False
    )
    grad_query_w = jnp.stack(
        [
            qkv_sum[:, :gw],
            qkv_sum[:, gw : 2 * gw],
            qkv_sum[:, 4 * gw : 5 * gw],
            qkv_sum[:, 5 * gw :],
        ]
    )
    grad_query_b = jnp.stack(
        [own_vec[:gw], own_vec[gw : 2 * gw], own_vec[4 * gw : 5 * gw], own_vec[5 * gw : 6 * gw]]
    )
    return (
        out_low[:words],
        out_low[words:],
        acc[:words],
        grad_ents,
        pos_sum,
        grad_query_w,
        grad_query_b,
        qkv_sum[:, 2 * gw : 3 * gw],
        qkv_sum[:, 3 * gw : 4 * gw],
        own_vec[3 * gw : 4 * gw],
        ffn_sum[:gw],
        vec[2],
        vec[0],
        vec[1],
        ffn_sum[gw : gw + width],
        own_vec[6 * gw :],
        ffn_sum[gw + width :],
        vec[5],
        vec[3],
        vec[4],
    )


def solution(mesh):
    rows = P(("dp", "tensor"), None)
    last = P(None, "tensor")
    placed = (
        P("dp", None),
        P("dp", None),
        P("dp", None, None),
        P("dp", None),
        P("dp", None),
        P(),
        P(None, None, "tensor"),
        last,
        last,
        last,
        P("tensor"),
        P("tensor", None),
        P(),
        P(),
        P(),
        last,
        P("tensor"),
        P("tensor", None),
        P(),
        P(),
        P(),
        rows,
        rows,
    )
    return jax.shard_map(
        shards,
        mesh=mesh,
        in_specs=placed,
        out_specs=(
            rows,
            rows,
            rows,
            rows,
            P(),
            P(None, None, "tensor"),
            last,
            last,
            last,
            P("tensor"),
            P("tensor", None),
            P(),
            P(),
            P(),
            last,
            P("tensor"),
            P("tensor", None),
            P(),
            P(),
            P(),
        ),
        check_vma=False,
    )
```

time: 1390 us -> 520 us (0.37)
  waiting for transfers between devices: 851 us -> 153 us
  matrix products: 224 us -> 84.7 us
  blocking collectives: 139 us -> 0 us
  Pallas kernels: 0 us -> 74.8 us
  starting transfers between devices: 1.91 us -> 52.9 us
    reduce_scatter x8 -> x0, waiting for transfers between devices: 446 us -> none  [the longest x1 112 us: shards(): lax.psum_scatter(normed_part[:word_total], 'tensor', scatter_dimension=0,...]
    psum x2 -> x0, waiting for transfers between devices: 273 us -> none  [the longest x1 137 us: shards(): lax.psum((grad_query_w, grad_query_b, grad_key_w, grad_value_w, grad_valu...]
    ppermute x0 -> x70, waiting for transfers between devices: none -> 153 us  [the longest x24 68.9 us: swap_bit(): return lax.ppermute(v, 'dp', [(i, i ^ 2 << k) for i in range(self.dp)])]
    all_gather x3 -> x0, waiting for transfers between devices: 131 us -> none  [the longest x1 44.1 us: shards(): lax.all_gather(attended_low[:word_share], 'tensor', axis=0, tiled=True)]
    dot_general x78 -> x39, matrix products: 194 us -> 84.7 us  [the longest x13 40.2 us: mm(): return jnp.dot(a, b, preferred_element_type=F32)]
    pallas_call x0 -> x8, Pallas kernels: none -> 74.8 us  [the longest x4 42.6 us: attn_backward(): pl.pallas_call(partial(attn_backward_kernel, words, gw, heads), out_shape...]
    all_gather x3 -> x0, blocking collectives: 74.6 us -> none  [the longest x1 25.3 us: shards(): lax.all_gather(mixed_low[word_share:], 'tensor', axis=0, tiled=True)]
    psum x2 -> x0, blocking collectives: 64.2 us -> none  [the longest x1 49.9 us: shards(): lax.psum((grad_gain_one, grad_bias_one, grad_out_b, grad_gain_two, grad_b...]
  transfers between devices with their start and end apart: 13 -> 70, of which waited for: 12 -> 28; matrix products, arithmetic and copies ran while one was open for 6% -> 21% of each run, Pallas kernels for 0% -> 15%
where the time goes in v1:
time: 520 us; the launch traced here: 510 us
  waiting for transfers between devices  153 us (29%)
  local copies, waits for them, and re-layouts  104 us (20%)
  matrix products  84.7 us (16%)
  Pallas kernels  74.8 us (14%)
  starting transfers between devices  52.9 us (10%)
  other arithmetic  37.8 us (7%)
    ppermute x24, waiting for transfers between devices, swap_bit(): return lax.ppermute(v, 'dp', [(i, i ^ 2 << k) for i in range(self.dp)])  68.9 us
    ppermute x12, waiting for transfers between devices, next_z(): return lax.ppermute(v, 'tensor', [(i, (i + 1) % n) for i in range(n)])  65.5 us
    unnamed x228, local copies, waits for them, and re-layouts  44.3 us
    pallas_call x4, Pallas kernels, attn_backward(): pl.pallas_call(partial(attn_backward_kernel, words, gw, heads), out_shape...  42.6 us
    dot_general x13, matrix products, mm(): return jnp.dot(a, b, preferred_element_type=F32)  40.2 us
    pallas_call x4, Pallas kernels, attn_forward(): pl.pallas_call(partial(attn_forward_kernel, words, ents, gw, heads), out_...  32.2 us
    ppermute x24, starting transfers between devices, swap_bit(): return lax.ppermute(v, 'dp', [(i, i ^ 2 << k) for i in range(self.dp)])  25.7 us
    dot_general x14, matrix products, mm_tn(): return lax.dot_general(a, b, TN, preferred_element_type=F32)  23.7 us
  transfers between devices with their start and end apart: 70, of which 28 were waited for; matrix products, arithmetic and copies ran while one was open for 21% of the time, Pallas kernels for 15%

profile of v1, /device:TPU:0, one launch (start us, length us, event | category | flops | bytes accessed | tf_op | source)
XLA Modules:
  0.0 510.5 jit_solution(17896873660644713931)
XLA Ops:
  3.7 3.1 collective-permute-start.4
  6.8 2.6 collective-permute-start.14
  10.7 2.3 fusion.109
  23.5 4.2 concatenate.76.w_ref
  46.2 8.1 %shard_map.374 = (bf16[512,768]{1,0:T(8,128)(2,1)S(1)}, bf16[128,768]{1,0:T(8,128)(2,1)S(1)}, bf16[640,192]{1,0:T(8,128)(2,1)S(1)}, f32[8,640]{1,0:T(8,128)S(1)}) custom-call(bf16[640,768]{1,0:T(8,128)(2,1)S(1)} %copy.95.rows_ref, bf16[768,1152]{1,0:T(8,128)(2,1)S(1)} %copy-done.2, f32[1,1152]{1,0:T(1,128)S(1)} %slice_convert_fusion.3.b_ref), custom_call_target="tpu_custom_call" | custom-call | flops 2013265920 | bytes 6291456 | tf_op jit(solution)/shard_map/pallas_call | solution.py:78
  59.3 2.3 copy.107
  69.8 8.4 %collective-permute-done.5 = bf16[192,1152]{1,0:T(8,128)(2,1)S(1)} collective-permute-done((bf16[192,1152]{1,0:T(8,128)(2,1)}, bf16[192,1152]{1,0:T(8,128)(2,1)S(1)}, u32[]{:S(2)}, u32[]{:S(2)}) %collective-permute-start.5) | collective-permute-done | bytes 442400 | tf_op jit(solution)/shard_map/ppermute | solution.py:247
  80.5 9.4 %collective-permute-done.6 = bf16[192,1152]{1,0:T(8,128)(2,1)S(1)} collective-permute-done((bf16[192,1152]{1,0:T(8,128)(2,1)S(1)}, bf16[192,1152]{1,0:T(8,128)(2,1)S(1)}, u32[]{:S(2)}, u32[]{:S(2)}) %collective-permute-start.6) | collective-permute-done | bytes 442400 | tf_op jit(solution)/shard_map/ppermute | solution.py:247
  93.6 8.1 %shard_map.375 = (bf16[512,768]{1,0:T(8,128)(2,1)S(1)}, bf16[128,768]{1,0:T(8,128)(2,1)S(1)}, bf16[640,192]{1,0:T(8,128)(2,1)S(1)}, f32[8,640]{1,0:T(8,128)S(1)}) custom-call(bf16[640,768]{1,0:T(8,128)(2,1)S(1)} %copy.95.rows_ref, bf16[768,1152]{1,0:T(8,128)(2,1)S(1)} %constant_dynamic-update-slice_fusion.28.w_ref, f32[1,1152]{1,0:T(1,128)S(1)} %slice_convert_fusion.2.b_ref), custom_call_target="tpu_custom_call" | custom-call | flops 2013265920 | bytes 6291456 | tf_op jit(solution)/shard_map/pallas_call | solution.py:78
  101.9 4.8 collective-permute-done.7
  108.7 8.1 %shard_map.376 = (bf16[512,768]{1,0:T(8,128)(2,1)S(1)}, bf16[128,768]{1,0:T(8,128)(2,1)S(1)}, bf16[640,192]{1,0:T(8,128)(2,1)S(1)}, f32[8,640]{1,0:T(8,128)S(1)}) custom-call(bf16[640,768]{1,0:T(8,128)(2,1)S(1)} %copy.95.rows_ref, bf16[768,1152]{1,0:T(8,128)(2,1)S(1)} %constant_dynamic-update-slice_fusion.20.w_ref, f32[1,1152]{1,0:T(1,128)S(1)} %slice_convert_fusion.1.b_ref), custom_call_target="tpu_custom_call" | custom-call | flops 2013265920 | bytes 6291456 | tf_op jit(solution)/shard_map/pallas_call | solution.py:78
  117.7 3.9 collective-permute-done.15
  123.3 8.1 %shard_map.377 = (bf16[512,768]{1,0:T(8,128)(2,1)S(1)}, bf16[128,768]{1,0:T(8,128)(2,1)S(1)}, bf16[640,192]{1,0:T(8,128)(2,1)S(1)}, f32[8,640]{1,0:T(8,128)S(1)}) custom-call(bf16[640,768]{1,0:T(8,128)(2,1)S(1)} %copy.95.rows_ref, bf16[768,1152]{1,0:T(8,128)(2,1)S(1)} %constant_dynamic-update-slice_fusion.12.w_ref, f32[1,1152]{1,0:T(1,128)S(1)} %slice_convert_fusion.b_ref), custom_call_target="tpu_custom_call" | custom-call | flops 2013265920 | bytes 6291456 | tf_op jit(solution)/shard_map/pallas_call | solution.py:78
  132.6 6.0 %collective-permute-done.23 = bf16[432,768]{1,0:T(8,128)(2,1)S(1)} collective-permute-done((bf16[432,768]{1,0:T(8,128)(2,1)S(1)}, bf16[432,768]{1,0:T(8,128)(2,1)S(1)}, u32[]{:S(2)}, u32[]{:S(2)}) %collective-permute-start.23) | collective-permute-done | bytes 663584 | tf_op jit(solution)/shard_map/ppermute | solution.py:247
  140.6 10.7 %collective-permute-done.24 = bf16[432,768]{1,0:T(8,128)(2,1)S(1)} collective-permute-done((bf16[432,768]{1,0:T(8,128)(2,1)S(1)}, bf16[432,768]{1,0:T(8,128)(2,1)S(1)}, u32[]{:S(2)}, u32[]{:S(2)}) %collective-permute-start.24) | collective-permute-done | bytes 663584 | tf_op jit(solution)/shard_map/ppermute | solution.py:260
  156.4 12.6 %multiply_convert_fusion.2 = (bf16[640,768]{1,0:T(8,128)(2,1)S(1)}, f32[640,768]{1,0:T(8,128)S(1)}, f32[640,768]{1,0:T(8,128)}) fusion(f32[768]{0:T(1024)S(1)} %fusion.85, bf16[640,768]{0,1:T(8,128)(2,1)S(1)} %fusion.28, bf16[1728,768]{1,0:T(8,128)(2,1)S(1)} %constant_dynamic-update-slice_fusion.24), kind=kOutput, calls=%fused_computation.69 | convolution fusion | flops 787415040 | bytes 7081984 | tf_op jit(solution)/shard_map/dot_general | solution.py:19
  170.2 5.8 %multiply_convert_fusion.1 = (bf16[640,768]{1,0:T(8,128)(2,1)S(1)}, f32[640,768]{1,0:T(8,128)S(1)}, f32[640,768]{1,0:T(8,128)S(1)}) fusion(f32[768]{0:T(1024)S(1)} %fusion.84, bf16[640,768]{0,1:T(8,128)(2,1)S(1)} %fusion.28, bf16[1728,768]{1,0:T(8,128)(2,1)S(1)} %constant_dynamic-update-slice_fusion.16), kind=kOutput, calls=%fused_computation.56 | convolution fusion | flops 787415040 | bytes 7081984 | tf_op jit(solution)/shard_map/dot_general | solution.py:19
  177.2 5.4 %multiply_convert_fusion.3 = (bf16[640,768]{1,0:T(8,128)(2,1)S(1)}, f32[640,768]{1,0:T(8,128)S(1)}, f32[640,768]{1,0:T(8,128)S(1)}) fusion(f32[768]{0:T(1024)S(1)} %copy-done.92, bf16[640,768]{0,1:T(8,128)(2,1)S(1)} %fusion.28, bf16[768,768]{1,0:T(8,128)(2,1)S(1)} %copy-done.63), kind=kOutput, calls=%fused_computation.82 | convolution fusion | flops 787415040 | bytes 7080960 | tf_op jit(solution)/shard_map/dot_general | solution.py:19
  183.8 6.4 %multiply_convert_fusion = (bf16[640,768]{1,0:T(8,128)(2,1)S(1)}, f32[640,768]{1,0:T(8,128)}, f32[640,768]{1,0:T(8,128)}) fusion(f32[768]{0:T(1024)S(1)} %fusion.83, bf16[640,768]{0,1:T(8,128)(2,1)S(1)} %fusion.28, bf16[1728,768]{1,0:T(8,128)(2,1)S(1)} %constant_dynamic-update-slice_fusion.8), kind=kOutput, calls=%fused_computation.43 | convolution fusion | flops 787415040 | bytes 7081984 | tf_op jit(solution)/shard_map/dot_general | solution.py:19
  193.8 2.5 fusion.101
  209.3 2.4 convert_reduce_fusion.1
  235.9 2.4 copy.113.acc_ref
  238.3 2.2 convolution_convert_fusion.13
  259.7 10.6 %shard_map.378 = (bf16[768,1152]{1,0:T(8,128)(2,1)S(1)}, f32[640,768]{1,0:T(8,128)S(1)}, f32[8,1152]{1,0:T(8,128)S(1)}) custom-call(bf16[768,640]{1,0:T(8,128)(2,1)S(1)} %copy-done.18, bf16[512,768]{1,0:T(8,128)(2,1)S(1)} %copy-done.25, bf16[128,768]{1,0:T(8,128)(2,1)S(1)} %copy-done.33, ...), custom_call_target="tpu_custom_call", output_to_operand_aliasing={{1}: (6, {})} | custom-call | flops 4655677440 | bytes 12582912 | tf_op jit(solution)/shard_map/pallas_call | solution.py:189
  271.5 10.7 %shard_map.379 = (bf16[768,1152]{1,0:T(8,128)(2,1)S(1)}, f32[640,768]{1,0:T(8,128)S(1)}, f32[8,1152]{1,0:T(8,128)S(1)}) custom-call(bf16[768,640]{1,0:T(8,128)(2,1)S(1)} %copy-done.18, bf16[512,768]{1,0:T(8,128)(2,1)S(1)} %copy-done.27, bf16[128,768]{1,0:T(8,128)(2,1)S(1)} %copy-done.35, ...), custom_call_target="tpu_custom_call", output_to_operand_aliasing={{1}: (6, {})} | custom-call | flops 4655677440 | bytes 12582912 | tf_op jit(solution)/shard_map/pallas_call | solution.py:189
  283.5 10.6 %shard_map.380 = (bf16[768,1152]{1,0:T(8,128)(2,1)S(1)}, f32[640,768]{1,0:T(8,128)S(1)}, f32[8,1152]{1,0:T(8,128)S(1)}) custom-call(bf16[768,640]{1,0:T(8,128)(2,1)S(1)} %copy-done.18, bf16[512,768]{1,0:T(8,128)(2,1)S(1)} %copy-done.29, bf16[128,768]{1,0:T(8,128)(2,1)S(1)} %copy-done.37, f32[8,640]{1,0:T(8,128)S(1)} %copy-done.39, ...), custom_call_target="tpu_custom_call", output_to_operand_aliasing={{1}: (6, {})} | custom-call | flops 4655677440 | bytes 12582912 | tf_op jit(solution)/shard_map/pallas_call | solution.py:189
  294.2 10.8 %shard_map.381 = (bf16[768,1152]{1,0:T(8,128)(2,1)S(1)}, f32[640,768]{1,0:T(8,128)S(1)}, f32[8,1152]{1,0:T(8,128)S(1)}) custom-call(bf16[768,640]{1,0:T(8,128)(2,1)S(1)} %copy-done.18, bf16[512,768]{1,0:T(8,128)(2,1)S(1)} %copy-done.23, bf16[128,768]{1,0:T(8,128)(2,1)S(1)} %copy-done.31, ...), custom_call_target="tpu_custom_call", output_to_operand_aliasing={{1}: (6, {})} | custom-call | flops 4655677440 | bytes 12582912 | tf_op jit(solution)/shard_map/pallas_call | solution.py:189
  320.8 2.3 collective-permute-done.51
  323.9 2.5 collective-permute-done.28
  327.4 3.8 collective-permute-done.29
  332.1 3.8 collective-permute-done.30
  339.6 2.3 collective-permute-start.31
  343.4 4.0 collective-permute-done.31
  348.2 3.9 collective-permute-done.32
  360.4 4.8 collective-permute-done.40
  369.0 6.6 %collective-permute-done.62 = bf16[432,768]{1,0:T(8,128)(2,1)S(1)} collective-permute-done((bf16[432,768]{1,0:T(8,128)(2,1)S(1)}, bf16[432,768]{1,0:T(8,128)(2,1)S(1)}, u32[]{:S(2)}, u32[]{:S(2)}) %collective-permute-start.62) | collective-permute-done | bytes 663584 | tf_op jit(solution)/shard_map/ppermute | solution.py:260
  378.0 2.7 collective-permute-start.54
  380.7 9.7 %collective-permute-done.44 = bf16[192,1152]{1,0:T(8,128)(2,1)S(1)} collective-permute-done((bf16[192,1152]{1,0:T(8,128)(2,1)S(1)}, bf16[192,1152]{1,0:T(8,128)(2,1)S(1)}, u32[]{:S(2)}, u32[]{:S(2)}) %collective-permute-start.44) | collective-permute-done | bytes 442400 | tf_op jit(solution)/shard_map/ppermute | solution.py:247
  392.6 8.6 %collective-permute-done.63 = bf16[432,768]{1,0:T(8,128)(2,1)S(1)} collective-permute-done((bf16[432,768]{1,0:T(8,128)(2,1)S(1)}, bf16[432,768]{1,0:T(8,128)(2,1)S(1)}, u32[]{:S(2)}, u32[]{:S(2)}) %collective-permute-start.63) | collective-permute-done | bytes 663584 | tf_op jit(solution)/shard_map/ppermute | solution.py:247
  402.0 2.8 collective-permute-start.64
  407.7 8.4 %collective-permute-done.45 = bf16[192,1152]{1,0:T(8,128)(2,1)S(1)} collective-permute-done((bf16[192,1152]{1,0:T(8,128)(2,1)S(1)}, bf16[192,1152]{1,0:T(8,128)(2,1)S(1)}, u32[]{:S(2)}, u32[]{:S(2)}) %collective-permute-start.45) | collective-permute-done | bytes 442400 | tf_op jit(solution)/shard_map/ppermute | solution.py:247
  420.0 4.6 collective-permute-done.64
  430.8 8.0 %collective-permute-done.54 = f32[16,768]{1,0:T(8,128)} collective-permute-done((f32[16,768]{1,0:T(8,128)}, f32[16,768]{1,0:T(8,128)}, u32[]{:S(2)}, u32[]{:S(2)}) %collective-permute-start.54) | collective-permute-done | bytes 49184 | tf_op jit(solution)/shard_map/ppermute | solution.py:254
  451.2 3.9 collective-permute-done.47
  455.2 13.6 %collective-permute-done.66 = bf16[432,768]{1,0:T(8,128)(2,1)S(1)} collective-permute-done((bf16[432,768]{1,0:T(8,128)(2,1)S(1)}, bf16[432,768]{1,0:T(8,128)(2,1)S(1)}, u32[]{:S(2)}, u32[]{:S(2)}) %collective-permute-start.66) | collective-permute-done | bytes 663584 | tf_op jit(solution)/shard_map/ppermute | solution.py:260
  473.6 14.8 %collective-permute-done.67 = bf16[432,768]{1,0:T(8,128)(2,1)} collective-permute-done((bf16[432,768]{1,0:T(8,128)(2,1)}, bf16[432,768]{1,0:T(8,128)(2,1)}, u32[]{:S(2)}, u32[]{:S(2)}) %collective-permute-start.67) | collective-permute-done | bytes 663584 | tf_op jit(solution)/shard_map/ppermute | solution.py:260
  490.2 3.3 copy.122
  503.9 4.3 fusion.107
  (553 shorter events, 216.5 us)
Async XLA Ops:
  3.7 58.8 %collective-permute-start.4 = (bf16[1,1920]{1,0:T(2,128)(2,1)}, bf16[1,1920]{1,0:T(2,128)(2,1)}, u32[]{:S(2)}, u32[]{:S(2)}) collective-permute-start(bf16[1,1920]{1,0:T(2,128)(2,1)} %broadcast_in_dim.22), channel_id=1, source_target_pairs={{0,1},{1,2},{2,3},{3,0},{4,5},{5,6},{6,7},{7,4},{8,9},{9,10},{10,1... | collective-permute-start | bytes 11528 | tf_op jit(solution)/shard_map/ppermute | solution.py:251
  6.8 56.5 %collective-permute-start.14 = (bf16[1,1920]{1,0:T(2,128)(2,1)}, bf16[1,1920]{1,0:T(2,128)(2,1)}, u32[]{:S(2)}, u32[]{:S(2)}) collective-permute-start(bf16[1,1920]{1,0:T(2,128)(2,1)} %broadcast_in_dim.22), channel_id=1, source_target_pairs={{0,2},{1,3},{2,0},{3,1},{4,6},{5,7},{6,4},{7,5},{8,10},{9,11},{10,... | collective-permute-start | bytes 11528 | tf_op jit(solution)/shard_map/ppermute | solution.py:251
  9.3 55.3 %collective-permute-start.22 = (bf16[1,1920]{1,0:T(2,128)(2,1)}, bf16[1,1920]{1,0:T(2,128)(2,1)}, u32[]{:S(2)}, u32[]{:S(2)}) collective-permute-start(bf16[1,1920]{1,0:T(2,128)(2,1)} %broadcast_in_dim.22), channel_id=1, source_target_pairs={{0,3},{1,0},{2,1},{3,2},{4,7},{5,4},{6,5},{7,6},{8,11},{9,8},{10,9... | collective-permute-start | bytes 11528 | tf_op jit(solution)/shard_map/ppermute | solution.py:251
  29.5 35.9 %collective-permute-start = (bf16[192,1152]{1,0:T(8,128)(2,1)}, bf16[192,1152]{1,0:T(8,128)(2,1)}, u32[]{:S(2)}, u32[]{:S(2)}) collective-permute-start(bf16[192,1152]{1,0:T(8,128)(2,1)} %constant_dynamic-slice_fusion.23), channel_id=1, source_target_pairs={{0,1},{1,2},{2,3},{3,0},{4,5},{5,6},{6,7},{7,4},{8,9},{9,10},{10,1... | collective-permute-start | bytes 1327112 | tf_op jit(solution)/shard_map/ppermute | solution.py:247
  65.3 12.8 %collective-permute-start.5 = (bf16[192,1152]{1,0:T(8,128)(2,1)}, bf16[192,1152]{1,0:T(8,128)(2,1)S(1)}, u32[]{:S(2)}, u32[]{:S(2)}) collective-permute-start(bf16[192,1152]{1,0:T(8,128)(2,1)} %collective-permute-done), channel_id=1, source_target_pairs={{0,1},{1,2},{2,3},{3,0},{4,5},{5,6},{6,7},{7,4},{8,9},{9,10},{10,1... | collective-permute-start | bytes 1327112 | tf_op jit(solution)/shard_map/ppermute | solution.py:247
  65.4 14.3 %collective-permute-start.1 = (bf16[192,1152]{1,0:T(8,128)(2,1)}, bf16[192,1152]{1,0:T(8,128)(2,1)S(1)}, u32[]{:S(2)}, u32[]{:S(2)}) collective-permute-start(bf16[192,1152]{1,0:T(8,128)(2,1)} %collective-permute-done), channel_id=1, source_target_pairs={{0,8},{4,12},{8,0},{12,4},{16,24},{20,28},{24,16},{28,20},{1,9},{5... | collective-permute-start | bytes 1327112 | tf_op jit(solution)/shard_map/ppermute | solution.py:260
  78.2 14.5 %collective-permute-start.11 = (bf16[192,1152]{1,0:T(8,128)(2,1)S(1)}, bf16[192,1152]{1,0:T(8,128)(2,1)S(1)}, u32[]{:S(2)}, u32[]{:S(2)}) collective-permute-start(bf16[192,1152]{1,0:T(8,128)(2,1)S(1)} %collective-permute-done.5), channel_id=1, source_target_pairs={{0,8},{4,12},{8,0},{12,4},{16,24},{20,28},{24,16},{28,20},{1,9},{5... | collective-permute-start | bytes 1327112 | tf_op jit(solution)/shard_map/ppermute | solution.py:260
  79.7 13.2 %collective-permute-start.12 = (bf16[192,1152]{1,0:T(8,128)(2,1)S(1)}, bf16[192,1152]{1,0:T(8,128)(2,1)S(1)}, u32[]{:S(2)}, u32[]{:S(2)}) collective-permute-start(bf16[192,1152]{1,0:T(8,128)(2,1)S(1)} %collective-permute-done.5), channel_id=1, source_target_pairs={{0,4},{4,0},{8,12},{12,8},{16,20},{20,16},{24,28},{28,24},{1,5},{5... | collective-permute-start | bytes 1327112 | tf_op jit(solution)/shard_map/ppermute | solution.py:257
  79.7 13.9 %collective-permute-start.3 = (bf16[192,1152]{1,0:T(8,128)(2,1)S(1)}, bf16[192,1152]{1,0:T(8,128)(2,1)S(1)}, u32[]{:S(2)}, u32[]{:S(2)}) collective-permute-start(bf16[192,1152]{1,0:T(8,128)(2,1)S(1)} %collective-permute-done.1), channel_id=1, source_target_pairs={{0,4},{4,0},{8,12},{12,8},{16,20},{20,16},{24,28},{28,24},{1,5},{5... | collective-permute-start | bytes 1327112 | tf_op jit(solution)/shard_map/ppermute | solution.py:257
  91.0 15.7 %collective-permute-start.7 = (bf16[432,768]{1,0:T(8,128)(2,1)S(1)}, bf16[432,768]{1,0:T(8,128)(2,1)S(1)}, u32[]{:S(2)}, u32[]{:S(2)}) collective-permute-start(bf16[432,768]{1,0:T(8,128)(2,1)S(1)} %constant_dynamic-slice_fusion.22), channel_id=1, source_target_pairs={{0,1},{1,2},{2,3},{3,0},{4,5},{5,6},{6,7},{7,4},{8,9},{9,10},{10,1... | collective-permute-start | bytes 1990664 | tf_op jit(solution)/shard_map/ppermute | solution.py:247
  92.7 14.2 %collective-permute-start.13 = (bf16[192,1152]{1,0:T(8,128)(2,1)S(1)}, bf16[192,1152]{1,0:T(8,128)(2,1)S(1)}, u32[]{:S(2)}, u32[]{:S(2)}) collective-permute-start(bf16[192,1152]{1,0:T(8,128)(2,1)S(1)} %collective-permute-done.11), channel_id=1, source_target_pairs={{0,4},{4,0},{8,12},{12,8},{16,20},{20,16},{24,28},{28,24},{1,5},{5... | collective-permute-start | bytes 1327112 | tf_op jit(solution)/shard_map/ppermute | solution.py:257
  92.9 14.0 %collective-permute-start.20 = (bf16[192,1152]{1,0:T(8,128)(2,1)S(1)}, bf16[192,1152]{1,0:T(8,128)(2,1)S(1)}, u32[]{:S(2)}, u32[]{:S(2)}) collective-permute-start(bf16[192,1152]{1,0:T(8,128)(2,1)S(1)} %collective-permute-done.6), channel_id=1, source_target_pairs={{0,4},{4,0},{8,12},{12,8},{16,20},{20,16},{24,28},{28,24},{1,5},{5... | collective-permute-start | bytes 1327112 | tf_op jit(solution)/shard_map/ppermute | solution.py:257
  101.7 21.5 %collective-permute-start.21 = (bf16[192,1152]{1,0:T(8,128)(2,1)S(1)}, bf16[192,1152]{1,0:T(8,128)(2,1)S(1)}, u32[]{:S(2)}, u32[]{:S(2)}) collective-permute-start(bf16[192,1152]{1,0:T(8,128)(2,1)S(1)} %collective-permute-done.19), channel_id=1, source_target_pairs={{0,4},{4,0},{8,12},{12,8},{16,20},{20,16},{24,28},{28,24},{1,5},{5... | collective-permute-start | bytes 1327112 | tf_op jit(solution)/shard_map/ppermute | solution.py:257
  106.7 14.9 %collective-permute-start.15 = (bf16[432,768]{1,0:T(8,128)(2,1)S(1)}, bf16[432,768]{1,0:T(8,128)(2,1)S(1)}, u32[]{:S(2)}, u32[]{:S(2)}) collective-permute-start(bf16[432,768]{1,0:T(8,128)(2,1)S(1)} %collective-permute-done.7), channel_id=1, source_target_pairs={{0,1},{1,2},{2,3},{3,0},{4,5},{5,6},{6,7},{7,4},{8,9},{9,10},{10,1... | collective-permute-start | bytes 1990664 | tf_op jit(solution)/shard_map/ppermute | solution.py:247
  107.1 24.4 %collective-permute-start.8 = (bf16[432,768]{1,0:T(8,128)(2,1)S(1)}, bf16[432,768]{1,0:T(8,128)(2,1)S(1)}, u32[]{:S(2)}, u32[]{:S(2)}) collective-permute-start(bf16[432,768]{1,0:T(8,128)(2,1)S(1)} %collective-permute-done.7), channel_id=1, source_target_pairs={{0,16},{4,20},{8,24},{12,28},{16,0},{20,4},{24,8},{28,12},{1,17},{... | collective-permute-start | bytes 1990664 | tf_op jit(solution)/shard_map/ppermute | solution.py:260
  116.8 15.7 %collective-permute-start.9 = (bf16[432,768]{1,0:T(8,128)(2,1)S(1)}, bf16[432,768]{1,0:T(8,128)(2,1)S(1)}, u32[]{:S(2)}, u32[]{:S(2)}) collective-permute-start(bf16[432,768]{1,0:T(8,128)(2,1)S(1)} %collective-permute-done.7), channel_id=1, source_target_pairs={{0,4},{4,0},{8,12},{12,8},{16,20},{20,16},{24,28},{28,24},{1,5},{5... | collective-permute-start | bytes 1990664 | tf_op jit(solution)/shard_map/ppermute | solution.py:257
  121.6 17.5 %collective-permute-start.16 = (bf16[432,768]{1,0:T(8,128)(2,1)S(1)}, bf16[432,768]{1,0:T(8,128)(2,1)S(1)}, u32[]{:S(2)}, u32[]{:S(2)}) collective-permute-start(bf16[432,768]{1,0:T(8,128)(2,1)S(1)} %collective-permute-done.15), channel_id=1, source_target_pairs={{0,16},{4,20},{8,24},{12,28},{16,0},{20,4},{24,8},{28,12},{1,17},{... | collective-permute-start | bytes 1990664 | tf_op jit(solution)/shard_map/ppermute | solution.py:260
  123.2 15.4 %collective-permute-start.23 = (bf16[432,768]{1,0:T(8,128)(2,1)S(1)}, bf16[432,768]{1,0:T(8,128)(2,1)S(1)}, u32[]{:S(2)}, u32[]{:S(2)}) collective-permute-start(bf16[432,768]{1,0:T(8,128)(2,1)S(1)} %collective-permute-done.15), channel_id=1, source_target_pairs={{0,1},{1,2},{2,3},{3,0},{4,5},{5,6},{6,7},{7,4},{8,9},{9,10},{10,1... | collective-permute-start | bytes 1990664 | tf_op jit(solution)/shard_map/ppermute | solution.py:247
  123.3 16.7 %collective-permute-start.17 = (bf16[432,768]{1,0:T(8,128)(2,1)S(1)}, bf16[432,768]{1,0:T(8,128)(2,1)S(1)}, u32[]{:S(2)}, u32[]{:S(2)}) collective-permute-start(bf16[432,768]{1,0:T(8,128)(2,1)S(1)} %collective-permute-done.15), channel_id=1, source_target_pairs={{0,4},{4,0},{8,12},{12,8},{16,20},{20,16},{24,28},{28,24},{1,5},{5... | collective-permute-start | bytes 1990664 | tf_op jit(solution)/shard_map/ppermute | solution.py:257
  138.6 12.7 %collective-permute-start.24 = (bf16[432,768]{1,0:T(8,128)(2,1)S(1)}, bf16[432,768]{1,0:T(8,128)(2,1)S(1)}, u32[]{:S(2)}, u32[]{:S(2)}) collective-permute-start(bf16[432,768]{1,0:T(8,128)(2,1)S(1)} %collective-permute-done.23), channel_id=1, source_target_pairs={{0,16},{4,20},{8,24},{12,28},{16,0},{20,4},{24,8},{28,12},{1,17},{... | collective-permute-start | bytes 1990664 | tf_op jit(solution)/shard_map/ppermute | solution.py:260
  139.1 12.3 %collective-permute-start.25 = (bf16[432,768]{1,0:T(8,128)(2,1)S(1)}, bf16[432,768]{1,0:T(8,128)(2,1)S(1)}, u32[]{:S(2)}, u32[]{:S(2)}) collective-permute-start(bf16[432,768]{1,0:T(8,128)(2,1)S(1)} %collective-permute-done.23), channel_id=1, source_target_pairs={{0,4},{4,0},{8,12},{12,8},{16,20},{20,16},{24,28},{28,24},{1,5},{5... | collective-permute-start | bytes 1990664 | tf_op jit(solution)/shard_map/ppermute | solution.py:257
  245.1 156.9 %collective-permute-start.55 = (bf16[864,768]{1,0:T(8,128)(2,1)}, bf16[864,768]{1,0:T(8,128)(2,1)}, u32[]{:S(2)}, u32[]{:S(2)}) collective-permute-start(bf16[864,768]{1,0:T(8,128)(2,1)} %constant_dynamic-slice_fusion.8), channel_id=1, source_target_pairs={{0,4},{4,0},{8,12},{12,8},{16,20},{20,16},{24,28},{28,24},{1,5},{5... | collective-permute-start | bytes 3981320 | tf_op jit(solution)/shard_map/ppermute | solution.py:257
  249.2 108.5 %collective-permute-start.59 = (bf16[864,768]{1,0:T(8,128)(2,1)}, bf16[864,768]{1,0:T(8,128)(2,1)}, u32[]{:S(2)}, u32[]{:S(2)}) collective-permute-start(bf16[864,768]{1,0:T(8,128)(2,1)} %constant_dynamic-slice_fusion.4), channel_id=1, source_target_pairs={{0,4},{4,0},{8,12},{12,8},{16,20},{20,16},{24,28},{28,24},{1,5},{5... | collective-permute-start | bytes 3981320 | tf_op jit(solution)/shard_map/ppermute | solution.py:257
  309.8 26.2 %collective-permute-start.35 = (bf16[384,1152]{1,0:T(8,128)(2,1)}, bf16[384,1152]{1,0:T(8,128)(2,1)}, u32[]{:S(2)}, u32[]{:S(2)}) collective-permute-start(bf16[384,1152]{1,0:T(8,128)(2,1)} %constant_dynamic-slice_fusion.16), channel_id=1, source_target_pairs={{0,4},{4,0},{8,12},{12,8},{16,20},{20,16},{24,28},{28,24},{1,5},{5... | collective-permute-start | bytes 2654216 | tf_op jit(solution)/shard_map/ppermute | solution.py:257
  331.5 23.7 %collective-permute-start.61 = (bf16[864,768]{1,0:T(8,128)(2,1)S(1)}, bf16[864,768]{1,0:T(8,128)(2,1)S(1)}, u32[]{:S(2)}, u32[]{:S(2)}) collective-permute-start(bf16[864,768]{1,0:T(8,128)(2,1)S(1)} %constant_dynamic-slice_fusion.2), channel_id=1, source_target_pairs={{0,4},{4,0},{8,12},{12,8},{16,20},{20,16},{24,28},{28,24},{1,5},{5... | collective-permute-start | bytes 3981320 | tf_op jit(solution)/shard_map/ppermute | solution.py:257
  352.1 23.6 %collective-permute-start.57 = (bf16[864,768]{1,0:T(8,128)(2,1)S(1)}, bf16[864,768]{1,0:T(8,128)(2,1)S(1)}, u32[]{:S(2)}, u32[]{:S(2)}) collective-permute-start(bf16[864,768]{1,0:T(8,128)(2,1)S(1)} %constant_dynamic-slice_fusion.6), channel_id=1, source_target_pairs={{0,4},{4,0},{8,12},{12,8},{16,20},{20,16},{24,28},{28,24},{1,5},{5... | collective-permute-start | bytes 3981320 | tf_op jit(solution)/shard_map/ppermute | solution.py:257
  355.2 12.6 %collective-permute-start.43 = (bf16[192,1152]{1,0:T(8,128)(2,1)S(1)}, bf16[192,1152]{1,0:T(8,128)(2,1)S(1)}, u32[]{:S(2)}, u32[]{:S(2)}) collective-permute-start(bf16[192,1152]{1,0:T(8,128)(2,1)S(1)} %add_convert_fusion.26), channel_id=1, source_target_pairs={{0,1},{1,2},{2,3},{3,0},{4,5},{5,6},{6,7},{7,4},{8,9},{9,10},{10,1... | collective-permute-start | bytes 1327112 | tf_op jit(solution)/shard_map/ppermute | solution.py:247
  357.7 17.8 %collective-permute-start.62 = (bf16[432,768]{1,0:T(8,128)(2,1)S(1)}, bf16[432,768]{1,0:T(8,128)(2,1)S(1)}, u32[]{:S(2)}, u32[]{:S(2)}) collective-permute-start(bf16[432,768]{1,0:T(8,128)(2,1)S(1)} %constant_dynamic-slice_fusion.1), channel_id=1, source_target_pairs={{0,16},{4,20},{8,24},{12,28},{16,0},{20,4},{24,8},{28,12},{1,17},{... | collective-permute-start | bytes 1990664 | tf_op jit(solution)/shard_map/ppermute | solution.py:260
  365.2 12.8 %collective-permute-start.38 = (bf16[192,1152]{1,0:T(8,128)(2,1)S(1)}, bf16[192,1152]{1,0:T(8,128)(2,1)S(1)}, u32[]{:S(2)}, u32[]{:S(2)}) collective-permute-start(bf16[192,1152]{1,0:T(8,128)(2,1)S(1)} %constant_dynamic-slice_fusion.13), channel_id=1, source_target_pairs={{0,8},{4,12},{8,0},{12,4},{16,24},{20,28},{24,16},{28,20},{1,9},{5... | collective-permute-start | bytes 1327112 | tf_op jit(solution)/shard_map/ppermute | solution.py:260
  367.9 23.9 %collective-permute-start.60 = (bf16[432,768]{1,0:T(8,128)(2,1)S(1)}, bf16[432,768]{1,0:T(8,128)(2,1)S(1)}, u32[]{:S(2)}, u32[]{:S(2)}) collective-permute-start(bf16[432,768]{1,0:T(8,128)(2,1)S(1)} %constant_dynamic-slice_fusion.3), channel_id=1, source_target_pairs={{0,16},{4,20},{8,24},{12,28},{16,0},{20,4},{24,8},{28,12},{1,17},{... | collective-permute-start | bytes 1990664 | tf_op jit(solution)/shard_map/ppermute | solution.py:260
  375.6 14.9 %collective-permute-start.44 = (bf16[192,1152]{1,0:T(8,128)(2,1)S(1)}, bf16[192,1152]{1,0:T(8,128)(2,1)S(1)}, u32[]{:S(2)}, u32[]{:S(2)}) collective-permute-start(bf16[192,1152]{1,0:T(8,128)(2,1)S(1)} %add_convert_fusion.25), channel_id=1, source_target_pairs={{0,1},{1,2},{2,3},{3,0},{4,5},{5,6},{6,7},{7,4},{8,9},{9,10},{10,1... | collective-permute-start | bytes 1327112 | tf_op jit(solution)/shard_map/ppermute | solution.py:247
  375.8 25.4 %collective-permute-start.63 = (bf16[432,768]{1,0:T(8,128)(2,1)S(1)}, bf16[432,768]{1,0:T(8,128)(2,1)S(1)}, u32[]{:S(2)}, u32[]{:S(2)}) collective-permute-start(bf16[432,768]{1,0:T(8,128)(2,1)S(1)} %add_convert_fusion.18), channel_id=1, source_target_pairs={{0,1},{1,2},{2,3},{3,0},{4,5},{5,6},{6,7},{7,4},{8,9},{9,10},{10,1... | collective-permute-start | bytes 1990664 | tf_op jit(solution)/shard_map/ppermute | solution.py:247
  378.0 60.8 %collective-permute-start.54 = (f32[16,768]{1,0:T(8,128)}, f32[16,768]{1,0:T(8,128)}, u32[]{:S(2)}, u32[]{:S(2)}) collective-permute-start(f32[16,768]{1,0:T(8,128)} %add.524), channel_id=1, source_target_pairs={{0,2},{1,3},{2,0},{3,1},{4,6},{5,7},{6,4},{7,5},{8,10},{9,11},{10,... | collective-permute-start | bytes 147464 | tf_op jit(solution)/shard_map/ppermute | solution.py:254
  390.4 16.1 %collective-permute-start.36 = (bf16[192,1152]{1,0:T(8,128)(2,1)S(1)}, bf16[192,1152]{1,0:T(8,128)(2,1)S(1)}, u32[]{:S(2)}, u32[]{:S(2)}) collective-permute-start(bf16[192,1152]{1,0:T(8,128)(2,1)S(1)} %constant_dynamic-slice_fusion.15), channel_id=1, source_target_pairs={{0,8},{4,12},{8,0},{12,4},{16,24},{20,28},{24,16},{28,20},{1,9},{5... | collective-permute-start | bytes 1327112 | tf_op jit(solution)/shard_map/ppermute | solution.py:260
  391.8 27.1 %collective-permute-start.58 = (bf16[432,768]{1,0:T(8,128)(2,1)S(1)}, bf16[432,768]{1,0:T(8,128)(2,1)S(1)}, u32[]{:S(2)}, u32[]{:S(2)}) collective-permute-start(bf16[432,768]{1,0:T(8,128)(2,1)S(1)} %constant_dynamic-slice_fusion.5), channel_id=1, source_target_pairs={{0,16},{4,20},{8,24},{12,28},{16,0},{20,4},{24,8},{28,12},{1,17},{... | collective-permute-start | bytes 1990664 | tf_op jit(solution)/shard_map/ppermute | solution.py:260
  401.2 14.9 %collective-permute-start.45 = (bf16[192,1152]{1,0:T(8,128)(2,1)S(1)}, bf16[192,1152]{1,0:T(8,128)(2,1)S(1)}, u32[]{:S(2)}, u32[]{:S(2)}) collective-permute-start(bf16[192,1152]{1,0:T(8,128)(2,1)S(1)} %add_convert_fusion.24), channel_id=1, source_target_pairs={{0,1},{1,2},{2,3},{3,0},{4,5},{5,6},{6,7},{7,4},{8,9},{9,10},{10,1... | collective-permute-start | bytes 1327112 | tf_op jit(solution)/shard_map/ppermute | solution.py:247
  402.0 22.5 %collective-permute-start.64 = (bf16[432,768]{1,0:T(8,128)(2,1)S(1)}, bf16[432,768]{1,0:T(8,128)(2,1)S(1)}, u32[]{:S(2)}, u32[]{:S(2)}) collective-permute-start(bf16[432,768]{1,0:T(8,128)(2,1)S(1)} %add_convert_fusion.17), channel_id=1, source_target_pairs={{0,1},{1,2},{2,3},{3,0},{4,5},{5,6},{6,7},{7,4},{8,9},{9,10},{10,1... | collective-permute-start | bytes 1990664 | tf_op jit(solution)/shard_map/ppermute | solution.py:247
  406.5 33.8 %collective-permute-start.33 = (bf16[128,768]{1,0:T(8,128)(2,1)S(1)}, bf16[128,768]{1,0:T(8,128)(2,1)S(1)}, u32[]{:S(2)}, u32[]{:S(2)}) collective-permute-start(bf16[128,768]{1,0:T(8,128)(2,1)S(1)} %maximum_select_fusion.2), channel_id=1, source_target_pairs={{0,8},{4,12},{8,0},{12,4},{16,24},{20,28},{24,16},{28,20},{1,9},{5... | collective-permute-start | bytes 589832 | tf_op jit(solution)/shard_map/ppermute | solution.py:260
  417.0 23.4 %collective-permute-start.46 = (bf16[192,1152]{1,0:T(8,128)(2,1)}, bf16[192,1152]{1,0:T(8,128)(2,1)}, u32[]{:S(2)}, u32[]{:S(2)}) collective-permute-start(bf16[192,1152]{1,0:T(8,128)(2,1)} %add_convert_fusion.23), channel_id=1, source_target_pairs={{0,16},{4,20},{8,24},{12,28},{16,0},{20,4},{24,8},{28,12},{1,17},{... | collective-permute-start | bytes 1327112 | tf_op jit(solution)/shard_map/ppermute | solution.py:260
  418.8 24.4 %collective-permute-start.56 = (bf16[432,768]{1,0:T(8,128)(2,1)}, bf16[432,768]{1,0:T(8,128)(2,1)}, u32[]{:S(2)}, u32[]{:S(2)}) collective-permute-start(bf16[432,768]{1,0:T(8,128)(2,1)} %constant_dynamic-slice_fusion.7), channel_id=1, source_target_pairs={{0,16},{4,20},{8,24},{12,28},{16,0},{20,4},{24,8},{28,12},{1,17},{... | collective-permute-start | bytes 1990664 | tf_op jit(solution)/shard_map/ppermute | solution.py:260
  425.6 17.6 %collective-permute-start.65 = (bf16[432,768]{1,0:T(8,128)(2,1)}, bf16[432,768]{1,0:T(8,128)(2,1)}, u32[]{:S(2)}, u32[]{:S(2)}) collective-permute-start(bf16[432,768]{1,0:T(8,128)(2,1)} %add_convert_fusion.16), channel_id=1, source_target_pairs={{0,1},{1,2},{2,3},{3,0},{4,5},{5,6},{6,7},{7,4},{8,9},{9,10},{10,1... | collective-permute-start | bytes 1990664 | tf_op jit(solution)/shard_map/ppermute | solution.py:247
  442.1 13.1 %collective-permute-start.47 = (bf16[192,1152]{1,0:T(8,128)(2,1)S(1)}, bf16[192,1152]{1,0:T(8,128)(2,1)S(1)}, u32[]{:S(2)}, u32[]{:S(2)}) collective-permute-start(bf16[192,1152]{1,0:T(8,128)(2,1)S(1)} %get-tuple-element.145), channel_id=1, source_target_pairs={{0,8},{4,12},{8,0},{12,4},{16,24},{20,28},{24,16},{28,20},{1,9},{5... | collective-permute-start | bytes 1327112 | tf_op jit(solution)/shard_map/ppermute | solution.py:260
  444.8 24.0 %collective-permute-start.66 = (bf16[432,768]{1,0:T(8,128)(2,1)S(1)}, bf16[432,768]{1,0:T(8,128)(2,1)S(1)}, u32[]{:S(2)}, u32[]{:S(2)}) collective-permute-start(bf16[432,768]{1,0:T(8,128)(2,1)S(1)} %add_convert_fusion.15), channel_id=1, source_target_pairs={{0,8},{4,12},{8,0},{12,4},{16,24},{20,28},{24,16},{28,20},{1,9},{5... | collective-permute-start | bytes 1990664 | tf_op jit(solution)/shard_map/ppermute | solution.py:260
  451.2 21.4 %collective-permute-start.48 = (bf16[192,1152]{1,0:T(8,128)(2,1)S(1)}, bf16[192,1152]{1,0:T(8,128)(2,1)S(1)}, u32[]{:S(2)}, u32[]{:S(2)}) collective-permute-start(bf16[192,1152]{1,0:T(8,128)(2,1)S(1)} %get-tuple-element.145), channel_id=1, source_target_pairs={{0,4},{4,0},{8,12},{12,8},{16,20},{20,16},{24,28},{28,24},{1,5},{5... | collective-permute-start | bytes 1327112 | tf_op jit(solution)/shard_map/ppermute | solution.py:257
  455.2 17.5 %collective-permute-start.49 = (bf16[192,1152]{1,0:T(8,128)(2,1)S(1)}, bf16[192,1152]{1,0:T(8,128)(2,1)S(1)}, u32[]{:S(2)}, u32[]{:S(2)}) collective-permute-start(bf16[192,1152]{1,0:T(8,128)(2,1)S(1)} %collective-permute-done.47), channel_id=1, source_target_pairs={{0,4},{4,0},{8,12},{12,8},{16,20},{20,16},{24,28},{28,24},{1,5},{5... | collective-permute-start | bytes 1327112 | tf_op jit(solution)/shard_map/ppermute | solution.py:257
  471.7 16.6 %collective-permute-start.67 = (bf16[432,768]{1,0:T(8,128)(2,1)}, bf16[432,768]{1,0:T(8,128)(2,1)}, u32[]{:S(2)}, u32[]{:S(2)}) collective-permute-start(bf16[432,768]{1,0:T(8,128)(2,1)} %get-tuple-element.137), channel_id=1, source_target_pairs={{0,16},{4,20},{8,24},{12,28},{16,0},{20,4},{24,8},{28,12},{1,17},{... | collective-permute-start | bytes 1990664 | tf_op jit(solution)/shard_map/ppermute | solution.py:260
  473.0 26.9 %collective-permute-start.68 = (bf16[432,768]{1,0:T(8,128)(2,1)}, bf16[432,768]{1,0:T(8,128)(2,1)}, u32[]{:S(2)}, u32[]{:S(2)}) collective-permute-start(bf16[432,768]{1,0:T(8,128)(2,1)} %get-tuple-element.137), channel_id=1, source_target_pairs={{0,4},{4,0},{8,12},{12,8},{16,20},{20,16},{24,28},{28,24},{1,5},{5... | collective-permute-start | bytes 1990664 | tf_op jit(solution)/shard_map/ppermute | solution.py:257
  488.4 13.5 %collective-permute-start.69 = (bf16[432,768]{1,0:T(8,128)(2,1)}, bf16[432,768]{1,0:T(8,128)(2,1)}, u32[]{:S(2)}, u32[]{:S(2)}) collective-permute-start(bf16[432,768]{1,0:T(8,128)(2,1)} %collective-permute-done.67), channel_id=1, source_target_pairs={{0,4},{4,0},{8,12},{12,8},{16,20},{20,16},{24,28},{28,24},{1,5},{5... | collective-permute-start | bytes 1990664 | tf_op jit(solution)/shard_map/ppermute | solution.py:257
  (126 other events, 893.5 us)

commit v2 on v1

v2 whole, which is shorter than its diff:
```python
from functools import partial

import jax
import jax.numpy as jnp
from jax import lax
from jax.experimental import pallas as pl
from jax.experimental.pallas import tpu as pltpu
from jax.sharding import PartitionSpec as P

HEAD_DIM = 64
SCALE = HEAD_DIM**-0.5
norm_epsilon = 1e-12
F32 = jnp.float32
BF16 = jnp.bfloat16
NT = (((1,), (1,)), ((), ()))
TN = (((0,), (0,)), ((), ()))
ERFC_STEP = 0.35
ERFC_POLY = (
    0.1396196249207051,
    0.13989555693599826,
    0.11957015144655456,
    0.10661400019997494,
    -0.025870835326937874,
    0.16337919550284652,
    -0.25954764983005574,
    0.14589250699009862,
    -0.029552569422939476,
)
ORDER = ((0, 0, 0), (0, 0, 1), (1, 0, 0), (0, 1, 1), (1, 0, 1), (1, 1, 1), (0, 1, 0), (1, 1, 0))
VMEM = pl.BlockSpec(memory_space=pltpu.VMEM)
SMEM = pl.BlockSpec(memory_space=pltpu.SMEM)
ANY = pl.BlockSpec(memory_space=pl.ANY)


def mm(a, b):
    return jnp.dot(a, b, preferred_element_type=F32)


def mm_nt(a, b):
    return lax.dot_general(a, b, NT, preferred_element_type=F32)


def mm_tn(a, b):
    return lax.dot_general(a, b, TN, preferred_element_type=F32)


def params(mib):
    return pltpu.CompilerParams(vmem_limit_bytes=mib << 20)


def cost(gflop, mbytes):
    return pl.CostEstimate(
        flops=int(gflop * 1e9), bytes_accessed=int(mbytes * 1e6), transcendentals=0
    )


def shape(dims, kind):
    return jax.ShapeDtypeStruct(dims, kind)


def start_kernel(info_ref, words_ref, ents_ref, spans_ref, table_ref, bias_ref, low_ref, turn_ref, resid_ref):
    words = words_ref.shape[0]
    low_words = words_ref[...]
    spans = spans_ref[0]
    begin = spans[:, 0:1]
    end = spans[:, 1:2]
    count = ents_ref.shape[0]
    position = lax.broadcasted_iota(jnp.int32, (count, words), 1)
    inside = jnp.where(jnp.logical_and(position >= begin, position < end), 1.0, 0.0).astype(BF16)
    share = 1.0 / (end - begin).astype(F32)
    rows = ents_ref[...].astype(F32) + mm(inside, table_ref[...]) * share
    low_ents = rows.astype(BF16)
    low_ref[:words] = low_words
    low_ref[words:] = low_ents
    turn_ref[:, :words] = low_words.T
    turn_ref[:, words:] = low_ents.T
    out_b = bias_ref[...].astype(F32)
    resid_ref[:words] = low_words.astype(F32) + out_b
    resid_ref[words:] = rows + out_b


def start_rows(info, word_in, entity_in, spans, table, out_b, words, ents):
    width = word_in.shape[1]
    total = words + ents
    whole = lambda i, info_ref: (0, 0)
    return pl.pallas_call(
        start_kernel,
        grid_spec=pltpu.PrefetchScalarGridSpec(
            num_scalar_prefetch=1,
            grid=(1,),
            in_specs=[
                pl.BlockSpec((words, width), lambda i, info_ref: (info_ref[0], 0)),
                pl.BlockSpec((ents, width), lambda i, info_ref: (info_ref[0], 0)),
                pl.BlockSpec((1, ents, 2), lambda i, info_ref: (info_ref[0], 0, 0)),
                pl.BlockSpec(table.shape, whole),
                pl.BlockSpec((1, width), whole),
            ],
            out_specs=[
                pl.BlockSpec((total, width), whole),
                pl.BlockSpec((width, total), whole),
                pl.BlockSpec((total, width), whole),
            ],
        ),
        out_shape=(shape((total, width), BF16), shape((width, total), BF16), shape((total, width), F32)),
        compiler_params=params(24),
        cost_estimate=cost(0.5, 8),
        name="start_rows",
    )(info, word_in, entity_in, spans, table, out_b)


def pack_kernel(info_ref, query_ref, key_ref, value_ref, out_ref, piece_ref):
    parts = (query_ref[0], query_ref[1], key_ref[...], value_ref[...], query_ref[2], query_ref[3], out_ref[...])
    piece_ref[...] = jnp.concatenate(parts, 1)


def pack_piece(info, query_w, key_w, value_w, out_turned):
    width, gw = key_w.shape
    unit = out_turned.shape[0]
    block = lambda i, info_ref: (info_ref[2], 0)
    return pl.pallas_call(
        pack_kernel,
        grid_spec=pltpu.PrefetchScalarGridSpec(
            num_scalar_prefetch=1,
            grid=(1,),
            in_specs=[
                pl.BlockSpec((4, unit, gw), lambda i, info_ref: (0, info_ref[2], 0)),
                pl.BlockSpec((unit, gw), block),
                pl.BlockSpec((unit, gw), block),
                pl.BlockSpec((unit, gw), lambda i, info_ref: (0, 0)),
            ],
            out_specs=pl.BlockSpec((unit, 7 * gw), lambda i, info_ref: (0, 0)),
        ),
        out_shape=shape((unit, 7 * gw), BF16),
        compiler_params=params(4),
        cost_estimate=cost(0.01, 1),
        name="pack_piece",
    )(info, query_w, key_w, value_w, out_turned)


def place_chunks(near_ref, far_ref, part, unit, targets, sem):
    stride = unit * len(targets)
    copies = []
    for core, source in enumerate((near_ref, far_ref)):
        for k, (first, second, half) in enumerate(ORDER):
            code = 4 * core + 2 * first + second
            place = (lax.bitwise_xor(part, jnp.int32(code)) * 2 + half) * unit
            for t, target in enumerate(targets):
                copies.append(
                    pltpu.make_async_copy(
                        source.at[pl.ds(k * stride + t * unit, unit)],
                        target.at[pl.ds(pl.multiple_of(place, 16), unit)],
                        sem,
                    )
                )
    for copy in copies:
        copy.start()
    return copies


def split_heads(words, gw, heads, pw_ref, pe_ref, qw_s, qe_s, k_s, v_s):
    half = 2 * gw
    for h in range(heads):
        o = h * HEAD_DIM
        e = o + HEAD_DIM
        qw_s[h, :words] = pw_ref[:, o:e]
        qw_s[h, words:] = pe_ref[:, half + o : half + e]
        qe_s[h, :words] = pw_ref[:, gw + o : gw + e]
        qe_s[h, words:] = pe_ref[:, half + gw + o : half + gw + e]
        k_s[h, :words] = pw_ref[:, half + o : half + e]
        k_s[h, words:] = pe_ref[:, o:e]
        v_s[h, :words] = pw_ref[:, half + gw + o : half + gw + e]
        v_s[h, words:] = pe_ref[:, gw + o : gw + e]


def attend_body(words, gw, heads, rows_ref, b_ref, acc_ref, w_ref, pw_ref, pe_ref, ctx_ref, lt_ref, out_ref, scratch):
    half = 2 * gw
    pw_ref[...] = (mm(rows_ref[:words], w_ref[:, : 4 * gw]) + b_ref[:, : 4 * gw].astype(F32)).astype(BF16)
    pe_ref[...] = (
        mm(rows_ref[words:], w_ref[:, half : 6 * gw]) + b_ref[:, half : 6 * gw].astype(F32)
    ).astype(BF16)
    split_heads(words, gw, heads, pw_ref, pe_ref, *scratch)
    qw_s, qe_s, k_s, v_s = scratch
    block = 128

    def step(qb, carry):
        rows = pl.ds(pl.multiple_of(qb * block, block), block)
        parts = []
        for h in range(heads):
            sw = mm_nt(qw_s[h, rows], k_s[h, :words])
            se = mm_nt(qe_s[h, rows], k_s[h, words:])
            top = jnp.maximum(jnp.max(sw, 1, keepdims=True), jnp.max(se, 1, keepdims=True))
            ew = jnp.exp((sw - top) * SCALE)
            ee = jnp.exp((se - top) * SCALE)
            total = jnp.sum(ew, 1, keepdims=True) + jnp.sum(ee, 1, keepdims=True)
            inv = 1.0 / total
            parts.append(
                mm((ew * inv).astype(BF16), v_s[h, :words]) + mm((ee * inv).astype(BF16), v_s[h, words:])
            )
            logt = top * SCALE + jnp.log(total)
            lt_ref[h : h + 1, rows] = jnp.broadcast_to(logt, (block, block)).T[0:1]
        ctx_ref[rows, :] = jnp.concatenate(parts, 1).astype(BF16)
        return carry

    lax.fori_loop(0, rows_ref.shape[0] // block, step, 0)
    out_ref[...] = acc_ref[...] + mm_nt(ctx_ref[...], w_ref[:, 6 * gw :])


def attend_own_kernel(
    words, gw, heads, rows_ref, b_ref, acc_ref, query_ref, key_ref, value_ref, ow_ref,
    w_ref, pw_ref, pe_ref, ctx_ref, lt_ref, out_ref, *scratch,
):
    parts = (query_ref[0], query_ref[1], key_ref[...], value_ref[...], query_ref[2], query_ref[3], ow_ref[...].T)
    for i, part in enumerate(parts):
        w_ref[:, i * gw : (i + 1) * gw] = part
    attend_body(words, gw, heads, rows_ref, b_ref, acc_ref, w_ref, pw_ref, pe_ref, ctx_ref, lt_ref, out_ref, scratch)


def attend_far_kernel(
    words, gw, heads, info_ref, rows_ref, b_ref, acc_ref, near_ref, far_ref,
    w_ref, pw_ref, pe_ref, ctx_ref, lt_ref, out_ref, *scratch,
):
    unit = w_ref.shape[0] // 16
    for copy in place_chunks(near_ref, far_ref, info_ref[2], unit, (w_ref,), scratch[-1]):
        copy.wait()
    attend_body(
        words, gw, heads, rows_ref, b_ref, acc_ref, w_ref, pw_ref, pe_ref, ctx_ref, lt_ref, out_ref, scratch[:-1]
    )


def attend_group(info, rows_low, bias, acc, weights, words, heads):
    total, width = rows_low.shape
    ents = total - words
    gw = heads * HEAD_DIM
    outs = (
        shape((width, 7 * gw), BF16),
        shape((words, 4 * gw), BF16),
        shape((ents, 4 * gw), BF16),
        shape((total, gw), BF16),
        shape((8, total), F32),
        shape((total, width), F32),
    )
    scratch = [pltpu.VMEM((heads, total, HEAD_DIM), BF16) for _ in range(4)]
    own = len(weights) == 4
    if own:
        body = partial(attend_own_kernel, words, gw, heads)
        args = (rows_low, bias, acc) + weights
        specs = [VMEM] * 7
        alias = {2: 5}
    else:
        body = partial(attend_far_kernel, words, gw, heads)
        args = (info, rows_low, bias, acc) + weights
        specs = [SMEM] + [VMEM] * 3 + [ANY] * 2
        alias = {3: 5}
        scratch.append(pltpu.SemaphoreType.DMA)
    return pl.pallas_call(
        body,
        in_specs=specs,
        out_specs=[VMEM] * 6,
        out_shape=outs,
        scratch_shapes=scratch,
        input_output_aliases=alias,
        compiler_params=params(28),
        cost_estimate=cost(8, 10),
        name="attend_own" if own else "attend_far",
    )(*args)


def gelu_pair(x):
    size = jnp.abs(x)
    t = 1.0 / (1.0 + ERFC_STEP * size)
    poly = jnp.full_like(x, ERFC_POLY[-1])
    for c in ERFC_POLY[-2::-1]:
        poly = poly * t + c
    bell = jnp.exp(x * x * -0.5)
    tail = poly * t * bell
    below = jnp.where(x >= 0, 1.0 - tail, tail)
    return x * below, below + x * (bell * 0.3989422804014327)


def norm_parts(values):
    centered = values - jnp.mean(values, 1, keepdims=True)
    inv = lax.rsqrt(jnp.mean(centered * centered, 1, keepdims=True) + norm_epsilon)
    return centered * inv, inv


def hidden_body(low, up_ref, down_ref, b_ref, at_ref, slope_ref):
    width = up_ref.shape[1]
    total = low.shape[0]
    block = 128
    upb = b_ref[...].astype(F32)
    act = []
    for i in range(total // block):
        lo = i * block
        pre = mm(low[lo : lo + block], up_ref[...]) + upb
        value, slope = gelu_pair(pre)
        slope_ref[lo : lo + block] = slope
        value = value.astype(BF16)
        at_ref[:, lo : lo + block] = value.T
        act.append(mm(value, down_ref[...]))
    return jnp.concatenate(act, 0)


def hidden_own_kernel(
    attended_ref, vec_ref, b_ref, up_ref, down_ref, low_ref, turn_ref, at_ref, slope_ref, out_ref
):
    scaled, _ = norm_parts(attended_ref[...])
    normed = scaled * vec_ref[0:1].astype(F32) + vec_ref[1:2].astype(F32)
    low = normed.astype(BF16)
    low_ref[...] = low
    turn_ref[...] = low.T
    out_ref[...] = normed + vec_ref[2:3].astype(F32)
    out_ref[...] += hidden_body(low_ref, up_ref, down_ref, b_ref, at_ref, slope_ref)


def hidden_own(attended, vec, bias, up, down):
    total, width = attended.shape
    ff = up.shape[1]
    return pl.pallas_call(
        hidden_own_kernel,
        in_specs=[VMEM] * 5,
        out_specs=[VMEM] * 5,
        out_shape=(
            shape((total, width), BF16),
            shape((width, total), BF16),
            shape((ff, total), BF16),
            shape((total, ff), F32),
            shape((total, width), F32),
        ),
        compiler_params=params(28),
        cost_estimate=cost(6, 12),
        name="hidden_own",
    )(attended, vec, bias, up, down)


def hidden_far_kernel(
    info_ref, low_ref, b_ref, acc_ref, near_ref, far_ref, up_ref, down_ref, at_ref, slope_ref, out_ref, sem
):
    unit = up_ref.shape[0] // 16
    for copy in place_chunks(near_ref, far_ref, info_ref[3], unit, (up_ref, down_ref), sem):
        copy.wait()
    out_ref[...] = acc_ref[...] + hidden_body(low_ref, up_ref, down_ref, b_ref, at_ref, slope_ref)


def hidden_far(info, low, bias, acc, near, far):
    total, width = low.shape
    return pl.pallas_call(
        hidden_far_kernel,
        in_specs=[SMEM] + [VMEM] * 3 + [ANY] * 2,
        out_specs=[VMEM] * 5,
        out_shape=(
            shape((width, width), BF16),
            shape((width, width), BF16),
            shape((width, total), BF16),
            shape((total, width), F32),
            shape((total, width), F32),
        ),
        scratch_shapes=[pltpu.SemaphoreType.DMA],
        input_output_aliases={3: 4},
        compiler_params=params(28),
        cost_estimate=cost(6, 12),
        name="hidden_far",
    )(info, low, bias, acc, near, far)


def norm_backward(grad_in, scaled, inv_std, gain_row):
    grad_gain = jnp.sum(grad_in * scaled, axis=0, keepdims=True)
    grad_shift = jnp.sum(grad_in, axis=0, keepdims=True)
    grad_scaled = grad_in * gain_row
    mean_first = jnp.mean(grad_scaled, axis=1, keepdims=True)
    mean_second = jnp.mean(grad_scaled * scaled, axis=1, keepdims=True)
    return inv_std * (grad_scaled - mean_first - scaled * mean_second), grad_gain, grad_shift


def loss_kernel(mixed_ref, vec_ref, mask_ref, cw_ref, ce_ref, ow_ref, oe_ref, low_ref, grad_ref, sums_ref):
    words = cw_ref.shape[0]
    scaled, inv = norm_parts(mixed_ref[...])
    gain = vec_ref[3:4].astype(F32)
    output = scaled * gain + vec_ref[4:5].astype(F32)
    ow_ref[...] = output[:words].astype(BF16)
    oe_ref[...] = output[words:].astype(BF16)
    cot = jnp.concatenate([cw_ref[...].astype(F32), ce_ref[...].astype(F32)], 0)
    grad, grad_gain, grad_shift = norm_backward(mask_ref[...] * cot, scaled, inv, gain)
    grad_ref[...] = grad
    low_ref[...] = grad.astype(BF16)
    sums_ref[0:1] = grad_gain
    sums_ref[1:2] = grad_shift
    sums_ref[2:3] = jnp.sum(grad, 0, keepdims=True)


def loss_back(mixed, vec, mask, cot_words, cot_ents):
    total, width = mixed.shape
    return pl.pallas_call(
        loss_kernel,
        in_specs=[VMEM] * 5,
        out_specs=[VMEM] * 5,
        out_shape=(
            shape(cot_words.shape, BF16),
            shape(cot_ents.shape, BF16),
            shape((total, width), BF16),
            shape((total, width), F32),
            shape((8, width), F32),
        ),
        compiler_params=params(28),
        cost_estimate=cost(3, 8),
        name="loss_back",
    )(mixed, vec, mask, cot_words, cot_ents)


def store_parts(value, ref, offset, stride, unit):
    for i in range(value.shape[0] // unit):
        ref[offset + i * stride : offset + i * stride + unit] = value[i * unit : (i + 1) * unit]


def hidden_back_kernel(
    info_ref, low_ref, at_ref, slope_ref, turn_ref, up_ref, down_ref, acc_ref, send_ref, keep_ref, out_ref, b_ref,
    full_s,
):
    unit = up_ref.shape[0] // 4
    half = full_s.shape[0] // 2
    low = low_ref[...]
    store_parts(mm(at_ref[...], low).astype(BF16), full_s, unit, 2 * unit, unit)
    pre = mm_nt(low, down_ref[...]) * slope_ref[...]
    pre_low = pre.astype(BF16)
    store_parts(mm(turn_ref[...], pre_low).astype(BF16), full_s, 0, 2 * unit, unit)
    core = info_ref[1]
    send_ref[...] = full_s[pl.ds(pl.multiple_of((1 - core) * half, 128), half)]
    keep_ref[...] = full_s[pl.ds(pl.multiple_of(core * half, 128), half)]
    out_ref[...] = acc_ref[...] + mm_nt(pre_low, up_ref[...])
    b_ref[...] = jnp.broadcast_to(jnp.sum(pre_low.astype(F32), 0, keepdims=True), b_ref.shape)


def hidden_back(info, mixed_low, act_t, slope, normed_t, up, down, acc):
    total, width = mixed_low.shape
    rows = up.shape[0]
    return pl.pallas_call(
        hidden_back_kernel,
        in_specs=[SMEM] + [VMEM] * 7,
        out_specs=[VMEM] * 4,
        out_shape=(
            shape((rows, width), BF16),
            shape((rows, width), BF16),
            shape((total, width), F32),
            shape((8, up.shape[1]), F32),
        ),
        scratch_shapes=[pltpu.VMEM((2 * rows, width), BF16)],
        input_output_aliases={7: 2},
        compiler_params=params(36),
        cost_estimate=cost(8, 14),
        name="hidden_back",
    )(info, mixed_low, act_t, slope, normed_t, up, down, acc)


def norm_back_kernel(attended_ref, grad_ref, vec_ref, out_ref, low_ref, turn_ref, sums_ref):
    scaled, inv = norm_parts(attended_ref[...])
    grad, grad_gain, grad_shift = norm_backward(grad_ref[...], scaled, inv, vec_ref[0:1].astype(F32))
    out_ref[...] = grad
    low = grad.astype(BF16)
    low_ref[...] = low
    turn_ref[...] = low.T
    sums_ref[0:1] = grad_gain
    sums_ref[1:2] = grad_shift
    sums_ref[2:3] = jnp.sum(grad, 0, keepdims=True)


def norm_back(attended, grad, vec):
    total, width = attended.shape
    return pl.pallas_call(
        norm_back_kernel,
        in_specs=[VMEM] * 3,
        out_specs=[VMEM] * 4,
        out_shape=(
            shape((total, width), F32),
            shape((total, width), BF16),
            shape((width, total), BF16),
            shape((8, width), F32),
        ),
        input_output_aliases={1: 0},
        compiler_params=params(24),
        cost_estimate=cost(3, 8),
        name="norm_back",
    )(attended, grad, vec)


def attend_back_kernel(
    words, gw, heads, info_ref, rt_ref, pw_ref, pe_ref, lt_ref, ctx_ref, low_ref, turn_ref, w_ref, acc_ref,
    send_ref, keep_ref, out_ref, db_ref,
    qw_s, qe_s, k_s, v_s, dc_s, p_s, ds_s, dpw_s, dpe_s, full_s,
):
    half = 2 * gw
    total = rt_ref.shape[1]
    split_heads(words, gw, heads, pw_ref, pe_ref, qw_s, qe_s, k_s, v_s)
    grad_ctx = mm(low_ref[...], w_ref[:, 6 * gw :]).astype(BF16)
    for h in range(heads):
        dc_s[h] = grad_ctx[:, h * HEAD_DIM : (h + 1) * HEAD_DIM]
    full_s[:, 6 * gw :] = mm(turn_ref[...], ctx_ref[...]).astype(BF16)
    block = 128
    for h in range(heads):
        o = h * HEAD_DIM
        e = o + HEAD_DIM

        def step(qb, carry):
            rows = pl.ds(pl.multiple_of(qb * block, block), block)
            logt = lt_ref[h : h + 1, rows]
            pw = jnp.exp(mm_nt(k_s[h, :words], qw_s[h, rows]) * SCALE - logt)
            pe = jnp.exp(mm_nt(k_s[h, words:], qe_s[h, rows]) * SCALE - logt)
            gw_ = mm_nt(v_s[h, :words], dc_s[h, rows])
            ge_ = mm_nt(v_s[h, words:], dc_s[h, rows])
            p_s[:words, rows] = pw.astype(BF16)
            p_s[words:, rows] = pe.astype(BF16)
            dot = jnp.sum(pw * gw_, 0, keepdims=True) + jnp.sum(pe * ge_, 0, keepdims=True)
            ds_s[:words, rows] = (pw * (gw_ - dot)).astype(BF16)
            ds_s[words:, rows] = (pe * (ge_ - dot)).astype(BF16)
            return carry

        lax.fori_loop(0, total // block, step, 0)
        dv = mm(p_s[...], dc_s[h]).astype(BF16)
        dkw = (mm(ds_s[:words], qw_s[h]) * SCALE).astype(BF16)
        dke = (mm(ds_s[words:], qe_s[h]) * SCALE).astype(BF16)
        dqw = (mm_tn(ds_s[:words], k_s[h, :words]) * SCALE).astype(BF16)
        dqe = (mm_tn(ds_s[words:], k_s[h, words:]) * SCALE).astype(BF16)
        dpw_s[:, o:e] = dqw[:words]
        dpw_s[:, gw + o : gw + e] = dqe[:words]
        dpw_s[:, half + o : half + e] = dkw
        dpw_s[:, half + gw + o : half + gw + e] = dv[:words]
        dpe_s[:, o:e] = dke
        dpe_s[:, gw + o : gw + e] = dv[words:]
        dpe_s[:, half + o : half + e] = dqw[words:]
        dpe_s[:, half + gw + o : half + gw + e] = dqe[words:]
    dpw = dpw_s[...]
    dpe = dpe_s[...]
    full_s[:, :half] = mm(rt_ref[:, :words], dpw[:, :half]).astype(BF16)
    full_s[:, half : 2 * half] = (
        mm(rt_ref[:, :words], dpw[:, half:]) + mm(rt_ref[:, words:], dpe[:, :half])
    ).astype(BF16)
    full_s[:, 2 * half : 3 * half] = mm(rt_ref[:, words:], dpe[:, half:]).astype(BF16)
    core = info_ref[1]
    rows = full_s.shape[0] // 2
    send_ref[...] = full_s[pl.ds(pl.multiple_of((1 - core) * rows, 128), rows)]
    keep_ref[...] = full_s[pl.ds(pl.multiple_of(core * rows, 128), rows)]
    out_ref[:words] = acc_ref[:words] + mm_nt(dpw, w_ref[:, : 2 * half])
    out_ref[words:] = acc_ref[words:] + mm_nt(dpe, w_ref[:, half : 3 * half])
    sw = jnp.sum(dpw.astype(F32), 0, keepdims=True)
    se = jnp.sum(dpe.astype(F32), 0, keepdims=True)
    db_ref[0:1, :half] = sw[:, :half]
    db_ref[0:1, half : 2 * half] = sw[:, half:] + se[:, :half]
    db_ref[0:1, 2 * half :] = se[:, half:]


def attend_back(info, rows_t, proj_w, proj_e, log_total, ctx, low, turned, weight, acc, heads):
    width, total = rows_t.shape
    words = proj_w.shape[0]
    ents = total - words
    gw = heads * HEAD_DIM
    return pl.pallas_call(
        partial(attend_back_kernel, words, gw, heads),
        in_specs=[SMEM] + [VMEM] * 9,
        out_specs=[VMEM] * 4,
        out_shape=(
            shape((width // 2, 7 * gw), BF16),
            shape((width // 2, 7 * gw), BF16),
            shape((total, width), F32),
            shape((8, 6 * gw), F32),
        ),
        scratch_shapes=[pltpu.VMEM((heads, total, HEAD_DIM), BF16) for _ in range(5)]
        + [
            pltpu.VMEM((total, total), BF16),
            pltpu.VMEM((total, total), BF16),
            pltpu.VMEM((words, 4 * gw), BF16),
            pltpu.VMEM((ents, 4 * gw), BF16),
            pltpu.VMEM((width, 7 * gw), BF16),
        ],
        input_output_aliases={9: 2},
        compiler_params=params(36),
        cost_estimate=cost(12, 14),
        name="attend_back",
    )(info, rows_t, proj_w, proj_e, log_total, ctx, low, turned, weight, acc)


def finish_kernel(info_ref, acc_ref, spans_ref, words_ref, ents_ref, pos_ref):
    words = words_ref.shape[0]
    count = ents_ref.shape[0]
    words_ref[...] = acc_ref[:words]
    grad = acc_ref[words:]
    ents_ref[...] = grad
    spans = spans_ref[0]
    begin = spans[:, 0:1]
    end = spans[:, 1:2]
    position = lax.broadcasted_iota(jnp.int32, (count, words), 1)
    inside = jnp.where(jnp.logical_and(position >= begin, position < end), 1.0, 0.0).astype(BF16)
    scaled = grad * (1.0 / (end - begin).astype(F32))
    high = scaled.astype(BF16)
    rest = (scaled - high.astype(F32)).astype(BF16)
    pos_ref[...] = (mm_tn(inside, high) + mm_tn(inside, rest)).astype(BF16)


def finish_rows(info, acc, spans, words):
    total, width = acc.shape
    ents = total - words
    whole = lambda i, info_ref: (0, 0)
    return pl.pallas_call(
        finish_kernel,
        grid_spec=pltpu.PrefetchScalarGridSpec(
            num_scalar_prefetch=1,
            grid=(1,),
            in_specs=[
                pl.BlockSpec((total, width), whole),
                pl.BlockSpec((1, ents, 2), lambda i, info_ref: (info_ref[0], 0, 0)),
            ],
            out_specs=[
                pl.BlockSpec((words, width), whole),
                pl.BlockSpec((ents, width), whole),
                pl.BlockSpec((words, width), whole),
            ],
        ),
        out_shape=(shape((words, width), F32), shape((ents, width), F32), shape((words, width), BF16)),
        compiler_params=params(16),
        cost_estimate=cost(0.5, 6),
        name="finish_rows",
    )(info, acc, spans)


def spread_query_kernel(info_ref, a_ref, b_ref, c_ref, d_ref, query_ref, key_ref, value_ref, out_ref):
    unit, width = a_ref.shape
    gw = width // 7
    part = info_ref[4]
    for i, ref in enumerate((a_ref, b_ref, c_ref, d_ref)):
        row = lax.bitwise_xor(part, jnp.int32(i))
        rows = pl.ds(pl.multiple_of(row * unit, 64), unit)
        value = ref[...].astype(F32)
        query_ref[0, rows] = value[:, :gw]
        query_ref[1, rows] = value[:, gw : 2 * gw]
        key_ref[rows] = value[:, 2 * gw : 3 * gw]
        value_ref[rows] = value[:, 3 * gw : 4 * gw]
        query_ref[2, rows] = value[:, 4 * gw : 5 * gw]
        query_ref[3, rows] = value[:, 5 * gw : 6 * gw]
        out_ref[rows] = value[:, 6 * gw :]


def spread_query(info, pieces):
    unit, width = pieces[0].shape
    gw = width // 7
    full = 4 * unit
    return pl.pallas_call(
        spread_query_kernel,
        in_specs=[SMEM] + [VMEM] * 4,
        out_specs=[VMEM] * 4,
        out_shape=(
            shape((4, full, gw), F32),
            shape((full, gw), F32),
            shape((full, gw), F32),
            shape((full, gw), F32),
        ),
        compiler_params=params(16),
        cost_estimate=cost(0.5, 7),
        name="spread_query",
    )(info, *pieces)


def spread_hidden_kernel(info_ref, a_ref, b_ref, c_ref, d_ref, up_ref, down_ref):
    unit = a_ref.shape[0] // 2
    part = info_ref[5]
    for i, ref in enumerate((a_ref, b_ref, c_ref, d_ref)):
        row = lax.bitwise_xor(part, jnp.int32(i))
        rows = pl.ds(pl.multiple_of(row * unit, 64), unit)
        up_ref[rows] = ref[:unit].astype(F32)
        down_ref[rows] = ref[unit:].astype(F32)


def spread_hidden(info, pieces):
    rows, width = pieces[0].shape
    out = shape((2 * rows, width), F32)
    return pl.pallas_call(
        spread_hidden_kernel,
        in_specs=[SMEM] + [VMEM] * 4,
        out_specs=[VMEM] * 2,
        out_shape=(out, out),
        compiler_params=params(16),
        cost_estimate=cost(0.5, 7),
        name="spread_hidden",
    )(info, *pieces)


class Links:
    def __init__(self):
        self.dp = lax.axis_size("dp")
        self.ring = lax.axis_size("tensor")
        dp_index = lax.axis_index("dp")
        self.z = lax.axis_index("tensor")
        self.core = dp_index % 2
        self.bits = (self.dp // 2).bit_length() - 1
        self.bit = [(dp_index // (2 << k)) % 2 for k in range(self.bits)]

    def shift_z(self, v, by):
        n = self.ring
        return lax.ppermute(v, "tensor", [(i, (i + by) % n) for i in range(n)])

    def swap_z(self, v, mask):
        return lax.ppermute(v, "tensor", [(i, i ^ mask) for i in range(self.ring)])

    def swap_core(self, v):
        return lax.ppermute(v, "dp", [(i, i ^ 1) for i in range(self.dp)])

    def swap_bit(self, v, k):
        return lax.ppermute(v, "dp", [(i, i ^ (2 << k)) for i in range(self.dp)])


def take_rows(v, start, size):
    return lax.dynamic_slice_in_dim(v, start, size, 0)


def after(value, *others):
    return lax.optimization_barrier((value,) + others)[0]


def gather_step(links, piece, first, second):
    unit = piece.shape[0] // 2
    low, high = piece[:unit], piece[unit:]
    low_first = links.swap_bit(low, first)
    high_second = links.swap_bit(high, second)
    high_both = links.swap_bit(jnp.concatenate([high, high_second], 0), first)
    low_both = links.swap_bit(jnp.concatenate([low, low_first], 0), second)
    near = jnp.concatenate([piece, low_first, high_second, high_both, low_both], 0)
    return near, links.swap_core(near)


def gather_stage(links, piece, first, second):
    groups = []
    for _ in range(links.ring - 1):
        piece = links.shift_z(piece, 1)
        groups.append(gather_step(links, piece, first, second))
    return groups, piece


def add_low(a, b):
    return (a.astype(F32) + b.astype(F32)).astype(BF16)


def join_rows(mine, other, flag):
    return jnp.where(flag == 0, jnp.concatenate([mine, other], 0), jnp.concatenate([other, mine], 0))


class Reduction:
    def __init__(self, links, k):
        self.links = links
        self.k = k
        self.acc = None

    def cores(self, send, keep):
        links, flag = self.links, self.links.bit[self.k]
        total = add_low(keep, links.swap_core(send))
        unit = total.shape[0] // 2
        return take_rows(total, flag * unit, unit), take_rows(total, (1 - flag) * unit, unit)

    def planes(self, mine, theirs):
        return add_low(mine, self.links.swap_bit(theirs, self.k))

    def ring(self, quarter):
        self.acc = quarter if self.acc is None else add_low(quarter, self.links.shift_z(self.acc, 1))
        return self.acc

    def rest(self):
        for j in range(self.links.bits):
            if j != self.k:
                self.acc = add_low(self.acc, self.links.swap_bit(self.acc, j))
        return self.acc

    def spread(self):
        links = self.links
        other = links.swap_bit(self.acc, self.k)
        return self.acc, other, links.swap_core(self.acc), links.swap_core(other)


def reduce_everywhere(links, v):
    v = v + links.swap_core(v)
    for j in range(links.bits):
        v = v + links.swap_bit(v, j)
    mask = 1
    while mask < links.ring:
        v = v + links.swap_z(v, mask)
        mask *= 2
    return v


def reduce_pos(links, v):
    flags = [(links.core, links.swap_core)] + [
        (links.bit[j], partial(links.swap_bit, k=j)) for j in range(min(2, links.bits))
    ]
    for flag, swap in flags:
        half = v.shape[0] // 2
        v = add_low(take_rows(v, flag * half, half), swap(take_rows(v, (1 - flag) * half, half)))
    for j in range(2, links.bits):
        v = add_low(v, links.swap_bit(v, j))
    mask = 1
    while mask < links.ring:
        v = add_low(v, links.swap_z(v, mask))
        mask *= 2
    for flag, swap in reversed(flags):
        v = join_rows(v, swap(v), flag)
    return v


def shards(
    word_in,
    entity_in,
    entity_spans,
    word_mask,
    entity_mask,
    pos_table,
    query_w,
    query_b,
    key_w,
    value_w,
    value_b,
    out_w,
    out_b,
    norm1_gain,
    norm1_bias,
    up_w,
    up_b,
    down_w,
    down_b,
    norm2_gain,
    norm2_bias,
    cot_words,
    cot_entities,
):
    links = Links()
    n = links.ring
    z = links.z
    words = cot_words.shape[0]
    ents = cot_entities.shape[0]
    width = word_in.shape[1]
    gw = key_w.shape[1]
    heads = gw // HEAD_DIM
    ff = up_w.shape[1]
    c, b0, b1 = links.core, links.bit[0], links.bit[1]
    part_q = 4 * c + 2 * b0 + b1
    part_f = 4 * c + 2 * b1 + b0
    info = jnp.stack([z, c, part_q, part_f, 2 * c + b0, 2 * c + b1, z, z]).astype(jnp.int32)
    unit = width // 8

    out_piece = lax.dynamic_slice_in_dim(out_w, part_q * unit, unit, 1).T
    piece_q = pack_piece(info, query_w, key_w, value_w, out_piece)
    query_groups, last_q = gather_stage(links, piece_q, 0, 1)
    small = unit // 2
    up_piece = take_rows(up_w, part_f * unit, unit)
    down_piece = take_rows(down_w, part_f * unit, unit)
    piece_f = jnp.concatenate([up_piece[:small], down_piece[:small], up_piece[small:], down_piece[small:]], 0)
    piece_f = after(piece_f, last_q)
    ffn_groups, _ = gather_stage(links, piece_f, 1, 0)
    bias_own = jnp.concatenate(
        [query_b[0], query_b[1], jnp.zeros((gw,), BF16), value_b, query_b[2], query_b[3], up_b]
    )[None]
    biases = [bias_own] + [links.shift_z(bias_own, r) for r in range(1, n)]

    rows_low, rows_t, acc = start_rows(
        info, word_in, entity_in, entity_spans, pos_table, out_b[None], words, ents
    )
    weights = []
    saved = []
    for r in range(n):
        source = (query_w, key_w, value_w, out_w) if r == 0 else query_groups[r - 1]
        w, pw, pe, ctx, lt, acc = attend_group(
            info, rows_low, biases[r][:, : 6 * gw], acc, source, words, heads
        )
        weights.append(w)
        saved.append((pw, pe, lt, ctx))
    attended = acc

    vec = jnp.stack([norm1_gain, norm1_bias, down_b, norm2_gain, norm2_bias] + [down_b] * 3)
    normed_low, normed_t, act, slope, acc = hidden_own(attended, vec, biases[0][:, 6 * gw :], up_w, down_w)
    ffn = [(up_w, down_w, act, slope)]
    for r in range(1, n):
        up, down, act, slope, acc = hidden_far(
            info, normed_low, biases[r][:, 6 * gw :], acc, *ffn_groups[r - 1]
        )
        ffn.append((up, down, act, slope))
    mask_row = jnp.concatenate(
        [
            lax.dynamic_index_in_dim(word_mask, z, 0, keepdims=False),
            lax.dynamic_index_in_dim(entity_mask, z, 0, keepdims=False),
        ]
    ).astype(F32)[:, None]
    out_words, out_ents, mixed_low, acc, sums_two = loss_back(acc, vec, mask_row, cot_words, cot_entities)

    order = list(range(1, n)) + [0]
    red_f = Reduction(links, 1)
    halves_f = []
    up_sums = [None] * n
    for i, r in enumerate(order):
        up, down, act, slope = ffn[r]
        if i >= 2:
            acc = after(acc, halves_f[i - 2][1])
        send, keep, acc, sums = hidden_back(info, mixed_low, act, slope, normed_t, up, down, acc)
        up_sums[r] = sums[0]
        halves_f.append(red_f.cores(send, keep))
    acc, attended_low, attended_t, sums_one = norm_back(attended, acc, vec)

    red_q = Reduction(links, 0)
    quarters_f = [red_f.planes(*halves_f[0])]
    red_f.ring(quarters_f[0])
    acc = after(acc, quarters_f[0], halves_f[-1][1])
    halves_q = []
    quarters_q = []
    query_sums = [None] * n
    for i, r in enumerate(order):
        if i == 1:
            quarters_f.append(red_f.planes(*halves_f[1]))
            acc = after(acc, red_f.ring(quarters_f[1]))
        elif i == 2:
            quarters_f.append(red_f.planes(*halves_f[2]))
            acc = after(acc, quarters_f[2], halves_q[0][1])
        elif i == 3:
            quarters_f.append(red_f.planes(*halves_f[3]))
            acc = after(acc, red_f.ring(quarters_f[2]), quarters_f[3], halves_q[1][1])
        pw, pe, lt, ctx = saved[r]
        send, keep, acc, sums = attend_back(
            info, rows_t, pw, pe, lt, ctx, attended_low, attended_t, weights[r], acc, heads
        )
        query_sums[r] = sums[0]
        halves_q.append(red_q.cores(send, keep))
    for i in range(n):
        quarters_q.append(red_q.planes(*halves_q[i]))
    grad_words, grad_ents, grad_pos = finish_rows(info, acc, entity_spans, words)
    red_f.ring(quarters_f[3])
    for i in range(n):
        red_q.ring(quarters_q[i])
    red_f.rest()
    red_q.rest()
    grad_up, grad_down = spread_hidden(info, red_f.spread())
    grad_query_w, grad_key_w, grad_value_w, grad_out_t = spread_query(info, red_q.spread())
    pos_sum = reduce_pos(links, grad_pos).astype(F32)

    group_vec = jnp.stack([jnp.concatenate([query_sums[r], up_sums[r]]) for r in range(n)])
    group_abs = jnp.take(group_vec, (z - jnp.arange(n)) % n, axis=0)
    flat = jnp.concatenate([sums_one[:3], sums_two[:3], group_abs.reshape(-1, width)], 0)
    vec_sum = reduce_everywhere(links, flat)
    own_vec = lax.dynamic_index_in_dim(vec_sum[6:].reshape(n, 6 * gw + ff), z, 0, keepdims=False)
    grad_query_b = jnp.stack(
        [own_vec[:gw], own_vec[gw : 2 * gw], own_vec[4 * gw : 5 * gw], own_vec[5 * gw : 6 * gw]]
    )
    return (
        out_words,
        out_ents,
        grad_words,
        grad_ents,
        pos_sum,
        grad_query_w,
        grad_query_b,
        grad_key_w,
        grad_value_w,
        own_vec[3 * gw : 4 * gw],
        grad_out_t.T,
        vec_sum[2],
        vec_sum[0],
        vec_sum[1],
        grad_up,
        own_vec[6 * gw :],
        grad_down,
        vec_sum[5],
        vec_sum[3],
        vec_sum[4],
    )


def solution(mesh):
    rows = P(("dp", "tensor"), None)
    last = P(None, "tensor")
    placed = (
        P("dp", None),
        P("dp", None),
        P("dp", None, None),
        P("dp", None),
        P("dp", None),
        P(),
        P(None, None, "tensor"),
        last,
        last,
        last,
        P("tensor"),
        P("tensor", None),
        P(),
        P(),
        P(),
        last,
        P("tensor"),
        P("tensor", None),
        P(),
        P(),
        P(),
        rows,
        rows,
    )
    return jax.shard_map(
        shards,
        mesh=mesh,
        in_specs=placed,
        out_specs=(
            rows,
            rows,
            rows,
            rows,
            P(),
            P(None, None, "tensor"),
            last,
            last,
            last,
            P("tensor"),
            P("tensor", None),
            P(),
            P(),
            P(),
            last,
            P("tensor"),
            P("tensor", None),
            P(),
            P(),
            P(),
        ),
        check_vma=False,
    )
```

time: 520 us -> 516 us (level)
  matrix products: 84.7 us -> 0 us
  Pallas kernels: 74.8 us -> 147 us
  waiting for transfers between devices: 153 us -> 98.6 us
  local copies, waits for them, and re-layouts: 104 us -> 153 us
  starting transfers between devices: 52.9 us -> 64.3 us
    dot_general x39 -> x0, matrix products: 84.7 us -> none  [the longest x13 40.2 us: mm(): return jnp.dot(a, b, preferred_element_type=F32)]
    pallas_call x8 -> x23, Pallas kernels: 74.8 us -> 147 us  [the longest x4 46.5 us: attend_back(): pl.pallas_call(partial(attend_back_kernel, words, gw, heads), in_specs=[S...]
    ppermute x12 -> x0, waiting for transfers between devices: 65.5 us -> none  [next_z(): return lax.ppermute(v, 'tensor', [(i, (i + 1) % n) for i in range(n)])]
    unnamed x228 -> x331, local copies, waits for them, and re-layouts: 44.3 us -> 91.1 us
    ppermute x3 -> x15, waiting for transfers between devices: 0.01 us -> 34.6 us  [shift_z(): return lax.ppermute(v, 'tensor', [(i, (i + by) % n) for i in range(n)])]
    ppermute x24 -> x42, starting transfers between devices: 25.7 us -> 45.7 us  [swap_bit(): return lax.ppermute(v, 'dp', [(i, i ^ 2 << k) for i in range(self.dp)])]
    ppermute x0 -> x7, local copies, waits for them, and re-layouts: none -> 13.8 us  [swap_core(): return lax.ppermute(v, 'dp', [(i, i ^ 1) for i in range(self.dp)])]
    ppermute x24 -> x42, waiting for transfers between devices: 68.9 us -> 57.3 us  [swap_bit(): return lax.ppermute(v, 'dp', [(i, i ^ 2 << k) for i in range(self.dp)])]
  transfers between devices with their start and end apart: 70 -> 82, of which waited for: 28 -> 28; matrix products, arithmetic and copies ran while one was open for 21% -> 24% of each run, Pallas kernels for 15% -> 26%
where the time goes in v2:
time: 516 us; the launch traced here: 506 us
  local copies, waits for them, and re-layouts  153 us (30%)
  Pallas kernels  147 us (28%)
  waiting for transfers between devices  98.6 us (19%)
  starting transfers between devices  64.3 us (12%)
  other arithmetic  40.5 us (8%)
    unnamed x331, local copies, waits for them, and re-layouts  91.1 us
    ppermute x42, waiting for transfers between devices, swap_bit(): return lax.ppermute(v, 'dp', [(i, i ^ 2 << k) for i in range(self.dp)])  57.3 us
    pallas_call x4, Pallas kernels, attend_back(): pl.pallas_call(partial(attend_back_kernel, words, gw, heads), in_specs=[S...  46.5 us
    ppermute x42, starting transfers between devices, swap_bit(): return lax.ppermute(v, 'dp', [(i, i ^ 2 << k) for i in range(self.dp)])  45.7 us
    pallas_call x4, Pallas kernels, attend_group(): pl.pallas_call(body, in_specs=specs, out_specs=[VMEM] * 6, out_shape=outs...  44.6 us
    ppermute x15, waiting for transfers between devices, shift_z(): return lax.ppermute(v, 'tensor', [(i, (i + by) % n) for i in range(n)])  34.6 us
    convert_element_type x23, other arithmetic, add_low(): return (a.astype(F32) + b.astype(F32)).astype(BF16)  21.2 us
    pallas_call x3, Pallas kernels, hidden_far(): pl.pallas_call(hidden_far_kernel, in_specs=[SMEM] + [VMEM] * 3 + [ANY] *...  19.8 us
  transfers between devices with their start and end apart: 82, of which 28 were waited for; matrix products, arithmetic and copies ran while one was open for 24% of the time, Pallas kernels for 26%

profile of v2, /device:TPU:0, one launch (start us, length us, event | category | flops | bytes accessed | tf_op | source)
XLA Modules:
  0.0 505.9 jit_solution(11590784486261593706)
XLA Ops:
  3.0 5.1 %collective-permute-start = (bf16[1,1920]{1,0:T(2,128)(2,1)S(1)}, bf16[1,1920]{1,0:T(2,128)(2,1)S(1)}, u32[]{:S(2)}, u32[]{:S(2)}) collective-permute-start(bf16[1,1920]{1,0:T(2,128)(2,1)S(1)} %broadcast_in_dim.22), channel_id=1, source_target_pairs={{0,3},{1,0},{2,1},{3,2},{4,7},{5,4},{6,5},{7,6},{8,11},{9,8},{10,9... | collective-permute-start | bytes 11528 | tf_op jit(solution)/shard_map/ppermute | solution.py:695
  13.8 2.5 collective-permute-start.3
  21.6 8.7 %attend_own.1 = (bf16[768,1344]{1,0:T(8,128)(2,1)S(1)}, bf16[512,768]{1,0:T(8,128)(2,1)S(1)}, bf16[128,768]{1,0:T(8,128)(2,1)S(1)}, bf16[640,192]{1,0:T(8,128)(2...) custom-call(bf16[640,768]{1,0:T(8,128)(2,1)S(1)} %get-tuple-element.124.rows_ref, ...), custom_call_target="tpu_custom_call", output_to_operand_aliasing={{5}: (2, {})} | custom-call | flops 8000000000 | bytes 10000000 | tf_op jit(solution)/shard_map/attend_own/pallas_call | solution.py:255
  46.7 2.5 collective-permute-done.5
  51.5 2.8 collective-permute-done.9
  57.4 3.5 collective-permute-done.11
  87.8 2.4 collective-permute-done.23
  107.1 2.7 collective-permute-done.29
  111.9 3.4 collective-permute-done.33
  119.7 2.3 copy.125.far_ref
  126.1 11.9 %attend_far.3 = (bf16[768,1344]{1,0:T(8,128)(2,1)S(1)}, bf16[512,768]{1,0:T(8,128)(2,1)S(1)}, bf16[128,768]{1,0:T(8,128)(2,1)S(1)}, bf16[640,192]{1,0:T(8,128)(2...) custom-call(s32[8]{0:T(128)S(1)} %stack.72.info_ref, ...), custom_call_target="tpu_custom_call", output_to_operand_aliasing={{5}: (3, {})} | custom-call | flops 8000000000 | bytes 10000000 | tf_op jit(solution)/shard_map/attend_far/pallas_call | solution.py:255
  156.4 11.9 %attend_far.4 = (bf16[768,1344]{1,0:T(8,128)(2,1)S(1)}, bf16[512,768]{1,0:T(8,128)(2,1)S(1)}, bf16[128,768]{1,0:T(8,128)(2,1)S(1)}, bf16[640,192]{1,0:T(8,128)(2...) custom-call(s32[8]{0:T(128)S(1)} %stack.72.info_ref, ...), custom_call_target="tpu_custom_call", output_to_operand_aliasing={{5}: (3, {})} | custom-call | flops 8000000000 | bytes 10000000 | tf_op jit(solution)/shard_map/attend_far/pallas_call | solution.py:255
  178.6 12.1 %attend_far.5 = (bf16[768,1344]{1,0:T(8,128)(2,1)S(1)}, bf16[512,768]{1,0:T(8,128)(2,1)S(1)}, bf16[128,768]{1,0:T(8,128)(2,1)S(1)}, bf16[640,192]{1,0:T(8,128)(2...) custom-call(s32[8]{0:T(128)S(1)} %stack.72.info_ref, ...), custom_call_target="tpu_custom_call", output_to_operand_aliasing={{5}: (3, {})} | custom-call | flops 8000000000 | bytes 10000000 | tf_op jit(solution)/shard_map/attend_far/pallas_call | solution.py:255
  196.0 4.5 hidden_own.1
  200.6 7.0 %hidden_far.3 = (bf16[768,768]{1,0:T(8,128)(2,1)S(1)}, bf16[768,768]{1,0:T(8,128)(2,1)S(1)}, bf16[768,640]{1,0:T(8,128)(2,1)S(1)}, f32[640,768]{1,0:T(8,128)S(1)}, f32[640,768]{1,0:T(8,128)S(1)}) custom-call(s32[8]{0:T(128)S(1)} %stack.72.info_ref, bf16[640,768]{1,0:T(8,128)(2,1)S(1)} %get-tuple-element.130.low_ref, ...), custom_call_target="tpu_custom_call", output_to_operand_aliasing={{4}: (3, {})} | custom-call | flops 6000000000 | bytes 12000000 | tf_op jit(solution)/shard_map/hidden_far/pallas_call | solution.py:346
  207.7 6.5 %hidden_far.4 = (bf16[768,768]{1,0:T(8,128)(2,1)S(1)}, bf16[768,768]{1,0:T(8,128)(2,1)S(1)}, bf16[768,640]{1,0:T(8,128)(2,1)S(1)}, f32[640,768]{1,0:T(8,128)S(1)}, f32[640,768]{1,0:T(8,128)S(1)}) custom-call(s32[8]{0:T(128)S(1)} %stack.72.info_ref, bf16[640,768]{1,0:T(8,128)(2,1)S(1)} %get-tuple-element.130.low_ref, ...), custom_call_target="tpu_custom_call", output_to_operand_aliasing={{4}: (3, {})} | custom-call | flops 6000000000 | bytes 12000000 | tf_op jit(solution)/shard_map/hidden_far/pallas_call | solution.py:346
  214.2 6.3 %hidden_far.5 = (bf16[768,768]{1,0:T(8,128)(2,1)S(1)}, bf16[768,768]{1,0:T(8,128)(2,1)S(1)}, bf16[768,640]{1,0:T(8,128)(2,1)S(1)}, f32[640,768]{1,0:T(8,128)S(1)}, f32[640,768]{1,0:T(8,128)S(1)}) custom-call(s32[8]{0:T(128)S(1)} %stack.72.info_ref, bf16[640,768]{1,0:T(8,128)(2,1)S(1)} %get-tuple-element.130.low_ref, ...), custom_call_target="tpu_custom_call", output_to_operand_aliasing={{4}: (3, {})} | custom-call | flops 6000000000 | bytes 12000000 | tf_op jit(solution)/shard_map/hidden_far/pallas_call | solution.py:346
  222.5 2.3 loss_back.1
  224.8 4.8 hidden_back.4
  230.1 4.9 hidden_back.5
  244.0 4.3 hidden_back.6
  248.4 4.4 hidden_back.7
  259.5 10.3 %collective-permute-done.43 = bf16[384,768]{1,0:T(8,128)(2,1)S(1)} collective-permute-done((bf16[384,768]{1,0:T(8,128)(2,1)S(1)}, bf16[384,768]{1,0:T(8,128)(2,1)S(1)}, u32[]{:S(2)}, u32[]{:S(2)}) %collective-permute-start.43) | collective-permute-done | bytes 589856 | tf_op jit(solution)/shard_map/ppermute | solution.py:704
  269.8 2.4 collective-permute-done.44
  276.1 11.7 %attend_back.4 = (bf16[384,1344]{1,0:T(8,128)(2,1)S(1)}, bf16[384,1344]{1,0:T(8,128)(2,1)S(1)}, f32[640,768]{1,0:T(8,128)S(1)}, f32[8,1152]{1,0:T(8,128)S(1)}) custom-call(s32[8]{0:T(128)S(1)} %stack.72.info_ref, bf16[768,640]{1,0:T(8,128)(2,1)S(1)} %copy-done.44, bf16[512,768]{1,0:T(8,128)(2,1)S(1)} %copy-done.91, ...), custom_call_target="tpu_custom_call", output_to_operand_aliasing={{2}: (9, {})} | custom-call | flops 12000000000 | bytes 14000000 | tf_op jit(solution)/shard_map/attend_back/pallas_call | solution.py:554
  303.7 11.5 %attend_back.5 = (bf16[384,1344]{1,0:T(8,128)(2,1)S(1)}, bf16[384,1344]{1,0:T(8,128)(2,1)S(1)}, f32[640,768]{1,0:T(8,128)S(1)}, f32[8,1152]{1,0:T(8,128)S(1)}) custom-call(s32[8]{0:T(128)S(1)} %stack.72.info_ref, bf16[768,640]{1,0:T(8,128)(2,1)S(1)} %copy-done.45, bf16[512,768]{1,0:T(8,128)(2,1)S(1)} %copy-done.93, ...), custom_call_target="tpu_custom_call", output_to_operand_aliasing={{2}: (9, {})} | custom-call | flops 12000000000 | bytes 14000000 | tf_op jit(solution)/shard_map/attend_back/pallas_call | solution.py:554
  322.4 2.4 add_convert_fusion.11
  324.9 2.7 copy.132
  339.1 11.6 %attend_back.6 = (bf16[384,1344]{1,0:T(8,128)(2,1)S(1)}, bf16[384,1344]{1,0:T(8,128)(2,1)S(1)}, f32[640,768]{1,0:T(8,128)S(1)}, f32[8,1152]{1,0:T(8,128)S(1)}) custom-call(s32[8]{0:T(128)S(1)} %stack.72.info_ref, bf16[768,640]{1,0:T(8,128)(2,1)S(1)} %copy-done.46, bf16[512,768]{1,0:T(8,128)(2,1)S(1)} %copy-done.89, ...), custom_call_target="tpu_custom_call", output_to_operand_aliasing={{2}: (9, {})} | custom-call | flops 12000000000 | bytes 14000000 | tf_op jit(solution)/shard_map/attend_back/pallas_call | solution.py:554
  354.0 2.6 add_convert_fusion.9
  363.9 11.7 %attend_back.7 = (bf16[384,1344]{1,0:T(8,128)(2,1)S(1)}, bf16[384,1344]{1,0:T(8,128)(2,1)S(1)}, f32[640,768]{1,0:T(8,128)S(1)}, f32[8,1152]{1,0:T(8,128)S(1)}) custom-call(s32[8]{0:T(128)S(1)} %stack.72.info_ref, bf16[768,640]{1,0:T(8,128)(2,1)S(1)} %copy-done.47, bf16[512,768]{1,0:T(8,128)(2,1)S(1)} %copy-done.87, ...), custom_call_target="tpu_custom_call", output_to_operand_aliasing={{2}: (9, {})} | custom-call | flops 12000000000 | bytes 14000000 | tf_op jit(solution)/shard_map/attend_back/pallas_call | solution.py:554
  375.6 2.5 finish_rows.1
  382.7 2.1 add_convert_fusion.20
  390.1 11.6 %collective-permute-done.65 = bf16[192,1344]{1,0:T(8,128)(2,1)} collective-permute-done((bf16[192,1344]{1,0:T(8,128)(2,1)}, bf16[192,1344]{1,0:T(8,128)(2,1)}, u32[]{:S(2)}, u32[]{:S(2)}) %collective-permute-start.65) | collective-permute-done | bytes 516128 | tf_op jit(solution)/shard_map/ppermute | solution.py:695
  401.7 2.2 add_convert_fusion.19
  410.7 9.3 %collective-permute-done.66 = bf16[192,1344]{1,0:T(8,128)(2,1)} collective-permute-done((bf16[192,1344]{1,0:T(8,128)(2,1)}, bf16[192,1344]{1,0:T(8,128)(2,1)}, u32[]{:S(2)}, u32[]{:S(2)}) %collective-permute-start.66) | collective-permute-done | bytes 516128 | tf_op jit(solution)/shard_map/ppermute | solution.py:695
  422.9 2.5 collective-permute-start.67
  428.6 2.6 collective-permute-done.53
  432.9 4.4 collective-permute-done.67
  440.1 4.2 collective-permute-done.78
  450.0 11.9 %collective-permute-done.56 = bf16[64,768]{1,0:T(8,128)(2,1)S(1)} collective-permute-done((bf16[64,768]{1,0:T(8,128)(2,1)S(1)}, bf16[64,768]{1,0:T(8,128)(2,1)S(1)}, u32[]{:S(2)}, u32[]{:S(2)}) %collective-permute-start.56) | collective-permute-done | bytes 98336 | tf_op jit(solution)/shard_map/ppermute | solution.py:704
  464.8 4.7 collective-permute-done.73
  470.8 2.9 collective-permute-done.74
  479.1 5.2 %collective-permute-done.76 = f32[16,768]{1,0:T(8,128)} collective-permute-done((f32[16,768]{1,0:T(8,128)}, f32[16,768]{1,0:T(8,128)}, u32[]{:S(2)}, u32[]{:S(2)}) %collective-permute-start.76) | collective-permute-done | bytes 49184 | tf_op jit(solution)/shard_map/ppermute | solution.py:698
  489.7 2.6 fusion
  492.4 3.0 spread_hidden.1
  499.1 2.2 copy.140
  501.2 2.3 copy.141
  (609 shorter events, 243.2 us)
Async XLA Ops:
  3.0 34.7 %collective-permute-start = (bf16[1,1920]{1,0:T(2,128)(2,1)S(1)}, bf16[1,1920]{1,0:T(2,128)(2,1)S(1)}, u32[]{:S(2)}, u32[]{:S(2)}) collective-permute-start(bf16[1,1920]{1,0:T(2,128)(2,1)S(1)} %broadcast_in_dim.22), channel_id=1, source_target_pairs={{0,3},{1,0},{2,1},{3,2},{4,7},{5,4},{6,5},{7,6},{8,11},{9,8},{10,9... | collective-permute-start | bytes 11528 | tf_op jit(solution)/shard_map/ppermute | solution.py:695
  8.1 29.6 %collective-permute-start.1 = (bf16[1,1920]{1,0:T(2,128)(2,1)S(1)}, bf16[1,1920]{1,0:T(2,128)(2,1)}, u32[]{:S(2)}, u32[]{:S(2)}) collective-permute-start(bf16[1,1920]{1,0:T(2,128)(2,1)S(1)} %broadcast_in_dim.22), channel_id=1, source_target_pairs={{0,2},{1,3},{2,0},{3,1},{4,6},{5,7},{6,4},{7,5},{8,10},{9,11},{10,... | collective-permute-start | bytes 11528 | tf_op jit(solution)/shard_map/ppermute | solution.py:695
  8.1 31.5 %collective-permute-start.2 = (bf16[1,1920]{1,0:T(2,128)(2,1)S(1)}, bf16[1,1920]{1,0:T(2,128)(2,1)}, u32[]{:S(2)}, u32[]{:S(2)}) collective-permute-start(bf16[1,1920]{1,0:T(2,128)(2,1)S(1)} %broadcast_in_dim.22), channel_id=1, source_target_pairs={{0,1},{1,2},{2,3},{3,0},{4,5},{5,6},{6,7},{7,4},{8,9},{9,10},{10,1... | collective-permute-start | bytes 11528 | tf_op jit(solution)/shard_map/ppermute | solution.py:695
  13.8 27.8 %collective-permute-start.3 = (bf16[96,1344]{1,0:T(8,128)(2,1)}, bf16[96,1344]{1,0:T(8,128)(2,1)}, u32[]{:S(2)}, u32[]{:S(2)}) collective-permute-start(bf16[96,1344]{1,0:T(8,128)(2,1)} %pack_piece.1), channel_id=1, source_target_pairs={{0,1},{1,2},{2,3},{3,0},{4,5},{5,6},{6,7},{7,4},{8,9},{9,10},{10,1... | collective-permute-start | bytes 774152 | tf_op jit(solution)/shard_map/ppermute | solution.py:695
  49.2 15.3 %collective-permute-start.6 = (bf16[96,1344]{1,0:T(8,128)(2,1)S(1)}, bf16[96,1344]{1,0:T(8,128)(2,1)S(1)}, u32[]{:S(2)}, u32[]{:S(2)}) collective-permute-start(bf16[96,1344]{1,0:T(8,128)(2,1)S(1)} %pad_maximum_fusion.7), channel_id=1, source_target_pairs={{0,8},{4,12},{8,0},{12,4},{16,24},{20,28},{24,16},{28,20},{1,9},{5... | collective-permute-start | bytes 774152 | tf_op jit(solution)/shard_map/ppermute | solution.py:704
  49.8 14.7 %collective-permute-start.7 = (bf16[96,1344]{1,0:T(8,128)(2,1)S(1)}, bf16[96,1344]{1,0:T(8,128)(2,1)S(1)}, u32[]{:S(2)}, u32[]{:S(2)}) collective-permute-start(bf16[96,1344]{1,0:T(8,128)(2,1)S(1)} %pad_maximum_fusion.8), channel_id=1, source_target_pairs={{0,16},{4,20},{8,24},{12,28},{16,0},{20,4},{24,8},{28,12},{1,17},{... | collective-permute-start | bytes 774152 | tf_op jit(solution)/shard_map/ppermute | solution.py:704
  66.0 52.4 %collective-permute-start.8 = (bf16[384,1344]{0,1:T(8,128)(2,1)}, bf16[384,1344]{0,1:T(8,128)(2,1)}, u32[]{:S(2)}, u32[]{:S(2)}) collective-permute-start(bf16[384,1344]{0,1:T(8,128)(2,1)} %copy.124), channel_id=1, source_target_pairs={{0,4},{4,0},{8,12},{12,8},{16,20},{20,16},{24,28},{28,24},{1,5},{5... | collective-permute-start | bytes 3096584 | tf_op jit(solution)/shard_map/ppermute | solution.py:701
  73.3 77.3 %collective-permute-start.14 = (bf16[384,1344]{0,1:T(8,128)(2,1)}, bf16[384,1344]{0,1:T(8,128)(2,1)}, u32[]{:S(2)}, u32[]{:S(2)}) collective-permute-start(bf16[384,1344]{0,1:T(8,128)(2,1)} %copy.126), channel_id=1, source_target_pairs={{0,4},{4,0},{8,12},{12,8},{16,20},{20,16},{24,28},{28,24},{1,5},{5... | collective-permute-start | bytes 3096584 | tf_op jit(solution)/shard_map/ppermute | solution.py:701
  86.3 12.1 %collective-permute-start.27 = (bf16[192,768]{1,0:T(8,128)(2,1)}, bf16[192,768]{1,0:T(8,128)(2,1)}, u32[]{:S(2)}, u32[]{:S(2)}) collective-permute-start(bf16[192,768]{1,0:T(8,128)(2,1)} %collective-permute-done.21), channel_id=1, source_target_pairs={{0,1},{1,2},{2,3},{3,0},{4,5},{5,6},{6,7},{7,4},{8,9},{9,10},{10,1... | collective-permute-start | bytes 884744 | tf_op jit(solution)/shard_map/ppermute | solution.py:695
  93.8 12.1 %collective-permute-start.25 = (bf16[192,768]{1,0:T(8,128)(2,1)S(1)}, bf16[192,768]{1,0:T(8,128)(2,1)S(1)}, u32[]{:S(2)}, u32[]{:S(2)}) collective-permute-start(bf16[192,768]{1,0:T(8,128)(2,1)S(1)} %pad_maximum_fusion.2), channel_id=1, source_target_pairs={{0,8},{4,12},{8,0},{12,4},{16,24},{20,28},{24,16},{28,20},{1,9},{5... | collective-permute-start | bytes 884744 | tf_op jit(solution)/shard_map/ppermute | solution.py:704
  101.8 73.5 %collective-permute-start.20 = (bf16[384,1344]{0,1:T(8,128)(2,1)}, bf16[384,1344]{0,1:T(8,128)(2,1)}, u32[]{:S(2)}, u32[]{:S(2)}) collective-permute-start(bf16[384,1344]{0,1:T(8,128)(2,1)} %copy.128), channel_id=1, source_target_pairs={{0,4},{4,0},{8,12},{12,8},{16,20},{20,16},{24,28},{28,24},{1,5},{5... | collective-permute-start | bytes 3096584 | tf_op jit(solution)/shard_map/ppermute | solution.py:701
  109.8 90.8 %collective-permute-start.26 = (bf16[768,768]{1,0:T(8,128)(2,1)}, bf16[768,768]{1,0:T(8,128)(2,1)}, u32[]{:S(2)}, u32[]{:S(2)}) collective-permute-start(bf16[768,768]{1,0:T(8,128)(2,1)} %constant_dynamic-update-slice_fusion.15.near_ref), channel_id=1, source_target_pairs={{0,4},{4,0},{8,12},{12,8},{16,20},{20,16},{24,28},{28,24},{1,5},{5... | collective-permute-start | bytes 3538952 | tf_op jit(solution)/shard_map/ppermute | solution.py:701
  115.3 25.0 %collective-permute-start.30 = (bf16[192,768]{1,0:T(8,128)(2,1)}, bf16[192,768]{1,0:T(8,128)(2,1)}, u32[]{:S(2)}, u32[]{:S(2)}) collective-permute-start(bf16[192,768]{1,0:T(8,128)(2,1)} %pad_maximum_fusion.3), channel_id=1, source_target_pairs={{0,16},{4,20},{8,24},{12,28},{16,0},{20,4},{24,8},{28,12},{1,17},{... | collective-permute-start | bytes 884744 | tf_op jit(solution)/shard_map/ppermute | solution.py:704
  118.3 24.5 %collective-permute-start.31 = (bf16[192,768]{1,0:T(8,128)(2,1)}, bf16[192,768]{1,0:T(8,128)(2,1)}, u32[]{:S(2)}, u32[]{:S(2)}) collective-permute-start(bf16[192,768]{1,0:T(8,128)(2,1)} %pad_maximum_fusion.4), channel_id=1, source_target_pairs={{0,8},{4,12},{8,0},{12,4},{16,24},{20,28},{24,16},{28,20},{1,9},{5... | collective-permute-start | bytes 884744 | tf_op jit(solution)/shard_map/ppermute | solution.py:704
  145.5 62.2 %collective-permute-start.32 = (bf16[768,768]{1,0:T(8,128)(2,1)}, bf16[768,768]{1,0:T(8,128)(2,1)}, u32[]{:S(2)}, u32[]{:S(2)}) collective-permute-start(bf16[768,768]{1,0:T(8,128)(2,1)} %constant_dynamic-update-slice_fusion.20.near_ref), channel_id=1, source_target_pairs={{0,4},{4,0},{8,12},{12,8},{16,20},{20,16},{24,28},{28,24},{1,5},{5... | collective-permute-start | bytes 3538952 | tf_op jit(solution)/shard_map/ppermute | solution.py:701
  148.0 23.7 %collective-permute-start.36 = (bf16[192,768]{1,0:T(8,128)(2,1)}, bf16[192,768]{1,0:T(8,128)(2,1)}, u32[]{:S(2)}, u32[]{:S(2)}) collective-permute-start(bf16[192,768]{1,0:T(8,128)(2,1)} %pad_maximum_fusion.5), channel_id=1, source_target_pairs={{0,16},{4,20},{8,24},{12,28},{16,0},{20,4},{24,8},{28,12},{1,17},{... | collective-permute-start | bytes 884744 | tf_op jit(solution)/shard_map/ppermute | solution.py:704
  150.7 22.9 %collective-permute-start.37 = (bf16[192,768]{1,0:T(8,128)(2,1)}, bf16[192,768]{1,0:T(8,128)(2,1)}, u32[]{:S(2)}, u32[]{:S(2)}) collective-permute-start(bf16[192,768]{1,0:T(8,128)(2,1)} %pad_maximum_fusion.6), channel_id=1, source_target_pairs={{0,8},{4,12},{8,0},{12,4},{16,24},{20,28},{24,16},{28,20},{1,9},{5... | collective-permute-start | bytes 884744 | tf_op jit(solution)/shard_map/ppermute | solution.py:704
  175.2 39.0 %collective-permute-start.38 = (bf16[768,768]{1,0:T(8,128)(2,1)}, bf16[768,768]{1,0:T(8,128)(2,1)}, u32[]{:S(2)}, u32[]{:S(2)}) collective-permute-start(bf16[768,768]{1,0:T(8,128)(2,1)} %constant_dynamic-update-slice_fusion.25.near_ref), channel_id=1, source_target_pairs={{0,4},{4,0},{8,12},{12,8},{16,20},{20,16},{24,28},{28,24},{1,5},{5... | collective-permute-start | bytes 3538952 | tf_op jit(solution)/shard_map/ppermute | solution.py:701
  239.4 15.7 %collective-permute-start.41 = (bf16[384,768]{1,0:T(8,128)(2,1)S(1)}, bf16[384,768]{1,0:T(8,128)(2,1)S(1)}, u32[]{:S(2)}, u32[]{:S(2)}) collective-permute-start(bf16[384,768]{1,0:T(8,128)(2,1)S(1)} %constant_dynamic-slice_fusion.13), channel_id=1, source_target_pairs={{0,16},{4,20},{8,24},{12,28},{16,0},{20,4},{24,8},{28,12},{1,17},{... | collective-permute-start | bytes 1769480 | tf_op jit(solution)/shard_map/ppermute | solution.py:704
  252.8 20.4 %collective-permute-start.42 = (bf16[768,768]{1,0:T(8,128)(2,1)S(1)}, bf16[768,768]{1,0:T(8,128)(2,1)S(1)}, u32[]{:S(2)}, u32[]{:S(2)}) collective-permute-start(bf16[768,768]{1,0:T(8,128)(2,1)S(1)} %get-tuple-element.190), channel_id=1, source_target_pairs={{0,4},{4,0},{8,12},{12,8},{16,20},{20,16},{24,28},{28,24},{1,5},{5... | collective-permute-start | bytes 3538952 | tf_op jit(solution)/shard_map/ppermute | solution.py:701
  254.2 15.6 %collective-permute-start.43 = (bf16[384,768]{1,0:T(8,128)(2,1)S(1)}, bf16[384,768]{1,0:T(8,128)(2,1)S(1)}, u32[]{:S(2)}, u32[]{:S(2)}) collective-permute-start(bf16[384,768]{1,0:T(8,128)(2,1)S(1)} %constant_dynamic-slice_fusion.12), channel_id=1, source_target_pairs={{0,16},{4,20},{8,24},{12,28},{16,0},{20,4},{24,8},{28,12},{1,17},{... | collective-permute-start | bytes 1769480 | tf_op jit(solution)/shard_map/ppermute | solution.py:704
  255.3 16.8 %collective-permute-start.44 = (bf16[384,768]{1,0:T(8,128)(2,1)S(1)}, bf16[384,768]{1,0:T(8,128)(2,1)S(1)}, u32[]{:S(2)}, u32[]{:S(2)}) collective-permute-start(bf16[384,768]{1,0:T(8,128)(2,1)S(1)} %add_convert_fusion.15), channel_id=1, source_target_pairs={{0,1},{1,2},{2,3},{3,0},{4,5},{5,6},{6,7},{7,4},{8,9},{9,10},{10,1... | collective-permute-start | bytes 1769480 | tf_op jit(solution)/shard_map/ppermute | solution.py:695
  256.0 31.8 %collective-permute-start.45 = (bf16[768,768]{1,0:T(8,128)(2,1)S(1)}, bf16[768,768]{1,0:T(8,128)(2,1)S(1)}, u32[]{:S(2)}, u32[]{:S(2)}) collective-permute-start(bf16[768,768]{1,0:T(8,128)(2,1)S(1)} %get-tuple-element.196), channel_id=1, source_target_pairs={{0,4},{4,0},{8,12},{12,8},{16,20},{20,16},{24,28},{28,24},{1,5},{5... | collective-permute-start | bytes 3538952 | tf_op jit(solution)/shard_map/ppermute | solution.py:701
  273.2 49.2 %collective-permute-start.48 = (bf16[384,768]{1,0:T(8,128)(2,1)}, bf16[384,768]{1,0:T(8,128)(2,1)}, u32[]{:S(2)}, u32[]{:S(2)}) collective-permute-start(bf16[384,768]{1,0:T(8,128)(2,1)} %add_convert_fusion.13), channel_id=1, source_target_pairs={{0,1},{1,2},{2,3},{3,0},{4,5},{5,6},{6,7},{7,4},{8,9},{9,10},{10,1... | collective-permute-start | bytes 1769480 | tf_op jit(solution)/shard_map/ppermute | solution.py:695
  274.5 79.5 %collective-permute-start.49 = (bf16[384,768]{1,0:T(8,128)(2,1)}, bf16[384,768]{1,0:T(8,128)(2,1)}, u32[]{:S(2)}, u32[]{:S(2)}) collective-permute-start(bf16[384,768]{1,0:T(8,128)(2,1)} %constant_dynamic-slice_fusion.11), channel_id=1, source_target_pairs={{0,16},{4,20},{8,24},{12,28},{16,0},{20,4},{24,8},{28,12},{1,17},{... | collective-permute-start | bytes 1769480 | tf_op jit(solution)/shard_map/ppermute | solution.py:704
  290.3 32.1 %collective-permute-start.46 = (bf16[384,768]{1,0:T(8,128)(2,1)}, bf16[384,768]{1,0:T(8,128)(2,1)}, u32[]{:S(2)}, u32[]{:S(2)}) collective-permute-start(bf16[384,768]{1,0:T(8,128)(2,1)} %constant_dynamic-slice_fusion.10), channel_id=1, source_target_pairs={{0,16},{4,20},{8,24},{12,28},{16,0},{20,4},{24,8},{28,12},{1,17},{... | collective-permute-start | bytes 1769480 | tf_op jit(solution)/shard_map/ppermute | solution.py:704
  293.1 31.7 %collective-permute-start.47 = (bf16[384,1344]{0,1:T(8,128)(2,1)}, bf16[384,1344]{0,1:T(8,128)(2,1)}, u32[]{:S(2)}, u32[]{:S(2)}) collective-permute-start(bf16[384,1344]{0,1:T(8,128)(2,1)} %copy.131), channel_id=1, source_target_pairs={{0,4},{4,0},{8,12},{12,8},{16,20},{20,16},{24,28},{28,24},{1,5},{5... | collective-permute-start | bytes 3096584 | tf_op jit(solution)/shard_map/ppermute | solution.py:701
  318.5 12.3 %collective-permute-start.50 = (bf16[384,1344]{0,1:T(8,128)(2,1)}, bf16[384,1344]{0,1:T(8,128)(2,1)}, u32[]{:S(2)}, u32[]{:S(2)}) collective-permute-start(bf16[384,1344]{0,1:T(8,128)(2,1)} %copy.133), channel_id=1, source_target_pairs={{0,4},{4,0},{8,12},{12,8},{16,20},{20,16},{24,28},{28,24},{1,5},{5... | collective-permute-start | bytes 3096584 | tf_op jit(solution)/shard_map/ppermute | solution.py:701
  324.9 29.1 %collective-permute-start.77 = (bf16[384,768]{1,0:T(8,128)(2,1)}, bf16[384,768]{1,0:T(8,128)(2,1)}, u32[]{:S(2)}, u32[]{:S(2)}) collective-permute-start(bf16[384,768]{1,0:T(8,128)(2,1)} %add_convert_fusion.11), channel_id=1, source_target_pairs={{0,1},{1,2},{2,3},{3,0},{4,5},{5,6},{6,7},{7,4},{8,9},{9,10},{10,1... | collective-permute-start | bytes 1769480 | tf_op jit(solution)/shard_map/ppermute | solution.py:695
  330.1 52.6 %collective-permute-start.64 = (bf16[192,1344]{1,0:T(8,128)(2,1)}, bf16[192,1344]{1,0:T(8,128)(2,1)}, u32[]{:S(2)}, u32[]{:S(2)}) collective-permute-start(bf16[192,1344]{1,0:T(8,128)(2,1)} %constant_dynamic-slice_fusion.9), channel_id=1, source_target_pairs={{0,8},{4,12},{8,0},{12,4},{16,24},{20,28},{24,16},{28,20},{1,9},{5... | collective-permute-start | bytes 1548296 | tf_op jit(solution)/shard_map/ppermute | solution.py:704
  333.8 56.3 %collective-permute-start.63 = (bf16[192,1344]{1,0:T(8,128)(2,1)}, bf16[192,1344]{1,0:T(8,128)(2,1)}, u32[]{:S(2)}, u32[]{:S(2)}) collective-permute-start(bf16[192,1344]{1,0:T(8,128)(2,1)} %constant_dynamic-slice_fusion.8), channel_id=1, source_target_pairs={{0,8},{4,12},{8,0},{12,4},{16,24},{20,28},{24,16},{28,20},{1,9},{5... | collective-permute-start | bytes 1548296 | tf_op jit(solution)/shard_map/ppermute | solution.py:704
  353.3 51.0 %collective-permute-start.61 = (bf16[384,1344]{0,1:T(8,128)(2,1)}, bf16[384,1344]{0,1:T(8,128)(2,1)}, u32[]{:S(2)}, u32[]{:S(2)}) collective-permute-start(bf16[384,1344]{0,1:T(8,128)(2,1)} %copy.138), channel_id=1, source_target_pairs={{0,4},{4,0},{8,12},{12,8},{16,20},{20,16},{24,28},{28,24},{1,5},{5... | collective-permute-start | bytes 3096584 | tf_op jit(solution)/shard_map/ppermute | solution.py:701
  381.7 26.0 %collective-permute-start.59 = (bf16[384,1344]{0,1:T(8,128)(2,1)}, bf16[384,1344]{0,1:T(8,128)(2,1)}, u32[]{:S(2)}, u32[]{:S(2)}) collective-permute-start(bf16[384,1344]{0,1:T(8,128)(2,1)} %copy.136), channel_id=1, source_target_pairs={{0,4},{4,0},{8,12},{12,8},{16,20},{20,16},{24,28},{28,24},{1,5},{5... | collective-permute-start | bytes 3096584 | tf_op jit(solution)/shard_map/ppermute | solution.py:701
  384.8 16.9 %collective-permute-start.65 = (bf16[192,1344]{1,0:T(8,128)(2,1)}, bf16[192,1344]{1,0:T(8,128)(2,1)}, u32[]{:S(2)}, u32[]{:S(2)}) collective-permute-start(bf16[192,1344]{1,0:T(8,128)(2,1)} %add_convert_fusion.20), channel_id=1, source_target_pairs={{0,1},{1,2},{2,3},{3,0},{4,5},{5,6},{6,7},{7,4},{8,9},{9,10},{10,1... | collective-permute-start | bytes 1548296 | tf_op jit(solution)/shard_map/ppermute | solution.py:695
  388.8 36.6 %collective-permute-start.52 = (bf16[128,768]{1,0:T(8,128)(2,1)}, bf16[128,768]{1,0:T(8,128)(2,1)}, u32[]{:S(2)}, u32[]{:S(2)}) collective-permute-start(bf16[128,768]{1,0:T(8,128)(2,1)} %constant_dynamic-slice_fusion.6), channel_id=1, source_target_pairs={{0,8},{4,12},{8,0},{12,4},{16,24},{20,28},{24,16},{28,20},{1,9},{5... | collective-permute-start | bytes 589832 | tf_op jit(solution)/shard_map/ppermute | solution.py:704
  404.0 16.1 %collective-permute-start.66 = (bf16[192,1344]{1,0:T(8,128)(2,1)}, bf16[192,1344]{1,0:T(8,128)(2,1)}, u32[]{:S(2)}, u32[]{:S(2)}) collective-permute-start(bf16[192,1344]{1,0:T(8,128)(2,1)} %add_convert_fusion.19), channel_id=1, source_target_pairs={{0,1},{1,2},{2,3},{3,0},{4,5},{5,6},{6,7},{7,4},{8,9},{9,10},{10,1... | collective-permute-start | bytes 1548296 | tf_op jit(solution)/shard_map/ppermute | solution.py:695
  406.4 15.2 %collective-permute-start.62 = (bf16[192,1344]{1,0:T(8,128)(2,1)S(1)}, bf16[192,1344]{1,0:T(8,128)(2,1)S(1)}, u32[]{:S(2)}, u32[]{:S(2)}) collective-permute-start(bf16[192,1344]{1,0:T(8,128)(2,1)S(1)} %constant_dynamic-slice_fusion.3), channel_id=1, source_target_pairs={{0,8},{4,12},{8,0},{12,4},{16,24},{20,28},{24,16},{28,20},{1,9},{5... | collective-permute-start | bytes 1548296 | tf_op jit(solution)/shard_map/ppermute | solution.py:704
  409.8 23.1 %collective-permute-start.60 = (bf16[192,1344]{1,0:T(8,128)(2,1)S(1)}, bf16[192,1344]{1,0:T(8,128)(2,1)S(1)}, u32[]{:S(2)}, u32[]{:S(2)}) collective-permute-start(bf16[192,1344]{1,0:T(8,128)(2,1)S(1)} %constant_dynamic-slice_fusion.4), channel_id=1, source_target_pairs={{0,8},{4,12},{8,0},{12,4},{16,24},{20,28},{24,16},{28,20},{1,9},{5... | collective-permute-start | bytes 1548296 | tf_op jit(solution)/shard_map/ppermute | solution.py:704
  422.9 14.5 %collective-permute-start.67 = (bf16[192,1344]{1,0:T(8,128)(2,1)S(1)}, bf16[192,1344]{1,0:T(8,128)(2,1)S(1)}, u32[]{:S(2)}, u32[]{:S(2)}) collective-permute-start(bf16[192,1344]{1,0:T(8,128)(2,1)S(1)} %add_convert_fusion.18), channel_id=1, source_target_pairs={{0,1},{1,2},{2,3},{3,0},{4,5},{5,6},{6,7},{7,4},{8,9},{9,10},{10,1... | collective-permute-start | bytes 1548296 | tf_op jit(solution)/shard_map/ppermute | solution.py:695
  427.1 36.8 %collective-permute-start.72 = (f32[16,768]{1,0:T(8,128)S(1)}, f32[16,768]{1,0:T(8,128)S(1)}, u32[]{:S(2)}, u32[]{:S(2)}) collective-permute-start(f32[16,768]{1,0:T(8,128)S(1)} %pad_maximum_fusion.13), channel_id=1, source_target_pairs={{0,4},{4,0},{8,12},{12,8},{16,20},{20,16},{24,28},{28,24},{1,5},{5... | collective-permute-start | bytes 147464 | tf_op jit(solution)/shard_map/ppermute | solution.py:701
  427.2 17.0 %collective-permute-start.78 = (bf16[384,768]{1,0:T(8,128)(2,1)S(1)}, bf16[384,768]{1,0:T(8,128)(2,1)S(1)}, u32[]{:S(2)}, u32[]{:S(2)}) collective-permute-start(bf16[384,768]{1,0:T(8,128)(2,1)S(1)} %copy-done.125), channel_id=1, source_target_pairs={{0,8},{4,12},{8,0},{12,4},{16,24},{20,28},{24,16},{28,20},{1,9},{5... | collective-permute-start | bytes 1769480 | tf_op jit(solution)/shard_map/ppermute | solution.py:704
  444.4 29.4 %collective-permute-start.79 = (bf16[384,768]{1,0:T(8,128)(2,1)S(1)}, bf16[384,768]{1,0:T(8,128)(2,1)S(1)}, u32[]{:S(2)}, u32[]{:S(2)}) collective-permute-start(bf16[384,768]{1,0:T(8,128)(2,1)S(1)} %add_convert_fusion.8.a_ref), channel_id=1, source_target_pairs={{0,16},{4,20},{8,24},{12,28},{16,0},{20,4},{24,8},{28,12},{1,17},{... | collective-permute-start | bytes 1769480 | tf_op jit(solution)/shard_map/ppermute | solution.py:704
  445.1 16.8 %collective-permute-start.56 = (bf16[64,768]{1,0:T(8,128)(2,1)S(1)}, bf16[64,768]{1,0:T(8,128)(2,1)S(1)}, u32[]{:S(2)}, u32[]{:S(2)}) collective-permute-start(bf16[64,768]{1,0:T(8,128)(2,1)S(1)} %add_convert_fusion.26), channel_id=1, source_target_pairs={{0,16},{4,20},{8,24},{12,28},{16,0},{20,4},{24,8},{28,12},{1,17},{... | collective-permute-start | bytes 294920 | tf_op jit(solution)/shard_map/ppermute | solution.py:704
  448.7 38.6 %collective-permute-start.69 = (bf16[192,1344]{1,0:T(8,128)(2,1)S(1)}, bf16[192,1344]{1,0:T(8,128)(2,1)S(1)}, u32[]{:S(2)}, u32[]{:S(2)}) collective-permute-start(bf16[192,1344]{1,0:T(8,128)(2,1)S(1)} %add_convert_fusion.16.a_ref), channel_id=1, source_target_pairs={{0,8},{4,12},{8,0},{12,4},{16,24},{20,28},{24,16},{28,20},{1,9},{5... | collective-permute-start | bytes 1548296 | tf_op jit(solution)/shard_map/ppermute | solution.py:704
  462.7 11.7 %collective-permute-start.57 = (bf16[128,768]{1,0:T(8,128)(2,1)}, bf16[128,768]{1,0:T(8,128)(2,1)}, u32[]{:S(2)}, u32[]{:S(2)}) collective-permute-start(bf16[128,768]{1,0:T(8,128)(2,1)} %maximum_select_fusion.2), channel_id=1, source_target_pairs={{0,8},{4,12},{8,0},{12,4},{16,24},{20,28},{24,16},{28,20},{1,9},{5... | collective-permute-start | bytes 589832 | tf_op jit(solution)/shard_map/ppermute | solution.py:704
  473.8 18.5 %collective-permute-start.80 = (bf16[384,768]{1,0:T(8,128)(2,1)S(1)}, bf16[384,768]{1,0:T(8,128)(2,1)S(1)}, u32[]{:S(2)}, u32[]{:S(2)}) collective-permute-start(bf16[384,768]{1,0:T(8,128)(2,1)S(1)} %add_convert_fusion.8.a_ref), channel_id=1, source_target_pairs={{0,4},{4,0},{8,12},{12,8},{16,20},{20,16},{24,28},{28,24},{1,5},{5... | collective-permute-start | bytes 1769480 | tf_op jit(solution)/shard_map/ppermute | solution.py:701
  473.8 18.5 %collective-permute-start.81 = (bf16[384,768]{1,0:T(8,128)(2,1)S(1)}, bf16[384,768]{1,0:T(8,128)(2,1)S(1)}, u32[]{:S(2)}, u32[]{:S(2)}) collective-permute-start(bf16[384,768]{1,0:T(8,128)(2,1)S(1)} %collective-permute-done.79.b_ref), channel_id=1, source_target_pairs={{0,4},{4,0},{8,12},{12,8},{16,20},{20,16},{24,28},{28,24},{1,5},{5... | collective-permute-start | bytes 1769480 | tf_op jit(solution)/shard_map/ppermute | solution.py:701
  476.4 13.3 %collective-permute-start.58 = (bf16[256,768]{1,0:T(8,128)(2,1)}, bf16[256,768]{1,0:T(8,128)(2,1)}, u32[]{:S(2)}, u32[]{:S(2)}) collective-permute-start(bf16[256,768]{1,0:T(8,128)(2,1)} %maximum_select_fusion.1), channel_id=1, source_target_pairs={{0,4},{4,0},{8,12},{12,8},{16,20},{20,16},{24,28},{28,24},{1,5},{5... | collective-permute-start | bytes 1179656 | tf_op jit(solution)/shard_map/ppermute | solution.py:701
  (183 other events, 934.9 us)

commit v3 on v1

v3 whole, which is shorter than its diff:
```python
from functools import partial

import jax
import jax.numpy as jnp
from jax import lax
from jax.experimental import pallas as pl
from jax.experimental.pallas import tpu as pltpu
from jax.sharding import PartitionSpec as P

HEAD_DIM = 64
SCALE = HEAD_DIM**-0.5
norm_epsilon = 1e-12
F32 = jnp.float32
BF16 = jnp.bfloat16
NT = (((1,), (1,)), ((), ()))
TN = (((0,), (0,)), ((), ()))
ERFC_STEP = 0.35
ERFC_POLY = (
    0.1396196249207051,
    0.13989555693599826,
    0.11957015144655456,
    0.10661400019997494,
    -0.025870835326937874,
    0.16337919550284652,
    -0.25954764983005574,
    0.14589250699009862,
    -0.029552569422939476,
)
CODES = (0, 2, 1, 3, 4, 6, 5, 7)
TILE = 16
VMEM = pl.BlockSpec(memory_space=pltpu.VMEM)
SMEM = pl.BlockSpec(memory_space=pltpu.SMEM)
HBM = pl.BlockSpec(memory_space=pltpu.HBM)
DMA = pltpu.SemaphoreType.DMA


def mm(a, b):
    return jnp.dot(a, b, preferred_element_type=F32)


def mm_nt(a, b):
    return lax.dot_general(a, b, NT, preferred_element_type=F32)


def mm_tn(a, b):
    return lax.dot_general(a, b, TN, preferred_element_type=F32)


def params(mib):
    return pltpu.CompilerParams(vmem_limit_bytes=mib << 20)


def cost(gflop, mbytes):
    return pl.CostEstimate(
        flops=int(gflop * 1e9), bytes_accessed=int(mbytes * 1e6), transcendentals=0
    )


def shape(dims, kind):
    return jax.ShapeDtypeStruct(dims, kind)


def start(pairs, sem):
    copies = [pltpu.make_async_copy(source, target, sem) for source, target in pairs]
    for copy in copies:
        copy.start()
    return copies


def wait(copies):
    for copy in copies:
        copy.wait()


def rows_at(first, size):
    return pl.ds(pl.multiple_of(first, TILE), size)


def place(pieces, part, unit, targets):
    pairs = []
    for piece, code in zip(pieces, CODES):
        row = lax.bitwise_xor(part, jnp.int32(code)) * unit
        for t, target in enumerate(targets):
            pairs.append((piece.at[pl.ds(t * unit, unit)], target.at[rows_at(row, unit)]))
    return pairs


def blocks_out(full_s, part, unit, first, send_ref, near_ref, pass_ref):
    second = 3 - first
    order = (0, second, first, 3)
    pairs = []
    for i, code in enumerate(order):
        mine = lax.bitwise_xor(part, jnp.int32(code)) * unit
        other = lax.bitwise_xor(part, jnp.int32(code + 4)) * unit
        keep = near_ref if i < 2 else pass_ref
        pairs.append((full_s.at[rows_at(other, unit)], send_ref.at[pl.ds(i * unit, unit)]))
        pairs.append((full_s.at[rows_at(mine, unit)], keep.at[pl.ds((i % 2) * unit, unit)]))
    return pairs


def pack_kernel(
    gw, info_ref, qb_ref, vb_ref, ub_ref, query_ref, key_ref, value_ref, ow_ref, up_ref, down_ref,
    w_ref, piece_ref, ffn_ref, w_s, sem,
):
    parts = (query_ref.at[0], query_ref.at[1], key_ref, value_ref, query_ref.at[2], query_ref.at[3], ow_ref)
    reads = start([(v, w_s.at[pl.ds(i * gw, gw)]) for i, v in enumerate(parts)], sem.at[0])
    part = info_ref[2]
    unit = ffn_ref.shape[0] // 2
    ffn = start(
        [(v.at[rows_at(part * unit, unit)], ffn_ref.at[pl.ds(i * unit, unit)]) for i, v in enumerate((up_ref, down_ref))],
        sem.at[1],
    )
    qb = qb_ref[...].astype(F32)
    none = jnp.zeros((1, gw), F32)
    first = jnp.concatenate([qb[0:1], qb[1:2], none, vb_ref[...].astype(F32)], 1)
    second = jnp.concatenate([qb[2:3], qb[3:4], none, none], 1)
    spare = w_s.shape[0] - 7 * gw
    row = lax.broadcasted_iota(jnp.int32, (spare, 4 * gw), 0)
    rows = jnp.where(row == 0, first, jnp.where(row == 1, second, jnp.where(row == 2, ub_ref[...].astype(F32), 0.0)))
    w_s[7 * gw :] = rows.astype(BF16)
    wait(reads)
    size = piece_ref.shape[0]
    piece = start([(w_s.at[rows_at(part * size, size)], piece_ref)], sem.at[2])
    whole = start([(w_s, w_ref)], sem.at[3])
    wait(piece)
    wait(ffn)
    wait(whole)


def pack(info, query_b, value_b, up_b, query_t, key_t, value_t, out_w, up_w, down_w, rows):
    gw, width = key_t.shape
    unit = up_w.shape[0] // 8
    return pl.pallas_call(
        partial(pack_kernel, gw),
        in_specs=[SMEM] + [VMEM] * 3 + [HBM] * 6,
        out_specs=[HBM] * 3,
        out_shape=(shape((rows, width), BF16), shape((rows // 8, width), BF16), shape((2 * unit, width), BF16)),
        scratch_shapes=[pltpu.VMEM((rows, width), BF16), DMA((4,))],
        compiler_params=params(12),
        cost_estimate=cost(0.01, 8),
        name="pack",
    )(info, query_b, value_b, up_b, query_t, key_t, value_t, out_w, up_w, down_w)


def start_kernel(info_ref, words_ref, ents_ref, spans_ref, table_ref, bias_ref, low_ref, resid_ref, w_s, e_s, t_s, sem):
    words, count = w_s.shape[0], e_s.shape[0]
    z = info_ref[0]
    ents = start(
        [(ents_ref.at[rows_at(z * count, count)], e_s), (table_ref, t_s)],
        sem.at[0],
    )
    reads = start([(words_ref.at[rows_at(z * words, words)], w_s)], sem.at[1])
    spans = spans_ref[z]
    begin = spans[:, 0:1]
    end = spans[:, 1:2]
    position = lax.broadcasted_iota(jnp.int32, (count, words), 1)
    inside = jnp.where(jnp.logical_and(position >= begin, position < end), 1.0, 0.0).astype(BF16)
    share = 1.0 / (end - begin).astype(F32)
    out_b = bias_ref[...].astype(F32)
    wait(ents)
    rows = e_s[...].astype(F32) + mm(inside, t_s[...]) * share
    low_ref[words:] = rows.astype(BF16)
    resid_ref[words:] = rows + out_b
    wait(reads)
    low_ref[:words] = w_s[...]
    resid_ref[:words] = w_s[...].astype(F32) + out_b


def start_rows(info, word_in, entity_in, spans, table, out_b, words, ents):
    width = word_in.shape[1]
    total = words + ents
    return pl.pallas_call(
        start_kernel,
        in_specs=[SMEM, HBM, HBM, VMEM, HBM, VMEM],
        out_specs=[VMEM] * 2,
        out_shape=(shape((total, width), BF16), shape((total, width), F32)),
        scratch_shapes=[
            pltpu.VMEM((words, width), BF16),
            pltpu.VMEM((ents, width), BF16),
            pltpu.VMEM(table.shape, BF16),
            DMA((2,)),
        ],
        compiler_params=params(16),
        cost_estimate=cost(0.5, 6),
        name="start_rows",
    )(info, word_in, entity_in, spans, table, out_b)


def split_heads(words, gw, heads, pw_ref, pe_ref, qw_s, qe_s, k_s, v_s):
    half = 2 * gw
    for h in range(heads):
        o = h * HEAD_DIM
        e = o + HEAD_DIM
        qw_s[h, :words] = pw_ref[:, o:e]
        qw_s[h, words:] = pe_ref[:, half + o : half + e]
        qe_s[h, :words] = pw_ref[:, gw + o : gw + e]
        qe_s[h, words:] = pe_ref[:, half + gw + o : half + gw + e]
        k_s[h, :words] = pw_ref[:, half + o : half + e]
        k_s[h, words:] = pe_ref[:, o:e]
        v_s[h, :words] = pw_ref[:, half + gw + o : half + gw + e]
        v_s[h, words:] = pe_ref[:, gw + o : gw + e]


def attend_kernel(words, gw, heads, count, info_ref, rows_ref, acc_ref, *refs):
    pieces = refs[:count]
    pw_ref, pe_ref, ctx_ref, lt_ref, bias_ref, out_ref, w_s, pw_s, pe_s, ctx_s, qw_s, qe_s, k_s, v_s, sem = refs[count:]
    half = 2 * gw
    if count == 1:
        wait(start([(pieces[0], w_s)], sem.at[0]))
    else:
        wait(start(place(pieces, info_ref[2], w_s.shape[0] // 8, (w_s,)), sem.at[0]))
    rows_b = w_s[7 * gw : 7 * gw + TILE]
    bias_ref[...] = rows_b
    rows_b = rows_b.astype(F32)
    bias_e = jnp.concatenate([rows_b[0:1, half:], rows_b[1:2, :half]], 1)
    pw_s[...] = (mm_nt(rows_ref[:words], w_s[: 4 * gw]) + rows_b[0:1]).astype(BF16)
    pe_s[...] = (mm_nt(rows_ref[words:], w_s[half : 6 * gw]) + bias_e).astype(BF16)
    saves = start([(pw_s, pw_ref), (pe_s, pe_ref)], sem.at[1])
    split_heads(words, gw, heads, pw_s, pe_s, qw_s, qe_s, k_s, v_s)
    block = 128

    def step(qb, carry):
        rows = pl.ds(pl.multiple_of(qb * block, block), block)
        parts = []
        for h in range(heads):
            sw = mm_nt(qw_s[h, rows], k_s[h, :words])
            se = mm_nt(qe_s[h, rows], k_s[h, words:])
            top = jnp.maximum(jnp.max(sw, 1, keepdims=True), jnp.max(se, 1, keepdims=True))
            ew = jnp.exp((sw - top) * SCALE)
            ee = jnp.exp((se - top) * SCALE)
            total = jnp.sum(ew, 1, keepdims=True) + jnp.sum(ee, 1, keepdims=True)
            inv = 1.0 / total
            parts.append(
                mm((ew * inv).astype(BF16), v_s[h, :words]) + mm((ee * inv).astype(BF16), v_s[h, words:])
            )
            logt = top * SCALE + jnp.log(total)
            lt_ref[h : h + 1, rows] = jnp.broadcast_to(logt, (block, block)).T[0:1]
        ctx_s[rows, :] = jnp.concatenate(parts, 1).astype(BF16)
        return carry

    lax.fori_loop(0, rows_ref.shape[0] // block, step, 0)
    last = start([(ctx_s, ctx_ref)], sem.at[2])
    out_ref[...] = acc_ref[...] + mm(ctx_s[...], w_s[6 * gw : 7 * gw])
    wait(saves)
    wait(last)


def attend(info, rows_low, acc, pieces, words, heads, rows):
    total, width = rows_low.shape
    ents = total - words
    gw = heads * HEAD_DIM
    count = len(pieces)
    return pl.pallas_call(
        partial(attend_kernel, words, gw, heads, count),
        in_specs=[SMEM] + [VMEM] * 2 + [HBM] * count,
        out_specs=[HBM] * 3 + [VMEM] * 3,
        out_shape=(
            shape((words, 4 * gw), BF16),
            shape((ents, 4 * gw), BF16),
            shape((total, gw), BF16),
            shape((8, total), F32),
            shape((TILE, width), BF16),
            shape((total, width), F32),
        ),
        scratch_shapes=[
            pltpu.VMEM((rows, width), BF16),
            pltpu.VMEM((words, 4 * gw), BF16),
            pltpu.VMEM((ents, 4 * gw), BF16),
            pltpu.VMEM((total, gw), BF16),
        ]
        + [pltpu.VMEM((heads, total, HEAD_DIM), BF16) for _ in range(4)]
        + [DMA((3,))],
        input_output_aliases={2: 5},
        compiler_params=params(24),
        cost_estimate=cost(8, 6),
        name="attend_own" if count == 1 else "attend_far",
    )(info, rows_low, acc, *pieces)


def gelu_pair(x):
    size = jnp.abs(x)
    t = 1.0 / (1.0 + ERFC_STEP * size)
    poly = jnp.full_like(x, ERFC_POLY[-1])
    for c in ERFC_POLY[-2::-1]:
        poly = poly * t + c
    bell = jnp.exp(x * x * -0.5)
    tail = poly * t * bell
    below = jnp.where(x >= 0, 1.0 - tail, tail)
    return x * below, below + x * (bell * 0.3989422804014327)


def norm_parts(values):
    centered = values - jnp.mean(values, 1, keepdims=True)
    inv = lax.rsqrt(jnp.mean(centered * centered, 1, keepdims=True) + norm_epsilon)
    return centered * inv, inv


def hidden_kernel(n, info_ref, attended_ref, vec_ref, wm_ref, em_ref, cw_ref, ce_ref, *refs):
    bias_refs, refs = refs[:n], refs[n:]
    up_own, down_own = refs[:2]
    pieces, refs = refs[2 : 2 + 8 * (n - 1)], refs[2 + 8 * (n - 1) :]
    low_ref, turn_ref, at_ref, slope_ref, ow_ref, oe_ref, mixed_ref, grad_ref, sums_ref, up_s, down_s, acc_s, b_s, sem = refs
    total, width = attended_ref.shape
    unit = width // 8
    part = info_ref[2]
    reads = [start([(up_own, up_s.at[0]), (down_own, down_s.at[0])], sem.at[0])]
    for r in range(1, n):
        reads.append(start(place(pieces[8 * (r - 1) : 8 * r], part, unit, (up_s.at[r], down_s.at[r])), sem.at[r]))
    for r in range(n):
        b_s[r] = bias_refs[r][2:3].astype(F32)
    scaled, _ = norm_parts(attended_ref[...])
    normed = scaled * vec_ref[0:1].astype(F32) + vec_ref[1:2].astype(F32)
    low = normed.astype(BF16)
    low_ref[...] = low
    turn_ref[...] = low.T
    acc_s[...] = normed + vec_ref[2:3].astype(F32)
    block = 128

    def group(r):
        for lo in range(0, total, block):
            pre = mm(low_ref[lo : lo + block], up_s[r]) + b_s[r]
            value, slope = gelu_pair(pre)
            slope_ref[r, lo : lo + block] = slope
            value = value.astype(BF16)
            at_ref[r, :, lo : lo + block] = value.T
            acc_s[lo : lo + block] += mm(value, down_s[r])

    for r in range(n):
        wait(reads[r])
        group(r)

    words = cw_ref.shape[0]
    z = info_ref[0]
    scaled, inv = norm_parts(acc_s[...])
    gain = vec_ref[3:4].astype(F32)
    output = scaled * gain + vec_ref[4:5].astype(F32)
    ow_ref[...] = output[:words].astype(BF16)
    oe_ref[...] = output[words:].astype(BF16)

    def column(ref, size):
        return jnp.broadcast_to(ref[pl.ds(z, 1), :].astype(F32), (128, size)).T[:, 0:1]

    cot = jnp.concatenate(
        [
            column(wm_ref, words) * cw_ref[...].astype(F32),
            column(em_ref, total - words) * ce_ref[...].astype(F32),
        ],
        0,
    )
    grad, grad_gain, grad_shift = norm_backward(cot, scaled, inv, gain)
    grad_ref[...] = grad
    mixed_ref[...] = grad.astype(BF16)
    sums_ref[0:1] = grad_gain
    sums_ref[1:2] = grad_shift
    sums_ref[2:3] = jnp.sum(grad, 0, keepdims=True)
    sums_ref[3:] = jnp.zeros((5, width), F32)


def hidden(info, attended, vec, word_mask, entity_mask, cot_words, cot_ents, biases, own, groups):
    total, width = attended.shape
    n = len(biases)
    pieces = [v for g in groups for v in g]
    return pl.pallas_call(
        partial(hidden_kernel, n),
        in_specs=[SMEM] + [VMEM] * (6 + n) + [HBM] * (2 + len(pieces)),
        out_specs=[VMEM] * 9,
        out_shape=(
            shape((total, width), BF16),
            shape((width, total), BF16),
            shape((n, width, total), BF16),
            shape((n, total, width), F32),
            shape(cot_words.shape, BF16),
            shape(cot_ents.shape, BF16),
            shape((total, width), BF16),
            shape((total, width), F32),
            shape((8, width), F32),
        ),
        scratch_shapes=[
            pltpu.VMEM((n, width, width), BF16),
            pltpu.VMEM((n, width, width), BF16),
            pltpu.VMEM((total, width), F32),
            pltpu.VMEM((n, 1, width), F32),
            DMA((n,)),
        ],
        compiler_params=params(48),
        cost_estimate=cost(22, 20),
        name="hidden",
    )(info, attended, vec, word_mask, entity_mask, cot_words, cot_ents, *biases, *own, *pieces)


def norm_backward(grad_in, scaled, inv_std, gain_row):
    grad_gain = jnp.sum(grad_in * scaled, axis=0, keepdims=True)
    grad_shift = jnp.sum(grad_in, axis=0, keepdims=True)
    grad_scaled = grad_in * gain_row
    mean_first = jnp.mean(grad_scaled, axis=1, keepdims=True)
    mean_second = jnp.mean(grad_scaled * scaled, axis=1, keepdims=True)
    return inv_std * (grad_scaled - mean_first - scaled * mean_second), grad_gain, grad_shift


def hidden_back_kernel(r, first, count, info_ref, low_ref, at_ref, slope_ref, turn_ref, acc_ref, *refs):
    pieces = refs[:count]
    send_ref, near_ref, pass_ref, out_ref, b_ref, up_s, down_s, full_s, sem = refs[count:]
    unit = up_s.shape[0] // 8
    part = info_ref[2]
    if count == 2:
        reads = start([(pieces[0], up_s), (pieces[1], down_s)], sem.at[0])
    else:
        reads = start(place(pieces, part, unit, (up_s, down_s)), sem.at[0])
    low = low_ref[...]
    grad_down = mm(at_ref[r], low).astype(BF16)
    for i in range(8):
        full_s[(2 * i + 1) * unit : (2 * i + 2) * unit] = grad_down[i * unit : (i + 1) * unit]
    wait(reads)
    pre_low = (mm_nt(low, down_s[...]) * slope_ref[r]).astype(BF16)
    grad_up = mm(turn_ref[...], pre_low).astype(BF16)
    for i in range(8):
        full_s[2 * i * unit : (2 * i + 1) * unit] = grad_up[i * unit : (i + 1) * unit]
    writes = start(blocks_out(full_s, part, 2 * unit, first, send_ref, near_ref, pass_ref), sem.at[1])
    out_ref[...] = acc_ref[...] + mm_nt(pre_low, up_s[...])
    b_ref[...] = jnp.broadcast_to(jnp.sum(pre_low.astype(F32), 0, keepdims=True), b_ref.shape)
    wait(writes)


def hidden_back(info, r, first, mixed_low, act_t, slope, normed_t, acc, pieces):
    total, width = mixed_low.shape
    count = len(pieces)
    return pl.pallas_call(
        partial(hidden_back_kernel, r, first, count),
        in_specs=[SMEM] + [VMEM] * 5 + [HBM] * count,
        out_specs=[HBM] * 3 + [VMEM] * 2,
        out_shape=(
            shape((width, width), BF16),
            shape((width // 2, width), BF16),
            shape((width // 2, width), BF16),
            shape((total, width), F32),
            shape((8, width), F32),
        ),
        scratch_shapes=[
            pltpu.VMEM((width, width), BF16),
            pltpu.VMEM((width, width), BF16),
            pltpu.VMEM((2 * width, width), BF16),
            DMA((2,)),
        ],
        input_output_aliases={5: 3},
        compiler_params=params(32),
        cost_estimate=cost(7, 8),
        name="hidden_back",
    )(info, mixed_low, act_t, slope, normed_t, acc, *pieces)


def norm_back_kernel(attended_ref, grad_ref, vec_ref, sums_ref, out_ref, low_ref, all_ref):
    scaled, inv = norm_parts(attended_ref[...])
    grad, grad_gain, grad_shift = norm_backward(grad_ref[...], scaled, inv, vec_ref[0:1].astype(F32))
    out_ref[...] = grad
    low_ref[...] = grad.astype(BF16)
    all_ref[...] = sums_ref[...]
    all_ref[3:4] = grad_gain
    all_ref[4:5] = grad_shift
    all_ref[5:6] = jnp.sum(grad, 0, keepdims=True)


def norm_back(attended, grad, vec, sums):
    total, width = attended.shape
    return pl.pallas_call(
        norm_back_kernel,
        in_specs=[VMEM] * 4,
        out_specs=[VMEM] * 3,
        out_shape=(shape((total, width), F32), shape((total, width), BF16), shape((8, width), F32)),
        input_output_aliases={1: 0},
        compiler_params=params(24),
        cost_estimate=cost(2, 6),
        name="norm_back",
    )(attended, grad, vec, sums)


def attend_back_kernel(words, gw, heads, first, count, info_ref, rows_ref, lt_ref, low_ref, up_ref, acc_ref, *refs):
    pw_ref, pe_ref, ctx_ref = refs[:3]
    pieces = refs[3 : 3 + count]
    (
        send_ref, near_ref, pass_ref, out_ref,
        w_s, pw_s, pe_s, ctx_s, qw_s, qe_s, k_s, v_s, dc_s, p_s, ds_s, dpw_s, dpe_s, full_s, sem,
    ) = refs[3 + count :]
    half = 2 * gw
    total = rows_ref.shape[0]
    part = info_ref[2]
    size = w_s.shape[0] // 8
    saved = start([(pw_ref, pw_s), (pe_ref, pe_s)], sem.at[0])
    if count == 1:
        reads = start([(pieces[0], w_s)], sem.at[1])
    else:
        reads = start(place(pieces, part, size, (w_s,)), sem.at[1])
    last = start([(ctx_ref, ctx_s)], sem.at[2])
    wait(saved)
    split_heads(words, gw, heads, pw_s, pe_s, qw_s, qe_s, k_s, v_s)
    wait(reads)
    grad_ctx = mm_nt(low_ref[...], w_s[6 * gw : 7 * gw]).astype(BF16)
    for h in range(heads):
        dc_s[h] = grad_ctx[:, h * HEAD_DIM : (h + 1) * HEAD_DIM]
    wait(last)
    full_s[6 * gw : 7 * gw] = mm_tn(ctx_s[...], low_ref[...]).astype(BF16)
    block = 128
    for h in range(heads):
        o = h * HEAD_DIM
        e = o + HEAD_DIM

        def step(qb, carry):
            rows = pl.ds(pl.multiple_of(qb * block, block), block)
            logt = lt_ref[h : h + 1, rows]
            pw = jnp.exp(mm_nt(k_s[h, :words], qw_s[h, rows]) * SCALE - logt)
            pe = jnp.exp(mm_nt(k_s[h, words:], qe_s[h, rows]) * SCALE - logt)
            gw_ = mm_nt(v_s[h, :words], dc_s[h, rows])
            ge_ = mm_nt(v_s[h, words:], dc_s[h, rows])
            p_s[:words, rows] = pw.astype(BF16)
            p_s[words:, rows] = pe.astype(BF16)
            dot = jnp.sum(pw * gw_, 0, keepdims=True) + jnp.sum(pe * ge_, 0, keepdims=True)
            ds_s[:words, rows] = (pw * (gw_ - dot)).astype(BF16)
            ds_s[words:, rows] = (pe * (ge_ - dot)).astype(BF16)
            return carry

        lax.fori_loop(0, total // block, step, 0)
        dv = mm(p_s[...], dc_s[h]).astype(BF16)
        dkw = (mm(ds_s[:words], qw_s[h]) * SCALE).astype(BF16)
        dke = (mm(ds_s[words:], qe_s[h]) * SCALE).astype(BF16)
        dqw = (mm_tn(ds_s[:words], k_s[h, :words]) * SCALE).astype(BF16)
        dqe = (mm_tn(ds_s[words:], k_s[h, words:]) * SCALE).astype(BF16)
        dpw_s[:, o:e] = dqw[:words]
        dpw_s[:, gw + o : gw + e] = dqe[:words]
        dpw_s[:, half + o : half + e] = dkw
        dpw_s[:, half + gw + o : half + gw + e] = dv[:words]
        dpe_s[:, o:e] = dke
        dpe_s[:, gw + o : gw + e] = dv[words:]
        dpe_s[:, half + o : half + e] = dqw[words:]
        dpe_s[:, half + gw + o : half + gw + e] = dqe[words:]
    dpw = dpw_s[...]
    dpe = dpe_s[...]
    rows_w = rows_ref[:words]
    rows_e = rows_ref[words:]
    full_s[:half] = mm_tn(dpw[:, :half], rows_w).astype(BF16)
    full_s[half : 2 * half] = (mm_tn(dpw[:, half:], rows_w) + mm_tn(dpe[:, :half], rows_e)).astype(BF16)
    full_s[2 * half : 3 * half] = mm_tn(dpe[:, half:], rows_e).astype(BF16)
    sw = jnp.sum(dpw.astype(F32), 0, keepdims=True)
    se = jnp.sum(dpe.astype(F32), 0, keepdims=True)
    sum_a = jnp.concatenate([sw[:, :half], sw[:, half:] + se[:, :half]], 1)
    sum_b = jnp.concatenate([se[:, half:], jnp.zeros((1, half), F32)], 1)
    spare = w_s.shape[0] - 7 * gw
    row = lax.broadcasted_iota(jnp.int32, (spare, 2 * half), 0)
    sums = jnp.where(row == 0, sum_a, jnp.where(row == 1, sum_b, jnp.where(row == 2, up_ref[0:1], 0.0)))
    full_s[7 * gw :] = sums.astype(BF16)
    writes = start(blocks_out(full_s, part, size, first, send_ref, near_ref, pass_ref), sem.at[3])
    out_ref[:words] = acc_ref[:words] + mm(dpw, w_s[: 2 * half])
    out_ref[words:] = acc_ref[words:] + mm(dpe, w_s[half : 3 * half])
    wait(writes)


def attend_back(info, first, rows_low, saved, low, up_sums, acc, pieces, words, heads, rows):
    total, width = rows_low.shape
    pw, pe, ctx, lt = saved
    ents = total - words
    gw = heads * HEAD_DIM
    count = len(pieces)
    return pl.pallas_call(
        partial(attend_back_kernel, words, gw, heads, first, count),
        in_specs=[SMEM] + [VMEM] * 5 + [HBM] * (3 + count),
        out_specs=[HBM] * 3 + [VMEM],
        out_shape=(
            shape((rows // 2, width), BF16),
            shape((rows // 4, width), BF16),
            shape((rows // 4, width), BF16),
            shape((total, width), F32),
        ),
        scratch_shapes=[
            pltpu.VMEM((rows, width), BF16),
            pltpu.VMEM((words, 4 * gw), BF16),
            pltpu.VMEM((ents, 4 * gw), BF16),
            pltpu.VMEM((total, gw), BF16),
        ]
        + [pltpu.VMEM((heads, total, HEAD_DIM), BF16) for _ in range(5)]
        + [
            pltpu.VMEM((total, total), BF16),
            pltpu.VMEM((total, total), BF16),
            pltpu.VMEM((words, 4 * gw), BF16),
            pltpu.VMEM((ents, 4 * gw), BF16),
            pltpu.VMEM((rows, width), BF16),
            DMA((4,)),
        ],
        input_output_aliases={5: 3},
        compiler_params=params(32),
        cost_estimate=cost(11, 8),
        name="attend_back",
    )(info, rows_low, lt, low, up_sums, acc, pw, pe, ctx, *pieces)


def finish_kernel(info_ref, acc_ref, spans_ref, words_ref, ents_ref, send_ref, near_ref, pass_ref, pos_s, sem):
    words = words_ref.shape[0]
    count = ents_ref.shape[0]
    grad = acc_ref[words:]
    ents_ref[...] = grad
    spans = spans_ref[info_ref[0]]
    begin = spans[:, 0:1]
    end = spans[:, 1:2]
    position = lax.broadcasted_iota(jnp.int32, (count, words), 1)
    inside = jnp.where(jnp.logical_and(position >= begin, position < end), 1.0, 0.0).astype(BF16)
    scaled = grad * (1.0 / (end - begin).astype(F32))
    high = scaled.astype(BF16)
    rest = (scaled - high.astype(F32)).astype(BF16)
    pos_s[...] = (mm_tn(inside, high) + mm_tn(inside, rest)).astype(BF16)
    writes = start(blocks_out(pos_s, info_ref[2], words // 8, 2, send_ref, near_ref, pass_ref), sem)
    words_ref[...] = acc_ref[:words]
    wait(writes)


def finish_rows(info, acc, spans, words):
    total, width = acc.shape
    ents = total - words
    return pl.pallas_call(
        finish_kernel,
        in_specs=[SMEM] + [VMEM] * 2,
        out_specs=[VMEM] * 2 + [HBM] * 3,
        out_shape=(
            shape((words, width), F32),
            shape((ents, width), F32),
            shape((words // 2, width), BF16),
            shape((words // 4, width), BF16),
            shape((words // 4, width), BF16),
        ),
        scratch_shapes=[pltpu.VMEM((words, width), BF16), DMA],
        compiler_params=params(16),
        cost_estimate=cost(0.5, 6),
        name="finish_rows",
    )(info, acc, spans)


def spread_query_kernel(info_ref, *refs):
    pieces = refs[:8]
    query_ref, key_ref, value_ref, out_ref, qb_ref, vb_ref, ub_ref, s, sem = refs[8:]
    wait(start(place(pieces, info_ref[2], s.shape[0] // 8, (s,)), sem))
    gw = key_ref.shape[0]
    for i, k in ((0, 0), (1, 1), (2, 4), (3, 5)):
        query_ref[i] = s[k * gw : (k + 1) * gw].astype(F32)
    key_ref[...] = s[2 * gw : 3 * gw].astype(F32)
    value_ref[...] = s[3 * gw : 4 * gw].astype(F32)
    out_ref[...] = s[6 * gw : 7 * gw].astype(F32)
    rows = s[7 * gw : 7 * gw + TILE].astype(F32)
    qb_ref[0:1] = rows[0:1, :gw]
    qb_ref[1:2] = rows[0:1, gw : 2 * gw]
    qb_ref[2:3] = rows[1:2, :gw]
    qb_ref[3:4] = rows[1:2, gw : 2 * gw]
    vb_ref[...] = rows[0:1, 3 * gw :]
    ub_ref[...] = rows[2:3]


def spread_query(info, pieces, gw):
    unit, width = pieces[0].shape
    flat = shape((gw, width), F32)
    return pl.pallas_call(
        spread_query_kernel,
        in_specs=[SMEM] + [HBM] * 8,
        out_specs=[VMEM] * 7,
        out_shape=(
            shape((4, gw, width), F32), flat, flat, flat,
            shape((4, gw), F32), shape((1, gw), F32), shape((1, width), F32),
        ),
        scratch_shapes=[pltpu.VMEM((8 * unit, width), BF16), DMA],
        compiler_params=params(16),
        cost_estimate=cost(0.5, 7),
        name="spread_query",
    )(info, *pieces)


def spread_hidden_kernel(info_ref, *refs):
    pieces = refs[:8]
    up_ref, down_ref, up_s, down_s, sem = refs[8:]
    wait(start(place(pieces, info_ref[2], up_ref.shape[0] // 8, (up_s, down_s)), sem))
    up_ref[...] = up_s[...].astype(F32)
    down_ref[...] = down_s[...].astype(F32)


def spread_hidden(info, pieces):
    rows, width = pieces[0].shape
    out = shape((4 * rows, width), F32)
    return pl.pallas_call(
        spread_hidden_kernel,
        in_specs=[SMEM] + [HBM] * 8,
        out_specs=[VMEM] * 2,
        out_shape=(out, out),
        scratch_shapes=[pltpu.VMEM((4 * rows, width), BF16)] * 2 + [DMA],
        compiler_params=params(16),
        cost_estimate=cost(0.5, 7),
        name="spread_hidden",
    )(info, *pieces)


def spread_pos_kernel(info_ref, *refs):
    pieces = refs[:8]
    pos_ref, s, sem = refs[8:]
    wait(start(place(pieces, info_ref[2], s.shape[0] // 8, (s,)), sem))
    pos_ref[...] = s[...].astype(F32)


def spread_pos(info, pieces):
    rows, width = pieces[0].shape
    return pl.pallas_call(
        spread_pos_kernel,
        in_specs=[SMEM] + [HBM] * 8,
        out_specs=VMEM,
        out_shape=shape((8 * rows, width), F32),
        scratch_shapes=[pltpu.VMEM((8 * rows, width), BF16), DMA],
        compiler_params=params(8),
        cost_estimate=cost(0.5, 3),
        name="spread_pos",
    )(info, *pieces)


class Links:
    def __init__(self):
        self.dp = lax.axis_size("dp")
        self.ring = lax.axis_size("tensor")
        dp_index = lax.axis_index("dp")
        self.z = lax.axis_index("tensor")
        self.core = dp_index % 2
        self.bits = (self.dp // 2).bit_length() - 1
        self.bit = [(dp_index // (2 << k)) % 2 for k in range(self.bits)]

    def shift_z(self, v, by):
        n = self.ring
        return lax.ppermute(v, "tensor", [(i, (i + by) % n) for i in range(n)])

    def swap_z(self, v, mask):
        return lax.ppermute(v, "tensor", [(i, i ^ mask) for i in range(self.ring)])

    def swap(self, v, code):
        return lax.ppermute(v, "dp", [(i, i ^ code) for i in range(self.dp)])

    def swap_core(self, v):
        return self.swap(v, 1)

    def swap_code(self, v, code):
        return self.swap(v, ((code >> 1) & 1) * 2 + (code & 1) * 4)


def after(value, *others):
    return lax.optimization_barrier((value,) + others)[0]


def gather_group(links, piece, first):
    second = 3 - first
    over = {first: links.swap_code(piece, first), second: links.swap_code(piece, second)}
    near = (piece, over[2], over[1], links.swap_code(over[first], second))
    return near + tuple(links.swap_core(v) for v in near)


def add_low(*parts):
    total = parts[0].astype(F32)
    for part in parts[1:]:
        total = total + part.astype(F32)
    return total.astype(BF16)


class Blocks:
    def __init__(self, links, first, send, near, far):
        self.links, self.first, self.near, self.far = links, first, near, far
        self.unit = near.shape[0] // 2
        self.got = links.swap_core(send)

    def one(self):
        u = self.unit
        value = add_low(self.far, self.got[2 * u :])
        self.a = self.links.swap_code(value, self.first)
        return value

    def two(self):
        u = self.unit
        value = add_low(self.near[u:], self.got[u : 2 * u], self.a[u:])
        self.parts = (self.a[:u], self.links.swap_code(value, 3 - self.first))
        return value

    def direct(self):
        u = self.unit
        first, second = self.first, 3 - self.first
        a = add_low(self.far[:u], self.got[2 * u : 3 * u])
        b = add_low(self.far[u:], self.got[3 * u :])
        c = add_low(self.near[u:], self.got[u : 2 * u])
        links = self.links
        self.parts = (links.swap_code(b, 3), links.swap_code(a, first), links.swap_code(c, second))

    def rest(self, *more):
        u = self.unit
        value = add_low(self.near[:u], self.got[:u], *self.parts, *more)
        for j in range(2, self.links.bits):
            value = add_low(value, self.links.swap(value, 2 << j))
        return value


def spread_all(links, value):
    near = (value, links.swap_code(value, 2), links.swap_code(value, 1), links.swap_code(value, 3))
    return near + tuple(links.swap_core(v) for v in near)


def reduce_everywhere(links, v):
    v = v + links.swap_core(v)
    for j in range(links.bits):
        v = v + links.swap(v, 2 << j)
    mask = 1
    while mask < links.ring:
        v = v + links.swap_z(v, mask)
        mask *= 2
    return v


def shards(
    word_in,
    entity_in,
    entity_spans,
    word_mask,
    entity_mask,
    pos_table,
    query_w,
    query_b,
    key_w,
    value_w,
    value_b,
    out_w,
    out_b,
    norm1_gain,
    norm1_bias,
    up_w,
    up_b,
    down_w,
    down_b,
    norm2_gain,
    norm2_bias,
    cot_words,
    cot_entities,
):
    links = Links()
    n = links.ring
    z = links.z
    words = cot_words.shape[0]
    ents = cot_entities.shape[0]
    width = word_in.shape[1]
    gw = key_w.shape[1]
    heads = gw // HEAD_DIM
    rows = -(-(7 * gw + 3) // (8 * TILE)) * 8 * TILE
    part = 4 * links.core + 2 * links.bit[0] + links.bit[1]
    info = jnp.stack([z, links.core, part, part]).astype(jnp.int32)

    own_w, piece_q, piece_f = pack(
        info, query_b, value_b[None], up_b[None], jnp.swapaxes(query_w, 1, 2), key_w.T, value_w.T, out_w, up_w, down_w, rows
    )
    shifted = []
    for _ in range(n - 1):
        piece_q = links.shift_z(piece_q, 1)
        shifted.append(piece_q)
    piece_f = after(piece_f, shifted[0])
    query_groups = [(own_w,)] + [gather_group(links, v, 1 + i % 2) for i, v in enumerate(shifted)]
    ffn_groups = []
    for i in range(n - 1):
        piece_f = links.shift_z(piece_f, 1)
        ffn_groups.append(gather_group(links, piece_f, 2 - i % 2))

    rows_low, acc = start_rows(info, word_in, entity_in, entity_spans, pos_table, out_b[None], words, ents)
    saved = []
    biases = []
    for r in range(n):
        pw, pe, ctx, lt, bias, acc = attend(info, rows_low, acc, query_groups[r], words, heads, rows)
        saved.append((pw, pe, ctx, lt))
        biases.append(bias)
    attended = acc

    vec = jnp.stack([norm1_gain, norm1_bias, down_b, norm2_gain, norm2_bias] + [down_b] * 3)
    _, normed_t, act_t, slope, out_words, out_ents, mixed_low, acc, sums = hidden(
        info, attended, vec, word_mask, entity_mask, cot_words, cot_entities, biases, (up_w, down_w), ffn_groups
    )

    order = list(range(1, n)) + [0]
    ffn_pieces = [(up_w, down_w)] + ffn_groups
    blocks_f = []
    up_sums = [None] * n
    for i, r in enumerate(order):
        first = 2 - i % 2
        send, near, far, acc, up_sums[r] = hidden_back(
            info, r, first, mixed_low, act_t, slope, normed_t, acc, ffn_pieces[r]
        )
        blocks_f.append(Blocks(links, first, send, near, far))
        if i:
            acc = after(acc, blocks_f[i - 1].one())
    acc, attended_low, sums = norm_back(attended, acc, vec, sums)

    last = n - 1
    blocks_q = []
    sent_f = []
    sent_q = []
    acc = after(acc, blocks_f[last].one(), *[b.two() for b in blocks_f[: n // 2]])
    pieces_f = None
    for i, r in enumerate(order):
        first = 1 + i % 2
        send, near, far, acc = attend_back(
            info, first, rows_low, saved[r], attended_low, up_sums[r], acc, query_groups[r], words, heads, rows
        )
        blocks_q.append(Blocks(links, first, send, near, far))
        if i == 0:
            ready = [b.two() for b in blocks_f[n // 2 :]]
            done = [b.rest() for b in blocks_f[: n // 2]]
            sent_f += [links.shift_z(v, -order[j]) for j, v in enumerate(done)]
            acc = after(acc, *ready, *done)
        elif i == 1:
            done = [b.rest() for b in blocks_f[n // 2 : last]]
            sent_f += [links.shift_z(v, -order[n // 2 + j]) for j, v in enumerate(done)]
            total_sums = reduce_everywhere(links, sums)
            acc = after(acc, *done, blocks_q[0].one())
        elif i == 2:
            value = blocks_f[last].rest(*sent_f)
            pieces_f = spread_all(links, value)
            acc = after(acc, value, blocks_q[0].two(), blocks_q[1].one(), total_sums)
    grad_words, grad_ents, *pos_blocks = finish_rows(info, acc, entity_spans, words)
    blocks_p = Blocks(links, 2, *pos_blocks)

    done = blocks_q[0].rest()
    sent_q.append(links.shift_z(done, -order[0]))
    blocks_q[1].two()
    blocks_q[2].direct()
    blocks_q[3].direct()
    blocks_p.direct()
    for j in range(1, last):
        sent_q.append(links.shift_z(blocks_q[j].rest(), -order[j]))
    grad_up, grad_down = spread_hidden(info, pieces_f)
    value = blocks_q[last].rest(*sent_q)
    pieces_q = spread_all(links, value)
    pos = blocks_p.rest()
    mask = 1
    while mask < n:
        pos = add_low(pos, links.swap_z(pos, mask))
        mask *= 2
    pieces_p = spread_all(links, pos)
    grad_query_t, grad_key_t, grad_value_t, grad_out, grad_query_b, grad_value_b, grad_up_b = spread_query(
        info, pieces_q, gw
    )
    pos_sum = spread_pos(info, pieces_p)
    return (
        out_words,
        out_ents,
        grad_words,
        grad_ents,
        pos_sum,
        jnp.swapaxes(grad_query_t, 1, 2),
        grad_query_b,
        grad_key_t.T,
        grad_value_t.T,
        grad_value_b[0],
        grad_out,
        total_sums[5],
        total_sums[3],
        total_sums[4],
        grad_up,
        grad_up_b[0],
        grad_down,
        total_sums[2],
        total_sums[0],
        total_sums[1],
    )


def solution(mesh):
    rows = P(("dp", "tensor"), None)
    last = P(None, "tensor")
    placed = (
        P("dp", None),
        P("dp", None),
        P("dp", None, None),
        P("dp", None),
        P("dp", None),
        P(),
        P(None, None, "tensor"),
        last,
        last,
        last,
        P("tensor"),
        P("tensor", None),
        P(),
        P(),
        P(),
        last,
        P("tensor"),
        P("tensor", None),
        P(),
        P(),
        P(),
        rows,
        rows,
    )
    return jax.shard_map(
        shards,
        mesh=mesh,
        in_specs=placed,
        out_specs=(
            rows,
            rows,
            rows,
            rows,
            P(),
            P(None, None, "tensor"),
            last,
            last,
            last,
            P("tensor"),
            P("tensor", None),
            P(),
            P(),
            P(),
            last,
            P("tensor"),
            P("tensor", None),
            P(),
            P(),
            P(),
        ),
        check_vma=False,
    )
```

time: 520 us -> 459 us (0.88); the launches traced: 510 us -> 455 us
  Pallas kernels: 74.8 us -> 180 us
  matrix products: 84.7 us -> 0 us
  local copies, waits for them, and re-layouts: 104 us -> 49.4 us
  starting transfers between devices: 52.9 us -> 83.9 us
  waiting for transfers between devices: 153 us -> 125 us
  other arithmetic: 37.8 us -> 14 us
    pallas_call x8 -> x20, Pallas kernels: 74.8 us -> 180 us  [the longest x4 54.4 us: attend_back(): pl.pallas_call(partial(attend_back_kernel, words, gw, heads, first, count...]
    dot_general x39 -> x0, matrix products: 84.7 us -> none  [the longest x13 40.2 us: mm(): return jnp.dot(a, b, preferred_element_type=F32)]
    ppermute x63 -> x96, waiting for transfers between devices: 137 us -> 67.2 us  [swap(): return lax.ppermute(v, 'dp', [(i, i ^ code) for i in range(self.dp)])]
    ppermute x63 -> x96, starting transfers between devices: 40.8 us -> 68.7 us  [swap(): return lax.ppermute(v, 'dp', [(i, i ^ code) for i in range(self.dp)])]
    ppermute x3 -> x12, waiting for transfers between devices: 0.01 us -> 26 us  [shift_z(): return lax.ppermute(v, 'tensor', [(i, (i + by) % n) for i in range(n)])]
    ppermute x4, waiting for transfers between devices: 15.9 us -> 31.6 us  [swap_z(): return lax.ppermute(v, 'tensor', [(i, i ^ mask) for i in range(self.ring)])]
    slice x18 -> x1, local copies, waits for them, and re-layouts: 15.3 us -> 0.64 us  [shards(): total_sums[1]]
    dynamic_slice x24 -> x0, local copies, waits for them, and re-layouts: 12.3 us -> none  [the longest x23 11.6 us: take_rows(): return lax.dynamic_slice_in_dim(v, start, size, 0)]
  transfers between devices with their start and end apart: 70 -> 112, of which waited for: 28 -> 25; matrix products, arithmetic and copies ran while one was open for 21% -> 3% of each run, Pallas kernels for 15% -> 30%
where the time goes in v3:
time: 459 us; the launch traced here: 455 us
  Pallas kernels  180 us (39%)
  waiting for transfers between devices  125 us (27%)
  starting transfers between devices  83.9 us (18%)
  local copies, waits for them, and re-layouts  49.4 us (11%)
  other arithmetic  14 us (3%)
    ppermute x96, starting transfers between devices, swap(): return lax.ppermute(v, 'dp', [(i, i ^ code) for i in range(self.dp)])  68.7 us
    ppermute x96, waiting for transfers between devices, swap(): return lax.ppermute(v, 'dp', [(i, i ^ code) for i in range(self.dp)])  67.2 us
    pallas_call x4, Pallas kernels, attend_back(): pl.pallas_call(partial(attend_back_kernel, words, gw, heads, first, count...  54.4 us
    unnamed x223, local copies, waits for them, and re-layouts  47.3 us
    pallas_call x4, Pallas kernels, attend(): pl.pallas_call(partial(attend_kernel, words, gw, heads, count), in_specs=...  43.9 us
    pallas_call x4, Pallas kernels, hidden_back(): pl.pallas_call(partial(hidden_back_kernel, r, first, count), in_specs=[SM...  32.6 us
    ppermute x4, waiting for transfers between devices, swap_z(): return lax.ppermute(v, 'tensor', [(i, i ^ mask) for i in range(self.ring)])  31.6 us
    pallas_call x1, Pallas kernels, hidden(): pl.pallas_call(partial(hidden_kernel, n), in_specs=[SMEM] + [VMEM] * (6 +...  29.1 us
  transfers between devices with their start and end apart: 112, of which 25 were waited for; matrix products, arithmetic and copies ran while one was open for 3% of the time, Pallas kernels for 30%

profile of v3, /device:TPU:0, one launch (start us, length us, event | category | flops | bytes accessed | tf_op | source)
XLA Modules:
  0.0 455.0 jit_solution(14446208787262353416)
XLA Ops:
  12.6 3.1 collective-permute-start
  15.6 8.5 %collective-permute-done.refs_0_.refs_3_ = bf16[176,768]{1,0:T(8,128)(2,1)S(1)} collective-permute-done((bf16[176,768]{1,0:T(8,128)(2,1)S(1)}, bf16[176,768]{1,0:T(8,128)(2,1)S(1)}, u32[]{:S(2)}, u32[]{:S(2)}) %collective-permute-start) | collective-permute-done | bytes 270368 | tf_op jit(solution)/shard_map/ppermute | solution.py:726
  29.1 6.1 %collective-permute-done.8.refs_0_.refs_3_ = bf16[176,768]{1,0:T(8,128)(2,1)S(1)} collective-permute-done((bf16[176,768]{1,0:T(8,128)(2,1)S(1)}, bf16[176,768]{1,0:T(8,128)(2,1)S(1)}, u32[]{:S(2)}, u32[]{:S(2)}) %collective-permute-start.8) | collective-permute-done | bytes 270368 | tf_op jit(solution)/shard_map/ppermute | solution.py:726
  39.7 1.9 collective-permute-done.24.refs_6_.refs_0_
  41.6 4.1 collective-permute-done.16.refs_0_.refs_3_
  55.1 5.4 %collective-permute-done.32.refs_14_.refs_0_ = bf16[192,768]{1,0:T(8,128)(2,1)} collective-permute-done((bf16[192,768]{1,0:T(8,128)(2,1)S(1)}, bf16[192,768]{1,0:T(8,128)(2,1)}, u32[]{:S(2)}, u32[]{:S(2)}) %collective-permute-start.32) | collective-permute-done | bytes 294944 | tf_op jit(solution)/shard_map/ppermute | solution.py:726
  68.6 1.8 collective-permute-done.17.refs_1_.refs_4_
  79.2 2.3 collective-permute-start.27
  82.7 10.3 %attend_own.1 = (bf16[512,768]{1,0:T(8,128)(2,1)S(1)}, bf16[128,768]{1,0:T(8,128)(2,1)S(1)}, bf16[640,192]{1,0:T(8,128)(2,1)S(1)}, f32[8,640]{1,0:T(8,128)S(1)},...) custom-call(s32[4]{0:T(128)S(1)} %pad_add_fusion.info_ref, ...), custom_call_target="tpu_custom_call", output_to_operand_aliasing={{5}: (2, {})} | custom-call | flops 8000000000 | bytes 6000000 | tf_op jit(solution)/shard_map/attend_own/pallas_call | solution.py:253
  106.6 11.3 %attend_far.3 = (bf16[512,768]{1,0:T(8,128)(2,1)S(1)}, bf16[128,768]{1,0:T(8,128)(2,1)S(1)}, bf16[640,192]{1,0:T(8,128)(2,1)S(1)}, f32[8,640]{1,0:T(8,128)S(1)},...) custom-call(s32[4]{0:T(128)S(1)} %pad_add_fusion.info_ref, ...), custom_call_target="tpu_custom_call", output_to_operand_aliasing={{5}: (2, {})} | custom-call | flops 8000000000 | bytes 6000000 | tf_op jit(solution)/shard_map/attend_far/pallas_call | solution.py:253
  121.2 11.2 %attend_far.4 = (bf16[512,768]{1,0:T(8,128)(2,1)S(1)}, bf16[128,768]{1,0:T(8,128)(2,1)S(1)}, bf16[640,192]{1,0:T(8,128)(2,1)S(1)}, f32[8,640]{1,0:T(8,128)S(1)},...) custom-call(s32[4]{0:T(128)S(1)} %pad_add_fusion.info_ref, ...), custom_call_target="tpu_custom_call", output_to_operand_aliasing={{5}: (2, {})} | custom-call | flops 8000000000 | bytes 6000000 | tf_op jit(solution)/shard_map/attend_far/pallas_call | solution.py:253
  134.5 11.2 %attend_far.5 = (bf16[512,768]{1,0:T(8,128)(2,1)S(1)}, bf16[128,768]{1,0:T(8,128)(2,1)S(1)}, bf16[640,192]{1,0:T(8,128)(2,1)S(1)}, f32[8,640]{1,0:T(8,128)S(1)},...) custom-call(s32[4]{0:T(128)S(1)} %pad_add_fusion.info_ref, ...), custom_call_target="tpu_custom_call", output_to_operand_aliasing={{5}: (2, {})} | custom-call | flops 8000000000 | bytes 6000000 | tf_op jit(solution)/shard_map/attend_far/pallas_call | solution.py:253
  148.9 29.1 %hidden.1 = (bf16[640,768]{1,0:T(8,128)(2,1)}, bf16[768,640]{1,0:T(8,128)(2,1)}, bf16[4,768,640]{2,1,0:T(8,128)(2,1)}, f32[4,640,768]{2,1,0:T(8,128)}, bf16[512,...) custom-call(s32[4]{0:T(128)S(1)} %pad_add_fusion.info_ref, ...), custom_call_target="tpu_custom_call" | custom-call | flops 22000001024 | bytes 20000000 | tf_op jit(solution)/shard_map/hidden/pallas_call | solution.py:363
  179.6 3.3 copy-done.79
  182.9 2.1 copy-done.80
  187.4 8.7 %hidden_back.4 = (bf16[768,768]{1,0:T(8,128)(2,1)S(1)}, bf16[384,768]{1,0:T(8,128)(2,1)S(1)}, bf16[384,768]{1,0:T(8,128)(2,1)S(1)}, f32[640,768]{1,0:T(8,128)S(1)}, f32[8,768]{1,0:T(8,128)S(1)}) custom-call(s32[4]{0:T(128)S(1)} %pad_add_fusion.info_ref, bf16[640,768]{1,0:T(8,128)(2,1)S(1)} %copy-done.83, ...), custom_call_target="tpu_custom_call", output_to_operand_aliasing={{3}: (5, {})} | custom-call | flops 7000000000 | bytes 8000000 | tf_op jit(solution)/shard_map/hidden_back/pallas_call | solution.py:427
  196.5 7.9 %hidden_back.5 = (bf16[768,768]{1,0:T(8,128)(2,1)S(1)}, bf16[384,768]{1,0:T(8,128)(2,1)S(1)}, bf16[384,768]{1,0:T(8,128)(2,1)S(1)}, f32[640,768]{1,0:T(8,128)S(1)}, f32[8,768]{1,0:T(8,128)S(1)}) custom-call(s32[4]{0:T(128)S(1)} %pad_add_fusion.info_ref, bf16[640,768]{1,0:T(8,128)(2,1)S(1)} %copy-done.83, ...), custom_call_target="tpu_custom_call", output_to_operand_aliasing={{3}: (5, {})} | custom-call | flops 7000000000 | bytes 8000000 | tf_op jit(solution)/shard_map/hidden_back/pallas_call | solution.py:427
  207.5 9.4 %hidden_back.6 = (bf16[768,768]{1,0:T(8,128)(2,1)S(1)}, bf16[384,768]{1,0:T(8,128)(2,1)S(1)}, bf16[384,768]{1,0:T(8,128)(2,1)S(1)}, f32[640,768]{1,0:T(8,128)S(1)}, f32[8,768]{1,0:T(8,128)S(1)}) custom-call(s32[4]{0:T(128)S(1)} %pad_add_fusion.info_ref, bf16[640,768]{1,0:T(8,128)(2,1)S(1)} %copy-done.83, ...), custom_call_target="tpu_custom_call", output_to_operand_aliasing={{3}: (5, {})} | custom-call | flops 7000000000 | bytes 8000000 | tf_op jit(solution)/shard_map/hidden_back/pallas_call | solution.py:427
  219.7 6.7 %hidden_back.7 = (bf16[768,768]{1,0:T(8,128)(2,1)S(1)}, bf16[384,768]{1,0:T(8,128)(2,1)S(1)}, bf16[384,768]{1,0:T(8,128)(2,1)S(1)}, f32[640,768]{1,0:T(8,128)S(1)}, f32[8,768]{1,0:T(8,128)S(1)}) custom-call(s32[4]{0:T(128)S(1)} %pad_add_fusion.info_ref, bf16[640,768]{1,0:T(8,128)(2,1)S(1)} %copy-done.83, ...), custom_call_target="tpu_custom_call", output_to_operand_aliasing={{3}: (5, {})} | custom-call | flops 7000000000 | bytes 8000000 | tf_op jit(solution)/shard_map/hidden_back/pallas_call | solution.py:427
  226.6 7.4 %collective-permute-done.53 = bf16[384,768]{1,0:T(8,128)(2,1)S(1)} collective-permute-done((bf16[384,768]{1,0:T(8,128)(2,1)S(1)}, bf16[384,768]{1,0:T(8,128)(2,1)S(1)}, u32[]{:S(2)}, u32[]{:S(2)}) %collective-permute-start.53) | collective-permute-done | bytes 589856 | tf_op jit(solution)/shard_map/ppermute | solution.py:732
  248.1 3.4 collective-permute-start.61
  254.0 10.5 %collective-permute-done.69 = f32[8,768]{1,0:T(8,128)S(1)} collective-permute-done((f32[8,768]{1,0:T(8,128)S(1)}, f32[8,768]{1,0:T(8,128)S(1)}, u32[]{:S(2)}, u32[]{:S(2)}) %collective-permute-start.69) | collective-permute-done | bytes 24608 | tf_op jit(solution)/shard_map/ppermute | solution.py:729
  264.7 13.7 %attend_back.4 = (bf16[704,768]{1,0:T(8,128)(2,1)S(1)}, bf16[352,768]{1,0:T(8,128)(2,1)S(1)}, bf16[352,768]{1,0:T(8,128)(2,1)S(1)}, f32[640,768]{1,0:T(8,128)S(1)}) custom-call(s32[4]{0:T(128)S(1)} %pad_add_fusion.info_ref, bf16[640,768]{1,0:T(8,128)(2,1)S(1)} %copy-done.22, ...), custom_call_target="tpu_custom_call", output_to_operand_aliasing={{3}: (5, {})} | custom-call | flops 11000000512 | bytes 8000000 | tf_op jit(solution)/shard_map/attend_back/pallas_call | solution.py:561
  280.2 13.4 %attend_back.5 = (bf16[704,768]{1,0:T(8,128)(2,1)S(1)}, bf16[352,768]{1,0:T(8,128)(2,1)S(1)}, bf16[352,768]{1,0:T(8,128)(2,1)S(1)}, f32[640,768]{1,0:T(8,128)S(1)}) custom-call(s32[4]{0:T(128)S(1)} %pad_add_fusion.info_ref, bf16[640,768]{1,0:T(8,128)(2,1)S(1)} %copy-done.22, ...), custom_call_target="tpu_custom_call", output_to_operand_aliasing={{3}: (5, {})} | custom-call | flops 11000000512 | bytes 8000000 | tf_op jit(solution)/shard_map/attend_back/pallas_call | solution.py:561
  295.2 4.3 collective-permute-start.63
  301.4 13.7 %attend_back.6 = (bf16[704,768]{1,0:T(8,128)(2,1)S(1)}, bf16[352,768]{1,0:T(8,128)(2,1)S(1)}, bf16[352,768]{1,0:T(8,128)(2,1)S(1)}, f32[640,768]{1,0:T(8,128)S(1)}) custom-call(s32[4]{0:T(128)S(1)} %pad_add_fusion.info_ref, bf16[640,768]{1,0:T(8,128)(2,1)S(1)} %copy-done.22, ...), custom_call_target="tpu_custom_call", output_to_operand_aliasing={{3}: (5, {})} | custom-call | flops 11000000512 | bytes 8000000 | tf_op jit(solution)/shard_map/attend_back/pallas_call | solution.py:561
  317.6 13.6 %attend_back.7 = (bf16[704,768]{1,0:T(8,128)(2,1)S(1)}, bf16[352,768]{1,0:T(8,128)(2,1)S(1)}, bf16[352,768]{1,0:T(8,128)(2,1)S(1)}, f32[640,768]{1,0:T(8,128)S(1)}) custom-call(s32[4]{0:T(128)S(1)} %pad_add_fusion.info_ref, bf16[640,768]{1,0:T(8,128)(2,1)S(1)} %copy-done.22, ...), custom_call_target="tpu_custom_call", output_to_operand_aliasing={{3}: (5, {})} | custom-call | flops 11000000512 | bytes 8000000 | tf_op jit(solution)/shard_map/attend_back/pallas_call | solution.py:561
  331.2 3.7 finish_rows.1
  340.8 11.3 %collective-permute-done.72 = bf16[64,768]{1,0:T(8,128)(2,1)S(1)} collective-permute-done((bf16[64,768]{1,0:T(8,128)(2,1)S(1)}, bf16[64,768]{1,0:T(8,128)(2,1)S(1)}, u32[]{:S(2)}, u32[]{:S(2)}) %collective-permute-start.72) | collective-permute-done | bytes 98336 | tf_op jit(solution)/shard_map/ppermute | solution.py:732
  352.1 2.8 collective-permute-start.94
  355.7 1.8 collective-permute-start.91
  357.6 4.8 %collective-permute-done.94 = bf16[176,768]{1,0:T(8,128)(2,1)S(1)} collective-permute-done((bf16[176,768]{1,0:T(8,128)(2,1)S(1)}, bf16[176,768]{1,0:T(8,128)(2,1)S(1)}, u32[]{:S(2)}, u32[]{:S(2)}) %collective-permute-start.94) | collective-permute-done | bytes 270368 | tf_op jit(solution)/shard_map/ppermute | solution.py:732
  362.4 2.8 collective-permute-start.107
  365.2 6.9 %collective-permute-done.95 = bf16[176,768]{1,0:T(8,128)(2,1)S(1)} collective-permute-done((bf16[176,768]{1,0:T(8,128)(2,1)S(1)}, bf16[176,768]{1,0:T(8,128)(2,1)S(1)}, u32[]{:S(2)}, u32[]{:S(2)}) %collective-permute-start.95) | collective-permute-done | bytes 270368 | tf_op jit(solution)/shard_map/ppermute | solution.py:732
  372.3 6.1 %collective-permute-done.91 = bf16[176,768]{1,0:T(8,128)(2,1)S(1)} collective-permute-done((bf16[176,768]{1,0:T(8,128)(2,1)S(1)}, bf16[176,768]{1,0:T(8,128)(2,1)S(1)}, u32[]{:S(2)}, u32[]{:S(2)}) %collective-permute-start.91) | collective-permute-done | bytes 270368 | tf_op jit(solution)/shard_map/ppermute | solution.py:732
  381.3 3.1 collective-permute-done.106.refs_2_
  384.5 10.6 %collective-permute-done.75 = bf16[64,768]{1,0:T(8,128)(2,1)S(1)} collective-permute-done((bf16[64,768]{1,0:T(8,128)(2,1)S(1)}, bf16[64,768]{1,0:T(8,128)(2,1)S(1)}, u32[]{:S(2)}, u32[]{:S(2)}) %collective-permute-start.75) | collective-permute-done | bytes 98336 | tf_op jit(solution)/shard_map/ppermute | solution.py:729
  395.1 2.2 collective-permute-start.85
  398.4 10.4 %collective-permute-done.76 = bf16[64,768]{1,0:T(8,128)(2,1)S(1)} collective-permute-done((bf16[64,768]{1,0:T(8,128)(2,1)S(1)}, bf16[64,768]{1,0:T(8,128)(2,1)S(1)}, u32[]{:S(2)}, u32[]{:S(2)}) %collective-permute-start.76) | collective-permute-done | bytes 98336 | tf_op jit(solution)/shard_map/ppermute | solution.py:729
  408.9 2.0 collective-permute-start.87
  412.0 5.1 %collective-permute-done.87 = bf16[176,768]{1,0:T(8,128)(2,1)S(1)} collective-permute-done((bf16[176,768]{1,0:T(8,128)(2,1)S(1)}, bf16[176,768]{1,0:T(8,128)(2,1)S(1)}, u32[]{:S(2)}, u32[]{:S(2)}) %collective-permute-start.87) | collective-permute-done | bytes 270368 | tf_op jit(solution)/shard_map/ppermute | solution.py:732
  417.5 2.4 collective-permute-start.100
  421.0 2.3 collective-permute-start.79
  423.6 11.7 %collective-permute-done.79.refs_3_ = bf16[64,768]{1,0:T(8,128)(2,1)S(1)} collective-permute-done((bf16[64,768]{1,0:T(8,128)(2,1)S(1)}, bf16[64,768]{1,0:T(8,128)(2,1)S(1)}, u32[]{:S(2)}, u32[]{:S(2)}) %collective-permute-start.79) | collective-permute-done | bytes 98336 | tf_op jit(solution)/shard_map/ppermute | solution.py:732
  437.4 2.6 collective-permute-done.77.refs_1_
  442.2 6.0 %spread_hidden.1 = (f32[768,768]{1,0:T(8,128)}, f32[768,768]{1,0:T(8,128)}) custom-call(s32[4]{0:T(128)S(1)} %pad_add_fusion.info_ref, bf16[192,768]{1,0:T(8,128)(2,1)S(1)} %add_convert_fusion.6.refs_0_, bf16[192,768]{1,0:T(8,128)(2,1)S(1)} %collective-permute-done.105.refs_1_, bf16[192,768]{1,0:T(8,128)(2,1)S(1)} %collective-permute-done.106.refs_2_, ...), custom_call_target="tpu_custom_call" | custom-call | flops 500000000 | bytes 7000000 | tf_op jit(solution)/shard_map/spread_hidden/pallas_call | solution.py:681
  448.2 2.8 spread_pos.1
  451.1 2.8 spread_query.1
  (462 shorter events, 123.7 us)
Async XLA Ops:
  24.2 17.5 %collective-permute-start.24 = (bf16[192,768]{1,0:T(8,128)(2,1)S(1)}, bf16[192,768]{1,0:T(8,128)(2,1)S(1)}, u32[]{:S(2)}, u32[]{:S(2)}) collective-permute-start(bf16[192,768]{1,0:T(8,128)(2,1)S(1)} %get-tuple-element.131), channel_id=1, source_target_pairs={{0,1},{1,2},{2,3},{3,0},{4,5},{5,6},{6,7},{7,4},{8,9},{9,10},{10,1... | collective-permute-start | bytes 884744 | tf_op jit(solution)/shard_map/ppermute | solution.py:726
  78.6 18.2 %collective-permute-start.29 = (bf16[192,768]{1,0:T(8,128)(2,1)}, bf16[192,768]{1,0:T(8,128)(2,1)S(1)}, u32[]{:S(2)}, u32[]{:S(2)}) collective-permute-start(bf16[192,768]{1,0:T(8,128)(2,1)} %collective-permute-done.25.refs_7_.refs_1_), channel_id=1, source_target_pairs={{0,4},{4,0},{8,12},{12,8},{16,20},{20,16},{24,28},{28,24},{1,5},{5... | collective-permute-start | bytes 884744 | tf_op jit(solution)/shard_map/ppermute | solution.py:732
  79.2 18.1 %collective-permute-start.27 = (bf16[192,768]{1,0:T(8,128)(2,1)}, bf16[192,768]{1,0:T(8,128)(2,1)S(1)}, u32[]{:S(2)}, u32[]{:S(2)}) collective-permute-start(bf16[192,768]{1,0:T(8,128)(2,1)} %collective-permute-done.25.refs_7_.refs_1_), channel_id=1, source_target_pairs={{0,16},{4,20},{8,24},{12,28},{16,0},{20,4},{24,8},{28,12},{1,17},{... | collective-permute-start | bytes 884744 | tf_op jit(solution)/shard_map/ppermute | solution.py:732
  81.5 15.2 %collective-permute-start.30 = (bf16[192,768]{1,0:T(8,128)(2,1)}, bf16[192,768]{1,0:T(8,128)(2,1)S(1)}, u32[]{:S(2)}, u32[]{:S(2)}) collective-permute-start(bf16[192,768]{1,0:T(8,128)(2,1)} %collective-permute-done.26.refs_8_.refs_2_), channel_id=1, source_target_pairs={{0,4},{4,0},{8,12},{12,8},{16,20},{20,16},{24,28},{28,24},{1,5},{5... | collective-permute-start | bytes 884744 | tf_op jit(solution)/shard_map/ppermute | solution.py:732
  81.5 15.9 %collective-permute-start.22 = (bf16[176,768]{1,0:T(8,128)(2,1)}, bf16[176,768]{1,0:T(8,128)(2,1)S(1)}, u32[]{:S(2)}, u32[]{:S(2)}) collective-permute-start(bf16[176,768]{1,0:T(8,128)(2,1)} %collective-permute-done.18.refs_2_.refs_5_), channel_id=1, source_target_pairs={{0,4},{4,0},{8,12},{12,8},{16,20},{20,16},{24,28},{28,24},{1,5},{5... | collective-permute-start | bytes 811016 | tf_op jit(solution)/shard_map/ppermute | solution.py:732
  82.0 17.5 %collective-permute-start.19 = (bf16[176,768]{1,0:T(8,128)(2,1)}, bf16[176,768]{1,0:T(8,128)(2,1)}, u32[]{:S(2)}, u32[]{:S(2)}) collective-permute-start(bf16[176,768]{1,0:T(8,128)(2,1)} %collective-permute-done.18.refs_2_.refs_5_), channel_id=1, source_target_pairs={{0,8},{4,12},{8,0},{12,4},{16,24},{20,28},{24,16},{28,20},{1,9},{5... | collective-permute-start | bytes 811016 | tf_op jit(solution)/shard_map/ppermute | solution.py:732
  96.7 22.5 %collective-permute-start.21 = (bf16[176,768]{1,0:T(8,128)(2,1)S(1)}, bf16[176,768]{1,0:T(8,128)(2,1)S(1)}, u32[]{:S(2)}, u32[]{:S(2)}) collective-permute-start(bf16[176,768]{1,0:T(8,128)(2,1)S(1)} %copy-done.59), channel_id=1, source_target_pairs={{0,4},{4,0},{8,12},{12,8},{16,20},{20,16},{24,28},{28,24},{1,5},{5... | collective-permute-start | bytes 811016 | tf_op jit(solution)/shard_map/ppermute | solution.py:732
  96.8 22.5 %collective-permute-start.15 = (bf16[176,768]{1,0:T(8,128)(2,1)}, bf16[176,768]{1,0:T(8,128)(2,1)S(1)}, u32[]{:S(2)}, u32[]{:S(2)}) collective-permute-start(bf16[176,768]{1,0:T(8,128)(2,1)} %collective-permute-done.11.refs_3_.refs_6_), channel_id=1, source_target_pairs={{0,4},{4,0},{8,12},{12,8},{16,20},{20,16},{24,28},{28,24},{1,5},{5... | collective-permute-start | bytes 811016 | tf_op jit(solution)/shard_map/ppermute | solution.py:732
  97.3 22.6 %collective-permute-start.44 = (bf16[192,768]{1,0:T(8,128)(2,1)}, bf16[192,768]{1,0:T(8,128)(2,1)S(1)}, u32[]{:S(2)}, u32[]{:S(2)}) collective-permute-start(bf16[192,768]{1,0:T(8,128)(2,1)} %collective-permute-done.40.refs_22_.refs_0_), channel_id=1, source_target_pairs={{0,4},{4,0},{8,12},{12,8},{16,20},{20,16},{24,28},{28,24},{1,5},{5... | collective-permute-start | bytes 884744 | tf_op jit(solution)/shard_map/ppermute | solution.py:732
  98.1 22.0 %collective-permute-start.42 = (bf16[192,768]{1,0:T(8,128)(2,1)}, bf16[192,768]{1,0:T(8,128)(2,1)S(1)}, u32[]{:S(2)}, u32[]{:S(2)}) collective-permute-start(bf16[192,768]{1,0:T(8,128)(2,1)} %collective-permute-done.40.refs_22_.refs_0_), channel_id=1, source_target_pairs={{0,16},{4,20},{8,24},{12,28},{16,0},{20,4},{24,8},{28,12},{1,17},{... | collective-permute-start | bytes 884744 | tf_op jit(solution)/shard_map/ppermute | solution.py:732
  99.5 21.0 %collective-permute-start.41 = (bf16[192,768]{1,0:T(8,128)(2,1)}, bf16[192,768]{1,0:T(8,128)(2,1)S(1)}, u32[]{:S(2)}, u32[]{:S(2)}) collective-permute-start(bf16[192,768]{1,0:T(8,128)(2,1)} %collective-permute-done.40.refs_22_.refs_0_), channel_id=1, source_target_pairs={{0,8},{4,12},{8,0},{12,4},{16,24},{20,28},{24,16},{28,20},{1,9},{5... | collective-permute-start | bytes 884744 | tf_op jit(solution)/shard_map/ppermute | solution.py:732
  133.3 14.6 %collective-permute-start.31 = (bf16[192,768]{1,0:T(8,128)(2,1)S(1)}, bf16[192,768]{1,0:T(8,128)(2,1)S(1)}, u32[]{:S(2)}, u32[]{:S(2)}) collective-permute-start(bf16[192,768]{1,0:T(8,128)(2,1)S(1)} %collective-permute-done.27.refs_9_.refs_3_), channel_id=1, source_target_pairs={{0,4},{4,0},{8,12},{12,8},{16,20},{20,16},{24,28},{28,24},{1,5},{5... | collective-permute-start | bytes 884744 | tf_op jit(solution)/shard_map/ppermute | solution.py:732
  133.3 14.6 %collective-permute-start.45 = (bf16[192,768]{1,0:T(8,128)(2,1)S(1)}, bf16[192,768]{1,0:T(8,128)(2,1)S(1)}, u32[]{:S(2)}, u32[]{:S(2)}) collective-permute-start(bf16[192,768]{1,0:T(8,128)(2,1)S(1)} %collective-permute-done.41.refs_23_.refs_1_), channel_id=1, source_target_pairs={{0,4},{4,0},{8,12},{12,8},{16,20},{20,16},{24,28},{28,24},{1,5},{5... | collective-permute-start | bytes 884744 | tf_op jit(solution)/shard_map/ppermute | solution.py:732
  133.8 14.1 %collective-permute-start.46 = (bf16[192,768]{1,0:T(8,128)(2,1)S(1)}, bf16[192,768]{1,0:T(8,128)(2,1)S(1)}, u32[]{:S(2)}, u32[]{:S(2)}) collective-permute-start(bf16[192,768]{1,0:T(8,128)(2,1)S(1)} %collective-permute-done.42.refs_24_.refs_2_), channel_id=1, source_target_pairs={{0,4},{4,0},{8,12},{12,8},{16,20},{20,16},{24,28},{28,24},{1,5},{5... | collective-permute-start | bytes 884744 | tf_op jit(solution)/shard_map/ppermute | solution.py:732
  206.0 29.8 %collective-permute-start.52 = (bf16[384,768]{1,0:T(8,128)(2,1)S(1)}, bf16[384,768]{1,0:T(8,128)(2,1)S(1)}, u32[]{:S(2)}, u32[]{:S(2)}) collective-permute-start(bf16[384,768]{1,0:T(8,128)(2,1)S(1)} %add_convert_fusion.3), channel_id=1, source_target_pairs={{0,8},{4,12},{8,0},{12,4},{16,24},{20,28},{24,16},{28,20},{1,9},{5... | collective-permute-start | bytes 1769480 | tf_op jit(solution)/shard_map/ppermute | solution.py:732
  216.9 21.5 %collective-permute-start.50 = (bf16[768,768]{1,0:T(8,128)(2,1)S(1)}, bf16[768,768]{1,0:T(8,128)(2,1)}, u32[]{:S(2)}, u32[]{:S(2)}) collective-permute-start(bf16[768,768]{1,0:T(8,128)(2,1)S(1)} %get-tuple-element.151), channel_id=1, source_target_pairs={{0,4},{4,0},{8,12},{12,8},{16,20},{20,16},{24,28},{28,24},{1,5},{5... | collective-permute-start | bytes 3538952 | tf_op jit(solution)/shard_map/ppermute | solution.py:732
  218.3 15.7 %collective-permute-start.53 = (bf16[384,768]{1,0:T(8,128)(2,1)S(1)}, bf16[384,768]{1,0:T(8,128)(2,1)S(1)}, u32[]{:S(2)}, u32[]{:S(2)}) collective-permute-start(bf16[384,768]{1,0:T(8,128)(2,1)S(1)} %add_convert_fusion.2), channel_id=1, source_target_pairs={{0,16},{4,20},{8,24},{12,28},{16,0},{20,4},{24,8},{28,12},{1,17},{... | collective-permute-start | bytes 1769480 | tf_op jit(solution)/shard_map/ppermute | solution.py:732
  226.5 26.9 %collective-permute-start.51 = (bf16[768,768]{1,0:T(8,128)(2,1)S(1)}, bf16[768,768]{1,0:T(8,128)(2,1)S(1)}, u32[]{:S(2)}, u32[]{:S(2)}) collective-permute-start(bf16[768,768]{1,0:T(8,128)(2,1)S(1)} %get-tuple-element.164), channel_id=1, source_target_pairs={{0,4},{4,0},{8,12},{12,8},{16,20},{20,16},{24,28},{28,24},{1,5},{5... | collective-permute-start | bytes 3538952 | tf_op jit(solution)/shard_map/ppermute | solution.py:732
  244.9 54.7 %collective-permute-start.62 = (bf16[192,768]{1,0:T(8,128)(2,1)S(1)}, bf16[192,768]{1,0:T(8,128)(2,1)S(1)}, u32[]{:S(2)}, u32[]{:S(2)}) collective-permute-start(bf16[192,768]{1,0:T(8,128)(2,1)S(1)} %add_convert_fusion.8), channel_id=1, source_target_pairs={{0,2},{1,3},{2,0},{3,1},{4,6},{5,7},{6,4},{7,5},{8,10},{9,11},{10,... | collective-permute-start | bytes 884744 | tf_op jit(solution)/shard_map/ppermute | solution.py:726
  248.1 67.0 %collective-permute-start.61 = (bf16[192,768]{1,0:T(8,128)(2,1)S(1)}, bf16[192,768]{1,0:T(8,128)(2,1)S(1)}, u32[]{:S(2)}, u32[]{:S(2)}) collective-permute-start(bf16[192,768]{1,0:T(8,128)(2,1)S(1)} %add_convert_fusion.9), channel_id=1, source_target_pairs={{0,3},{1,0},{2,1},{3,2},{4,7},{5,4},{6,5},{7,6},{8,11},{9,8},{10,9... | collective-permute-start | bytes 884744 | tf_op jit(solution)/shard_map/ppermute | solution.py:726
  251.5 27.5 %collective-permute-start.54 = (bf16[384,768]{1,0:T(8,128)(2,1)S(1)}, bf16[384,768]{1,0:T(8,128)(2,1)S(1)}, u32[]{:S(2)}, u32[]{:S(2)}) collective-permute-start(bf16[384,768]{1,0:T(8,128)(2,1)S(1)} %add_convert_fusion.1), channel_id=1, source_target_pairs={{0,8},{4,12},{8,0},{12,4},{16,24},{20,28},{24,16},{28,20},{1,9},{5... | collective-permute-start | bytes 1769480 | tf_op jit(solution)/shard_map/ppermute | solution.py:732
  253.5 25.0 %collective-permute-start.55 = (bf16[384,768]{1,0:T(8,128)(2,1)S(1)}, bf16[384,768]{1,0:T(8,128)(2,1)S(1)}, u32[]{:S(2)}, u32[]{:S(2)}) collective-permute-start(bf16[384,768]{1,0:T(8,128)(2,1)S(1)} %add_convert_fusion), channel_id=1, source_target_pairs={{0,16},{4,20},{8,24},{12,28},{16,0},{20,4},{24,8},{28,12},{1,17},{... | collective-permute-start | bytes 1769480 | tf_op jit(solution)/shard_map/ppermute | solution.py:732
  278.4 16.8 %collective-permute-start.59 = (bf16[704,768]{1,0:T(8,128)(2,1)S(1)}, bf16[704,768]{1,0:T(8,128)(2,1)S(1)}, u32[]{:S(2)}, u32[]{:S(2)}) collective-permute-start(bf16[704,768]{1,0:T(8,128)(2,1)S(1)} %get-tuple-element.180), channel_id=1, source_target_pairs={{0,4},{4,0},{8,12},{12,8},{16,20},{20,16},{24,28},{28,24},{1,5},{5... | collective-permute-start | bytes 3244040 | tf_op jit(solution)/shard_map/ppermute | solution.py:732
  278.6 36.5 %collective-permute-start.60 = (bf16[192,768]{1,0:T(8,128)(2,1)S(1)}, bf16[192,768]{1,0:T(8,128)(2,1)S(1)}, u32[]{:S(2)}, u32[]{:S(2)}) collective-permute-start(bf16[192,768]{1,0:T(8,128)(2,1)S(1)} %add_convert_fusion.10), channel_id=1, source_target_pairs={{0,8},{4,12},{8,0},{12,4},{16,24},{20,28},{24,16},{28,20},{1,9},{5... | collective-permute-start | bytes 884744 | tf_op jit(solution)/shard_map/ppermute | solution.py:732
  293.6 23.8 %collective-permute-start.65 = (bf16[704,768]{1,0:T(8,128)(2,1)S(1)}, bf16[704,768]{1,0:T(8,128)(2,1)S(1)}, u32[]{:S(2)}, u32[]{:S(2)}) collective-permute-start(bf16[704,768]{1,0:T(8,128)(2,1)S(1)} %get-tuple-element.188), channel_id=1, source_target_pairs={{0,4},{4,0},{8,12},{12,8},{16,20},{20,16},{24,28},{28,24},{1,5},{5... | collective-permute-start | bytes 3244040 | tf_op jit(solution)/shard_map/ppermute | solution.py:732
  295.2 20.0 %collective-permute-start.63 = (bf16[192,768]{1,0:T(8,128)(2,1)S(1)}, bf16[192,768]{1,0:T(8,128)(2,1)S(1)}, u32[]{:S(2)}, u32[]{:S(2)}) collective-permute-start(bf16[192,768]{1,0:T(8,128)(2,1)S(1)} %add_convert_fusion.7), channel_id=1, source_target_pairs={{0,1},{1,2},{2,3},{3,0},{4,5},{5,6},{6,7},{7,4},{8,9},{9,10},{10,1... | collective-permute-start | bytes 884744 | tf_op jit(solution)/shard_map/ppermute | solution.py:726
  299.6 15.9 %collective-permute-start.64 = (bf16[352,768]{1,0:T(8,128)(2,1)S(1)}, bf16[352,768]{1,0:T(8,128)(2,1)S(1)}, u32[]{:S(2)}, u32[]{:S(2)}) collective-permute-start(bf16[352,768]{1,0:T(8,128)(2,1)S(1)} %add_convert_fusion.5), channel_id=1, source_target_pairs={{0,16},{4,20},{8,24},{12,28},{16,0},{20,4},{24,8},{28,12},{1,17},{... | collective-permute-start | bytes 1622024 | tf_op jit(solution)/shard_map/ppermute | solution.py:732
  315.1 23.7 %collective-permute-start.93 = (bf16[704,768]{1,0:T(8,128)(2,1)S(1)}, bf16[704,768]{1,0:T(8,128)(2,1)S(1)}, u32[]{:S(2)}, u32[]{:S(2)}) collective-permute-start(bf16[704,768]{1,0:T(8,128)(2,1)S(1)} %get-tuple-element.205), channel_id=1, source_target_pairs={{0,4},{4,0},{8,12},{12,8},{16,20},{20,16},{24,28},{28,24},{1,5},{5... | collective-permute-start | bytes 3244040 | tf_op jit(solution)/shard_map/ppermute | solution.py:732
  315.7 21.1 %collective-permute-start.88 = (bf16[176,768]{1,0:T(8,128)(2,1)S(1)}, bf16[176,768]{1,0:T(8,128)(2,1)S(1)}, u32[]{:S(2)}, u32[]{:S(2)}) collective-permute-start(bf16[176,768]{1,0:T(8,128)(2,1)S(1)} %add_convert_fusion.25), channel_id=1, source_target_pairs={{0,8},{4,12},{8,0},{12,4},{16,24},{20,28},{24,16},{28,20},{1,9},{5... | collective-permute-start | bytes 811016 | tf_op jit(solution)/shard_map/ppermute | solution.py:732
  335.2 20.0 %collective-permute-start.90 = (bf16[352,768]{1,0:T(8,128)(2,1)S(1)}, bf16[352,768]{1,0:T(8,128)(2,1)S(1)}, u32[]{:S(2)}, u32[]{:S(2)}) collective-permute-start(bf16[352,768]{1,0:T(8,128)(2,1)S(1)} %add_convert_fusion.4), channel_id=1, source_target_pairs={{0,8},{4,12},{8,0},{12,4},{16,24},{20,28},{24,16},{28,20},{1,9},{5... | collective-permute-start | bytes 1622024 | tf_op jit(solution)/shard_map/ppermute | solution.py:732
  336.8 42.2 %collective-permute-start.84 = (bf16[704,768]{1,0:T(8,128)(2,1)S(1)}, bf16[704,768]{1,0:T(8,128)(2,1)S(1)}, u32[]{:S(2)}, u32[]{:S(2)}) collective-permute-start(bf16[704,768]{1,0:T(8,128)(2,1)S(1)} %get-tuple-element.201), channel_id=1, source_target_pairs={{0,4},{4,0},{8,12},{12,8},{16,20},{20,16},{24,28},{28,24},{1,5},{5... | collective-permute-start | bytes 3244040 | tf_op jit(solution)/shard_map/ppermute | solution.py:732
  337.0 15.1 %collective-permute-start.72 = (bf16[64,768]{1,0:T(8,128)(2,1)S(1)}, bf16[64,768]{1,0:T(8,128)(2,1)S(1)}, u32[]{:S(2)}, u32[]{:S(2)}) collective-permute-start(bf16[64,768]{1,0:T(8,128)(2,1)S(1)} %get-tuple-element.228), channel_id=1, source_target_pairs={{0,24},{4,28},{8,16},{12,20},{16,8},{20,12},{24,0},{28,4},{1,25},{... | collective-permute-start | bytes 294920 | tf_op jit(solution)/shard_map/ppermute | solution.py:732
  337.9 17.0 %collective-permute-start.73 = (bf16[64,768]{1,0:T(8,128)(2,1)S(1)}, bf16[64,768]{1,0:T(8,128)(2,1)S(1)}, u32[]{:S(2)}, u32[]{:S(2)}) collective-permute-start(bf16[64,768]{1,0:T(8,128)(2,1)S(1)} %get-tuple-element.229), channel_id=1, source_target_pairs={{0,8},{4,12},{8,0},{12,4},{16,24},{20,28},{24,16},{28,20},{1,9},{5... | collective-permute-start | bytes 294920 | tf_op jit(solution)/shard_map/ppermute | solution.py:732
  338.8 16.9 %collective-permute-start.74 = (bf16[64,768]{1,0:T(8,128)(2,1)S(1)}, bf16[64,768]{1,0:T(8,128)(2,1)S(1)}, u32[]{:S(2)}, u32[]{:S(2)}) collective-permute-start(bf16[64,768]{1,0:T(8,128)(2,1)S(1)} %get-tuple-element.230), channel_id=1, source_target_pairs={{0,16},{4,20},{8,24},{12,28},{16,0},{20,4},{24,8},{28,12},{1,17},{... | collective-permute-start | bytes 294920 | tf_op jit(solution)/shard_map/ppermute | solution.py:732
  354.9 17.1 %collective-permute-start.95 = (bf16[176,768]{1,0:T(8,128)(2,1)S(1)}, bf16[176,768]{1,0:T(8,128)(2,1)S(1)}, u32[]{:S(2)}, u32[]{:S(2)}) collective-permute-start(bf16[176,768]{1,0:T(8,128)(2,1)S(1)} %get-tuple-element.225), channel_id=1, source_target_pairs={{0,16},{4,20},{8,24},{12,28},{16,0},{20,4},{24,8},{28,12},{1,17},{... | collective-permute-start | bytes 811016 | tf_op jit(solution)/shard_map/ppermute | solution.py:732
  355.1 16.9 %collective-permute-start.96 = (bf16[176,768]{1,0:T(8,128)(2,1)S(1)}, bf16[176,768]{1,0:T(8,128)(2,1)S(1)}, u32[]{:S(2)}, u32[]{:S(2)}) collective-permute-start(bf16[176,768]{1,0:T(8,128)(2,1)S(1)} %get-tuple-element.227), channel_id=1, source_target_pairs={{0,8},{4,12},{8,0},{12,4},{16,24},{20,28},{24,16},{28,20},{1,9},{5... | collective-permute-start | bytes 811016 | tf_op jit(solution)/shard_map/ppermute | solution.py:732
  355.7 22.6 %collective-permute-start.91 = (bf16[176,768]{1,0:T(8,128)(2,1)S(1)}, bf16[176,768]{1,0:T(8,128)(2,1)S(1)}, u32[]{:S(2)}, u32[]{:S(2)}) collective-permute-start(bf16[176,768]{1,0:T(8,128)(2,1)S(1)} %add_convert_fusion.20), channel_id=1, source_target_pairs={{0,16},{4,20},{8,24},{12,28},{16,0},{20,4},{24,8},{28,12},{1,17},{... | collective-permute-start | bytes 811016 | tf_op jit(solution)/shard_map/ppermute | solution.py:732
  362.4 18.4 %collective-permute-start.107 = (bf16[192,768]{1,0:T(8,128)(2,1)S(1)}, bf16[192,768]{1,0:T(8,128)(2,1)S(1)}, u32[]{:S(2)}, u32[]{:S(2)}) collective-permute-start(bf16[192,768]{1,0:T(8,128)(2,1)S(1)} %add_convert_fusion.6.refs_0_), channel_id=1, source_target_pairs={{0,24},{4,28},{8,16},{12,20},{16,8},{20,12},{24,0},{28,4},{1,25},{... | collective-permute-start | bytes 884744 | tf_op jit(solution)/shard_map/ppermute | solution.py:732
  372.0 25.3 %collective-permute-start.105 = (bf16[192,768]{1,0:T(8,128)(2,1)S(1)}, bf16[192,768]{1,0:T(8,128)(2,1)S(1)}, u32[]{:S(2)}, u32[]{:S(2)}) collective-permute-start(bf16[192,768]{1,0:T(8,128)(2,1)S(1)} %add_convert_fusion.6.refs_0_), channel_id=1, source_target_pairs={{0,8},{4,12},{8,0},{12,4},{16,24},{20,28},{24,16},{28,20},{1,9},{5... | collective-permute-start | bytes 884744 | tf_op jit(solution)/shard_map/ppermute | solution.py:732
  378.3 19.1 %collective-permute-start.89 = (bf16[176,768]{1,0:T(8,128)(2,1)S(1)}, bf16[176,768]{1,0:T(8,128)(2,1)S(1)}, u32[]{:S(2)}, u32[]{:S(2)}) collective-permute-start(bf16[176,768]{1,0:T(8,128)(2,1)S(1)} %add_convert_fusion.21), channel_id=1, source_target_pairs={{0,3},{1,0},{2,1},{3,2},{4,7},{5,4},{6,5},{7,6},{8,11},{9,8},{10,9... | collective-permute-start | bytes 811016 | tf_op jit(solution)/shard_map/ppermute | solution.py:726
  379.0 16.1 %collective-permute-start.75 = (bf16[64,768]{1,0:T(8,128)(2,1)S(1)}, bf16[64,768]{1,0:T(8,128)(2,1)S(1)}, u32[]{:S(2)}, u32[]{:S(2)}) collective-permute-start(bf16[64,768]{1,0:T(8,128)(2,1)S(1)} %add_convert_fusion.28), channel_id=1, source_target_pairs={{0,1},{1,0},{2,3},{3,2},{4,5},{5,4},{6,7},{7,6},{8,9},{9,8},{10,11... | collective-permute-start | bytes 294920 | tf_op jit(solution)/shard_map/ppermute | solution.py:729
  380.8 30.1 %collective-permute-start.97 = (bf16[176,768]{1,0:T(8,128)(2,1)S(1)}, bf16[176,768]{1,0:T(8,128)(2,1)S(1)}, u32[]{:S(2)}, u32[]{:S(2)}) collective-permute-start(bf16[176,768]{1,0:T(8,128)(2,1)S(1)} %add_convert_fusion.15), channel_id=1, source_target_pairs={{0,1},{1,2},{2,3},{3,0},{4,5},{5,6},{6,7},{7,4},{8,9},{9,10},{10,1... | collective-permute-start | bytes 811016 | tf_op jit(solution)/shard_map/ppermute | solution.py:726
  384.4 26.4 %collective-permute-start.92 = (bf16[176,768]{1,0:T(8,128)(2,1)S(1)}, bf16[176,768]{1,0:T(8,128)(2,1)S(1)}, u32[]{:S(2)}, u32[]{:S(2)}) collective-permute-start(bf16[176,768]{1,0:T(8,128)(2,1)S(1)} %add_convert_fusion.19), channel_id=1, source_target_pairs={{0,2},{1,3},{2,0},{3,1},{4,6},{5,7},{6,4},{7,5},{8,10},{9,11},{10,... | collective-permute-start | bytes 811016 | tf_op jit(solution)/shard_map/ppermute | solution.py:726
  395.1 16.3 %collective-permute-start.85 = (bf16[176,768]{1,0:T(8,128)(2,1)S(1)}, bf16[176,768]{1,0:T(8,128)(2,1)S(1)}, u32[]{:S(2)}, u32[]{:S(2)}) collective-permute-start(bf16[176,768]{1,0:T(8,128)(2,1)S(1)} %get-tuple-element.222), channel_id=1, source_target_pairs={{0,24},{4,28},{8,16},{12,20},{16,8},{20,12},{24,0},{28,4},{1,25},{... | collective-permute-start | bytes 811016 | tf_op jit(solution)/shard_map/ppermute | solution.py:732
  417.5 23.0 %collective-permute-start.100 = (bf16[176,768]{1,0:T(8,128)(2,1)S(1)}, bf16[176,768]{1,0:T(8,128)(2,1)S(1)}, u32[]{:S(2)}, u32[]{:S(2)}) collective-permute-start(bf16[176,768]{1,0:T(8,128)(2,1)S(1)} %add_convert_fusion.14.refs_0_), channel_id=1, source_target_pairs={{0,24},{4,28},{8,16},{12,20},{16,8},{20,12},{24,0},{28,4},{1,25},{... | collective-permute-start | bytes 811016 | tf_op jit(solution)/shard_map/ppermute | solution.py:732
  419.9 20.7 %collective-permute-start.99 = (bf16[176,768]{1,0:T(8,128)(2,1)S(1)}, bf16[176,768]{1,0:T(8,128)(2,1)S(1)}, u32[]{:S(2)}, u32[]{:S(2)}) collective-permute-start(bf16[176,768]{1,0:T(8,128)(2,1)S(1)} %add_convert_fusion.14.refs_0_), channel_id=1, source_target_pairs={{0,16},{4,20},{8,24},{12,28},{16,0},{20,4},{24,8},{28,12},{1,17},{... | collective-permute-start | bytes 811016 | tf_op jit(solution)/shard_map/ppermute | solution.py:732
  420.2 20.9 %collective-permute-start.98 = (bf16[176,768]{1,0:T(8,128)(2,1)S(1)}, bf16[176,768]{1,0:T(8,128)(2,1)S(1)}, u32[]{:S(2)}, u32[]{:S(2)}) collective-permute-start(bf16[176,768]{1,0:T(8,128)(2,1)S(1)} %add_convert_fusion.14.refs_0_), channel_id=1, source_target_pairs={{0,8},{4,12},{8,0},{12,4},{16,24},{20,28},{24,16},{28,20},{1,9},{5... | collective-permute-start | bytes 811016 | tf_op jit(solution)/shard_map/ppermute | solution.py:732
  421.0 14.3 %collective-permute-start.79 = (bf16[64,768]{1,0:T(8,128)(2,1)S(1)}, bf16[64,768]{1,0:T(8,128)(2,1)S(1)}, u32[]{:S(2)}, u32[]{:S(2)}) collective-permute-start(bf16[64,768]{1,0:T(8,128)(2,1)S(1)} %add_convert_fusion.26.refs_0_), channel_id=1, source_target_pairs={{0,24},{4,28},{8,16},{12,20},{16,8},{20,12},{24,0},{28,4},{1,25},{... | collective-permute-start | bytes 294920 | tf_op jit(solution)/shard_map/ppermute | solution.py:732
  (175 other events, 1547.1 us)

commit v4 on v3

--- a/solution.py
+++ b/solution.py
@@ -26,7 +26,6 @@
     0.14589250699009862,
     -0.029552569422939476,
 )
-CODES = (0, 2, 1, 3, 4, 6, 5, 7)
 TILE = 16
 VMEM = pl.BlockSpec(memory_space=pltpu.VMEM)
 SMEM = pl.BlockSpec(memory_space=pltpu.SMEM)
@@ -76,25 +75,33 @@
     return pl.ds(pl.multiple_of(first, TILE), size)
 
 
-def place(pieces, part, unit, targets):
+def place(pieces, info_ref, unit, targets, skip=0):
+    part, first = info_ref[2], info_ref[3]
+    second = 3 - first
     pairs = []
-    for piece, code in zip(pieces, CODES):
+    for piece, code in zip(pieces, (0, first, second, 3, 4, 4 + second, 4 + first, 7)):
         row = lax.bitwise_xor(part, jnp.int32(code)) * unit
         for t, target in enumerate(targets):
-            pairs.append((piece.at[pl.ds(t * unit, unit)], target.at[rows_at(row, unit)]))
+            pairs.append((piece.at[pl.ds(skip + t * unit, unit)], target.at[rows_at(row, unit)]))
     return pairs
 
 
-def blocks_out(full_s, part, unit, first, send_ref, near_ref, pass_ref):
+def blocks_out(sources, info_ref, send_ref, near_ref, pass_ref):
+    part, first = info_ref[2], info_ref[3]
     second = 3 - first
-    order = (0, second, first, 3)
+    keep = (0, second, first, 3)
+    send = (4, 4 + first, 4 + second, 7)
+    total = sum(unit for _, unit in sources)
     pairs = []
-    for i, code in enumerate(order):
-        mine = lax.bitwise_xor(part, jnp.int32(code)) * unit
-        other = lax.bitwise_xor(part, jnp.int32(code + 4)) * unit
-        keep = near_ref if i < 2 else pass_ref
-        pairs.append((full_s.at[rows_at(other, unit)], send_ref.at[pl.ds(i * unit, unit)]))
-        pairs.append((full_s.at[rows_at(mine, unit)], keep.at[pl.ds((i % 2) * unit, unit)]))
+    for i in range(4):
+        done = 0
+        for source, unit in sources:
+            other = lax.bitwise_xor(part, jnp.int32(send[i])) * unit
+            mine = lax.bitwise_xor(part, jnp.int32(keep[i])) * unit
+            to = near_ref if i < 2 else pass_ref
+            pairs.append((source.at[rows_at(other, unit)], send_ref.at[pl.ds(i * total + done, unit)]))
+            pairs.append((source.at[rows_at(mine, unit)], to.at[pl.ds((i % 2) * total + done, unit)]))
+            done += unit
     return pairs
 
 
@@ -208,7 +215,7 @@
     if count == 1:
         wait(start([(pieces[0], w_s)], sem.at[0]))
     else:
-        wait(start(place(pieces, info_ref[2], w_s.shape[0] // 8, (w_s,)), sem.at[0]))
+        wait(start(place(pieces, info_ref, w_s.shape[0] // 8, (w_s,)), sem.at[0]))
     rows_b = w_s[7 * gw : 7 * gw + TILE]
     bias_ref[...] = rows_b
     rows_b = rows_b.astype(F32)
@@ -298,14 +305,13 @@
 def hidden_kernel(n, info_ref, attended_ref, vec_ref, wm_ref, em_ref, cw_ref, ce_ref, *refs):
     bias_refs, refs = refs[:n], refs[n:]
     up_own, down_own = refs[:2]
-    pieces, refs = refs[2 : 2 + 8 * (n - 1)], refs[2 + 8 * (n - 1) :]
-    low_ref, turn_ref, at_ref, slope_ref, ow_ref, oe_ref, mixed_ref, grad_ref, sums_ref, up_s, down_s, acc_s, b_s, sem = refs
+    pieces, refs = refs[2:10], refs[10:]
+    turn_ref, at_ref, slope_ref, up_s, down_s, ow_ref, oe_ref, mixed_ref, grad_ref, sums_ref, low_ref, acc_s, b_s, sem = refs
     total, width = attended_ref.shape
     unit = width // 8
-    part = info_ref[2]
     reads = [start([(up_own, up_s.at[0]), (down_own, down_s.at[0])], sem.at[0])]
     for r in range(1, n):
-        reads.append(start(place(pieces[8 * (r - 1) : 8 * r], part, unit, (up_s.at[r], down_s.at[r])), sem.at[r]))
+        reads.append(start(place(pieces, info_ref, unit, (up_s.at[r], down_s.at[r]), 2 * unit * (r - 1)), sem.at[r]))
     for r in range(n):
         b_s[r] = bias_refs[r][2:3].astype(F32)
     scaled, _ = norm_parts(attended_ref[...])
@@ -356,19 +362,19 @@
     sums_ref[3:] = jnp.zeros((5, width), F32)
 
 
-def hidden(info, attended, vec, word_mask, entity_mask, cot_words, cot_ents, biases, own, groups):
+def hidden(info, attended, vec, word_mask, entity_mask, cot_words, cot_ents, biases, own, pieces):
     total, width = attended.shape
     n = len(biases)
-    pieces = [v for g in groups for v in g]
     return pl.pallas_call(
         partial(hidden_kernel, n),
         in_specs=[SMEM] + [VMEM] * (6 + n) + [HBM] * (2 + len(pieces)),
-        out_specs=[VMEM] * 9,
+        out_specs=[VMEM] * 10,
         out_shape=(
-            shape((total, width), BF16),
             shape((width, total), BF16),
             shape((n, width, total), BF16),
             shape((n, total, width), F32),
+            shape((n, width, width), BF16),
+            shape((n, width, width), BF16),
             shape(cot_words.shape, BF16),
             shape(cot_ents.shape, BF16),
             shape((total, width), BF16),
@@ -376,8 +382,7 @@
             shape((8, width), F32),
         ),
         scratch_shapes=[
-            pltpu.VMEM((n, width, width), BF16),
-            pltpu.VMEM((n, width, width), BF16),
+            pltpu.VMEM((total, width), BF16),
             pltpu.VMEM((total, width), F32),
             pltpu.VMEM((n, 1, width), F32),
             DMA((n,)),
@@ -397,55 +402,47 @@
     return inv_std * (grad_scaled - mean_first - scaled * mean_second), grad_gain, grad_shift
 
 
-def hidden_back_kernel(r, first, count, info_ref, low_ref, at_ref, slope_ref, turn_ref, acc_ref, *refs):
-    pieces = refs[:count]
-    send_ref, near_ref, pass_ref, out_ref, b_ref, up_s, down_s, full_s, sem = refs[count:]
-    unit = up_s.shape[0] // 8
-    part = info_ref[2]
-    if count == 2:
-        reads = start([(pieces[0], up_s), (pieces[1], down_s)], sem.at[0])
-    else:
-        reads = start(place(pieces, part, unit, (up_s, down_s)), sem.at[0])
+def hidden_back_kernel(
+    pair, info_ref, low_ref, at_ref, slope_ref, turn_ref, up_ref, down_ref, acc_ref,
+    send_ref, near_ref, pass_ref, out_ref, b_ref, *refs,
+):
+    full, sem = refs[:-1], refs[-1]
+    unit = turn_ref.shape[0] // 8
     low = low_ref[...]
-    grad_down = mm(at_ref[r], low).astype(BF16)
-    for i in range(8):
-        full_s[(2 * i + 1) * unit : (2 * i + 2) * unit] = grad_down[i * unit : (i + 1) * unit]
-    wait(reads)
-    pre_low = (mm_nt(low, down_s[...]) * slope_ref[r]).astype(BF16)
-    grad_up = mm(turn_ref[...], pre_low).astype(BF16)
-    for i in range(8):
-        full_s[2 * i * unit : (2 * i + 1) * unit] = grad_up[i * unit : (i + 1) * unit]
-    writes = start(blocks_out(full_s, part, 2 * unit, first, send_ref, near_ref, pass_ref), sem.at[1])
-    out_ref[...] = acc_ref[...] + mm_nt(pre_low, up_s[...])
-    b_ref[...] = jnp.broadcast_to(jnp.sum(pre_low.astype(F32), 0, keepdims=True), b_ref.shape)
-    wait(writes)
-
-
-def hidden_back(info, r, first, mixed_low, act_t, slope, normed_t, acc, pieces):
+    out_ref[...] = acc_ref[...]
+    for k, r in enumerate(pair):
+        grad_down = mm(at_ref[r], low).astype(BF16)
+        for i in range(8):
+            full[k][(2 * i + 1) * unit : (2 * i + 2) * unit] = grad_down[i * unit : (i + 1) * unit]
+        pre_low = (mm_nt(low, down_ref[r]) * slope_ref[r]).astype(BF16)
+        grad_up = mm(turn_ref[...], pre_low).astype(BF16)
+        for i in range(8):
+            full[k][2 * i * unit : (2 * i + 1) * unit] = grad_up[i * unit : (i + 1) * unit]
+        b_ref[8 * k : 8 * k + 8] = jnp.broadcast_to(jnp.sum(pre_low.astype(F32), 0, keepdims=True), (8, b_ref.shape[1]))
+        out_ref[...] += mm_nt(pre_low, up_ref[r])
+    wait(start(blocks_out([(f, 2 * unit) for f in full], info_ref, send_ref, near_ref, pass_ref), sem))
+
+
+def hidden_back(info, pair, mixed_low, act_t, slope, normed_t, up, down, acc):
     total, width = mixed_low.shape
-    count = len(pieces)
+    k = len(pair)
     return pl.pallas_call(
-        partial(hidden_back_kernel, r, first, count),
-        in_specs=[SMEM] + [VMEM] * 5 + [HBM] * count,
+        partial(hidden_back_kernel, pair),
+        in_specs=[SMEM] + [VMEM] * 7,
         out_specs=[HBM] * 3 + [VMEM] * 2,
         out_shape=(
-            shape((width, width), BF16),
-            shape((width // 2, width), BF16),
-            shape((width // 2, width), BF16),
+            shape((k * width, width), BF16),
+            shape((k * width // 2, width), BF16),
+            shape((k * width // 2, width), BF16),
             shape((total, width), F32),
-            shape((8, width), F32),
+            shape((8 * k, width), F32),
         ),
-        scratch_shapes=[
-            pltpu.VMEM((width, width), BF16),
-            pltpu.VMEM((width, width), BF16),
-            pltpu.VMEM((2 * width, width), BF16),
-            DMA((2,)),
-        ],
-        input_output_aliases={5: 3},
-        compiler_params=params(32),
-        cost_estimate=cost(7, 8),
+        scratch_shapes=[pltpu.VMEM((2 * width, width), BF16) for _ in pair] + [DMA],
+        input_output_aliases={7: 3},
+        compiler_params=params(24),
+        cost_estimate=cost(7 * k, 8 * k),
         name="hidden_back",
-    )(info, mixed_low, act_t, slope, normed_t, acc, *pieces)
+    )(info, mixed_low, act_t, slope, normed_t, up, down, acc)
 
 
 def norm_back_kernel(attended_ref, grad_ref, vec_ref, sums_ref, out_ref, low_ref, all_ref):
@@ -473,22 +470,24 @@
     )(attended, grad, vec, sums)
 
 
-def attend_back_kernel(words, gw, heads, first, count, info_ref, rows_ref, lt_ref, low_ref, up_ref, acc_ref, *refs):
+def attend_back_kernel(words, gw, heads, final, count, info_ref, rows_ref, lt_ref, low_ref, up_ref, acc_ref, *refs):
     pw_ref, pe_ref, ctx_ref = refs[:3]
-    pieces = refs[3 : 3 + count]
+    pieces, refs = refs[3 : 3 + count], refs[3 + count :]
+    if final:
+        spans_ref, send_ref, near_ref, pass_ref, words_ref, ents_ref, pos_s, *refs = refs
+    else:
+        send_ref, near_ref, pass_ref, out_ref, *refs = refs
     (
-        send_ref, near_ref, pass_ref, out_ref,
         w_s, pw_s, pe_s, ctx_s, qw_s, qe_s, k_s, v_s, dc_s, p_s, ds_s, dpw_s, dpe_s, full_s, sem,
-    ) = refs[3 + count :]
+    ) = refs
     half = 2 * gw
     total = rows_ref.shape[0]
-    part = info_ref[2]
     size = w_s.shape[0] // 8
     saved = start([(pw_ref, pw_s), (pe_ref, pe_s)], sem.at[0])
     if count == 1:
         reads = start([(pieces[0], w_s)], sem.at[1])
     else:
-        reads = start(place(pieces, part, size, (w_s,)), sem.at[1])
+        reads = start(place(pieces, info_ref, size, (w_s,)), sem.at[1])
     last = start([(ctx_ref, ctx_s)], sem.at[2])
     wait(saved)
     split_heads(words, gw, heads, pw_s, pe_s, qw_s, qe_s, k_s, v_s)
@@ -546,29 +545,49 @@
     row = lax.broadcasted_iota(jnp.int32, (spare, 2 * half), 0)
     sums = jnp.where(row == 0, sum_a, jnp.where(row == 1, sum_b, jnp.where(row == 2, up_ref[0:1], 0.0)))
     full_s[7 * gw :] = sums.astype(BF16)
-    writes = start(blocks_out(full_s, part, size, first, send_ref, near_ref, pass_ref), sem.at[3])
-    out_ref[:words] = acc_ref[:words] + mm(dpw, w_s[: 2 * half])
-    out_ref[words:] = acc_ref[words:] + mm(dpe, w_s[half : 3 * half])
+    if final:
+        grad = acc_ref[words:] + mm(dpe, w_s[half : 3 * half])
+        ents_ref[...] = grad
+        spans = spans_ref[info_ref[0]]
+        begin = spans[:, 0:1]
+        end = spans[:, 1:2]
+        position = lax.broadcasted_iota(jnp.int32, (total - words, words), 1)
+        inside = jnp.where(jnp.logical_and(position >= begin, position < end), 1.0, 0.0).astype(BF16)
+        scaled = grad * (1.0 / (end - begin).astype(F32))
+        high = scaled.astype(BF16)
+        rest = (scaled - high.astype(F32)).astype(BF16)
+        pos_s[...] = (mm_tn(inside, high) + mm_tn(inside, rest)).astype(BF16)
+        sources = [(full_s, size), (pos_s, words // 8)]
+        writes = start(blocks_out(sources, info_ref, send_ref, near_ref, pass_ref), sem.at[3])
+        words_ref[...] = acc_ref[:words] + mm(dpw, w_s[: 2 * half])
+    else:
+        writes = start(blocks_out([(full_s, size)], info_ref, send_ref, near_ref, pass_ref), sem.at[3])
+        out_ref[:words] = acc_ref[:words] + mm(dpw, w_s[: 2 * half])
+        out_ref[words:] = acc_ref[words:] + mm(dpe, w_s[half : 3 * half])
     wait(writes)
 
 
-def attend_back(info, first, rows_low, saved, low, up_sums, acc, pieces, words, heads, rows):
+def attend_back(info, rows_low, saved, low, up_sums, acc, pieces, words, heads, rows, spans=None):
     total, width = rows_low.shape
     pw, pe, ctx, lt = saved
     ents = total - words
     gw = heads * HEAD_DIM
     count = len(pieces)
+    final = spans is not None
+    moved = rows + words if final else rows
+    grads = (shape((words, width), F32), shape((ents, width), F32)) if final else (shape((total, width), F32),)
     return pl.pallas_call(
-        partial(attend_back_kernel, words, gw, heads, first, count),
-        in_specs=[SMEM] + [VMEM] * 5 + [HBM] * (3 + count),
-        out_specs=[HBM] * 3 + [VMEM],
+        partial(attend_back_kernel, words, gw, heads, final, count),
+        in_specs=[SMEM] + [VMEM] * 5 + [HBM] * (3 + count) + [VMEM] * final,
+        out_specs=[HBM] * 3 + [VMEM] * len(grads),
         out_shape=(
-            shape((rows // 2, width), BF16),
-            shape((rows // 4, width), BF16),
-            shape((rows // 4, width), BF16),
-            shape((total, width), F32),
-        ),
-        scratch_shapes=[
+            shape((moved // 2, width), BF16),
+            shape((moved // 4, width), BF16),
+            shape((moved // 4, width), BF16),
+        )
+        + grads,
+        scratch_shapes=[pltpu.VMEM((words, width), BF16)] * final
+        + [
             pltpu.VMEM((rows, width), BF16),
             pltpu.VMEM((words, 4 * gw), BF16),
             pltpu.VMEM((ents, 4 * gw), BF16),
@@ -583,57 +602,17 @@
             pltpu.VMEM((rows, width), BF16),
             DMA((4,)),
         ],
-        input_output_aliases={5: 3},
+        input_output_aliases={} if final else {5: 3},
         compiler_params=params(32),
         cost_estimate=cost(11, 8),
         name="attend_back",
-    )(info, rows_low, lt, low, up_sums, acc, pw, pe, ctx, *pieces)
-
-
-def finish_kernel(info_ref, acc_ref, spans_ref, words_ref, ents_ref, send_ref, near_ref, pass_ref, pos_s, sem):
-    words = words_ref.shape[0]
-    count = ents_ref.shape[0]
-    grad = acc_ref[words:]
-    ents_ref[...] = grad
-    spans = spans_ref[info_ref[0]]
-    begin = spans[:, 0:1]
-    end = spans[:, 1:2]
-    position = lax.broadcasted_iota(jnp.int32, (count, words), 1)
-    inside = jnp.where(jnp.logical_and(position >= begin, position < end), 1.0, 0.0).astype(BF16)
-    scaled = grad * (1.0 / (end - begin).astype(F32))
-    high = scaled.astype(BF16)
-    rest = (scaled - high.astype(F32)).astype(BF16)
-    pos_s[...] = (mm_tn(inside, high) + mm_tn(inside, rest)).astype(BF16)
-    writes = start(blocks_out(pos_s, info_ref[2], words // 8, 2, send_ref, near_ref, pass_ref), sem)
-    words_ref[...] = acc_ref[:words]
-    wait(writes)
-
-
-def finish_rows(info, acc, spans, words):
-    total, width = acc.shape
-    ents = total - words
-    return pl.pallas_call(
-        finish_kernel,
-        in_specs=[SMEM] + [VMEM] * 2,
-        out_specs=[VMEM] * 2 + [HBM] * 3,
-        out_shape=(
-            shape((words, width), F32),
-            shape((ents, width), F32),
-            shape((words // 2, width), BF16),
-            shape((words // 4, width), BF16),
-            shape((words // 4, width), BF16),
-        ),
-        scratch_shapes=[pltpu.VMEM((words, width), BF16), DMA],
-        compiler_params=params(16),
-        cost_estimate=cost(0.5, 6),
-        name="finish_rows",
-    )(info, acc, spans)
+    )(info, rows_low, lt, low, up_sums, acc, pw, pe, ctx, *pieces, *((spans,) if final else ()))
 
 
 def spread_query_kernel(info_ref, *refs):
     pieces = refs[:8]
     query_ref, key_ref, value_ref, out_ref, qb_ref, vb_ref, ub_ref, s, sem = refs[8:]
-    wait(start(place(pieces, info_ref[2], s.shape[0] // 8, (s,)), sem))
+    wait(start(place(pieces, info_ref, s.shape[0] // 8, (s,)), sem))
     gw = key_ref.shape[0]
     for i, k in ((0, 0), (1, 1), (2, 4), (3, 5)):
         query_ref[i] = s[k * gw : (k + 1) * gw].astype(F32)
@@ -670,7 +649,7 @@
 def spread_hidden_kernel(info_ref, *refs):
     pieces = refs[:8]
     up_ref, down_ref, up_s, down_s, sem = refs[8:]
-    wait(start(place(pieces, info_ref[2], up_ref.shape[0] // 8, (up_s, down_s)), sem))
+    wait(start(place(pieces, info_ref, up_ref.shape[0] // 8, (up_s, down_s)), sem))
     up_ref[...] = up_s[...].astype(F32)
     down_ref[...] = down_s[...].astype(F32)
 
@@ -693,7 +672,7 @@
 def spread_pos_kernel(info_ref, *refs):
     pieces = refs[:8]
     pos_ref, s, sem = refs[8:]
-    wait(start(place(pieces, info_ref[2], s.shape[0] // 8, (s,)), sem))
+    wait(start(place(pieces, info_ref, s.shape[0] // 8, (s,)), sem))
     pos_ref[...] = s[...].astype(F32)
 
 
@@ -734,19 +713,19 @@
     def swap_core(self, v):
         return self.swap(v, 1)
 
-    def swap_code(self, v, code):
-        return self.swap(v, ((code >> 1) & 1) * 2 + (code & 1) * 4)
+    def first(self, v):
+        return lax.ppermute(v, "dp", [(i, i ^ (4 if i % 2 else 2)) for i in range(self.dp)])
+
+    def second(self, v):
+        return lax.ppermute(v, "dp", [(i, i ^ (2 if i % 2 else 4)) for i in range(self.dp)])
 
 
 def after(value, *others):
     return lax.optimization_barrier((value,) + others)[0]
 
 
-def gather_group(links, piece, first):
-    second = 3 - first
-    over = {first: links.swap_code(piece, first), second: links.swap_code(piece, second)}
-    near = (piece, over[2], over[1], links.swap_code(over[first], second))
-    return near + tuple(links.swap_core(v) for v in near)
+def sync(*values):
+    return lax.optimization_barrier(values)
 
 
 def add_low(*parts):
@@ -757,54 +736,22 @@
 
 
 class Blocks:
-    def __init__(self, links, first, send, near, far):
-        self.links, self.first, self.near, self.far = links, first, near, far
+    def __init__(self, links, send, near, far):
+        self.links, self.send, self.near, self.far = links, send, near, far
         self.unit = near.shape[0] // 2
-        self.got = links.swap_core(send)
 
     def one(self):
-        u = self.unit
-        value = add_low(self.far, self.got[2 * u :])
-        self.a = self.links.swap_code(value, self.first)
-        return value
+        return add_low(self.far, self.got[2 * self.unit :])
 
     def two(self):
         u = self.unit
-        value = add_low(self.near[u:], self.got[u : 2 * u], self.a[u:])
-        self.parts = (self.a[:u], self.links.swap_code(value, 3 - self.first))
-        return value
-
-    def direct(self):
-        u = self.unit
-        first, second = self.first, 3 - self.first
-        a = add_low(self.far[:u], self.got[2 * u : 3 * u])
-        b = add_low(self.far[u:], self.got[3 * u :])
-        c = add_low(self.near[u:], self.got[u : 2 * u])
-        links = self.links
-        self.parts = (links.swap_code(b, 3), links.swap_code(a, first), links.swap_code(c, second))
-
-    def rest(self, *more):
-        u = self.unit
-        value = add_low(self.near[:u], self.got[:u], *self.parts, *more)
+        return add_low(self.near[u:], self.got[u : 2 * u], self.a[u:])
+
+    def rest(self, low, high, *more):
+        value = add_low(self.near[low:high], self.got[low:high], self.a[low:high], self.b[low:high], *more)
         for j in range(2, self.links.bits):
             value = add_low(value, self.links.swap(value, 2 << j))
         return value
-
-
-def spread_all(links, value):
-    near = (value, links.swap_code(value, 2), links.swap_code(value, 1), links.swap_code(value, 3))
-    return near + tuple(links.swap_core(v) for v in near)
-
-
-def reduce_everywhere(links, v):
-    v = v + links.swap_core(v)
-    for j in range(links.bits):
-        v = v + links.swap(v, 2 << j)
-    mask = 1
-    while mask < links.ring:
-        v = v + links.swap_z(v, mask)
-        mask *= 2
-    return v
 
 
 def shards(
@@ -842,100 +789,137 @@
     heads = gw // HEAD_DIM
     rows = -(-(7 * gw + 3) // (8 * TILE)) * 8 * TILE
     part = 4 * links.core + 2 * links.bit[0] + links.bit[1]
-    info = jnp.stack([z, links.core, part, part]).astype(jnp.int32)
+    info = jnp.stack([z, links.core, part, 2 - links.core]).astype(jnp.int32)
 
     own_w, piece_q, piece_f = pack(
         info, query_b, value_b[None], up_b[None], jnp.swapaxes(query_w, 1, 2), key_w.T, value_w.T, out_w, up_w, down_w, rows
     )
-    shifted = []
-    for _ in range(n - 1):
-        piece_q = links.shift_z(piece_q, 1)
-        shifted.append(piece_q)
-    piece_f = after(piece_f, shifted[0])
-    query_groups = [(own_w,)] + [gather_group(links, v, 1 + i % 2) for i, v in enumerate(shifted)]
-    ffn_groups = []
-    for i in range(n - 1):
-        piece_f = links.shift_z(piece_f, 1)
-        ffn_groups.append(gather_group(links, piece_f, 2 - i % 2))
-
+    first, second, core, shift = links.first, links.second, links.swap_core, links.shift_z
+    v1, v2, v3 = (shift(piece_q, r) for r in range(1, n))
     rows_low, acc = start_rows(info, word_in, entity_in, entity_spans, pos_table, out_b[None], words, ents)
     saved = []
     biases = []
-    for r in range(n):
-        pw, pe, ctx, lt, bias, acc = attend(info, rows_low, acc, query_groups[r], words, heads, rows)
+
+    def attend_one(acc, pieces):
+        pw, pe, ctx, lt, bias, acc = attend(info, rows_low, acc, pieces, words, heads, rows)
         saved.append((pw, pe, ctx, lt))
         biases.append(bias)
-    attended = acc
+        return acc
+
+    acc = attend_one(acc, (own_w,))
+    acc, v1, piece_f = sync(acc, v1, piece_f)
+    a1, b1, f1 = first(v1), second(v1), shift(piece_f, 1)
+    acc, v1, a1, b1, v2, v3, piece_f = sync(acc, v1, a1, b1, v2, v3, piece_f)
+    c1, kv, ka, kb, a2, b2 = second(a1), core(v1), core(a1), core(b1), first(v2), second(v2)
+    acc, c1, kv, ka, kb, a2, b2, piece_f, v3 = sync(acc, c1, kv, ka, kb, a2, b2, piece_f, v3)
+    kc, f2, f3 = core(c1), shift(piece_f, 2), shift(piece_f, 3)
+    acc, kc, a2, v3 = sync(acc, kc, a2, v3)
+    group_1 = (v1, a1, b1, c1, kv, ka, kb, kc)
+
+    c2, a3, b3 = second(a2), first(v3), second(v3)
+    acc = attend_one(acc, group_1)
+    acc, c2, a3, b3, f1, f2, f3 = sync(acc, c2, a3, b3, f1, f2, f3)
+    kv, ka, kb, kc = core(v2), core(a2), core(b2), core(c2)
+    acc, kv, ka, kb, kc, far_f, a3, v3 = sync(acc, kv, ka, kb, kc, jnp.concatenate([f1, f2, f3], 0), a3, v3)
+    group_2 = (v2, a2, b2, c2, kv, ka, kb, kc)
+
+    c3, af, bf, kv, ka = second(a3), first(far_f), second(far_f), core(v3), core(a3)
+    acc = attend_one(acc, group_2)
+    acc, c3, af, bf, kv, ka = sync(acc, c3, af, bf, kv, ka)
+    kb, kc = core(b3), core(c3)
+    acc, kb, kc, af, bf, far_f = sync(acc, kb, kc, af, bf, far_f)
+    group_3 = (v3, a3, b3, c3, kv, ka, kb, kc)
+
+    cf, kv, ka, kb = second(af), core(far_f), core(af), core(bf)
+    acc = attend_one(acc, group_3)
+    attended, cf, kv, ka, kb = sync(acc, cf, kv, ka, kb)
+    ffn_pieces = (far_f, af, bf, cf, kv, ka, kb, core(cf))
+    query_groups = ((own_w,), group_1, group_2, group_3)
 
     vec = jnp.stack([norm1_gain, norm1_bias, down_b, norm2_gain, norm2_bias] + [down_b] * 3)
-    _, normed_t, act_t, slope, out_words, out_ents, mixed_low, acc, sums = hidden(
-        info, attended, vec, word_mask, entity_mask, cot_words, cot_entities, biases, (up_w, down_w), ffn_groups
+    normed_t, act_t, slope, up, down, out_words, out_ents, mixed_low, acc, sums = hidden(
+        info, attended, vec, word_mask, entity_mask, cot_words, cot_entities, biases, (up_w, down_w), ffn_pieces
     )
 
-    order = list(range(1, n)) + [0]
-    ffn_pieces = [(up_w, down_w)] + ffn_groups
-    blocks_f = []
+    size = width // 4
+    unit = rows // 8
     up_sums = [None] * n
-    for i, r in enumerate(order):
-        first = 2 - i % 2
-        send, near, far, acc, up_sums[r] = hidden_back(
-            info, r, first, mixed_low, act_t, slope, normed_t, acc, ffn_pieces[r]
+
+    def ffn_pair(pair, acc):
+        send, near, far, acc, up_sum = hidden_back(info, pair, mixed_low, act_t, slope, normed_t, up, down, acc)
+        for k, r in enumerate(pair):
+            up_sums[r] = up_sum[8 * k : 8 * k + 8]
+        return Blocks(links, send, near, far), acc
+
+    fa, acc = ffn_pair((1, 2), acc)
+    fa.got = core(fa.send)
+    fb, acc = ffn_pair((3, 0), acc)
+    acc, fa.got = sync(acc, fa.got)
+    one_a = fa.one()
+    acc, attended_low, sums = norm_back(attended, acc, vec, sums)
+    acc, one_a, sums = sync(acc, one_a, sums)
+
+    def back(r, acc, spans=None):
+        send, near, far, *acc = attend_back(
+            info, rows_low, saved[r], attended_low, up_sums[r], acc, query_groups[r], words, heads, rows, spans
         )
-        blocks_f.append(Blocks(links, first, send, near, far))
-        if i:
-            acc = after(acc, blocks_f[i - 1].one())
-    acc, attended_low, sums = norm_back(attended, acc, vec, sums)
-
-    last = n - 1
-    blocks_q = []
-    sent_f = []
-    sent_q = []
-    acc = after(acc, blocks_f[last].one(), *[b.two() for b in blocks_f[: n // 2]])
-    pieces_f = None
-    for i, r in enumerate(order):
-        first = 1 + i % 2
-        send, near, far, acc = attend_back(
-            info, first, rows_low, saved[r], attended_low, up_sums[r], acc, query_groups[r], words, heads, rows
-        )
-        blocks_q.append(Blocks(links, first, send, near, far))
-        if i == 0:
-            ready = [b.two() for b in blocks_f[n // 2 :]]
-            done = [b.rest() for b in blocks_f[: n // 2]]
-            sent_f += [links.shift_z(v, -order[j]) for j, v in enumerate(done)]
-            acc = after(acc, *ready, *done)
-        elif i == 1:
-            done = [b.rest() for b in blocks_f[n // 2 : last]]
-            sent_f += [links.shift_z(v, -order[n // 2 + j]) for j, v in enumerate(done)]
-            total_sums = reduce_everywhere(links, sums)
-            acc = after(acc, *done, blocks_q[0].one())
-        elif i == 2:
-            value = blocks_f[last].rest(*sent_f)
-            pieces_f = spread_all(links, value)
-            acc = after(acc, value, blocks_q[0].two(), blocks_q[1].one(), total_sums)
-    grad_words, grad_ents, *pos_blocks = finish_rows(info, acc, entity_spans, words)
-    blocks_p = Blocks(links, 2, *pos_blocks)
-
-    done = blocks_q[0].rest()
-    sent_q.append(links.shift_z(done, -order[0]))
-    blocks_q[1].two()
-    blocks_q[2].direct()
-    blocks_q[3].direct()
-    blocks_p.direct()
-    for j in range(1, last):
-        sent_q.append(links.shift_z(blocks_q[j].rest(), -order[j]))
-    grad_up, grad_down = spread_hidden(info, pieces_f)
-    value = blocks_q[last].rest(*sent_q)
-    pieces_q = spread_all(links, value)
-    pos = blocks_p.rest()
-    mask = 1
-    while mask < n:
-        pos = add_low(pos, links.swap_z(pos, mask))
-        mask *= 2
-    pieces_p = spread_all(links, pos)
+        return Blocks(links, send, near, far), *acc
+
+    fa.a, fb.got, more = first(one_a), core(fb.send), core(sums)
+    q1, acc = back(1, acc)
+    acc, fa.a, fb.got, more = sync(acc, fa.a, fb.got, more)
+    acc, two_a, one_b, sums = sync(acc, fa.two(), fb.one(), sums + more)
+
+    fa.b, fb.a, q1.got, more = second(two_a), first(one_b), core(q1.send), links.swap(sums, 2)
+    q2, acc = back(2, acc)
+    acc, fa.b, fb.a, q1.got, more = sync(acc, fa.b, fb.a, q1.got, more)
+    acc, r1, r2, two_b, one_1, sums = sync(
+        acc, fa.rest(0, size), fa.rest(size, 2 * size), fb.two(), q1.one(), sums + more
+    )
+
+    z1, z2, fb.b, q1.a, q2.got = shift(r1, -1), shift(r2, -2), second(two_b), first(one_1), core(q2.send)
+    q3, acc = back(3, acc)
+    acc, z1, z2, fb.b, q1.a, q2.got = sync(acc, z1, z2, fb.b, q1.a, q2.got)
+    acc, r3, two_1, one_2 = sync(acc, fb.rest(0, size), q1.two(), q2.one())
+
+    z3, q1.b, q2.a, q3.got, more = shift(r3, -3), second(two_1), first(one_2), core(q3.send), links.swap(sums, 4)
+    q4, grad_words, grad_ents = back(0, acc, entity_spans)
+    q4.send, z3, q1.b, q2.a, q3.got, more = sync(q4.send, z3, q1.b, q2.a, q3.got, more)
+
+    q4.got = core(q4.send)
+    value_1, two_2, one_3 = q1.rest(0, unit), q2.two(), q3.one()
+    y1, q2.b, q3.a = shift(value_1, -1), second(two_2), first(one_3)
+    sums = sums + more
+    for j in range(2, links.bits):
+        sums = sums + links.swap(sums, 2 << j)
+    own_f = fb.rest(size, 2 * size, z1, z2, z3)
+    q4.got, q2.b, q3.a, sums, own_f = sync(q4.got, q2.b, q3.a, sums, own_f)
+
+    q4.a, y2, q3.b, ga = first(q4.one()), shift(q2.rest(0, unit), -2), second(q3.two()), first(own_f)
+    q4.a, q3.b, y1, ga, own_f, sums = sync(q4.a, q3.b, y1, ga, own_f, sums)
+
+    q4.b, y3, gb, more = second(q4.two()), shift(q3.rest(0, unit), -3), second(own_f), links.swap_z(sums, 1)
+    q4.b, y2, gb, more, ga, sums = sync(q4.b, y2, gb, more, ga, sums)
+
+    pos = q4.rest(unit, unit + words // 8)
+    p1, p2, p3 = (links.swap_z(pos, mask) for mask in (1, 2, 3))
+    gc = second(ga)
+    sums = sums + more
+    p1, p2, p3, y3, gc, pos, sums = sync(p1, p2, p3, y3, gc, pos, sums)
+
+    pos = ((pos.astype(F32) + p1.astype(F32)) + (p2.astype(F32) + p3.astype(F32))).astype(BF16)
+    own_q = q4.rest(0, unit, y1, y2, y3)
+    qa, qb, pa, pb, more = first(own_q), second(own_q), first(pos), second(pos), links.swap_z(sums, 2)
+    total_sums = sums + more
+    qa, qb, pa, pb, own_q, pos, own_f, ga, gb, gc = sync(qa, qb, pa, pb, own_q, pos, own_f, ga, gb, gc)
+    near_q = (own_q, qa, qb, second(qa))
+    near_p = (pos, pa, pb, second(pa))
+    near_f = (own_f, ga, gb, gc)
+    grad_up, grad_down = spread_hidden(info, near_f + tuple(core(v) for v in near_f))
+    pos_sum = spread_pos(info, near_p + tuple(core(v) for v in near_p))
     grad_query_t, grad_key_t, grad_value_t, grad_out, grad_query_b, grad_value_b, grad_up_b = spread_query(
-        info, pieces_q, gw
+        info, near_q + tuple(core(v) for v in near_q), gw
     )
-    pos_sum = spread_pos(info, pieces_p)
     return (
         out_words,
         out_ents,

time: 459 us -> 398 us (0.87)
  waiting for transfers between devices: 125 us -> 93.7 us
  Pallas kernels: 180 us -> 164 us
  other arithmetic: 14 us -> 4.54 us
    ppermute x96 -> x37, starting transfers between devices: 68.7 us -> 9.14 us  [swap(): return lax.ppermute(v, 'dp', [(i, i ^ code) for i in range(self.dp)])]
    ppermute x96 -> x37, waiting for transfers between devices: 67.2 us -> 10.4 us  [swap(): return lax.ppermute(v, 'dp', [(i, i ^ code) for i in range(self.dp)])]
    ppermute x0 -> x33, waiting for transfers between devices: none -> 45.8 us  [the longest x20 40.5 us: second(): lax.ppermute(v, 'dp', [(i, i ^ (2 if i % 2 else 4)) for i in range(self.d...]
    ppermute x0 -> x33, starting transfers between devices: none -> 34.6 us  [the longest x20 21.5 us: second(): lax.ppermute(v, 'dp', [(i, i ^ (2 if i % 2 else 4)) for i in range(self.d...]
    ppermute x4 -> x5, waiting for transfers between devices: 31.6 us -> 8.86 us  [swap_z(): return lax.ppermute(v, 'tensor', [(i, i ^ mask) for i in range(self.ring)])]
    ppermute x12, starting transfers between devices: 13.4 us -> 29.3 us  [shift_z(): return lax.ppermute(v, 'tensor', [(i, (i + by) % n) for i in range(n)])]
    pallas_call x9 -> x6, Pallas kernels: 90.7 us -> 75 us  [the longest x4 57 us: attend_back(): pl.pallas_call(partial(attend_back_kernel, words, gw, heads, final, count...]
    convert_element_type x26 -> x20, other arithmetic: 13.3 us -> 3.71 us  [add_low(): return total.astype(BF16)]
  transfers between devices with their start and end apart: 112 -> 87, of which waited for: 25 -> 25; matrix products, arithmetic and copies ran while one was open for 3% -> 2% of each run, Pallas kernels for 30% -> 31%
where the time goes in v4:
time: 398 us; the launch traced here: 393 us
  Pallas kernels  164 us (41%)
  waiting for transfers between devices  93.7 us (24%)
  starting transfers between devices  81.8 us (21%)
  local copies, waits for them, and re-layouts  46.2 us (12%)
  other arithmetic  4.54 us (1%)
    pallas_call x4, Pallas kernels, attend_back(): pl.pallas_call(partial(attend_back_kernel, words, gw, heads, final, count...  57 us
    pallas_call x4, Pallas kernels, attend(): pl.pallas_call(partial(attend_kernel, words, gw, heads, count), in_specs=...  43.5 us
    unnamed x223, local copies, waits for them, and re-layouts  41 us
    ppermute x20, waiting for transfers between devices, second(): lax.ppermute(v, 'dp', [(i, i ^ (2 if i % 2 else 4)) for i in range(self.d...  40.5 us
    ppermute x12, starting transfers between devices, shift_z(): return lax.ppermute(v, 'tensor', [(i, (i + by) % n) for i in range(n)])  29.3 us
    pallas_call x1, Pallas kernels, hidden(): pl.pallas_call(partial(hidden_kernel, n), in_specs=[SMEM] + [VMEM] * (6 +...  28.6 us
    ppermute x12, waiting for transfers between devices, shift_z(): return lax.ppermute(v, 'tensor', [(i, (i + by) % n) for i in range(n)])  28.6 us
    ppermute x20, starting transfers between devices, second(): lax.ppermute(v, 'dp', [(i, i ^ (2 if i % 2 else 4)) for i in range(self.d...  21.5 us
  transfers between devices with their start and end apart: 87, of which 25 were waited for; matrix products, arithmetic and copies ran while one was open for 2% of the time, Pallas kernels for 31%

profile of v4, /device:TPU:0, one launch (start us, length us, event | category | flops | bytes accessed | tf_op | source)
XLA Modules:
  0.0 392.6 jit_solution(6682181200342451303)
XLA Ops:
  9.5 2.2 pack.1
  13.8 5.1 %collective-permute-start.4 = (bf16[176,768]{1,0:T(8,128)(2,1)}, bf16[176,768]{1,0:T(8,128)(2,1)}, u32[]{:S(2)}, u32[]{:S(2)}) collective-permute-start(bf16[176,768]{1,0:T(8,128)(2,1)} %get-tuple-element.231), channel_id=1, source_target_pairs={{0,3},{1,0},{2,1},{3,2},{4,7},{5,4},{6,5},{7,6},{8,11},{9,8},{10,9... | collective-permute-start | bytes 811016 | tf_op jit(solution)/shard_map/ppermute | solution.py:705
  23.9 10.3 %attend_own.1 = (bf16[512,768]{1,0:T(8,128)(2,1)S(1)}, bf16[128,768]{1,0:T(8,128)(2,1)S(1)}, bf16[640,192]{1,0:T(8,128)(2,1)S(1)}, f32[8,640]{1,0:T(8,128)S(1)},...) custom-call(s32[4]{0:T(128)S(1)} %pad_add_fusion.info_ref, ...), custom_call_target="tpu_custom_call", output_to_operand_aliasing={{5}: (2, {})} | custom-call | flops 8000000000 | bytes 6000000 | tf_op jit(solution)/shard_map/attend_own/pallas_call | solution.py:260
  40.5 1.7 collective-permute-done.3.refs_0_.refs_3_
  42.2 4.1 %collective-permute-done.2.refs_2_.refs_5_ = bf16[176,768]{1,0:T(8,128)(2,1)S(1)} collective-permute-done((bf16[176,768]{1,0:T(8,128)(2,1)}, bf16[176,768]{1,0:T(8,128)(2,1)S(1)}, u32[]{:S(2)}, u32[]{:S(2)}) %collective-permute-start.2) | collective-permute-done | bytes 270368 | tf_op jit(solution)/shard_map/ppermute | solution.py:720
  49.7 5.7 %collective-permute-start.15 = (bf16[192,768]{1,0:T(8,128)(2,1)S(1)}, bf16[192,768]{1,0:T(8,128)(2,1)S(1)}, u32[]{:S(2)}, u32[]{:S(2)}) collective-permute-start(bf16[192,768]{1,0:T(8,128)(2,1)S(1)} %copy-done.21), channel_id=1, source_target_pairs={{0,1},{1,2},{2,3},{3,0},{4,5},{5,6},{6,7},{7,4},{8,9},{9,10},{10,1... | collective-permute-start | bytes 884744 | tf_op jit(solution)/shard_map/ppermute | solution.py:705
  55.4 3.7 collective-permute-done.10.refs_2_.refs_5_
  59.2 2.7 collective-permute-start.17
  61.9 5.7 %collective-permute-start.16 = (bf16[192,768]{1,0:T(8,128)(2,1)S(1)}, bf16[192,768]{1,0:T(8,128)(2,1)S(1)}, u32[]{:S(2)}, u32[]{:S(2)}) collective-permute-start(bf16[192,768]{1,0:T(8,128)(2,1)S(1)} %copy-done.21), channel_id=1, source_target_pairs={{0,2},{1,3},{2,0},{3,1},{4,6},{5,7},{6,4},{7,5},{8,10},{9,11},{10,... | collective-permute-start | bytes 884744 | tf_op jit(solution)/shard_map/ppermute | solution.py:705
  70.2 11.1 %attend_far.3 = (bf16[512,768]{1,0:T(8,128)(2,1)S(1)}, bf16[128,768]{1,0:T(8,128)(2,1)S(1)}, bf16[640,192]{1,0:T(8,128)(2,1)S(1)}, f32[8,640]{1,0:T(8,128)S(1)},...) custom-call(s32[4]{0:T(128)S(1)} %pad_add_fusion.info_ref, ...), custom_call_target="tpu_custom_call", output_to_operand_aliasing={{5}: (2, {})} | custom-call | flops 8000000000 | bytes 6000000 | tf_op jit(solution)/shard_map/attend_far/pallas_call | solution.py:260
  81.8 6.0 %collective-permute-done.16 = bf16[192,768]{1,0:T(8,128)(2,1)S(1)} collective-permute-done((bf16[192,768]{1,0:T(8,128)(2,1)S(1)}, bf16[192,768]{1,0:T(8,128)(2,1)S(1)}, u32[]{:S(2)}, u32[]{:S(2)}) %collective-permute-start.16) | collective-permute-done | bytes 294944 | tf_op jit(solution)/shard_map/ppermute | solution.py:705
  93.9 11.1 %attend_far.4 = (bf16[512,768]{1,0:T(8,128)(2,1)S(1)}, bf16[128,768]{1,0:T(8,128)(2,1)S(1)}, bf16[640,192]{1,0:T(8,128)(2,1)S(1)}, f32[8,640]{1,0:T(8,128)S(1)},...) custom-call(s32[4]{0:T(128)S(1)} %pad_add_fusion.info_ref, ...), custom_call_target="tpu_custom_call", output_to_operand_aliasing={{5}: (2, {})} | custom-call | flops 8000000000 | bytes 6000000 | tf_op jit(solution)/shard_map/attend_far/pallas_call | solution.py:260
  107.1 7.9 %collective-permute-done.22.refs_3_.refs_6_ = bf16[176,768]{1,0:T(8,128)(2,1)S(1)} collective-permute-done((bf16[176,768]{1,0:T(8,128)(2,1)S(1)}, bf16[176,768]{1,0:T(8,128)(2,1)S(1)}, u32[]{:S(2)}, u32[]{:S(2)}) %collective-permute-start.22) | collective-permute-done | bytes 270368 | tf_op jit(solution)/shard_map/ppermute | solution.py:720
  118.9 11.1 %attend_far.5 = (bf16[512,768]{1,0:T(8,128)(2,1)S(1)}, bf16[128,768]{1,0:T(8,128)(2,1)S(1)}, bf16[640,192]{1,0:T(8,128)(2,1)S(1)}, f32[8,640]{1,0:T(8,128)S(1)},...) custom-call(s32[4]{0:T(128)S(1)} %pad_add_fusion.info_ref, ...), custom_call_target="tpu_custom_call", output_to_operand_aliasing={{5}: (2, {})} | custom-call | flops 8000000000 | bytes 6000000 | tf_op jit(solution)/shard_map/attend_far/pallas_call | solution.py:260
  140.8 28.6 %hidden.1 = (bf16[768,640]{1,0:T(8,128)(2,1)}, bf16[4,768,640]{2,1,0:T(8,128)(2,1)}, f32[4,640,768]{2,1,0:T(8,128)}, bf16[4,768,768]{2,1,0:T(8,128)(2,1)}, bf16[...) custom-call(s32[4]{0:T(128)S(1)} %pad_add_fusion.info_ref, ...), custom_call_target="tpu_custom_call" | custom-call | flops 22000001024 | bytes 20000000 | tf_op jit(solution)/shard_map/hidden/pallas_call | solution.py:368
  171.0 3.3 copy-done.68
  174.3 2.3 copy-done.69
  176.6 2.3 copy-done.70
  179.0 2.1 copy-done.71
  183.5 9.2 %hidden_back.2 = (bf16[1536,768]{1,0:T(8,128)(2,1)S(1)}, bf16[768,768]{1,0:T(8,128)(2,1)S(1)}, bf16[768,768]{1,0:T(8,128)(2,1)S(1)}, f32[640,768]{1,0:T(8,128)S(1)}, f32[16,768]{1,0:T(8,128)S(1)}) custom-call(s32[4]{0:T(128)S(1)} %pad_add_fusion.info_ref, bf16[640,768]{1,0:T(8,128)(2,1)S(1)} %copy-done.73, ...), custom_call_target="tpu_custom_call", output_to_operand_aliasing={{3}: (7, {})} | custom-call | flops 14000000000 | bytes 16000000 | tf_op jit(solution)/shard_map/hidden_back/pallas_call | solution.py:429
  194.3 1.5 copy-done.67
  195.9 8.8 %hidden_back.3 = (bf16[1536,768]{1,0:T(8,128)(2,1)S(1)}, bf16[768,768]{1,0:T(8,128)(2,1)S(1)}, bf16[768,768]{1,0:T(8,128)(2,1)S(1)}, f32[640,768]{1,0:T(8,128)S(1)}, f32[16,768]{1,0:T(8,128)S(1)}) custom-call(s32[4]{0:T(128)S(1)} %pad_add_fusion.info_ref, bf16[640,768]{1,0:T(8,128)(2,1)S(1)} %copy-done.73, ...), custom_call_target="tpu_custom_call", output_to_operand_aliasing={{3}: (7, {})} | custom-call | flops 14000000000 | bytes 16000000 | tf_op jit(solution)/shard_map/hidden_back/pallas_call | solution.py:429
  208.2 13.5 %attend_back.4 = (bf16[704,768]{1,0:T(8,128)(2,1)S(1)}, bf16[352,768]{1,0:T(8,128)(2,1)S(1)}, bf16[352,768]{1,0:T(8,128)(2,1)S(1)}, f32[640,768]{1,0:T(8,128)S(1)}) custom-call(s32[4]{0:T(128)S(1)} %pad_add_fusion.info_ref, bf16[640,768]{1,0:T(8,128)(2,1)S(1)} %copy-done.16, ...), custom_call_target="tpu_custom_call", output_to_operand_aliasing={{3}: (5, {})} | custom-call | flops 11000000512 | bytes 8000000 | tf_op jit(solution)/shard_map/attend_back/pallas_call | solution.py:579
  227.0 13.4 %attend_back.5 = (bf16[704,768]{1,0:T(8,128)(2,1)S(1)}, bf16[352,768]{1,0:T(8,128)(2,1)S(1)}, bf16[352,768]{1,0:T(8,128)(2,1)S(1)}, f32[640,768]{1,0:T(8,128)S(1)}) custom-call(s32[4]{0:T(128)S(1)} %pad_add_fusion.info_ref, bf16[640,768]{1,0:T(8,128)(2,1)S(1)} %copy-done.16, f32[8,640]{1,0:T(8,128)S(1)} %copy-done.101, ...), custom_call_target="tpu_custom_call", output_to_operand_aliasing={{3}: (5, {})} | custom-call | flops 11000000512 | bytes 8000000 | tf_op jit(solution)/shard_map/attend_back/pallas_call | solution.py:579
  240.4 5.9 %collective-permute-done.41 = f32[8,768]{1,0:T(8,128)S(1)} collective-permute-done((f32[8,768]{1,0:T(8,128)S(1)}, f32[8,768]{1,0:T(8,128)S(1)}, u32[]{:S(2)}, u32[]{:S(2)}) %collective-permute-start.41) | collective-permute-done | bytes 24608 | tf_op jit(solution)/shard_map/ppermute | solution.py:711
  247.2 5.0 %collective-permute-start.43 = (bf16[192,768]{1,0:T(8,128)(2,1)S(1)}, bf16[192,768]{1,0:T(8,128)(2,1)S(1)}, u32[]{:S(2)}, u32[]{:S(2)}) collective-permute-start(bf16[192,768]{1,0:T(8,128)(2,1)S(1)} %get-tuple-element.356), channel_id=1, source_target_pairs={{0,2},{1,3},{2,0},{3,1},{4,6},{5,7},{6,4},{7,5},{8,10},{9,11},{10,... | collective-permute-start | bytes 884744 | tf_op jit(solution)/shard_map/ppermute | solution.py:705
  254.5 13.6 %attend_back.6 = (bf16[704,768]{1,0:T(8,128)(2,1)S(1)}, bf16[352,768]{1,0:T(8,128)(2,1)S(1)}, bf16[352,768]{1,0:T(8,128)(2,1)S(1)}, f32[640,768]{1,0:T(8,128)S(1)}) custom-call(s32[4]{0:T(128)S(1)} %pad_add_fusion.info_ref, bf16[640,768]{1,0:T(8,128)(2,1)S(1)} %copy-done.16, f32[8,640]{1,0:T(8,128)S(1)} %copy-done.99, ...), custom_call_target="tpu_custom_call", output_to_operand_aliasing={{3}: (5, {})} | custom-call | flops 11000000512 | bytes 8000000 | tf_op jit(solution)/shard_map/attend_back/pallas_call | solution.py:579
  269.0 1.6 collective-permute-done.43
  273.7 16.5 %attend_back.7 = (bf16[960,768]{1,0:T(8,128)(2,1)S(1)}, bf16[480,768]{1,0:T(8,128)(2,1)S(1)}, bf16[480,768]{1,0:T(8,128)(2,1)S(1)}, f32[512,768]{1,0:T(8,128)}, f32[128,768]{1,0:T(8,128)}) custom-call(s32[4]{0:T(128)S(1)} %pad_add_fusion.info_ref, bf16[640,768]{1,0:T(8,128)(2,1)S(1)} %copy-done.16, f32[8,640]{1,0:T(8,128)S(1)} %get-tuple-element.297.lt_ref, ...), custom_call_target="tpu_custom_call" | custom-call | flops 11000000512 | bytes 8000000 | tf_op jit(solution)/shard_map/attend_back/pallas_call | solution.py:579
  292.9 8.2 %collective-permute-done.53 = bf16[176,768]{1,0:T(8,128)(2,1)S(1)} collective-permute-done((bf16[176,768]{1,0:T(8,128)(2,1)S(1)}, bf16[176,768]{1,0:T(8,128)(2,1)S(1)}, u32[]{:S(2)}, u32[]{:S(2)}) %collective-permute-start.53) | collective-permute-done | bytes 270368 | tf_op jit(solution)/shard_map/ppermute | solution.py:720
  301.1 1.7 collective-permute-done.54
  304.3 3.0 collective-permute-start.57
  309.7 3.1 collective-permute-done.57
  312.8 5.1 %collective-permute-done.56 = bf16[176,768]{1,0:T(8,128)(2,1)S(1)} collective-permute-done((bf16[176,768]{1,0:T(8,128)(2,1)S(1)}, bf16[176,768]{1,0:T(8,128)(2,1)S(1)}, u32[]{:S(2)}, u32[]{:S(2)}) %collective-permute-start.56) | collective-permute-done | bytes 270368 | tf_op jit(solution)/shard_map/ppermute | solution.py:720
  317.8 2.8 collective-permute-done.58.refs_1_
  323.1 3.6 collective-permute-start.62
  326.8 15.3 %collective-permute-done.60 = bf16[176,768]{1,0:T(8,128)(2,1)S(1)} collective-permute-done((bf16[176,768]{1,0:T(8,128)(2,1)S(1)}, bf16[176,768]{1,0:T(8,128)(2,1)S(1)}, u32[]{:S(2)}, u32[]{:S(2)}) %collective-permute-start.60) | collective-permute-done | bytes 270368 | tf_op jit(solution)/shard_map/ppermute | solution.py:705
  343.3 4.3 %collective-permute-start.63 = (bf16[64,768]{1,0:T(8,128)(2,1)S(1)}, bf16[64,768]{1,0:T(8,128)(2,1)S(1)}, u32[]{:S(2)}, u32[]{:S(2)}) collective-permute-start(bf16[64,768]{1,0:T(8,128)(2,1)S(1)} %add_convert_fusion.21), channel_id=1, source_target_pairs={{0,1},{1,0},{2,3},{3,2},{4,5},{5,4},{6,7},{7,6},{8,9},{9,8},{10,11... | collective-permute-start | bytes 294920 | tf_op jit(solution)/shard_map/ppermute | solution.py:708
  347.6 3.1 collective-permute-done.65
  350.7 2.0 collective-permute-done.64
  354.5 1.6 collective-permute-start.71
  357.2 6.1 %collective-permute-done.71.refs_2_ = bf16[64,768]{1,0:T(8,128)(2,1)S(1)} collective-permute-done((bf16[64,768]{1,0:T(8,128)(2,1)S(1)}, bf16[64,768]{1,0:T(8,128)(2,1)S(1)}, u32[]{:S(2)}, u32[]{:S(2)}) %collective-permute-start.71) | collective-permute-done | bytes 98336 | tf_op jit(solution)/shard_map/ppermute | solution.py:720
  364.9 3.8 collective-permute-done.82
  369.5 1.7 collective-permute-start.72
  371.2 5.5 %collective-permute-done.72.refs_3_ = bf16[64,768]{1,0:T(8,128)(2,1)S(1)} collective-permute-done((bf16[64,768]{1,0:T(8,128)(2,1)S(1)}, bf16[64,768]{1,0:T(8,128)(2,1)S(1)}, u32[]{:S(2)}, u32[]{:S(2)}) %collective-permute-start.72) | collective-permute-done | bytes 98336 | tf_op jit(solution)/shard_map/ppermute | solution.py:720
  379.8 2.8 spread_pos.1
  382.7 6.0 %spread_hidden.1 = (f32[768,768]{1,0:T(8,128)}, f32[768,768]{1,0:T(8,128)}) custom-call(s32[4]{0:T(128)S(1)} %pad_add_fusion.info_ref, bf16[192,768]{1,0:T(8,128)(2,1)S(1)} %add_convert_fusion.9.refs_0_, bf16[192,768]{1,0:T(8,128)(2,1)S(1)} %collective-permute-done.58.refs_1_, bf16[192,768]{1,0:T(8,128)(2,1)S(1)} %collective-permute-done.61.refs_2_, ...), custom_call_target="tpu_custom_call" | custom-call | flops 500000000 | bytes 7000000 | tf_op jit(solution)/shard_map/spread_hidden/pallas_call | solution.py:660
  388.8 2.8 spread_query.1
  (407 shorter events, 91.8 us)
Async XLA Ops:
  13.8 26.7 %collective-permute-start.4 = (bf16[176,768]{1,0:T(8,128)(2,1)}, bf16[176,768]{1,0:T(8,128)(2,1)}, u32[]{:S(2)}, u32[]{:S(2)}) collective-permute-start(bf16[176,768]{1,0:T(8,128)(2,1)} %get-tuple-element.231), channel_id=1, source_target_pairs={{0,3},{1,0},{2,1},{3,2},{4,7},{5,4},{6,5},{7,6},{8,11},{9,8},{10,9... | collective-permute-start | bytes 811016 | tf_op jit(solution)/shard_map/ppermute | solution.py:705
  18.8 23.3 %collective-permute-start.3 = (bf16[176,768]{1,0:T(8,128)(2,1)}, bf16[176,768]{1,0:T(8,128)(2,1)}, u32[]{:S(2)}, u32[]{:S(2)}) collective-permute-start(bf16[176,768]{1,0:T(8,128)(2,1)} %get-tuple-element.231), channel_id=1, source_target_pairs={{0,2},{1,3},{2,0},{3,1},{4,6},{5,7},{6,4},{7,5},{8,10},{9,11},{10,... | collective-permute-start | bytes 811016 | tf_op jit(solution)/shard_map/ppermute | solution.py:705
  18.8 18.6 %collective-permute-start = (bf16[176,768]{1,0:T(8,128)(2,1)}, bf16[176,768]{1,0:T(8,128)(2,1)}, u32[]{:S(2)}, u32[]{:S(2)}) collective-permute-start(bf16[176,768]{1,0:T(8,128)(2,1)} %get-tuple-element.231), channel_id=1, source_target_pairs={{0,1},{1,2},{2,3},{3,0},{4,5},{5,6},{6,7},{7,4},{8,9},{9,10},{10,1... | collective-permute-start | bytes 811016 | tf_op jit(solution)/shard_map/ppermute | solution.py:705
  48.4 10.7 %collective-permute-start.10 = (bf16[176,768]{1,0:T(8,128)(2,1)}, bf16[176,768]{1,0:T(8,128)(2,1)S(1)}, u32[]{:S(2)}, u32[]{:S(2)}) collective-permute-start(bf16[176,768]{1,0:T(8,128)(2,1)} %collective-permute-done.3.refs_0_.refs_3_), channel_id=1, source_target_pairs={{0,16},{4,12},{8,24},{12,4},{16,0},{20,28},{24,8},{28,20},{1,17},{... | collective-permute-start | bytes 811016 | tf_op jit(solution)/shard_map/ppermute | solution.py:720
  49.7 20.0 %collective-permute-start.15 = (bf16[192,768]{1,0:T(8,128)(2,1)S(1)}, bf16[192,768]{1,0:T(8,128)(2,1)S(1)}, u32[]{:S(2)}, u32[]{:S(2)}) collective-permute-start(bf16[192,768]{1,0:T(8,128)(2,1)S(1)} %copy-done.21), channel_id=1, source_target_pairs={{0,1},{1,2},{2,3},{3,0},{4,5},{5,6},{6,7},{7,4},{8,9},{9,10},{10,1... | collective-permute-start | bytes 884744 | tf_op jit(solution)/shard_map/ppermute | solution.py:705
  59.2 22.2 %collective-permute-start.17 = (bf16[192,768]{1,0:T(8,128)(2,1)S(1)}, bf16[192,768]{1,0:T(8,128)(2,1)S(1)}, u32[]{:S(2)}, u32[]{:S(2)}) collective-permute-start(bf16[192,768]{1,0:T(8,128)(2,1)S(1)} %copy-done.21), channel_id=1, source_target_pairs={{0,3},{1,0},{2,1},{3,2},{4,7},{5,4},{6,5},{7,6},{8,11},{9,8},{10,9... | collective-permute-start | bytes 884744 | tf_op jit(solution)/shard_map/ppermute | solution.py:705
  61.9 25.9 %collective-permute-start.16 = (bf16[192,768]{1,0:T(8,128)(2,1)S(1)}, bf16[192,768]{1,0:T(8,128)(2,1)S(1)}, u32[]{:S(2)}, u32[]{:S(2)}) collective-permute-start(bf16[192,768]{1,0:T(8,128)(2,1)S(1)} %copy-done.21), channel_id=1, source_target_pairs={{0,2},{1,3},{2,0},{3,1},{4,6},{5,7},{6,4},{7,5},{8,10},{9,11},{10,... | collective-permute-start | bytes 884744 | tf_op jit(solution)/shard_map/ppermute | solution.py:705
  67.7 20.2 %collective-permute-start.14 = (bf16[176,768]{1,0:T(8,128)(2,1)}, bf16[176,768]{1,0:T(8,128)(2,1)S(1)}, u32[]{:S(2)}, u32[]{:S(2)}) collective-permute-start(bf16[176,768]{1,0:T(8,128)(2,1)} %collective-permute-done.4.refs_0_.refs_3_), channel_id=1, source_target_pairs={{0,16},{4,12},{8,24},{12,4},{16,0},{20,28},{24,8},{28,20},{1,17},{... | collective-permute-start | bytes 811016 | tf_op jit(solution)/shard_map/ppermute | solution.py:720
  69.2 19.1 %collective-permute-start.13 = (bf16[176,768]{1,0:T(8,128)(2,1)}, bf16[176,768]{1,0:T(8,128)(2,1)S(1)}, u32[]{:S(2)}, u32[]{:S(2)}) collective-permute-start(bf16[176,768]{1,0:T(8,128)(2,1)} %collective-permute-done.4.refs_0_.refs_3_), channel_id=1, source_target_pairs={{0,8},{4,20},{8,0},{12,28},{16,24},{20,4},{24,16},{28,12},{1,9},{5... | collective-permute-start | bytes 811016 | tf_op jit(solution)/shard_map/ppermute | solution.py:717
  69.7 18.6 %collective-permute-start.12 = (bf16[176,768]{1,0:T(8,128)(2,1)S(1)}, bf16[176,768]{1,0:T(8,128)(2,1)S(1)}, u32[]{:S(2)}, u32[]{:S(2)}) collective-permute-start(bf16[176,768]{1,0:T(8,128)(2,1)S(1)} %collective-permute-done.9.refs_1_.refs_4_), channel_id=1, source_target_pairs={{0,16},{4,12},{8,24},{12,4},{16,0},{20,28},{24,8},{28,20},{1,17},{... | collective-permute-start | bytes 811016 | tf_op jit(solution)/shard_map/ppermute | solution.py:720
  90.1 24.8 %collective-permute-start.24 = (bf16[576,768]{1,0:T(8,128)(2,1)S(1)}, bf16[576,768]{1,0:T(8,128)(2,1)S(1)}, u32[]{:S(2)}, u32[]{:S(2)}) collective-permute-start(bf16[576,768]{1,0:T(8,128)(2,1)S(1)} %pad_maximum_fusion.refs_6_), channel_id=1, source_target_pairs={{0,16},{4,12},{8,24},{12,4},{16,0},{20,28},{24,8},{28,20},{1,17},{... | collective-permute-start | bytes 2654216 | tf_op jit(solution)/shard_map/ppermute | solution.py:720
  91.6 23.3 %collective-permute-start.23 = (bf16[576,768]{1,0:T(8,128)(2,1)S(1)}, bf16[576,768]{1,0:T(8,128)(2,1)S(1)}, u32[]{:S(2)}, u32[]{:S(2)}) collective-permute-start(bf16[576,768]{1,0:T(8,128)(2,1)S(1)} %pad_maximum_fusion.refs_6_), channel_id=1, source_target_pairs={{0,8},{4,20},{8,0},{12,28},{16,24},{20,4},{24,16},{28,12},{1,9},{5... | collective-permute-start | bytes 2654216 | tf_op jit(solution)/shard_map/ppermute | solution.py:717
  92.2 14.9 %collective-permute-start.26 = (bf16[176,768]{1,0:T(8,128)(2,1)S(1)}, bf16[176,768]{1,0:T(8,128)(2,1)S(1)}, u32[]{:S(2)}, u32[]{:S(2)}) collective-permute-start(bf16[176,768]{1,0:T(8,128)(2,1)S(1)} %collective-permute-done.13.refs_1_.refs_4_), channel_id=1, source_target_pairs={{0,4},{4,0},{8,12},{12,8},{16,20},{20,16},{24,28},{28,24},{1,5},{5... | collective-permute-start | bytes 811016 | tf_op jit(solution)/shard_map/ppermute | solution.py:711
  92.2 22.8 %collective-permute-start.22 = (bf16[176,768]{1,0:T(8,128)(2,1)S(1)}, bf16[176,768]{1,0:T(8,128)(2,1)S(1)}, u32[]{:S(2)}, u32[]{:S(2)}) collective-permute-start(bf16[176,768]{1,0:T(8,128)(2,1)S(1)} %collective-permute-done.13.refs_1_.refs_4_), channel_id=1, source_target_pairs={{0,16},{4,12},{8,24},{12,4},{16,0},{20,28},{24,8},{28,20},{1,17},{... | collective-permute-start | bytes 811016 | tf_op jit(solution)/shard_map/ppermute | solution.py:720
  92.7 14.4 %collective-permute-start.25 = (bf16[176,768]{1,0:T(8,128)(2,1)}, bf16[176,768]{1,0:T(8,128)(2,1)S(1)}, u32[]{:S(2)}, u32[]{:S(2)}) collective-permute-start(bf16[176,768]{1,0:T(8,128)(2,1)} %collective-permute-done.4.refs_0_.refs_3_), channel_id=1, source_target_pairs={{0,4},{4,0},{8,12},{12,8},{16,20},{20,16},{24,28},{28,24},{1,5},{5... | collective-permute-start | bytes 811016 | tf_op jit(solution)/shard_map/ppermute | solution.py:711
  116.7 17.5 %collective-permute-start.30 = (bf16[576,768]{1,0:T(8,128)(2,1)S(1)}, bf16[576,768]{1,0:T(8,128)(2,1)S(1)}, u32[]{:S(2)}, u32[]{:S(2)}) collective-permute-start(bf16[576,768]{1,0:T(8,128)(2,1)S(1)} %pad_maximum_fusion.refs_6_), channel_id=1, source_target_pairs={{0,4},{4,0},{8,12},{12,8},{16,20},{20,16},{24,28},{28,24},{1,5},{5... | collective-permute-start | bytes 2654216 | tf_op jit(solution)/shard_map/ppermute | solution.py:711
  116.8 18.3 %collective-permute-start.32 = (bf16[576,768]{1,0:T(8,128)(2,1)S(1)}, bf16[576,768]{1,0:T(8,128)(2,1)S(1)}, u32[]{:S(2)}, u32[]{:S(2)}) collective-permute-start(bf16[576,768]{1,0:T(8,128)(2,1)S(1)} %collective-permute-done.24.refs_8_), channel_id=1, source_target_pairs={{0,4},{4,0},{8,12},{12,8},{16,20},{20,16},{24,28},{28,24},{1,5},{5... | collective-permute-start | bytes 2654216 | tf_op jit(solution)/shard_map/ppermute | solution.py:711
  117.2 17.9 %collective-permute-start.31 = (bf16[576,768]{1,0:T(8,128)(2,1)S(1)}, bf16[576,768]{1,0:T(8,128)(2,1)S(1)}, u32[]{:S(2)}, u32[]{:S(2)}) collective-permute-start(bf16[576,768]{1,0:T(8,128)(2,1)S(1)} %collective-permute-done.23.refs_7_), channel_id=1, source_target_pairs={{0,4},{4,0},{8,12},{12,8},{16,20},{20,16},{24,28},{28,24},{1,5},{5... | collective-permute-start | bytes 2654216 | tf_op jit(solution)/shard_map/ppermute | solution.py:711
  117.3 17.8 %collective-permute-start.29 = (bf16[576,768]{1,0:T(8,128)(2,1)S(1)}, bf16[576,768]{1,0:T(8,128)(2,1)}, u32[]{:S(2)}, u32[]{:S(2)}) collective-permute-start(bf16[576,768]{1,0:T(8,128)(2,1)S(1)} %collective-permute-done.23.refs_7_), channel_id=1, source_target_pairs={{0,16},{4,12},{8,24},{12,4},{16,0},{20,28},{24,8},{28,20},{1,17},{... | collective-permute-start | bytes 2654216 | tf_op jit(solution)/shard_map/ppermute | solution.py:720
  194.0 10.9 %collective-permute-start.34 = (bf16[1536,768]{1,0:T(8,128)(2,1)S(1)}, bf16[1536,768]{1,0:T(8,128)(2,1)S(1)}, u32[]{:S(2)}, u32[]{:S(2)}) collective-permute-start(bf16[1536,768]{1,0:T(8,128)(2,1)S(1)} %get-tuple-element.307), channel_id=1, source_target_pairs={{0,4},{4,0},{8,12},{12,8},{16,20},{20,16},{24,28},{28,24},{1,5},{5... | collective-permute-start | bytes 7077896 | tf_op jit(solution)/shard_map/ppermute | solution.py:711
  204.7 17.5 %collective-permute-start.36 = (bf16[1536,768]{1,0:T(8,128)(2,1)S(1)}, bf16[1536,768]{1,0:T(8,128)(2,1)S(1)}, u32[]{:S(2)}, u32[]{:S(2)}) collective-permute-start(bf16[1536,768]{1,0:T(8,128)(2,1)S(1)} %get-tuple-element.326), channel_id=1, source_target_pairs={{0,4},{4,0},{8,12},{12,8},{16,20},{20,16},{24,28},{28,24},{1,5},{5... | collective-permute-start | bytes 7077896 | tf_op jit(solution)/shard_map/ppermute | solution.py:711
  206.8 16.3 %collective-permute-start.35 = (bf16[768,768]{1,0:T(8,128)(2,1)S(1)}, bf16[768,768]{1,0:T(8,128)(2,1)S(1)}, u32[]{:S(2)}, u32[]{:S(2)}) collective-permute-start(bf16[768,768]{1,0:T(8,128)(2,1)S(1)} %add_convert_fusion.1), channel_id=1, source_target_pairs={{0,8},{4,20},{8,0},{12,28},{16,24},{20,4},{24,16},{28,12},{1,9},{5... | collective-permute-start | bytes 3538952 | tf_op jit(solution)/shard_map/ppermute | solution.py:717
  208.0 14.2 %collective-permute-start.37 = (f32[8,768]{1,0:T(8,128)S(1)}, f32[8,768]{1,0:T(8,128)S(1)}, u32[]{:S(2)}, u32[]{:S(2)}) collective-permute-start(f32[8,768]{1,0:T(8,128)S(1)} %get-tuple-element.327), channel_id=1, source_target_pairs={{0,4},{4,0},{8,12},{12,8},{16,20},{20,16},{24,28},{28,24},{1,5},{5... | collective-permute-start | bytes 73736 | tf_op jit(solution)/shard_map/ppermute | solution.py:711
  221.8 18.7 %collective-permute-start.40 = (bf16[704,768]{1,0:T(8,128)(2,1)S(1)}, bf16[704,768]{1,0:T(8,128)(2,1)S(1)}, u32[]{:S(2)}, u32[]{:S(2)}) collective-permute-start(bf16[704,768]{1,0:T(8,128)(2,1)S(1)} %get-tuple-element.341), channel_id=1, source_target_pairs={{0,4},{4,0},{8,12},{12,8},{16,20},{20,16},{24,28},{28,24},{1,5},{5... | collective-permute-start | bytes 3244040 | tf_op jit(solution)/shard_map/ppermute | solution.py:711
  223.7 22.6 %collective-permute-start.39 = (bf16[768,768]{1,0:T(8,128)(2,1)S(1)}, bf16[768,768]{1,0:T(8,128)(2,1)S(1)}, u32[]{:S(2)}, u32[]{:S(2)}) collective-permute-start(bf16[768,768]{1,0:T(8,128)(2,1)S(1)} %add_convert_fusion), channel_id=1, source_target_pairs={{0,8},{4,20},{8,0},{12,28},{16,24},{20,4},{24,16},{28,12},{1,9},{5... | collective-permute-start | bytes 3538952 | tf_op jit(solution)/shard_map/ppermute | solution.py:717
  224.9 21.5 %collective-permute-start.41 = (f32[8,768]{1,0:T(8,128)S(1)}, f32[8,768]{1,0:T(8,128)S(1)}, u32[]{:S(2)}, u32[]{:S(2)}) collective-permute-start(f32[8,768]{1,0:T(8,128)S(1)} %add.204), channel_id=1, source_target_pairs={{0,8},{4,12},{8,0},{12,4},{16,24},{20,28},{24,16},{28,20},{1,9},{5... | collective-permute-start | bytes 73736 | tf_op jit(solution)/shard_map/ppermute | solution.py:711
  225.8 20.5 %collective-permute-start.38 = (bf16[384,768]{1,0:T(8,128)(2,1)S(1)}, bf16[384,768]{1,0:T(8,128)(2,1)S(1)}, u32[]{:S(2)}, u32[]{:S(2)}) collective-permute-start(bf16[384,768]{1,0:T(8,128)(2,1)S(1)} %add_convert_fusion.4), channel_id=1, source_target_pairs={{0,16},{4,12},{8,24},{12,4},{16,0},{20,28},{24,8},{28,20},{1,17},{... | collective-permute-start | bytes 1769480 | tf_op jit(solution)/shard_map/ppermute | solution.py:720
  240.3 27.8 %collective-permute-start.46 = (bf16[704,768]{1,0:T(8,128)(2,1)S(1)}, bf16[704,768]{1,0:T(8,128)(2,1)S(1)}, u32[]{:S(2)}, u32[]{:S(2)}) collective-permute-start(bf16[704,768]{1,0:T(8,128)(2,1)S(1)} %get-tuple-element.359), channel_id=1, source_target_pairs={{0,4},{4,0},{8,12},{12,8},{16,20},{20,16},{24,28},{28,24},{1,5},{5... | collective-permute-start | bytes 3244040 | tf_op jit(solution)/shard_map/ppermute | solution.py:711
  247.2 21.8 %collective-permute-start.42 = (bf16[192,768]{1,0:T(8,128)(2,1)S(1)}, bf16[192,768]{1,0:T(8,128)(2,1)S(1)}, u32[]{:S(2)}, u32[]{:S(2)}) collective-permute-start(bf16[192,768]{1,0:T(8,128)(2,1)S(1)} %get-tuple-element.355), channel_id=1, source_target_pairs={{0,3},{1,0},{2,1},{3,2},{4,7},{5,4},{6,5},{7,6},{8,11},{9,8},{10,9... | collective-permute-start | bytes 884744 | tf_op jit(solution)/shard_map/ppermute | solution.py:705
  247.2 23.3 %collective-permute-start.43 = (bf16[192,768]{1,0:T(8,128)(2,1)S(1)}, bf16[192,768]{1,0:T(8,128)(2,1)S(1)}, u32[]{:S(2)}, u32[]{:S(2)}) collective-permute-start(bf16[192,768]{1,0:T(8,128)(2,1)S(1)} %get-tuple-element.356), channel_id=1, source_target_pairs={{0,2},{1,3},{2,0},{3,1},{4,6},{5,7},{6,4},{7,5},{8,10},{9,11},{10,... | collective-permute-start | bytes 884744 | tf_op jit(solution)/shard_map/ppermute | solution.py:705
  252.2 18.4 %collective-permute-start.45 = (bf16[352,768]{1,0:T(8,128)(2,1)S(1)}, bf16[352,768]{1,0:T(8,128)(2,1)S(1)}, u32[]{:S(2)}, u32[]{:S(2)}) collective-permute-start(bf16[352,768]{1,0:T(8,128)(2,1)S(1)} %add_convert_fusion.7), channel_id=1, source_target_pairs={{0,8},{4,20},{8,0},{12,28},{16,24},{20,4},{24,16},{28,12},{1,9},{5... | collective-permute-start | bytes 1622024 | tf_op jit(solution)/shard_map/ppermute | solution.py:717
  253.2 17.4 %collective-permute-start.44 = (bf16[384,768]{1,0:T(8,128)(2,1)S(1)}, bf16[384,768]{1,0:T(8,128)(2,1)S(1)}, u32[]{:S(2)}, u32[]{:S(2)}) collective-permute-start(bf16[384,768]{1,0:T(8,128)(2,1)S(1)} %add_convert_fusion.3), channel_id=1, source_target_pairs={{0,16},{4,12},{8,24},{12,4},{16,0},{20,28},{24,8},{28,20},{1,17},{... | collective-permute-start | bytes 1769480 | tf_op jit(solution)/shard_map/ppermute | solution.py:720
  268.1 22.1 %collective-permute-start.51 = (f32[8,768]{1,0:T(8,128)S(1)}, f32[8,768]{1,0:T(8,128)S(1)}, u32[]{:S(2)}, u32[]{:S(2)}) collective-permute-start(f32[8,768]{1,0:T(8,128)S(1)} %add.214), channel_id=1, source_target_pairs={{0,16},{4,20},{8,24},{12,28},{16,0},{20,4},{24,8},{28,12},{1,17},{... | collective-permute-start | bytes 73736 | tf_op jit(solution)/shard_map/ppermute | solution.py:711
  269.0 21.2 %collective-permute-start.50 = (bf16[704,768]{1,0:T(8,128)(2,1)S(1)}, bf16[704,768]{1,0:T(8,128)(2,1)S(1)}, u32[]{:S(2)}, u32[]{:S(2)}) collective-permute-start(bf16[704,768]{1,0:T(8,128)(2,1)S(1)} %get-tuple-element.377), channel_id=1, source_target_pairs={{0,4},{4,0},{8,12},{12,8},{16,20},{20,16},{24,28},{28,24},{1,5},{5... | collective-permute-start | bytes 3244040 | tf_op jit(solution)/shard_map/ppermute | solution.py:711
  271.0 19.2 %collective-permute-start.48 = (bf16[176,768]{1,0:T(8,128)(2,1)S(1)}, bf16[176,768]{1,0:T(8,128)(2,1)S(1)}, u32[]{:S(2)}, u32[]{:S(2)}) collective-permute-start(bf16[176,768]{1,0:T(8,128)(2,1)S(1)} %add_convert_fusion.19), channel_id=1, source_target_pairs={{0,16},{4,12},{8,24},{12,4},{16,0},{20,28},{24,8},{28,20},{1,17},{... | collective-permute-start | bytes 811016 | tf_op jit(solution)/shard_map/ppermute | solution.py:720
  271.8 18.4 %collective-permute-start.47 = (bf16[192,768]{1,0:T(8,128)(2,1)S(1)}, bf16[192,768]{1,0:T(8,128)(2,1)S(1)}, u32[]{:S(2)}, u32[]{:S(2)}) collective-permute-start(bf16[192,768]{1,0:T(8,128)(2,1)S(1)} %add_convert_fusion.10), channel_id=1, source_target_pairs={{0,1},{1,2},{2,3},{3,0},{4,5},{5,6},{6,7},{7,4},{8,9},{9,10},{10,1... | collective-permute-start | bytes 884744 | tf_op jit(solution)/shard_map/ppermute | solution.py:705
  272.7 17.6 %collective-permute-start.49 = (bf16[352,768]{1,0:T(8,128)(2,1)S(1)}, bf16[352,768]{1,0:T(8,128)(2,1)S(1)}, u32[]{:S(2)}, u32[]{:S(2)}) collective-permute-start(bf16[352,768]{1,0:T(8,128)(2,1)S(1)} %add_convert_fusion.6), channel_id=1, source_target_pairs={{0,8},{4,20},{8,0},{12,28},{16,24},{20,4},{24,16},{28,12},{1,9},{5... | collective-permute-start | bytes 1622024 | tf_op jit(solution)/shard_map/ppermute | solution.py:717
  290.3 12.6 %collective-permute-start.52 = (bf16[960,768]{1,0:T(8,128)(2,1)S(1)}, bf16[960,768]{1,0:T(8,128)(2,1)S(1)}, u32[]{:S(2)}, u32[]{:S(2)}) collective-permute-start(bf16[960,768]{1,0:T(8,128)(2,1)S(1)} %get-tuple-element.379), channel_id=1, source_target_pairs={{0,4},{4,0},{8,12},{12,8},{16,20},{20,16},{24,28},{28,24},{1,5},{5... | collective-permute-start | bytes 4423688 | tf_op jit(solution)/shard_map/ppermute | solution.py:711
  290.5 12.3 %collective-permute-start.54 = (bf16[352,768]{1,0:T(8,128)(2,1)S(1)}, bf16[352,768]{1,0:T(8,128)(2,1)S(1)}, u32[]{:S(2)}, u32[]{:S(2)}) collective-permute-start(bf16[352,768]{1,0:T(8,128)(2,1)S(1)} %add_convert_fusion.5), channel_id=1, source_target_pairs={{0,8},{4,20},{8,0},{12,28},{16,24},{20,4},{24,16},{28,12},{1,9},{5... | collective-permute-start | bytes 1622024 | tf_op jit(solution)/shard_map/ppermute | solution.py:717
  303.0 17.6 %collective-permute-start.55 = (bf16[480,768]{1,0:T(8,128)(2,1)S(1)}, bf16[480,768]{1,0:T(8,128)(2,1)S(1)}, u32[]{:S(2)}, u32[]{:S(2)}) collective-permute-start(bf16[480,768]{1,0:T(8,128)(2,1)S(1)} %add_convert_fusion.2), channel_id=1, source_target_pairs={{0,8},{4,20},{8,0},{12,28},{16,24},{20,4},{24,16},{28,12},{1,9},{5... | collective-permute-start | bytes 2211848 | tf_op jit(solution)/shard_map/ppermute | solution.py:717
  307.3 13.3 %collective-permute-start.58 = (bf16[192,768]{1,0:T(8,128)(2,1)S(1)}, bf16[192,768]{1,0:T(8,128)(2,1)S(1)}, u32[]{:S(2)}, u32[]{:S(2)}) collective-permute-start(bf16[192,768]{1,0:T(8,128)(2,1)S(1)} %add_convert_fusion.9.refs_0_), channel_id=1, source_target_pairs={{0,8},{4,20},{8,0},{12,28},{16,24},{20,4},{24,16},{28,12},{1,9},{5... | collective-permute-start | bytes 884744 | tf_op jit(solution)/shard_map/ppermute | solution.py:717
  320.6 21.6 %collective-permute-start.61 = (bf16[192,768]{1,0:T(8,128)(2,1)S(1)}, bf16[192,768]{1,0:T(8,128)(2,1)S(1)}, u32[]{:S(2)}, u32[]{:S(2)}) collective-permute-start(bf16[192,768]{1,0:T(8,128)(2,1)S(1)} %add_convert_fusion.9.refs_0_), channel_id=1, source_target_pairs={{0,16},{4,12},{8,24},{12,4},{16,0},{20,28},{24,8},{28,20},{1,17},{... | collective-permute-start | bytes 884744 | tf_op jit(solution)/shard_map/ppermute | solution.py:720
  321.6 20.6 %collective-permute-start.59 = (bf16[240,768]{1,0:T(8,128)(2,1)S(1)}, bf16[240,768]{1,0:T(8,128)(2,1)S(1)}, u32[]{:S(2)}, u32[]{:S(2)}) collective-permute-start(bf16[240,768]{1,0:T(8,128)(2,1)S(1)} %add_convert_fusion.8), channel_id=1, source_target_pairs={{0,16},{4,12},{8,24},{12,4},{16,0},{20,28},{24,8},{28,20},{1,17},{... | collective-permute-start | bytes 1105928 | tf_op jit(solution)/shard_map/ppermute | solution.py:720
  323.0 19.2 %collective-permute-start.60 = (bf16[176,768]{1,0:T(8,128)(2,1)S(1)}, bf16[176,768]{1,0:T(8,128)(2,1)S(1)}, u32[]{:S(2)}, u32[]{:S(2)}) collective-permute-start(bf16[176,768]{1,0:T(8,128)(2,1)S(1)} %add_convert_fusion.15), channel_id=1, source_target_pairs={{0,2},{1,3},{2,0},{3,1},{4,6},{5,7},{6,4},{7,5},{8,10},{9,11},{10,... | collective-permute-start | bytes 811016 | tf_op jit(solution)/shard_map/ppermute | solution.py:705
  323.1 19.1 %collective-permute-start.62 = (f32[8,768]{1,0:T(8,128)S(1)}, f32[8,768]{1,0:T(8,128)S(1)}, u32[]{:S(2)}, u32[]{:S(2)}) collective-permute-start(f32[8,768]{1,0:T(8,128)S(1)} %add.224), channel_id=1, source_target_pairs={{0,1},{1,0},{2,3},{3,2},{4,5},{5,4},{6,7},{7,6},{8,9},{9,8},{10,11... | collective-permute-start | bytes 73736 | tf_op jit(solution)/shard_map/ppermute | solution.py:708
  326.8 20.8 %collective-permute-start.66 = (bf16[176,768]{1,0:T(8,128)(2,1)S(1)}, bf16[176,768]{1,0:T(8,128)(2,1)S(1)}, u32[]{:S(2)}, u32[]{:S(2)}) collective-permute-start(bf16[176,768]{1,0:T(8,128)(2,1)S(1)} %add_convert_fusion.14), channel_id=1, source_target_pairs={{0,1},{1,2},{2,3},{3,0},{4,5},{5,6},{6,7},{7,4},{8,9},{9,10},{10,1... | collective-permute-start | bytes 811016 | tf_op jit(solution)/shard_map/ppermute | solution.py:705
  364.7 13.8 %collective-permute-start.83 = (bf16[192,768]{1,0:T(8,128)(2,1)S(1)}, bf16[192,768]{1,0:T(8,128)(2,1)S(1)}, u32[]{:S(2)}, u32[]{:S(2)}) collective-permute-start(bf16[192,768]{1,0:T(8,128)(2,1)S(1)} %add_convert_fusion.9.refs_0_), channel_id=1, source_target_pairs={{0,4},{4,0},{8,12},{12,8},{16,20},{20,16},{24,28},{28,24},{1,5},{5... | collective-permute-start | bytes 884744 | tf_op jit(solution)/shard_map/ppermute | solution.py:711
  378.2 10.6 %collective-permute-start.79 = (bf16[176,768]{1,0:T(8,128)(2,1)S(1)}, bf16[176,768]{1,0:T(8,128)(2,1)S(1)}, u32[]{:S(2)}, u32[]{:S(2)}) collective-permute-start(bf16[176,768]{1,0:T(8,128)(2,1)S(1)} %collective-permute-done.68.refs_1_), channel_id=1, source_target_pairs={{0,4},{4,0},{8,12},{12,8},{16,20},{20,16},{24,28},{28,24},{1,5},{5... | collective-permute-start | bytes 811016 | tf_op jit(solution)/shard_map/ppermute | solution.py:711
  (150 other events, 1361.2 us)

commit v5 on v4

--- a/solution.py
+++ b/solution.py
@@ -59,6 +59,14 @@
     return jax.ShapeDtypeStruct(dims, kind)
 
 
+def far(values):
+    return tuple(pltpu.with_memory_space_constraint(v, pltpu.HBM) for v in values)
+
+
+def far_shape(dims, kind):
+    return pltpu.HBM(dims, kind)
+
+
 def start(pairs, sem):
     copies = [pltpu.make_async_copy(source, target, sem) for source, target in pairs]
     for copy in copies:
@@ -105,48 +113,61 @@
     return pairs
 
 
+def own_parts(query_ref, key_ref, value_ref, out_ref):
+    return (query_ref.at[0], query_ref.at[1], key_ref, value_ref, query_ref.at[2], query_ref.at[3], out_ref)
+
+
+def spare_rows(qb_ref, vb_ref, ub_ref, spare):
+    qb = qb_ref[...].astype(F32)
+    none = jnp.zeros((1, qb.shape[1]), F32)
+    first = jnp.concatenate([qb[0:1], qb[1:2], none, vb_ref[...].astype(F32)], 1)
+    second = jnp.concatenate([qb[2:3], qb[3:4], none, none], 1)
+    row = lax.broadcasted_iota(jnp.int32, (spare, first.shape[1]), 0)
+    rows = jnp.where(row == 0, first, jnp.where(row == 1, second, jnp.where(row == 2, ub_ref[...].astype(F32), 0.0)))
+    return rows.astype(BF16)
+
+
 def pack_kernel(
     gw, info_ref, qb_ref, vb_ref, ub_ref, query_ref, key_ref, value_ref, ow_ref, up_ref, down_ref,
-    w_ref, piece_ref, ffn_ref, w_s, sem,
+    piece_ref, ffn_ref, w_s, f_s, sem,
 ):
-    parts = (query_ref.at[0], query_ref.at[1], key_ref, value_ref, query_ref.at[2], query_ref.at[3], ow_ref)
-    reads = start([(v, w_s.at[pl.ds(i * gw, gw)]) for i, v in enumerate(parts)], sem.at[0])
     part = info_ref[2]
-    unit = ffn_ref.shape[0] // 2
+    size = piece_ref.shape[0]
+    low = lax.div(part * size, jnp.int32(gw))
+    copies = []
+    for i, ref in enumerate(own_parts(query_ref, key_ref, value_ref, ow_ref)):
+        needed = jnp.logical_or(low == i, low + 1 == i)
+        copies.append((needed, pltpu.make_async_copy(ref, w_s.at[pl.ds(i * gw, gw)], sem.at[0])))
+    for needed, copy in copies:
+        pl.when(needed)(copy.start)
+    unit = f_s.shape[0] // 2
     ffn = start(
-        [(v.at[rows_at(part * unit, unit)], ffn_ref.at[pl.ds(i * unit, unit)]) for i, v in enumerate((up_ref, down_ref))],
+        [(v.at[rows_at(part * unit, unit)], f_s.at[pl.ds(i * unit, unit)]) for i, v in enumerate((up_ref, down_ref))],
         sem.at[1],
     )
-    qb = qb_ref[...].astype(F32)
-    none = jnp.zeros((1, gw), F32)
-    first = jnp.concatenate([qb[0:1], qb[1:2], none, vb_ref[...].astype(F32)], 1)
-    second = jnp.concatenate([qb[2:3], qb[3:4], none, none], 1)
-    spare = w_s.shape[0] - 7 * gw
-    row = lax.broadcasted_iota(jnp.int32, (spare, 4 * gw), 0)
-    rows = jnp.where(row == 0, first, jnp.where(row == 1, second, jnp.where(row == 2, ub_ref[...].astype(F32), 0.0)))
-    w_s[7 * gw :] = rows.astype(BF16)
-    wait(reads)
-    size = piece_ref.shape[0]
+    w_s[7 * gw :] = spare_rows(qb_ref, vb_ref, ub_ref, w_s.shape[0] - 7 * gw)
+    for needed, copy in copies:
+        pl.when(needed)(copy.wait)
     piece = start([(w_s.at[rows_at(part * size, size)], piece_ref)], sem.at[2])
-    whole = start([(w_s, w_ref)], sem.at[3])
+    wait(ffn)
+    last = start([(f_s, ffn_ref)], sem.at[3])
     wait(piece)
-    wait(ffn)
-    wait(whole)
-
-
-def pack(info, query_b, value_b, up_b, query_t, key_t, value_t, out_w, up_w, down_w, rows):
-    gw, width = key_t.shape
+    wait(last)
+
+
+def pack(info, biases, own, up_w, down_w, rows):
+    gw, width = own[1].shape
     unit = up_w.shape[0] // 8
     return pl.pallas_call(
         partial(pack_kernel, gw),
         in_specs=[SMEM] + [VMEM] * 3 + [HBM] * 6,
-        out_specs=[HBM] * 3,
-        out_shape=(shape((rows, width), BF16), shape((rows // 8, width), BF16), shape((2 * unit, width), BF16)),
-        scratch_shapes=[pltpu.VMEM((rows, width), BF16), DMA((4,))],
-        compiler_params=params(12),
-        cost_estimate=cost(0.01, 8),
+        out_specs=[HBM] * 2,
+        out_shape=(far_shape((rows // 8, width), BF16), far_shape((2 * unit, width), BF16)),
+        scratch_shapes=[pltpu.VMEM((rows, width), BF16), pltpu.VMEM((2 * unit, width), BF16), DMA((4,))],
+        compiler_params=params(4),
+        cost_estimate=cost(0.01, 3),
         name="pack",
-    )(info, query_b, value_b, up_b, query_t, key_t, value_t, out_w, up_w, down_w)
+    )(info, *biases, *far(own + (up_w, down_w)))
 
 
 def start_kernel(info_ref, words_ref, ents_ref, spans_ref, table_ref, bias_ref, low_ref, resid_ref, w_s, e_s, t_s, sem):
@@ -187,10 +208,10 @@
             pltpu.VMEM(table.shape, BF16),
             DMA((2,)),
         ],
-        compiler_params=params(16),
+        compiler_params=params(6),
         cost_estimate=cost(0.5, 6),
         name="start_rows",
-    )(info, word_in, entity_in, spans, table, out_b)
+    )(info, *far((word_in, entity_in)), spans, *far((table,)), out_b)
 
 
 def split_heads(words, gw, heads, pw_ref, pe_ref, qw_s, qe_s, k_s, v_s):
@@ -198,10 +219,10 @@
     for h in range(heads):
         o = h * HEAD_DIM
         e = o + HEAD_DIM
-        qw_s[h, :words] = pw_ref[:, o:e]
-        qw_s[h, words:] = pe_ref[:, half + o : half + e]
-        qe_s[h, :words] = pw_ref[:, gw + o : gw + e]
-        qe_s[h, words:] = pe_ref[:, half + gw + o : half + gw + e]
+        qw_s[h, :words] = pw_ref[:, o:e] * SCALE
+        qw_s[h, words:] = pe_ref[:, half + o : half + e] * SCALE
+        qe_s[h, :words] = pw_ref[:, gw + o : gw + e] * SCALE
+        qe_s[h, words:] = pe_ref[:, half + gw + o : half + gw + e] * SCALE
         k_s[h, :words] = pw_ref[:, half + o : half + e]
         k_s[h, words:] = pe_ref[:, o:e]
         v_s[h, :words] = pw_ref[:, half + gw + o : half + gw + e]
@@ -209,11 +230,15 @@
 
 
 def attend_kernel(words, gw, heads, count, info_ref, rows_ref, acc_ref, *refs):
+    own = count == 4
+    small, refs = (refs[:3], refs[3:]) if own else ((), refs)
     pieces = refs[:count]
     pw_ref, pe_ref, ctx_ref, lt_ref, bias_ref, out_ref, w_s, pw_s, pe_s, ctx_s, qw_s, qe_s, k_s, v_s, sem = refs[count:]
     half = 2 * gw
-    if count == 1:
-        wait(start([(pieces[0], w_s)], sem.at[0]))
+    if own:
+        reads = start([(v, w_s.at[pl.ds(i * gw, gw)]) for i, v in enumerate(own_parts(*pieces))], sem.at[0])
+        w_s[7 * gw :] = spare_rows(*small, w_s.shape[0] - 7 * gw)
+        wait(reads)
     else:
         wait(start(place(pieces, info_ref, w_s.shape[0] // 8, (w_s,)), sem.at[0]))
     rows_b = w_s[7 * gw : 7 * gw + TILE]
@@ -233,14 +258,14 @@
             sw = mm_nt(qw_s[h, rows], k_s[h, :words])
             se = mm_nt(qe_s[h, rows], k_s[h, words:])
             top = jnp.maximum(jnp.max(sw, 1, keepdims=True), jnp.max(se, 1, keepdims=True))
-            ew = jnp.exp((sw - top) * SCALE)
-            ee = jnp.exp((se - top) * SCALE)
+            ew = jnp.exp(sw - top)
+            ee = jnp.exp(se - top)
             total = jnp.sum(ew, 1, keepdims=True) + jnp.sum(ee, 1, keepdims=True)
             inv = 1.0 / total
             parts.append(
                 mm((ew * inv).astype(BF16), v_s[h, :words]) + mm((ee * inv).astype(BF16), v_s[h, words:])
             )
-            logt = top * SCALE + jnp.log(total)
+            logt = top + jnp.log(total)
             lt_ref[h : h + 1, rows] = jnp.broadcast_to(logt, (block, block)).T[0:1]
         ctx_s[rows, :] = jnp.concatenate(parts, 1).astype(BF16)
         return carry
@@ -252,19 +277,19 @@
     wait(last)
 
 
-def attend(info, rows_low, acc, pieces, words, heads, rows):
+def attend(info, rows_low, acc, pieces, words, heads, rows, small=()):
     total, width = rows_low.shape
     ents = total - words
     gw = heads * HEAD_DIM
     count = len(pieces)
     return pl.pallas_call(
         partial(attend_kernel, words, gw, heads, count),
-        in_specs=[SMEM] + [VMEM] * 2 + [HBM] * count,
+        in_specs=[SMEM] + [VMEM] * (2 + len(small)) + [HBM] * count,
         out_specs=[HBM] * 3 + [VMEM] * 3,
         out_shape=(
-            shape((words, 4 * gw), BF16),
-            shape((ents, 4 * gw), BF16),
-            shape((total, gw), BF16),
+            far_shape((words, 4 * gw), BF16),
+            far_shape((ents, 4 * gw), BF16),
+            far_shape((total, gw), BF16),
             shape((8, total), F32),
             shape((TILE, width), BF16),
             shape((total, width), F32),
@@ -278,10 +303,10 @@
         + [pltpu.VMEM((heads, total, HEAD_DIM), BF16) for _ in range(4)]
         + [DMA((3,))],
         input_output_aliases={2: 5},
-        compiler_params=params(24),
+        compiler_params=params(11),
         cost_estimate=cost(8, 6),
-        name="attend_own" if count == 1 else "attend_far",
-    )(info, rows_low, acc, *pieces)
+        name="attend_own" if small else "attend_far",
+    )(info, rows_low, acc, *small, *far(pieces))
 
 
 def gelu_pair(x):
@@ -305,13 +330,14 @@
 def hidden_kernel(n, info_ref, attended_ref, vec_ref, wm_ref, em_ref, cw_ref, ce_ref, *refs):
     bias_refs, refs = refs[:n], refs[n:]
     up_own, down_own = refs[:2]
-    pieces, refs = refs[2:10], refs[10:]
+    pieces, refs = (refs[2:10], refs[10:18]), refs[18:]
     turn_ref, at_ref, slope_ref, up_s, down_s, ow_ref, oe_ref, mixed_ref, grad_ref, sums_ref, low_ref, acc_s, b_s, sem = refs
     total, width = attended_ref.shape
     unit = width // 8
     reads = [start([(up_own, up_s.at[0]), (down_own, down_s.at[0])], sem.at[0])]
     for r in range(1, n):
-        reads.append(start(place(pieces, info_ref, unit, (up_s.at[r], down_s.at[r]), 2 * unit * (r - 1)), sem.at[r]))
+        held, skip = pieces[r // 3], 2 * unit * ((r - 1) % 2)
+        reads.append(start(place(held, info_ref, unit, (up_s.at[r], down_s.at[r]), skip), sem.at[r]))
     for r in range(n):
         b_s[r] = bias_refs[r][2:3].astype(F32)
     scaled, _ = norm_parts(attended_ref[...])
@@ -387,10 +413,10 @@
             pltpu.VMEM((n, 1, width), F32),
             DMA((n,)),
         ],
-        compiler_params=params(48),
+        compiler_params=params(18),
         cost_estimate=cost(22, 20),
         name="hidden",
-    )(info, attended, vec, word_mask, entity_mask, cot_words, cot_ents, *biases, *own, *pieces)
+    )(info, attended, vec, word_mask, entity_mask, cot_words, cot_ents, *biases, *far(own), *far(pieces))
 
 
 def norm_backward(grad_in, scaled, inv_std, gain_row):
@@ -431,15 +457,15 @@
         in_specs=[SMEM] + [VMEM] * 7,
         out_specs=[HBM] * 3 + [VMEM] * 2,
         out_shape=(
-            shape((k * width, width), BF16),
-            shape((k * width // 2, width), BF16),
-            shape((k * width // 2, width), BF16),
+            far_shape((k * width, width), BF16),
+            far_shape((k * width // 2, width), BF16),
+            far_shape((k * width // 2, width), BF16),
             shape((total, width), F32),
             shape((8 * k, width), F32),
         ),
         scratch_shapes=[pltpu.VMEM((2 * width, width), BF16) for _ in pair] + [DMA],
         input_output_aliases={7: 3},
-        compiler_params=params(24),
+        compiler_params=params(12),
         cost_estimate=cost(7 * k, 8 * k),
         name="hidden_back",
     )(info, mixed_low, act_t, slope, normed_t, up, down, acc)
@@ -464,7 +490,7 @@
         out_specs=[VMEM] * 3,
         out_shape=(shape((total, width), F32), shape((total, width), BF16), shape((8, width), F32)),
         input_output_aliases={1: 0},
-        compiler_params=params(24),
+        compiler_params=params(8),
         cost_estimate=cost(2, 6),
         name="norm_back",
     )(attended, grad, vec, sums)
@@ -484,8 +510,8 @@
     total = rows_ref.shape[0]
     size = w_s.shape[0] // 8
     saved = start([(pw_ref, pw_s), (pe_ref, pe_s)], sem.at[0])
-    if count == 1:
-        reads = start([(pieces[0], w_s)], sem.at[1])
+    if count == 4:
+        reads = start([(v, w_s.at[pl.ds(i * gw, gw)]) for i, v in enumerate(own_parts(*pieces))], sem.at[1])
     else:
         reads = start(place(pieces, info_ref, size, (w_s,)), sem.at[1])
     last = start([(ctx_ref, ctx_s)], sem.at[2])
@@ -505,8 +531,8 @@
         def step(qb, carry):
             rows = pl.ds(pl.multiple_of(qb * block, block), block)
             logt = lt_ref[h : h + 1, rows]
-            pw = jnp.exp(mm_nt(k_s[h, :words], qw_s[h, rows]) * SCALE - logt)
-            pe = jnp.exp(mm_nt(k_s[h, words:], qe_s[h, rows]) * SCALE - logt)
+            pw = jnp.exp(mm_nt(k_s[h, :words], qw_s[h, rows]) - logt)
+            pe = jnp.exp(mm_nt(k_s[h, words:], qe_s[h, rows]) - logt)
             gw_ = mm_nt(v_s[h, :words], dc_s[h, rows])
             ge_ = mm_nt(v_s[h, words:], dc_s[h, rows])
             p_s[:words, rows] = pw.astype(BF16)
@@ -518,8 +544,8 @@
 
         lax.fori_loop(0, total // block, step, 0)
         dv = mm(p_s[...], dc_s[h]).astype(BF16)
-        dkw = (mm(ds_s[:words], qw_s[h]) * SCALE).astype(BF16)
-        dke = (mm(ds_s[words:], qe_s[h]) * SCALE).astype(BF16)
+        dkw = mm(ds_s[:words], qw_s[h]).astype(BF16)
+        dke = mm(ds_s[words:], qe_s[h]).astype(BF16)
         dqw = (mm_tn(ds_s[:words], k_s[h, :words]) * SCALE).astype(BF16)
         dqe = (mm_tn(ds_s[words:], k_s[h, words:]) * SCALE).astype(BF16)
         dpw_s[:, o:e] = dqw[:words]
@@ -581,9 +607,9 @@
         in_specs=[SMEM] + [VMEM] * 5 + [HBM] * (3 + count) + [VMEM] * final,
         out_specs=[HBM] * 3 + [VMEM] * len(grads),
         out_shape=(
-            shape((moved // 2, width), BF16),
-            shape((moved // 4, width), BF16),
-            shape((moved // 4, width), BF16),
+            far_shape((moved // 2, width), BF16),
+            far_shape((moved // 4, width), BF16),
+            far_shape((moved // 4, width), BF16),
         )
         + grads,
         scratch_shapes=[pltpu.VMEM((words, width), BF16)] * final
@@ -603,10 +629,10 @@
             DMA((4,)),
         ],
         input_output_aliases={} if final else {5: 3},
-        compiler_params=params(32),
+        compiler_params=params(20),
         cost_estimate=cost(11, 8),
         name="attend_back",
-    )(info, rows_low, lt, low, up_sums, acc, pw, pe, ctx, *pieces, *((spans,) if final else ()))
+    )(info, rows_low, lt, low, up_sums, acc, *far((pw, pe, ctx)), *far(pieces), *((spans,) if final else ()))
 
 
 def spread_query_kernel(info_ref, *refs):
@@ -640,10 +666,10 @@
             shape((4, gw), F32), shape((1, gw), F32), shape((1, width), F32),
         ),
         scratch_shapes=[pltpu.VMEM((8 * unit, width), BF16), DMA],
-        compiler_params=params(16),
+        compiler_params=params(8),
         cost_estimate=cost(0.5, 7),
         name="spread_query",
-    )(info, *pieces)
+    )(info, *far(pieces))
 
 
 def spread_hidden_kernel(info_ref, *refs):
@@ -663,10 +689,10 @@
         out_specs=[VMEM] * 2,
         out_shape=(out, out),
         scratch_shapes=[pltpu.VMEM((4 * rows, width), BF16)] * 2 + [DMA],
-        compiler_params=params(16),
+        compiler_params=params(9),
         cost_estimate=cost(0.5, 7),
         name="spread_hidden",
-    )(info, *pieces)
+    )(info, *far(pieces))
 
 
 def spread_pos_kernel(info_ref, *refs):
@@ -684,10 +710,10 @@
         out_specs=VMEM,
         out_shape=shape((8 * rows, width), F32),
         scratch_shapes=[pltpu.VMEM((8 * rows, width), BF16), DMA],
-        compiler_params=params(8),
+        compiler_params=params(4),
         cost_estimate=cost(0.5, 3),
         name="spread_pos",
-    )(info, *pieces)
+    )(info, *far(pieces))
 
 
 class Links:
@@ -791,50 +817,53 @@
     part = 4 * links.core + 2 * links.bit[0] + links.bit[1]
     info = jnp.stack([z, links.core, part, 2 - links.core]).astype(jnp.int32)
 
-    own_w, piece_q, piece_f = pack(
-        info, query_b, value_b[None], up_b[None], jnp.swapaxes(query_w, 1, 2), key_w.T, value_w.T, out_w, up_w, down_w, rows
-    )
+    small = (query_b, value_b[None], up_b[None])
+    own = (jnp.swapaxes(query_w, 1, 2), key_w.T, value_w.T, out_w)
+    piece_q, piece_f = pack(info, small, own, up_w, down_w, rows)
     first, second, core, shift = links.first, links.second, links.swap_core, links.shift_z
-    v1, v2, v3 = (shift(piece_q, r) for r in range(1, n))
     rows_low, acc = start_rows(info, word_in, entity_in, entity_spans, pos_table, out_b[None], words, ents)
-    saved = []
-    biases = []
-
-    def attend_one(acc, pieces):
-        pw, pe, ctx, lt, bias, acc = attend(info, rows_low, acc, pieces, words, heads, rows)
-        saved.append((pw, pe, ctx, lt))
-        biases.append(bias)
+    saved = [None] * n
+    biases = [None] * n
+
+    def attend_one(r, acc, pieces, small=()):
+        pw, pe, ctx, lt, biases[r], acc = attend(info, rows_low, acc, pieces, words, heads, rows, small)
+        saved[r] = (pw, pe, ctx, lt)
         return acc
 
-    acc = attend_one(acc, (own_w,))
-    acc, v1, piece_f = sync(acc, v1, piece_f)
-    a1, b1, f1 = first(v1), second(v1), shift(piece_f, 1)
-    acc, v1, a1, b1, v2, v3, piece_f = sync(acc, v1, a1, b1, v2, v3, piece_f)
-    c1, kv, ka, kb, a2, b2 = second(a1), core(v1), core(a1), core(b1), first(v2), second(v2)
-    acc, c1, kv, ka, kb, a2, b2, piece_f, v3 = sync(acc, c1, kv, ka, kb, a2, b2, piece_f, v3)
-    kc, f2, f3 = core(c1), shift(piece_f, 2), shift(piece_f, 3)
-    acc, kc, a2, v3 = sync(acc, kc, a2, v3)
+    v1, v3 = shift(piece_q, 1), shift(piece_q, 3)
+    acc = attend_one(0, acc, own, small)
+    acc, v1, v3, piece_f = sync(acc, v1, v3, piece_f)
+    a1, b1, v2, f1, f3 = first(v1), second(v1), shift(v1, 1), shift(piece_f, 1), shift(piece_f, 3)
+    acc, v1, a1, b1, v3 = sync(acc, v1, a1, b1, v3)
+    c1, kv, ka, kb, a3, b3 = second(a1), core(v1), core(a1), core(b1), first(v3), second(v3)
+    acc, c1, kv, ka, kb, v2, f1, f3, v3 = sync(acc, c1, kv, ka, kb, v2, f1, f3, v3)
+    kc, f2 = core(c1), shift(f1, 1)
+    acc, kc, a3, b3, v2, f3 = sync(acc, kc, a3, b3, v2, f3)
     group_1 = (v1, a1, b1, c1, kv, ka, kb, kc)
 
-    c2, a3, b3 = second(a2), first(v3), second(v3)
-    acc = attend_one(acc, group_1)
-    acc, c2, a3, b3, f1, f2, f3 = sync(acc, c2, a3, b3, f1, f2, f3)
-    kv, ka, kb, kc = core(v2), core(a2), core(b2), core(c2)
-    acc, kv, ka, kb, kc, far_f, a3, v3 = sync(acc, kv, ka, kb, kc, jnp.concatenate([f1, f2, f3], 0), a3, v3)
+    c3, a2, b2, ag, bg = second(a3), first(v2), second(v2), first(f3), second(f3)
+    acc = attend_one(1, acc, group_1)
+    acc, c3, a2, b2, ag, bg, f1, f2 = sync(acc, c3, a2, b2, ag, bg, f1, f2)
+    kv, ka, kb, kc = core(v3), core(a3), core(b3), core(c3)
+    far_f = jnp.concatenate([f1, f2], 0)
+    acc, kv, ka, kb, kc, far_f, a2, ag, v2 = sync(acc, kv, ka, kb, kc, far_f, a2, ag, v2)
+    group_3 = (v3, a3, b3, c3, kv, ka, kb, kc)
+
+    c2, cg, af, kv, ka = second(a2), second(ag), first(far_f), core(v2), core(a2)
+    acc = attend_one(3, acc, group_3)
+    acc, c2, cg, af, kv, ka, b2, far_f = sync(acc, c2, cg, af, kv, ka, b2, far_f)
+    kb, kc = core(b2), core(c2)
+    acc, kb, kc, far_f, af, f3, ag, bg = sync(acc, kb, kc, far_f, af, f3, ag, bg)
     group_2 = (v2, a2, b2, c2, kv, ka, kb, kc)
 
-    c3, af, bf, kv, ka = second(a3), first(far_f), second(far_f), core(v3), core(a3)
-    acc = attend_one(acc, group_2)
-    acc, c3, af, bf, kv, ka = sync(acc, c3, af, bf, kv, ka)
-    kb, kc = core(b3), core(c3)
-    acc, kb, kc, af, bf, far_f = sync(acc, kb, kc, af, bf, far_f)
-    group_3 = (v3, a3, b3, c3, kv, ka, kb, kc)
-
-    cf, kv, ka, kb = second(af), core(far_f), core(af), core(bf)
-    acc = attend_one(acc, group_3)
-    attended, cf, kv, ka, kb = sync(acc, cf, kv, ka, kb)
-    ffn_pieces = (far_f, af, bf, cf, kv, ka, kb, core(cf))
-    query_groups = ((own_w,), group_1, group_2, group_3)
+    bf, cf, kv_g, ka_g, kb_g = second(far_f), second(af), core(f3), core(ag), core(bg)
+    acc = attend_one(2, acc, group_2)
+    acc, bf, cf, kv_g, ka_g, kb_g, cg, af, far_f = sync(acc, bf, cf, kv_g, ka_g, kb_g, cg, af, far_f)
+    attended = acc
+    ffn_pieces = (
+        far_f, af, bf, cf, core(far_f), core(af), core(bf), core(cf), f3, ag, bg, cg, kv_g, ka_g, kb_g, core(cg)
+    )
+    query_groups = (own, group_1, group_2, group_3)
 
     vec = jnp.stack([norm1_gain, norm1_bias, down_b, norm2_gain, norm2_bias] + [down_b] * 3)
     normed_t, act_t, slope, up, down, out_words, out_ents, mixed_low, acc, sums = hidden(
@@ -845,80 +874,91 @@
     unit = rows // 8
     up_sums = [None] * n
 
-    def ffn_pair(pair, acc):
-        send, near, far, acc, up_sum = hidden_back(info, pair, mixed_low, act_t, slope, normed_t, up, down, acc)
-        for k, r in enumerate(pair):
+    def ffn_blocks(group, acc):
+        send, near, rest, acc, up_sum = hidden_back(info, group, mixed_low, act_t, slope, normed_t, up, down, acc)
+        for k, r in enumerate(group):
             up_sums[r] = up_sum[8 * k : 8 * k + 8]
-        return Blocks(links, send, near, far), acc
-
-    fa, acc = ffn_pair((1, 2), acc)
-    fa.got = core(fa.send)
-    fb, acc = ffn_pair((3, 0), acc)
-    acc, fa.got = sync(acc, fa.got)
-    one_a = fa.one()
-    acc, attended_low, sums = norm_back(attended, acc, vec, sums)
-    acc, one_a, sums = sync(acc, one_a, sums)
+        return Blocks(links, send, near, rest), acc
 
     def back(r, acc, spans=None):
-        send, near, far, *acc = attend_back(
+        send, near, rest, *acc = attend_back(
             info, rows_low, saved[r], attended_low, up_sums[r], acc, query_groups[r], words, heads, rows, spans
         )
-        return Blocks(links, send, near, far), *acc
-
-    fa.a, fb.got, more = first(one_a), core(fb.send), core(sums)
-    q1, acc = back(1, acc)
-    acc, fa.a, fb.got, more = sync(acc, fa.a, fb.got, more)
-    acc, two_a, one_b, sums = sync(acc, fa.two(), fb.one(), sums + more)
-
-    fa.b, fb.a, q1.got, more = second(two_a), first(one_b), core(q1.send), links.swap(sums, 2)
-    q2, acc = back(2, acc)
-    acc, fa.b, fb.a, q1.got, more = sync(acc, fa.b, fb.a, q1.got, more)
-    acc, r1, r2, two_b, one_1, sums = sync(
-        acc, fa.rest(0, size), fa.rest(size, 2 * size), fb.two(), q1.one(), sums + more
-    )
-
-    z1, z2, fb.b, q1.a, q2.got = shift(r1, -1), shift(r2, -2), second(two_b), first(one_1), core(q2.send)
+        return Blocks(links, send, near, rest), *acc
+
+    fa, acc = ffn_blocks((2, 1), acc)
+    fa.got = core(fa.send)
+    fb, acc = ffn_blocks((3,), acc)
+    acc, fa.got = sync(acc, fa.got)
+    acc, one_a = sync(acc, fa.one())
+
+    fa.a, fb.got = first(one_a), core(fb.send)
+    fc, acc = ffn_blocks((0,), acc)
+    acc, fb.got = sync(acc, fb.got)
+    one_b = fb.one()
+    acc, attended_low, sums = norm_back(attended, acc, vec, sums)
+    more = core(sums)
+    acc, one_b, sums, more = sync(acc, one_b, sums, more)
+    sums = sums + more
+
+    fb.a, fc.got, more = first(one_b), core(fc.send), links.swap(sums, 2)
+    q1, acc = back(2, acc)
+    acc, fa.a, fb.a, fc.got, more = sync(acc, fa.a, fb.a, fc.got, more)
+    acc, two_a, two_b, one_c, sums = sync(acc, fa.two(), fb.two(), fc.one(), sums + more)
+
+    fa.b, fb.b, fc.a, q1.got = second(two_a), second(two_b), first(one_c), core(q1.send)
+    q2, acc = back(1, acc)
+    acc, fa.b, fb.b, fc.a, q1.got = sync(acc, fa.b, fb.b, fc.a, q1.got)
+    q2.got = core(q2.send)
+    acc, r2, r1, r3, two_c, one_1, q2.got = sync(
+        acc, fa.rest(0, size), fa.rest(size, 2 * size), fb.rest(0, size), fc.two(), q1.one(), q2.got
+    )
+
+    z2, z1, z3, q1.a, fc.b = shift(r2, -2), shift(r1, -1), shift(r3, -3), first(one_1), second(two_c)
     q3, acc = back(3, acc)
-    acc, z1, z2, fb.b, q1.a, q2.got = sync(acc, z1, z2, fb.b, q1.a, q2.got)
-    acc, r3, two_1, one_2 = sync(acc, fb.rest(0, size), q1.two(), q2.one())
-
-    z3, q1.b, q2.a, q3.got, more = shift(r3, -3), second(two_1), first(one_2), core(q3.send), links.swap(sums, 4)
+    acc, z2, z1, z3, q1.a, fc.b = sync(acc, z2, z1, z3, q1.a, fc.b)
+    acc, own_f, two_1, one_2 = sync(acc, fc.rest(0, size, z1, z2, z3), q1.two(), q2.one())
+
+    ga, gb, q1.b, q2.a, q3.got = first(own_f), second(own_f), second(two_1), first(one_2), core(q3.send)
     q4, grad_words, grad_ents = back(0, acc, entity_spans)
-    q4.send, z3, q1.b, q2.a, q3.got, more = sync(q4.send, z3, q1.b, q2.a, q3.got, more)
-
+    q4.send, ga, gb, q1.b, q2.a, q3.got, sums = sync(q4.send, ga, gb, q1.b, q2.a, q3.got, sums)
+
+    y1, q2.b, q3.a = shift(q1.rest(0, unit), -2), second(q2.two()), first(q3.one())
     q4.got = core(q4.send)
-    value_1, two_2, one_3 = q1.rest(0, unit), q2.two(), q3.one()
-    y1, q2.b, q3.a = shift(value_1, -1), second(two_2), first(one_3)
+    q4.a = first(q4.one())
+    q4.a, q2.b, q3.a, y1, ga, sums = sync(q4.a, q2.b, q3.a, y1, ga, sums)
+
+    q4.b, q3.b, y2, gc, more = (
+        second(q4.two()), second(q3.two()), shift(q2.rest(0, unit), -1), second(ga), links.swap(sums, 4)
+    )
+    q4.b, q3.b, y2, gc, more, own_f, ga, gb = sync(q4.b, q3.b, y2, gc, more, own_f, ga, gb)
     sums = sums + more
     for j in range(2, links.bits):
         sums = sums + links.swap(sums, 2 << j)
-    own_f = fb.rest(size, 2 * size, z1, z2, z3)
-    q4.got, q2.b, q3.a, sums, own_f = sync(q4.got, q2.b, q3.a, sums, own_f)
-
-    q4.a, y2, q3.b, ga = first(q4.one()), shift(q2.rest(0, unit), -2), second(q3.two()), first(own_f)
-    q4.a, q3.b, y1, ga, own_f, sums = sync(q4.a, q3.b, y1, ga, own_f, sums)
-
-    q4.b, y3, gb, more = second(q4.two()), shift(q3.rest(0, unit), -3), second(own_f), links.swap_z(sums, 1)
-    q4.b, y2, gb, more, ga, sums = sync(q4.b, y2, gb, more, ga, sums)
 
     pos = q4.rest(unit, unit + words // 8)
     p1, p2, p3 = (links.swap_z(pos, mask) for mask in (1, 2, 3))
-    gc = second(ga)
-    sums = sums + more
-    p1, p2, p3, y3, gc, pos, sums = sync(p1, p2, p3, y3, gc, pos, sums)
+    y3 = shift(q3.rest(0, unit), -3)
+    near_f = (own_f, ga, gb, gc)
+    far_f = tuple(core(v) for v in near_f)
+    p1, p2, p3, y3, pos, sums, *far_f = sync(p1, p2, p3, y3, pos, sums, *far_f)
 
     pos = ((pos.astype(F32) + p1.astype(F32)) + (p2.astype(F32) + p3.astype(F32))).astype(BF16)
     own_q = q4.rest(0, unit, y1, y2, y3)
-    qa, qb, pa, pb, more = first(own_q), second(own_q), first(pos), second(pos), links.swap_z(sums, 2)
-    total_sums = sums + more
-    qa, qb, pa, pb, own_q, pos, own_f, ga, gb, gc = sync(qa, qb, pa, pb, own_q, pos, own_f, ga, gb, gc)
+    pa, pb, qa, qb, more = first(pos), second(pos), first(own_q), second(own_q), links.swap_z(sums, 1)
+    grad_up, grad_down = spread_hidden(info, near_f + tuple(far_f))
+    qa, qb, pa, pb, more, own_q, pos, grad_up, grad_down = sync(qa, qb, pa, pb, more, own_q, pos, grad_up, grad_down)
+
+    sums = sums + more
+    more = links.swap_z(sums, 2)
     near_q = (own_q, qa, qb, second(qa))
     near_p = (pos, pa, pb, second(pa))
-    near_f = (own_f, ga, gb, gc)
-    grad_up, grad_down = spread_hidden(info, near_f + tuple(core(v) for v in near_f))
-    pos_sum = spread_pos(info, near_p + tuple(core(v) for v in near_p))
+    far_q = tuple(core(v) for v in near_q)
+    far_p = tuple(core(v) for v in near_p)
+    total_sums = sums + more
+    pos_sum = spread_pos(info, near_p + far_p)
     grad_query_t, grad_key_t, grad_value_t, grad_out, grad_query_b, grad_value_b, grad_up_b = spread_query(
-        info, near_q + tuple(core(v) for v in near_q), gw
+        info, near_q + far_q, gw
     )
     return (
         out_words,

time: 398 us -> 352 us (0.88)
  local copies, waits for them, and re-layouts: 46.2 us -> 13.5 us
  waiting for transfers between devices: 93.7 us -> 84.7 us
    unnamed x223 -> x175, local copies, waits for them, and re-layouts: 41 us -> 7.69 us
    ppermute x20 -> x23, waiting for transfers between devices: 40.5 us -> 25 us  [second(): lax.ppermute(v, 'dp', [(i, i ^ (2 if i % 2 else 4)) for i in range(self.d...]
    pallas_call x1, Pallas kernels: 28.6 us -> 19.8 us  [hidden(): pl.pallas_call(partial(hidden_kernel, n), in_specs=[SMEM] + [VMEM] * (6 +...]
    ppermute x12, starting transfers between devices: 29.3 us -> 22.8 us  [shift_z(): return lax.ppermute(v, 'tensor', [(i, (i + by) % n) for i in range(n)])]
    ppermute x20 -> x23, starting transfers between devices: 21.5 us -> 26.6 us  [second(): lax.ppermute(v, 'dp', [(i, i ^ (2 if i % 2 else 4)) for i in range(self.d...]
    ppermute x37 -> x42, waiting for transfers between devices: 10.4 us -> 15.3 us  [swap(): return lax.ppermute(v, 'dp', [(i, i ^ code) for i in range(self.dp)])]
    ppermute x5, starting transfers between devices: 8.77 us -> 4.53 us  [swap_z(): return lax.ppermute(v, 'tensor', [(i, i ^ mask) for i in range(self.ring)])]
    pallas_call x4, Pallas kernels: 57 us -> 61.1 us  [attend_back(): pl.pallas_call(partial(attend_back_kernel, words, gw, heads, final, count...]
  transfers between devices with their start and end apart: 87 -> 97, of which waited for: 25 -> 28; matrix products, arithmetic and copies ran while one was open for 2% -> 3% of each run, Pallas kernels for 31% -> 36%
where the time goes in v5:
time: 352 us; the launch traced here: 348 us
  Pallas kernels  163 us (46%)
  waiting for transfers between devices  84.7 us (24%)
  starting transfers between devices  79.2 us (22%)
  local copies, waits for them, and re-layouts  13.5 us (4%)
  other arithmetic  5.44 us (2%)
    pallas_call x4, Pallas kernels, attend_back(): pl.pallas_call(partial(attend_back_kernel, words, gw, heads, final, count...  61.1 us
    pallas_call x4, Pallas kernels, attend(): pl.pallas_call(partial(attend_kernel, words, gw, heads, count), in_specs=...  44 us
    ppermute x12, waiting for transfers between devices, shift_z(): return lax.ppermute(v, 'tensor', [(i, (i + by) % n) for i in range(n)])  31.1 us
    ppermute x23, starting transfers between devices, second(): lax.ppermute(v, 'dp', [(i, i ^ (2 if i % 2 else 4)) for i in range(self.d...  26.6 us
    ppermute x23, waiting for transfers between devices, second(): lax.ppermute(v, 'dp', [(i, i ^ (2 if i % 2 else 4)) for i in range(self.d...  25 us
    ppermute x12, starting transfers between devices, shift_z(): return lax.ppermute(v, 'tensor', [(i, (i + by) % n) for i in range(n)])  22.8 us
    pallas_call x3, Pallas kernels, hidden_back(): pl.pallas_call(partial(hidden_back_kernel, pair), in_specs=[SMEM] + [VMEM...  19.9 us
    pallas_call x1, Pallas kernels, hidden(): pl.pallas_call(partial(hidden_kernel, n), in_specs=[SMEM] + [VMEM] * (6 +...  19.8 us
  transfers between devices with their start and end apart: 97, of which 28 were waited for; matrix products, arithmetic and copies ran while one was open for 3% of the time, Pallas kernels for 36%

profile of v5, /device:TPU:0, one launch (start us, length us, event | category | flops | bytes accessed | tf_op | source)
XLA Modules:
  0.0 347.7 jit_solution(13087450124189835276)
XLA Ops:
  2.8 2.4 pack.1
  5.3 5.1 %collective-permute-start.1 = (bf16[176,768]{1,0:T(8,128)(2,1)}, bf16[176,768]{1,0:T(8,128)(2,1)}, u32[]{:S(2)}, u32[]{:S(2)}) collective-permute-start(bf16[176,768]{1,0:T(8,128)(2,1)} %get-tuple-element.253), channel_id=1, source_target_pairs={{0,3},{1,0},{2,1},{3,2},{4,7},{5,4},{6,5},{7,6},{8,11},{9,8},{10,9... | collective-permute-start | bytes 811016 | tf_op jit(solution)/shard_map/ppermute | solution.py:731
  10.6 2.2 start_rows.1
  12.9 10.9 %attend_own.1 = (bf16[512,768]{1,0:T(8,128)(2,1)}, bf16[128,768]{1,0:T(8,128)(2,1)}, bf16[640,192]{1,0:T(8,128)(2,1)}, f32[8,640]{1,0:T(8,128)S(1)}, bf16[16,768...) custom-call(s32[4]{0:T(128)S(1)} %pad_add_fusion.info_ref, ...), custom_call_target="tpu_custom_call", output_to_operand_aliasing={{5}: (2, {})} | custom-call | flops 8000000000 | bytes 6000000 | tf_op jit(solution)/shard_map/attend_own/pallas_call | solution.py:285
  23.8 3.9 %collective-permute-start.10 = (bf16[192,768]{1,0:T(8,128)(2,1)S(1)}, bf16[192,768]{1,0:T(8,128)(2,1)S(1)}, u32[]{:S(2)}, u32[]{:S(2)}) collective-permute-start(bf16[192,768]{1,0:T(8,128)(2,1)S(1)} %copy-done.64), channel_id=1, source_target_pairs={{0,3},{1,0},{2,1},{3,2},{4,7},{5,4},{6,5},{7,6},{8,11},{9,8},{10,9... | collective-permute-start | bytes 884744 | tf_op jit(solution)/shard_map/ppermute | solution.py:731
  27.7 1.5 collective-permute-start.3
  30.7 5.8 %collective-permute-done.3.refs_2_.refs_5_ = bf16[176,768]{1,0:T(8,128)(2,1)S(1)} collective-permute-done((bf16[176,768]{1,0:T(8,128)(2,1)}, bf16[176,768]{1,0:T(8,128)(2,1)S(1)}, u32[]{:S(2)}, u32[]{:S(2)}) %collective-permute-start.3) | collective-permute-done | bytes 270368 | tf_op jit(solution)/shard_map/ppermute | solution.py:746
  37.1 5.0 %collective-permute-done.8.refs_0_.refs_3_ = bf16[176,768]{1,0:T(8,128)(2,1)S(1)} collective-permute-done((bf16[176,768]{1,0:T(8,128)(2,1)}, bf16[176,768]{1,0:T(8,128)(2,1)S(1)}, u32[]{:S(2)}, u32[]{:S(2)}) %collective-permute-start.8) | collective-permute-done | bytes 270368 | tf_op jit(solution)/shard_map/ppermute | solution.py:731
  42.9 3.3 collective-permute-done.9
  46.3 2.3 collective-permute-done.4.refs_3_.refs_6_
  48.6 1.5 collective-permute-start.19
  53.1 6.1 %collective-permute-done.13.refs_2_.refs_5_ = bf16[176,768]{1,0:T(8,128)(2,1)S(1)} collective-permute-done((bf16[176,768]{1,0:T(8,128)(2,1)}, bf16[176,768]{1,0:T(8,128)(2,1)S(1)}, u32[]{:S(2)}, u32[]{:S(2)}) %collective-permute-start.13) | collective-permute-done | bytes 270368 | tf_op jit(solution)/shard_map/ppermute | solution.py:746
  59.2 1.6 collective-permute-start.16
  63.3 1.5 collective-permute-start.14
  64.9 11.0 %attend_far.3 = (bf16[512,768]{1,0:T(8,128)(2,1)}, bf16[128,768]{1,0:T(8,128)(2,1)}, bf16[640,192]{1,0:T(8,128)(2,1)}, f32[8,640]{1,0:T(8,128)S(1)}, bf16[16,768...) custom-call(s32[4]{0:T(128)S(1)} %pad_add_fusion.info_ref, ...), custom_call_target="tpu_custom_call", output_to_operand_aliasing={{5}: (2, {})} | custom-call | flops 8000000000 | bytes 6000000 | tf_op jit(solution)/shard_map/attend_far/pallas_call | solution.py:285
  80.4 1.5 collective-permute-start.25
  82.4 11.0 %attend_far.4 = (bf16[512,768]{1,0:T(8,128)(2,1)}, bf16[128,768]{1,0:T(8,128)(2,1)}, bf16[640,192]{1,0:T(8,128)(2,1)}, f32[8,640]{1,0:T(8,128)S(1)}, bf16[16,768...) custom-call(s32[4]{0:T(128)S(1)} %pad_add_fusion.info_ref, ...), custom_call_target="tpu_custom_call", output_to_operand_aliasing={{5}: (2, {})} | custom-call | flops 8000000000 | bytes 6000000 | tf_op jit(solution)/shard_map/attend_far/pallas_call | solution.py:285
  99.5 11.2 %attend_far.5 = (bf16[512,768]{1,0:T(8,128)(2,1)}, bf16[128,768]{1,0:T(8,128)(2,1)}, bf16[640,192]{1,0:T(8,128)(2,1)}, f32[8,640]{1,0:T(8,128)S(1)}, bf16[16,768...) custom-call(s32[4]{0:T(128)S(1)} %pad_add_fusion.info_ref, ...), custom_call_target="tpu_custom_call", output_to_operand_aliasing={{5}: (2, {})} | custom-call | flops 8000000000 | bytes 6000000 | tf_op jit(solution)/shard_map/attend_far/pallas_call | solution.py:285
  110.8 3.2 collective-permute-done.32.refs_9_
  120.5 19.8 %hidden.1 = (bf16[768,640]{1,0:T(8,128)(2,1)S(1)}, bf16[4,768,640]{2,1,0:T(8,128)(2,1)S(1)}, f32[4,640,768]{2,1,0:T(8,128)S(1)}, bf16[4,768,768]{2,1,0:T(8,128)(...) custom-call(s32[4]{0:T(128)S(1)} %pad_add_fusion.info_ref, ...), custom_call_target="tpu_custom_call" | custom-call | flops 22000001024 | bytes 20000000 | tf_op jit(solution)/shard_map/hidden/pallas_call | solution.py:394
  140.3 9.4 %hidden_back.3 = (bf16[1536,768]{1,0:T(8,128)(2,1)}, bf16[768,768]{1,0:T(8,128)(2,1)}, bf16[768,768]{1,0:T(8,128)(2,1)}, f32[640,768]{1,0:T(8,128)S(1)}, f32[16,768]{1,0:T(8,128)S(1)}) custom-call(s32[4]{0:T(128)S(1)} %pad_add_fusion.info_ref, bf16[640,768]{1,0:T(8,128)(2,1)S(1)} %get-tuple-element.331.low_ref, ...), custom_call_target="tpu_custom_call", output_to_operand_aliasing={{3}: (7, {})} | custom-call | flops 14000000000 | bytes 16000000 | tf_op jit(solution)/shard_map/hidden_back/pallas_call | solution.py:455
  149.9 5.3 %hidden_back.4 = (bf16[768,768]{1,0:T(8,128)(2,1)}, bf16[384,768]{1,0:T(8,128)(2,1)}, bf16[384,768]{1,0:T(8,128)(2,1)}, f32[640,768]{1,0:T(8,128)S(1)}, f32[8,768]{1,0:T(8,128)S(1)}) custom-call(s32[4]{0:T(128)S(1)} %pad_add_fusion.info_ref, bf16[640,768]{1,0:T(8,128)(2,1)S(1)} %get-tuple-element.331.low_ref, ...), custom_call_target="tpu_custom_call", output_to_operand_aliasing={{3}: (7, {})} | custom-call | flops 7000000000 | bytes 8000000 | tf_op jit(solution)/shard_map/hidden_back/pallas_call | solution.py:455
  156.1 5.2 %hidden_back.5 = (bf16[768,768]{1,0:T(8,128)(2,1)}, bf16[384,768]{1,0:T(8,128)(2,1)}, bf16[384,768]{1,0:T(8,128)(2,1)}, f32[640,768]{1,0:T(8,128)S(1)}, f32[8,768]{1,0:T(8,128)S(1)}) custom-call(s32[4]{0:T(128)S(1)} %pad_add_fusion.info_ref, bf16[640,768]{1,0:T(8,128)(2,1)S(1)} %get-tuple-element.331.low_ref, ...), custom_call_target="tpu_custom_call", output_to_operand_aliasing={{3}: (7, {})} | custom-call | flops 7000000000 | bytes 8000000 | tf_op jit(solution)/shard_map/hidden_back/pallas_call | solution.py:455
  167.5 14.9 %attend_back.4 = (bf16[704,768]{1,0:T(8,128)(2,1)}, bf16[352,768]{1,0:T(8,128)(2,1)}, bf16[352,768]{1,0:T(8,128)(2,1)}, f32[640,768]{1,0:T(8,128)S(1)}) custom-call(s32[4]{0:T(128)S(1)} %pad_add_fusion.info_ref, bf16[640,768]{1,0:T(8,128)(2,1)S(1)} %get-tuple-element.250.rows_ref, f32[8,640]{1,0:T(8,128)S(1)} %copy-done.9, ...), custom_call_target="tpu_custom_call", output_to_operand_aliasing={{3}: (5, {})} | custom-call | flops 11000000512 | bytes 8000000 | tf_op jit(solution)/shard_map/attend_back/pallas_call | solution.py:605
  182.5 2.0 collective-permute-done.45
  189.1 14.7 %attend_back.5 = (bf16[704,768]{1,0:T(8,128)(2,1)}, bf16[352,768]{1,0:T(8,128)(2,1)}, bf16[352,768]{1,0:T(8,128)(2,1)}, f32[640,768]{1,0:T(8,128)S(1)}) custom-call(s32[4]{0:T(128)S(1)} %pad_add_fusion.info_ref, bf16[640,768]{1,0:T(8,128)(2,1)S(1)} %get-tuple-element.250.rows_ref, f32[8,640]{1,0:T(8,128)S(1)} %copy-done.7, ...), custom_call_target="tpu_custom_call", output_to_operand_aliasing={{3}: (5, {})} | custom-call | flops 11000000512 | bytes 8000000 | tf_op jit(solution)/shard_map/attend_back/pallas_call | solution.py:605
  208.0 1.8 collective-permute-start.54
  212.4 14.7 %attend_back.6 = (bf16[704,768]{1,0:T(8,128)(2,1)}, bf16[352,768]{1,0:T(8,128)(2,1)}, bf16[352,768]{1,0:T(8,128)(2,1)}, f32[640,768]{1,0:T(8,128)S(1)}) custom-call(s32[4]{0:T(128)S(1)} %pad_add_fusion.info_ref, bf16[640,768]{1,0:T(8,128)(2,1)S(1)} %get-tuple-element.250.rows_ref, ...), custom_call_target="tpu_custom_call", output_to_operand_aliasing={{3}: (5, {})} | custom-call | flops 11000000512 | bytes 8000000 | tf_op jit(solution)/shard_map/attend_back/pallas_call | solution.py:605
  230.8 1.5 collective-permute-start.59
  233.3 1.5 collective-permute-start.61
  234.9 16.7 %attend_back.7 = (bf16[960,768]{1,0:T(8,128)(2,1)}, bf16[480,768]{1,0:T(8,128)(2,1)}, bf16[480,768]{1,0:T(8,128)(2,1)}, f32[512,768]{1,0:T(8,128)}, f32[128,768]{1,0:T(8,128)}) custom-call(s32[4]{0:T(128)S(1)} %pad_add_fusion.info_ref, bf16[640,768]{1,0:T(8,128)(2,1)S(1)} %get-tuple-element.250.rows_ref, f32[8,640]{1,0:T(8,128)S(1)} %copy-done.11, ...), custom_call_target="tpu_custom_call" | custom-call | flops 11000000512 | bytes 8000000 | tf_op jit(solution)/shard_map/attend_back/pallas_call | solution.py:605
  252.5 2.7 collective-permute-done.63
  256.3 1.5 collective-permute-start.65
  257.8 6.8 %collective-permute-start.67 = (bf16[176,768]{1,0:T(8,128)(2,1)S(1)}, bf16[176,768]{1,0:T(8,128)(2,1)S(1)}, u32[]{:S(2)}, u32[]{:S(2)}) collective-permute-start(bf16[176,768]{1,0:T(8,128)(2,1)S(1)} %add_convert_fusion.19), channel_id=1, source_target_pairs={{0,2},{1,3},{2,0},{3,1},{4,6},{5,7},{6,4},{7,5},{8,10},{9,11},{10,... | collective-permute-start | bytes 811016 | tf_op jit(solution)/shard_map/ppermute | solution.py:731
  265.7 10.9 %collective-permute-done.67 = bf16[176,768]{1,0:T(8,128)(2,1)S(1)} collective-permute-done((bf16[176,768]{1,0:T(8,128)(2,1)S(1)}, bf16[176,768]{1,0:T(8,128)(2,1)S(1)}, u32[]{:S(2)}, u32[]{:S(2)}) %collective-permute-start.67) | collective-permute-done | bytes 270368 | tf_op jit(solution)/shard_map/ppermute | solution.py:731
  280.3 1.9 collective-permute-start.70
  283.5 7.4 %collective-permute-done.72 = f32[8,768]{1,0:T(8,128)S(1)} collective-permute-done((f32[8,768]{1,0:T(8,128)S(1)}, f32[8,768]{1,0:T(8,128)S(1)}, u32[]{:S(2)}, u32[]{:S(2)}) %collective-permute-start.72) | collective-permute-done | bytes 24608 | tf_op jit(solution)/shard_map/ppermute | solution.py:737
  291.0 2.3 collective-permute-start.75
  293.3 1.5 collective-permute-start.74
  296.0 2.2 collective-permute-done.75
  298.2 3.3 collective-permute-done.74
  301.8 10.7 %collective-permute-done.76 = bf16[176,768]{1,0:T(8,128)(2,1)S(1)} collective-permute-done((bf16[176,768]{1,0:T(8,128)(2,1)S(1)}, bf16[176,768]{1,0:T(8,128)(2,1)S(1)}, u32[]{:S(2)}, u32[]{:S(2)}) %collective-permute-start.76) | collective-permute-done | bytes 270368 | tf_op jit(solution)/shard_map/ppermute | solution.py:731
  317.1 4.6 %spread_hidden.1 = (f32[768,768]{1,0:T(8,128)}, f32[768,768]{1,0:T(8,128)}) custom-call(s32[4]{0:T(128)S(1)} %pad_add_fusion.info_ref, bf16[192,768]{1,0:T(8,128)(2,1)} %copy-done.12, bf16[192,768]{1,0:T(8,128)(2,1)} %copy-done.30, bf16[192,768]{1,0:T(8,128)(2,1)} %copy-done.29, bf16[192,768]{1,0:T(8,128)(2,1)} %copy-done.31, bf16[192,768]{1,0:T(8,128)(2,1)} %copy-done.32, ...), custom_call_target="tpu_custom_call" | custom-call | flops 500000000 | bytes 7000000 | tf_op jit(solution)/shard_map/spread_hidden/pallas_call | solution.py:686
  321.7 2.1 collective-permute-done.84.refs_2_
  325.7 4.7 %collective-permute-done.96 = f32[8,768]{1,0:T(8,128)S(1)} collective-permute-done((f32[8,768]{1,0:T(8,128)S(1)}, f32[8,768]{1,0:T(8,128)S(1)}, u32[]{:S(2)}, u32[]{:S(2)}) %collective-permute-start.96) | collective-permute-done | bytes 24608 | tf_op jit(solution)/shard_map/ppermute | solution.py:734
  332.3 3.8 %collective-permute-done.86.refs_3_ = bf16[64,768]{1,0:T(8,128)(2,1)S(1)} collective-permute-done((bf16[64,768]{1,0:T(8,128)(2,1)S(1)}, bf16[64,768]{1,0:T(8,128)(2,1)S(1)}, u32[]{:S(2)}, u32[]{:S(2)}) %collective-permute-start.86) | collective-permute-done | bytes 98336 | tf_op jit(solution)/shard_map/ppermute | solution.py:746
  338.1 3.0 spread_pos.1
  342.8 4.1 %spread_query.1 = (f32[4,192,768]{2,1,0:T(8,128)}, f32[192,768]{1,0:T(8,128)}, f32[192,768]{1,0:T(8,128)}, f32[192,768]{1,0:T(8,128)}, f32[4,192]{1,0:T(4,128)}, /*index=5*/f32[1,192]{1,0:T(1,128)}, f32[1,768]{1,0:T(1,128)S(1)}) custom-call(s32[4]{0:T(128)S(1)} %pad_add_fusion.info_ref, bf16[176,768]{1,0:T(8,128)(2,1)} %copy-done.15, ...), custom_call_target="tpu_custom_call" | custom-call | flops 500000000 | bytes 7000000 | tf_op jit(solution)/shard_map/spread_query/pallas_call | solution.py:660
  (380 shorter events, 73.2 us)
Async XLA Ops:
  5.3 18.5 %collective-permute-start.1 = (bf16[176,768]{1,0:T(8,128)(2,1)}, bf16[176,768]{1,0:T(8,128)(2,1)}, u32[]{:S(2)}, u32[]{:S(2)}) collective-permute-start(bf16[176,768]{1,0:T(8,128)(2,1)} %get-tuple-element.253), channel_id=1, source_target_pairs={{0,3},{1,0},{2,1},{3,2},{4,7},{5,4},{6,5},{7,6},{8,11},{9,8},{10,9... | collective-permute-start | bytes 811016 | tf_op jit(solution)/shard_map/ppermute | solution.py:731
  10.4 13.4 %collective-permute-start = (bf16[176,768]{1,0:T(8,128)(2,1)}, bf16[176,768]{1,0:T(8,128)(2,1)}, u32[]{:S(2)}, u32[]{:S(2)}) collective-permute-start(bf16[176,768]{1,0:T(8,128)(2,1)} %get-tuple-element.253), channel_id=1, source_target_pairs={{0,1},{1,2},{2,3},{3,0},{4,5},{5,6},{6,7},{7,4},{8,9},{9,10},{10,1... | collective-permute-start | bytes 811016 | tf_op jit(solution)/shard_map/ppermute | solution.py:731
  23.8 18.2 %collective-permute-start.10 = (bf16[192,768]{1,0:T(8,128)(2,1)S(1)}, bf16[192,768]{1,0:T(8,128)(2,1)S(1)}, u32[]{:S(2)}, u32[]{:S(2)}) collective-permute-start(bf16[192,768]{1,0:T(8,128)(2,1)S(1)} %copy-done.64), channel_id=1, source_target_pairs={{0,3},{1,0},{2,1},{3,2},{4,7},{5,4},{6,5},{7,6},{8,11},{9,8},{10,9... | collective-permute-start | bytes 884744 | tf_op jit(solution)/shard_map/ppermute | solution.py:731
  30.7 11.4 %collective-permute-start.8 = (bf16[176,768]{1,0:T(8,128)(2,1)}, bf16[176,768]{1,0:T(8,128)(2,1)S(1)}, u32[]{:S(2)}, u32[]{:S(2)}) collective-permute-start(bf16[176,768]{1,0:T(8,128)(2,1)} %collective-permute-done.refs_0_.refs_3_), channel_id=1, source_target_pairs={{0,1},{1,2},{2,3},{3,0},{4,5},{5,6},{6,7},{7,4},{8,9},{9,10},{10,1... | collective-permute-start | bytes 811016 | tf_op jit(solution)/shard_map/ppermute | solution.py:731
  30.7 15.6 %collective-permute-start.9 = (bf16[192,768]{1,0:T(8,128)(2,1)S(1)}, bf16[192,768]{1,0:T(8,128)(2,1)S(1)}, u32[]{:S(2)}, u32[]{:S(2)}) collective-permute-start(bf16[192,768]{1,0:T(8,128)(2,1)S(1)} %copy-done.64), channel_id=1, source_target_pairs={{0,1},{1,2},{2,3},{3,0},{4,5},{5,6},{6,7},{7,4},{8,9},{9,10},{10,1... | collective-permute-start | bytes 884744 | tf_op jit(solution)/shard_map/ppermute | solution.py:731
  48.6 14.7 %collective-permute-start.19 = (bf16[192,768]{1,0:T(8,128)(2,1)S(1)}, bf16[192,768]{1,0:T(8,128)(2,1)S(1)}, u32[]{:S(2)}, u32[]{:S(2)}) collective-permute-start(bf16[192,768]{1,0:T(8,128)(2,1)S(1)} %collective-permute-done.9), channel_id=1, source_target_pairs={{0,1},{1,2},{2,3},{3,0},{4,5},{5,6},{6,7},{7,4},{8,9},{9,10},{10,1... | collective-permute-start | bytes 884744 | tf_op jit(solution)/shard_map/ppermute | solution.py:731
  59.2 16.7 %collective-permute-start.16 = (bf16[176,768]{1,0:T(8,128)(2,1)S(1)}, bf16[176,768]{1,0:T(8,128)(2,1)S(1)}, u32[]{:S(2)}, u32[]{:S(2)}) collective-permute-start(bf16[176,768]{1,0:T(8,128)(2,1)S(1)} %collective-permute-done.8.refs_0_.refs_3_), channel_id=1, source_target_pairs={{0,16},{4,12},{8,24},{12,4},{16,0},{20,28},{24,8},{28,20},{1,17},{... | collective-permute-start | bytes 811016 | tf_op jit(solution)/shard_map/ppermute | solution.py:746
  60.8 15.2 %collective-permute-start.15 = (bf16[176,768]{1,0:T(8,128)(2,1)S(1)}, bf16[176,768]{1,0:T(8,128)(2,1)S(1)}, u32[]{:S(2)}, u32[]{:S(2)}) collective-permute-start(bf16[176,768]{1,0:T(8,128)(2,1)S(1)} %collective-permute-done.8.refs_0_.refs_3_), channel_id=1, source_target_pairs={{0,8},{4,20},{8,0},{12,28},{16,24},{20,4},{24,16},{28,12},{1,9},{5... | collective-permute-start | bytes 811016 | tf_op jit(solution)/shard_map/ppermute | solution.py:743
  61.3 15.4 %collective-permute-start.18 = (bf16[192,768]{1,0:T(8,128)(2,1)S(1)}, bf16[192,768]{1,0:T(8,128)(2,1)S(1)}, u32[]{:S(2)}, u32[]{:S(2)}) collective-permute-start(bf16[192,768]{1,0:T(8,128)(2,1)S(1)} %collective-permute-done.10.refs_14_), channel_id=1, source_target_pairs={{0,16},{4,12},{8,24},{12,4},{16,0},{20,28},{24,8},{28,20},{1,17},{... | collective-permute-start | bytes 884744 | tf_op jit(solution)/shard_map/ppermute | solution.py:746
  61.9 14.8 %collective-permute-start.17 = (bf16[192,768]{1,0:T(8,128)(2,1)S(1)}, bf16[192,768]{1,0:T(8,128)(2,1)S(1)}, u32[]{:S(2)}, u32[]{:S(2)}) collective-permute-start(bf16[192,768]{1,0:T(8,128)(2,1)S(1)} %collective-permute-done.10.refs_14_), channel_id=1, source_target_pairs={{0,8},{4,20},{8,0},{12,28},{16,24},{20,4},{24,16},{28,12},{1,9},{5... | collective-permute-start | bytes 884744 | tf_op jit(solution)/shard_map/ppermute | solution.py:743
  63.3 13.2 %collective-permute-start.14 = (bf16[176,768]{1,0:T(8,128)(2,1)S(1)}, bf16[176,768]{1,0:T(8,128)(2,1)S(1)}, u32[]{:S(2)}, u32[]{:S(2)}) collective-permute-start(bf16[176,768]{1,0:T(8,128)(2,1)S(1)} %collective-permute-done.12.refs_1_.refs_4_), channel_id=1, source_target_pairs={{0,16},{4,12},{8,24},{12,4},{16,0},{20,28},{24,8},{28,20},{1,17},{... | collective-permute-start | bytes 811016 | tf_op jit(solution)/shard_map/ppermute | solution.py:746
  78.9 14.5 %collective-permute-start.28 = (bf16[176,768]{1,0:T(8,128)(2,1)S(1)}, bf16[176,768]{1,0:T(8,128)(2,1)S(1)}, u32[]{:S(2)}, u32[]{:S(2)}) collective-permute-start(bf16[176,768]{1,0:T(8,128)(2,1)S(1)} %collective-permute-done.15.refs_1_.refs_4_), channel_id=1, source_target_pairs={{0,4},{4,0},{8,12},{12,8},{16,20},{20,16},{24,28},{28,24},{1,5},{5... | collective-permute-start | bytes 811016 | tf_op jit(solution)/shard_map/ppermute | solution.py:737
  79.0 14.4 %collective-permute-start.24 = (bf16[176,768]{1,0:T(8,128)(2,1)S(1)}, bf16[176,768]{1,0:T(8,128)(2,1)S(1)}, u32[]{:S(2)}, u32[]{:S(2)}) collective-permute-start(bf16[176,768]{1,0:T(8,128)(2,1)S(1)} %collective-permute-done.15.refs_1_.refs_4_), channel_id=1, source_target_pairs={{0,16},{4,12},{8,24},{12,4},{16,0},{20,28},{24,8},{28,20},{1,17},{... | collective-permute-start | bytes 811016 | tf_op jit(solution)/shard_map/ppermute | solution.py:746
  80.2 13.2 %collective-permute-start.27 = (bf16[176,768]{1,0:T(8,128)(2,1)S(1)}, bf16[176,768]{1,0:T(8,128)(2,1)S(1)}, u32[]{:S(2)}, u32[]{:S(2)}) collective-permute-start(bf16[176,768]{1,0:T(8,128)(2,1)S(1)} %collective-permute-done.8.refs_0_.refs_3_), channel_id=1, source_target_pairs={{0,4},{4,0},{8,12},{12,8},{16,20},{20,16},{24,28},{28,24},{1,5},{5... | collective-permute-start | bytes 811016 | tf_op jit(solution)/shard_map/ppermute | solution.py:737
  80.4 13.1 %collective-permute-start.25 = (bf16[192,768]{1,0:T(8,128)(2,1)S(1)}, bf16[192,768]{1,0:T(8,128)(2,1)}, u32[]{:S(2)}, u32[]{:S(2)}) collective-permute-start(bf16[192,768]{1,0:T(8,128)(2,1)S(1)} %collective-permute-done.17.refs_15_), channel_id=1, source_target_pairs={{0,16},{4,12},{8,24},{12,4},{16,0},{20,28},{24,8},{28,20},{1,17},{... | collective-permute-start | bytes 884744 | tf_op jit(solution)/shard_map/ppermute | solution.py:746
  81.9 12.6 %collective-permute-start.26 = (bf16[384,768]{1,0:T(8,128)(2,1)}, bf16[384,768]{1,0:T(8,128)(2,1)}, u32[]{:S(2)}, u32[]{:S(2)}) collective-permute-start(bf16[384,768]{1,0:T(8,128)(2,1)} %pad_maximum_fusion.refs_6_), channel_id=1, source_target_pairs={{0,8},{4,20},{8,0},{12,28},{16,24},{20,4},{24,16},{28,12},{1,9},{5... | collective-permute-start | bytes 1769480 | tf_op jit(solution)/shard_map/ppermute | solution.py:743
  96.6 14.1 %collective-permute-start.33 = (bf16[192,768]{1,0:T(8,128)(2,1)S(1)}, bf16[192,768]{1,0:T(8,128)(2,1)S(1)}, u32[]{:S(2)}, u32[]{:S(2)}) collective-permute-start(bf16[192,768]{1,0:T(8,128)(2,1)S(1)} %collective-permute-done.10.refs_14_), channel_id=1, source_target_pairs={{0,4},{4,0},{8,12},{12,8},{16,20},{20,16},{24,28},{28,24},{1,5},{5... | collective-permute-start | bytes 884744 | tf_op jit(solution)/shard_map/ppermute | solution.py:737
  97.0 13.8 %collective-permute-start.34 = (bf16[192,768]{1,0:T(8,128)(2,1)S(1)}, bf16[192,768]{1,0:T(8,128)(2,1)S(1)}, u32[]{:S(2)}, u32[]{:S(2)}) collective-permute-start(bf16[192,768]{1,0:T(8,128)(2,1)S(1)} %collective-permute-done.17.refs_15_), channel_id=1, source_target_pairs={{0,4},{4,0},{8,12},{12,8},{16,20},{20,16},{24,28},{28,24},{1,5},{5... | collective-permute-start | bytes 884744 | tf_op jit(solution)/shard_map/ppermute | solution.py:737
  97.1 13.7 %collective-permute-start.35 = (bf16[192,768]{1,0:T(8,128)(2,1)S(1)}, bf16[192,768]{1,0:T(8,128)(2,1)S(1)}, u32[]{:S(2)}, u32[]{:S(2)}) collective-permute-start(bf16[192,768]{1,0:T(8,128)(2,1)S(1)} %collective-permute-done.18.refs_16_), channel_id=1, source_target_pairs={{0,4},{4,0},{8,12},{12,8},{16,20},{20,16},{24,28},{28,24},{1,5},{5... | collective-permute-start | bytes 884744 | tf_op jit(solution)/shard_map/ppermute | solution.py:737
  97.5 13.3 %collective-permute-start.31 = (bf16[384,768]{1,0:T(8,128)(2,1)}, bf16[384,768]{1,0:T(8,128)(2,1)}, u32[]{:S(2)}, u32[]{:S(2)}) collective-permute-start(bf16[384,768]{1,0:T(8,128)(2,1)} %pad_maximum_fusion.refs_6_), channel_id=1, source_target_pairs={{0,16},{4,12},{8,24},{12,4},{16,0},{20,28},{24,8},{28,20},{1,17},{... | collective-permute-start | bytes 1769480 | tf_op jit(solution)/shard_map/ppermute | solution.py:746
  98.7 15.3 %collective-permute-start.32 = (bf16[384,768]{1,0:T(8,128)(2,1)}, bf16[384,768]{1,0:T(8,128)(2,1)}, u32[]{:S(2)}, u32[]{:S(2)}) collective-permute-start(bf16[384,768]{1,0:T(8,128)(2,1)} %collective-permute-done.26.refs_7_), channel_id=1, source_target_pairs={{0,16},{4,12},{8,24},{12,4},{16,0},{20,28},{24,8},{28,20},{1,17},{... | collective-permute-start | bytes 1769480 | tf_op jit(solution)/shard_map/ppermute | solution.py:746
  161.3 23.2 %collective-permute-start.46 = (bf16[768,768]{1,0:T(8,128)(2,1)}, bf16[768,768]{1,0:T(8,128)(2,1)S(1)}, u32[]{:S(2)}, u32[]{:S(2)}) collective-permute-start(bf16[768,768]{1,0:T(8,128)(2,1)} %get-tuple-element.367), channel_id=1, source_target_pairs={{0,4},{4,0},{8,12},{12,8},{16,20},{20,16},{24,28},{28,24},{1,5},{5... | collective-permute-start | bytes 3538952 | tf_op jit(solution)/shard_map/ppermute | solution.py:737
  161.4 23.1 %collective-permute-start.44 = (bf16[768,768]{1,0:T(8,128)(2,1)S(1)}, bf16[768,768]{1,0:T(8,128)(2,1)S(1)}, u32[]{:S(2)}, u32[]{:S(2)}) collective-permute-start(bf16[768,768]{1,0:T(8,128)(2,1)S(1)} %add_convert_fusion), channel_id=1, source_target_pairs={{0,8},{4,20},{8,0},{12,28},{16,24},{20,4},{24,16},{28,12},{1,9},{5... | collective-permute-start | bytes 3538952 | tf_op jit(solution)/shard_map/ppermute | solution.py:743
  165.5 17.1 %collective-permute-start.47 = (f32[8,768]{1,0:T(8,128)S(1)}, f32[8,768]{1,0:T(8,128)S(1)}, u32[]{:S(2)}, u32[]{:S(2)}) collective-permute-start(f32[8,768]{1,0:T(8,128)S(1)} %add.211), channel_id=1, source_target_pairs={{0,8},{4,12},{8,0},{12,4},{16,24},{20,28},{24,16},{28,20},{1,9},{5... | collective-permute-start | bytes 73736 | tf_op jit(solution)/shard_map/ppermute | solution.py:737
  166.8 17.7 %collective-permute-start.45 = (bf16[384,768]{1,0:T(8,128)(2,1)S(1)}, bf16[384,768]{1,0:T(8,128)(2,1)S(1)}, u32[]{:S(2)}, u32[]{:S(2)}) collective-permute-start(bf16[384,768]{1,0:T(8,128)(2,1)S(1)} %add_convert_fusion.4), channel_id=1, source_target_pairs={{0,8},{4,20},{8,0},{12,28},{16,24},{20,4},{24,16},{28,12},{1,9},{5... | collective-permute-start | bytes 1769480 | tf_op jit(solution)/shard_map/ppermute | solution.py:743
  182.4 21.5 %collective-permute-start.51 = (bf16[704,768]{1,0:T(8,128)(2,1)}, bf16[704,768]{1,0:T(8,128)(2,1)S(1)}, u32[]{:S(2)}, u32[]{:S(2)}) collective-permute-start(bf16[704,768]{1,0:T(8,128)(2,1)} %get-tuple-element.386), channel_id=1, source_target_pairs={{0,4},{4,0},{8,12},{12,8},{16,20},{20,16},{24,28},{28,24},{1,5},{5... | collective-permute-start | bytes 3244040 | tf_op jit(solution)/shard_map/ppermute | solution.py:737
  185.7 18.3 %collective-permute-start.49 = (bf16[192,768]{1,0:T(8,128)(2,1)S(1)}, bf16[192,768]{1,0:T(8,128)(2,1)S(1)}, u32[]{:S(2)}, u32[]{:S(2)}) collective-permute-start(bf16[192,768]{1,0:T(8,128)(2,1)S(1)} %add_convert_fusion.14), channel_id=1, source_target_pairs={{0,16},{4,12},{8,24},{12,4},{16,0},{20,28},{24,8},{28,20},{1,17},{... | collective-permute-start | bytes 884744 | tf_op jit(solution)/shard_map/ppermute | solution.py:746
  187.0 17.7 %collective-permute-start.48 = (bf16[384,768]{1,0:T(8,128)(2,1)S(1)}, bf16[384,768]{1,0:T(8,128)(2,1)S(1)}, u32[]{:S(2)}, u32[]{:S(2)}) collective-permute-start(bf16[384,768]{1,0:T(8,128)(2,1)S(1)} %get-tuple-element.383), channel_id=1, source_target_pairs={{0,16},{4,12},{8,24},{12,4},{16,0},{20,28},{24,8},{28,20},{1,17},{... | collective-permute-start | bytes 1769480 | tf_op jit(solution)/shard_map/ppermute | solution.py:746
  187.8 16.8 %collective-permute-start.50 = (bf16[384,768]{1,0:T(8,128)(2,1)S(1)}, bf16[384,768]{1,0:T(8,128)(2,1)S(1)}, u32[]{:S(2)}, u32[]{:S(2)}) collective-permute-start(bf16[384,768]{1,0:T(8,128)(2,1)S(1)} %get-tuple-element.385), channel_id=1, source_target_pairs={{0,8},{4,20},{8,0},{12,28},{16,24},{20,4},{24,16},{28,12},{1,9},{5... | collective-permute-start | bytes 1769480 | tf_op jit(solution)/shard_map/ppermute | solution.py:743
  206.9 20.5 %collective-permute-start.53 = (bf16[192,768]{1,0:T(8,128)(2,1)S(1)}, bf16[192,768]{1,0:T(8,128)(2,1)S(1)}, u32[]{:S(2)}, u32[]{:S(2)}) collective-permute-start(bf16[192,768]{1,0:T(8,128)(2,1)S(1)} %get-tuple-element.400), channel_id=1, source_target_pairs={{0,2},{1,3},{2,0},{3,1},{4,6},{5,7},{6,4},{7,5},{8,10},{9,11},{10,... | collective-permute-start | bytes 884744 | tf_op jit(solution)/shard_map/ppermute | solution.py:731
  208.0 20.4 %collective-permute-start.54 = (bf16[192,768]{1,0:T(8,128)(2,1)S(1)}, bf16[192,768]{1,0:T(8,128)(2,1)S(1)}, u32[]{:S(2)}, u32[]{:S(2)}) collective-permute-start(bf16[192,768]{1,0:T(8,128)(2,1)S(1)} %get-tuple-element.401), channel_id=1, source_target_pairs={{0,3},{1,0},{2,1},{3,2},{4,7},{5,4},{6,5},{7,6},{8,11},{9,8},{10,9... | collective-permute-start | bytes 884744 | tf_op jit(solution)/shard_map/ppermute | solution.py:731
  209.8 19.8 %collective-permute-start.55 = (bf16[192,768]{1,0:T(8,128)(2,1)S(1)}, bf16[192,768]{1,0:T(8,128)(2,1)S(1)}, u32[]{:S(2)}, u32[]{:S(2)}) collective-permute-start(bf16[192,768]{1,0:T(8,128)(2,1)S(1)} %add_convert_fusion.11), channel_id=1, source_target_pairs={{0,1},{1,2},{2,3},{3,0},{4,5},{5,6},{6,7},{7,4},{8,9},{9,10},{10,1... | collective-permute-start | bytes 884744 | tf_op jit(solution)/shard_map/ppermute | solution.py:731
  210.4 19.2 %collective-permute-start.57 = (bf16[192,768]{1,0:T(8,128)(2,1)S(1)}, bf16[192,768]{1,0:T(8,128)(2,1)S(1)}, u32[]{:S(2)}, u32[]{:S(2)}) collective-permute-start(bf16[192,768]{1,0:T(8,128)(2,1)S(1)} %add_convert_fusion.10), channel_id=1, source_target_pairs={{0,16},{4,12},{8,24},{12,4},{16,0},{20,28},{24,8},{28,20},{1,17},{... | collective-permute-start | bytes 884744 | tf_op jit(solution)/shard_map/ppermute | solution.py:746
  211.7 17.9 %collective-permute-start.56 = (bf16[352,768]{1,0:T(8,128)(2,1)S(1)}, bf16[352,768]{1,0:T(8,128)(2,1)S(1)}, u32[]{:S(2)}, u32[]{:S(2)}) collective-permute-start(bf16[352,768]{1,0:T(8,128)(2,1)S(1)} %add_convert_fusion.7), channel_id=1, source_target_pairs={{0,8},{4,20},{8,0},{12,28},{16,24},{20,4},{24,16},{28,12},{1,9},{5... | collective-permute-start | bytes 1622024 | tf_op jit(solution)/shard_map/ppermute | solution.py:743
  228.4 23.2 %collective-permute-start.62 = (bf16[704,768]{1,0:T(8,128)(2,1)S(1)}, bf16[704,768]{1,0:T(8,128)(2,1)S(1)}, u32[]{:S(2)}, u32[]{:S(2)}) collective-permute-start(bf16[704,768]{1,0:T(8,128)(2,1)S(1)} %copy-done.57), channel_id=1, source_target_pairs={{0,4},{4,0},{8,12},{12,8},{16,20},{20,16},{24,28},{28,24},{1,5},{5... | collective-permute-start | bytes 3244040 | tf_op jit(solution)/shard_map/ppermute | solution.py:737
  230.8 20.8 %collective-permute-start.59 = (bf16[192,768]{1,0:T(8,128)(2,1)S(1)}, bf16[192,768]{1,0:T(8,128)(2,1)S(1)}, u32[]{:S(2)}, u32[]{:S(2)}) collective-permute-start(bf16[192,768]{1,0:T(8,128)(2,1)S(1)} %add_convert_fusion.9.refs_0_), channel_id=1, source_target_pairs={{0,16},{4,12},{8,24},{12,4},{16,0},{20,28},{24,8},{28,20},{1,17},{... | collective-permute-start | bytes 884744 | tf_op jit(solution)/shard_map/ppermute | solution.py:746
  232.3 19.3 %collective-permute-start.58 = (bf16[192,768]{1,0:T(8,128)(2,1)S(1)}, bf16[192,768]{1,0:T(8,128)(2,1)S(1)}, u32[]{:S(2)}, u32[]{:S(2)}) collective-permute-start(bf16[192,768]{1,0:T(8,128)(2,1)S(1)} %add_convert_fusion.9.refs_0_), channel_id=1, source_target_pairs={{0,8},{4,20},{8,0},{12,28},{16,24},{20,4},{24,16},{28,12},{1,9},{5... | collective-permute-start | bytes 884744 | tf_op jit(solution)/shard_map/ppermute | solution.py:743
  232.8 18.8 %collective-permute-start.60 = (bf16[176,768]{1,0:T(8,128)(2,1)S(1)}, bf16[176,768]{1,0:T(8,128)(2,1)S(1)}, u32[]{:S(2)}, u32[]{:S(2)}) collective-permute-start(bf16[176,768]{1,0:T(8,128)(2,1)S(1)} %add_convert_fusion.21), channel_id=1, source_target_pairs={{0,16},{4,12},{8,24},{12,4},{16,0},{20,28},{24,8},{28,20},{1,17},{... | collective-permute-start | bytes 811016 | tf_op jit(solution)/shard_map/ppermute | solution.py:746
  233.3 18.3 %collective-permute-start.61 = (bf16[352,768]{1,0:T(8,128)(2,1)S(1)}, bf16[352,768]{1,0:T(8,128)(2,1)S(1)}, u32[]{:S(2)}, u32[]{:S(2)}) collective-permute-start(bf16[352,768]{1,0:T(8,128)(2,1)S(1)} %add_convert_fusion.6), channel_id=1, source_target_pairs={{0,8},{4,20},{8,0},{12,28},{16,24},{20,4},{24,16},{28,12},{1,9},{5... | collective-permute-start | bytes 1622024 | tf_op jit(solution)/shard_map/ppermute | solution.py:743
  251.9 24.7 %collective-permute-start.66 = (bf16[352,768]{1,0:T(8,128)(2,1)S(1)}, bf16[352,768]{1,0:T(8,128)(2,1)S(1)}, u32[]{:S(2)}, u32[]{:S(2)}) collective-permute-start(bf16[352,768]{1,0:T(8,128)(2,1)S(1)} %add_convert_fusion.5), channel_id=1, source_target_pairs={{0,8},{4,20},{8,0},{12,28},{16,24},{20,4},{24,16},{28,12},{1,9},{5... | collective-permute-start | bytes 1622024 | tf_op jit(solution)/shard_map/ppermute | solution.py:743
  255.4 21.2 %collective-permute-start.64 = (bf16[480,768]{1,0:T(8,128)(2,1)S(1)}, bf16[480,768]{1,0:T(8,128)(2,1)S(1)}, u32[]{:S(2)}, u32[]{:S(2)}) collective-permute-start(bf16[480,768]{1,0:T(8,128)(2,1)S(1)} %add_convert_fusion.1), channel_id=1, source_target_pairs={{0,8},{4,20},{8,0},{12,28},{16,24},{20,4},{24,16},{28,12},{1,9},{5... | collective-permute-start | bytes 2211848 | tf_op jit(solution)/shard_map/ppermute | solution.py:743
  257.8 18.8 %collective-permute-start.67 = (bf16[176,768]{1,0:T(8,128)(2,1)S(1)}, bf16[176,768]{1,0:T(8,128)(2,1)S(1)}, u32[]{:S(2)}, u32[]{:S(2)}) collective-permute-start(bf16[176,768]{1,0:T(8,128)(2,1)S(1)} %add_convert_fusion.19), channel_id=1, source_target_pairs={{0,2},{1,3},{2,0},{3,1},{4,6},{5,7},{6,4},{7,5},{8,10},{9,11},{10,... | collective-permute-start | bytes 811016 | tf_op jit(solution)/shard_map/ppermute | solution.py:731
  276.8 14.2 %collective-permute-start.71 = (bf16[192,768]{1,0:T(8,128)(2,1)S(1)}, bf16[192,768]{1,0:T(8,128)(2,1)S(1)}, u32[]{:S(2)}, u32[]{:S(2)}) collective-permute-start(bf16[192,768]{1,0:T(8,128)(2,1)S(1)} %collective-permute-done.58.refs_1_), channel_id=1, source_target_pairs={{0,16},{4,12},{8,24},{12,4},{16,0},{20,28},{24,8},{28,20},{1,17},{... | collective-permute-start | bytes 884744 | tf_op jit(solution)/shard_map/ppermute | solution.py:746
  278.0 13.0 %collective-permute-start.68 = (bf16[240,768]{1,0:T(8,128)(2,1)S(1)}, bf16[240,768]{1,0:T(8,128)(2,1)S(1)}, u32[]{:S(2)}, u32[]{:S(2)}) collective-permute-start(bf16[240,768]{1,0:T(8,128)(2,1)S(1)} %add_convert_fusion.8), channel_id=1, source_target_pairs={{0,16},{4,12},{8,24},{12,4},{16,0},{20,28},{24,8},{28,20},{1,17},{... | collective-permute-start | bytes 1105928 | tf_op jit(solution)/shard_map/ppermute | solution.py:746
  279.2 11.7 %collective-permute-start.69 = (bf16[176,768]{1,0:T(8,128)(2,1)S(1)}, bf16[176,768]{1,0:T(8,128)(2,1)S(1)}, u32[]{:S(2)}, u32[]{:S(2)}) collective-permute-start(bf16[176,768]{1,0:T(8,128)(2,1)S(1)} %add_convert_fusion.18), channel_id=1, source_target_pairs={{0,16},{4,12},{8,24},{12,4},{16,0},{20,28},{24,8},{28,20},{1,17},{... | collective-permute-start | bytes 811016 | tf_op jit(solution)/shard_map/ppermute | solution.py:746
  295.5 16.9 %collective-permute-start.77 = (bf16[192,768]{1,0:T(8,128)(2,1)S(1)}, bf16[192,768]{1,0:T(8,128)(2,1)S(1)}, u32[]{:S(2)}, u32[]{:S(2)}) collective-permute-start(bf16[192,768]{1,0:T(8,128)(2,1)S(1)} %add_convert_fusion.9.refs_0_), channel_id=1, source_target_pairs={{0,4},{4,0},{8,12},{12,8},{16,20},{20,16},{24,28},{28,24},{1,5},{5... | collective-permute-start | bytes 884744 | tf_op jit(solution)/shard_map/ppermute | solution.py:737
  295.5 16.9 %collective-permute-start.78 = (bf16[192,768]{1,0:T(8,128)(2,1)S(1)}, bf16[192,768]{1,0:T(8,128)(2,1)S(1)}, u32[]{:S(2)}, u32[]{:S(2)}) collective-permute-start(bf16[192,768]{1,0:T(8,128)(2,1)S(1)} %collective-permute-done.58.refs_1_), channel_id=1, source_target_pairs={{0,4},{4,0},{8,12},{12,8},{16,20},{20,16},{24,28},{28,24},{1,5},{5... | collective-permute-start | bytes 884744 | tf_op jit(solution)/shard_map/ppermute | solution.py:737
  298.2 14.3 %collective-permute-start.79 = (bf16[192,768]{1,0:T(8,128)(2,1)S(1)}, bf16[192,768]{1,0:T(8,128)(2,1)S(1)}, u32[]{:S(2)}, u32[]{:S(2)}) collective-permute-start(bf16[192,768]{1,0:T(8,128)(2,1)S(1)} %collective-permute-done.59.refs_2_), channel_id=1, source_target_pairs={{0,4},{4,0},{8,12},{12,8},{16,20},{20,16},{24,28},{28,24},{1,5},{5... | collective-permute-start | bytes 884744 | tf_op jit(solution)/shard_map/ppermute | solution.py:737
  (136 other events, 1470.6 us)

commit v6 on v5

--- a/solution.py
+++ b/solution.py
@@ -261,16 +261,15 @@
             ew = jnp.exp(sw - top)
             ee = jnp.exp(se - top)
             total = jnp.sum(ew, 1, keepdims=True) + jnp.sum(ee, 1, keepdims=True)
-            inv = 1.0 / total
             parts.append(
-                mm((ew * inv).astype(BF16), v_s[h, :words]) + mm((ee * inv).astype(BF16), v_s[h, words:])
+                (mm(ew.astype(BF16), v_s[h, :words]) + mm(ee.astype(BF16), v_s[h, words:])) * (1.0 / total)
             )
             logt = top + jnp.log(total)
             lt_ref[h : h + 1, rows] = jnp.broadcast_to(logt, (block, block)).T[0:1]
         ctx_s[rows, :] = jnp.concatenate(parts, 1).astype(BF16)
         return carry
 
-    lax.fori_loop(0, rows_ref.shape[0] // block, step, 0)
+    lax.fori_loop(0, rows_ref.shape[0] // block, step, 0, unroll=True)
     last = start([(ctx_s, ctx_ref)], sem.at[2])
     out_ref[...] = acc_ref[...] + mm(ctx_s[...], w_s[6 * gw : 7 * gw])
     wait(saves)
@@ -303,7 +302,7 @@
         + [pltpu.VMEM((heads, total, HEAD_DIM), BF16) for _ in range(4)]
         + [DMA((3,))],
         input_output_aliases={2: 5},
-        compiler_params=params(11),
+        compiler_params=params(16),
         cost_estimate=cost(8, 6),
         name="attend_own" if small else "attend_far",
     )(info, rows_low, acc, *small, *far(pieces))
@@ -523,26 +522,19 @@
         dc_s[h] = grad_ctx[:, h * HEAD_DIM : (h + 1) * HEAD_DIM]
     wait(last)
     full_s[6 * gw : 7 * gw] = mm_tn(ctx_s[...], low_ref[...]).astype(BF16)
-    block = 128
     for h in range(heads):
         o = h * HEAD_DIM
         e = o + HEAD_DIM
-
-        def step(qb, carry):
-            rows = pl.ds(pl.multiple_of(qb * block, block), block)
-            logt = lt_ref[h : h + 1, rows]
-            pw = jnp.exp(mm_nt(k_s[h, :words], qw_s[h, rows]) - logt)
-            pe = jnp.exp(mm_nt(k_s[h, words:], qe_s[h, rows]) - logt)
-            gw_ = mm_nt(v_s[h, :words], dc_s[h, rows])
-            ge_ = mm_nt(v_s[h, words:], dc_s[h, rows])
-            p_s[:words, rows] = pw.astype(BF16)
-            p_s[words:, rows] = pe.astype(BF16)
-            dot = jnp.sum(pw * gw_, 0, keepdims=True) + jnp.sum(pe * ge_, 0, keepdims=True)
-            ds_s[:words, rows] = (pw * (gw_ - dot)).astype(BF16)
-            ds_s[words:, rows] = (pe * (ge_ - dot)).astype(BF16)
-            return carry
-
-        lax.fori_loop(0, total // block, step, 0)
+        logt = lt_ref[h : h + 1]
+        pw = jnp.exp(mm_nt(k_s[h, :words], qw_s[h]) - logt)
+        pe = jnp.exp(mm_nt(k_s[h, words:], qe_s[h]) - logt)
+        gw_ = mm_nt(v_s[h, :words], dc_s[h])
+        ge_ = mm_nt(v_s[h, words:], dc_s[h])
+        p_s[:words] = pw.astype(BF16)
+        p_s[words:] = pe.astype(BF16)
+        dot = jnp.sum(pw * gw_, 0, keepdims=True) + jnp.sum(pe * ge_, 0, keepdims=True)
+        ds_s[:words] = (pw * (gw_ - dot)).astype(BF16)
+        ds_s[words:] = (pe * (ge_ - dot)).astype(BF16)
         dv = mm(p_s[...], dc_s[h]).astype(BF16)
         dkw = mm(ds_s[:words], qw_s[h]).astype(BF16)
         dke = mm(ds_s[words:], qe_s[h]).astype(BF16)
@@ -629,7 +621,7 @@
             DMA((4,)),
         ],
         input_output_aliases={} if final else {5: 3},
-        compiler_params=params(20),
+        compiler_params=params(24),
         cost_estimate=cost(11, 8),
         name="attend_back",
     )(info, rows_low, lt, low, up_sums, acc, *far((pw, pe, ctx)), *far(pieces), *((spans,) if final else ()))
@@ -831,12 +823,14 @@
         return acc
 
     v1, v3 = shift(piece_q, 1), shift(piece_q, 3)
+    acc, piece_f = sync(acc, piece_f)
+    f1, f3 = shift(piece_f, 1), shift(piece_f, 3)
     acc = attend_one(0, acc, own, small)
-    acc, v1, v3, piece_f = sync(acc, v1, v3, piece_f)
-    a1, b1, v2, f1, f3 = first(v1), second(v1), shift(v1, 1), shift(piece_f, 1), shift(piece_f, 3)
-    acc, v1, a1, b1, v3 = sync(acc, v1, a1, b1, v3)
+    acc, v1, v3 = sync(acc, v1, v3)
+    a1, b1, v2 = first(v1), second(v1), shift(v1, 1)
+    acc, v1, a1, b1, v3, f1, f3 = sync(acc, v1, a1, b1, v3, f1, f3)
     c1, kv, ka, kb, a3, b3 = second(a1), core(v1), core(a1), core(b1), first(v3), second(v3)
-    acc, c1, kv, ka, kb, v2, f1, f3, v3 = sync(acc, c1, kv, ka, kb, v2, f1, f3, v3)
+    acc, c1, kv, ka, kb, v2, f1, v3 = sync(acc, c1, kv, ka, kb, v2, f1, v3)
     kc, f2 = core(c1), shift(f1, 1)
     acc, kc, a3, b3, v2, f3 = sync(acc, kc, a3, b3, v2, f3)
     group_1 = (v1, a1, b1, c1, kv, ka, kb, kc)
@@ -896,70 +890,76 @@
     fc, acc = ffn_blocks((0,), acc)
     acc, fb.got = sync(acc, fb.got)
     one_b = fb.one()
+    fc.got = core(fc.send)
     acc, attended_low, sums = norm_back(attended, acc, vec, sums)
     more = core(sums)
-    acc, one_b, sums, more = sync(acc, one_b, sums, more)
-    sums = sums + more
-
-    fb.a, fc.got, more = first(one_b), core(fc.send), links.swap(sums, 2)
+    acc, one_b, sums, more, fc.got = sync(acc, one_b, sums, more, fc.got)
+    acc, one_c, sums = sync(acc, fc.one(), sums + more)
+
+    fb.a, fc.a, more = first(one_b), first(one_c), links.swap(sums, 2)
     q1, acc = back(2, acc)
-    acc, fa.a, fb.a, fc.got, more = sync(acc, fa.a, fb.a, fc.got, more)
-    acc, two_a, two_b, one_c, sums = sync(acc, fa.two(), fb.two(), fc.one(), sums + more)
-
-    fa.b, fb.b, fc.a, q1.got = second(two_a), second(two_b), first(one_c), core(q1.send)
+    acc, fa.a, fb.a, fc.a, more = sync(acc, fa.a, fb.a, fc.a, more)
+    q1.got = core(q1.send)
+    acc, two_a, two_b, two_c, sums, q1.got = sync(acc, fa.two(), fb.two(), fc.two(), sums + more, q1.got)
+    acc, one_1 = sync(acc, q1.one())
+
+    fa.b, fb.b, fc.b, q1.a, more = second(two_a), second(two_b), second(two_c), first(one_1), links.swap(sums, 4)
     q2, acc = back(1, acc)
-    acc, fa.b, fb.b, fc.a, q1.got = sync(acc, fa.b, fb.b, fc.a, q1.got)
+    acc, fa.b, fb.b, fc.b, q1.a, more = sync(acc, fa.b, fb.b, fc.b, q1.a, more)
     q2.got = core(q2.send)
-    acc, r2, r1, r3, two_c, one_1, q2.got = sync(
-        acc, fa.rest(0, size), fa.rest(size, 2 * size), fb.rest(0, size), fc.two(), q1.one(), q2.got
-    )
-
-    z2, z1, z3, q1.a, fc.b = shift(r2, -2), shift(r1, -1), shift(r3, -3), first(one_1), second(two_c)
-    q3, acc = back(3, acc)
-    acc, z2, z1, z3, q1.a, fc.b = sync(acc, z2, z1, z3, q1.a, fc.b)
-    acc, own_f, two_1, one_2 = sync(acc, fc.rest(0, size, z1, z2, z3), q1.two(), q2.one())
-
-    ga, gb, q1.b, q2.a, q3.got = first(own_f), second(own_f), second(two_1), first(one_2), core(q3.send)
-    q4, grad_words, grad_ents = back(0, acc, entity_spans)
-    q4.send, ga, gb, q1.b, q2.a, q3.got, sums = sync(q4.send, ga, gb, q1.b, q2.a, q3.got, sums)
-
-    y1, q2.b, q3.a = shift(q1.rest(0, unit), -2), second(q2.two()), first(q3.one())
-    q4.got = core(q4.send)
-    q4.a = first(q4.one())
-    q4.a, q2.b, q3.a, y1, ga, sums = sync(q4.a, q2.b, q3.a, y1, ga, sums)
-
-    q4.b, q3.b, y2, gc, more = (
-        second(q4.two()), second(q3.two()), shift(q2.rest(0, unit), -1), second(ga), links.swap(sums, 4)
-    )
-    q4.b, q3.b, y2, gc, more, own_f, ga, gb = sync(q4.b, q3.b, y2, gc, more, own_f, ga, gb)
     sums = sums + more
     for j in range(2, links.bits):
         sums = sums + links.swap(sums, 2 << j)
-
-    pos = q4.rest(unit, unit + words // 8)
-    p1, p2, p3 = (links.swap_z(pos, mask) for mask in (1, 2, 3))
-    y3 = shift(q3.rest(0, unit), -3)
+    acc, r2, r1, r3, two_1, q2.got, sums = sync(
+        acc, fa.rest(0, size), fa.rest(size, 2 * size), fb.rest(0, size), q1.two(), q2.got, sums
+    )
+    acc, one_2 = sync(acc, q2.one())
+
+    z2, z1, z3, q1.b, q2.a = shift(r2, -2), shift(r1, -1), shift(r3, -3), second(two_1), first(one_2)
+    q3, acc = back(3, acc)
+    acc, z2, z1, z3, q1.b, q2.a = sync(acc, z2, z1, z3, q1.b, q2.a)
+    q3.got = core(q3.send)
+    acc, own_f, value_1, two_2, q3.got = sync(
+        acc, fc.rest(0, size, z1, z2, z3), q1.rest(0, unit), q2.two(), q3.got
+    )
+    acc, one_3 = sync(acc, q3.one())
+
+    y1, ga, gb, q2.b, q3.a = shift(value_1, -2), first(own_f), second(own_f), second(two_2), first(one_3)
+    q4, grad_words, grad_ents = back(0, acc, entity_spans)
+    q4.send, y1, ga, gb, q2.b, q3.a, sums = sync(q4.send, y1, ga, gb, q2.b, q3.a, sums)
+
+    q4.got = core(q4.send)
+    y2, q3.b, gc = shift(q2.rest(0, unit), -1), second(q3.two()), second(ga)
+    q4.a = first(q4.one())
+    q4.a, q3.b, y2, gc, own_f, ga, gb, sums = sync(q4.a, q3.b, y2, gc, own_f, ga, gb, sums)
+
+    y3, q4.b = shift(q3.rest(0, unit), -3), second(q4.two())
     near_f = (own_f, ga, gb, gc)
     far_f = tuple(core(v) for v in near_f)
-    p1, p2, p3, y3, pos, sums, *far_f = sync(p1, p2, p3, y3, pos, sums, *far_f)
+    q4.b, y3, sums, *far_f = sync(q4.b, y3, sums, *far_f)
+
+    pos = q4.rest(unit, unit + words // 8)
+    own_q = q4.rest(0, unit, y1, y2, y3)
+    p1, p2, p3 = (links.swap_z(pos, mask) for mask in (1, 2, 3))
+    qa, qb = first(own_q), second(own_q)
+    grad_up, grad_down = spread_hidden(info, near_f + tuple(far_f))
+    p1, p2, p3, qa, qb, own_q, pos, sums, grad_up, grad_down = sync(
+        p1, p2, p3, qa, qb, own_q, pos, sums, grad_up, grad_down
+    )
 
     pos = ((pos.astype(F32) + p1.astype(F32)) + (p2.astype(F32) + p3.astype(F32))).astype(BF16)
-    own_q = q4.rest(0, unit, y1, y2, y3)
-    pa, pb, qa, qb, more = first(pos), second(pos), first(own_q), second(own_q), links.swap_z(sums, 1)
-    grad_up, grad_down = spread_hidden(info, near_f + tuple(far_f))
-    qa, qb, pa, pb, more, own_q, pos, grad_up, grad_down = sync(qa, qb, pa, pb, more, own_q, pos, grad_up, grad_down)
-
+    pa, pb, qc, more = first(pos), second(pos), second(qa), links.swap_z(sums, 1)
+    kv, ka, kb = core(own_q), core(qa), core(qb)
+    pa, pb, qc, more, kv, ka, kb, pos = sync(pa, pb, qc, more, kv, ka, kb, pos)
     sums = sums + more
-    more = links.swap_z(sums, 2)
-    near_q = (own_q, qa, qb, second(qa))
-    near_p = (pos, pa, pb, second(pa))
-    far_q = tuple(core(v) for v in near_q)
-    far_p = tuple(core(v) for v in near_p)
+    pc, more, kc = second(pa), links.swap_z(sums, 2), core(qc)
+    kp = tuple(core(v) for v in (pos, pa, pb))
+    grad_query_t, grad_key_t, grad_value_t, grad_out, grad_query_b, grad_value_b, grad_up_b = spread_query(
+        info, (own_q, qa, qb, qc, kv, ka, kb, kc), gw
+    )
     total_sums = sums + more
-    pos_sum = spread_pos(info, near_p + far_p)
-    grad_query_t, grad_key_t, grad_value_t, grad_out, grad_query_b, grad_value_b, grad_up_b = spread_query(
-        info, near_q + far_q, gw
-    )
+    grad_query_t, pc, *kp = sync(grad_query_t, pc, *kp)
+    pos_sum = spread_pos(info, (pos, pa, pb, pc, *kp, core(pc)))
     return (
         out_words,
         out_ents,

time: 352 us -> 344 us (0.977)
  Pallas kernels: 163 us -> 143 us
  starting transfers between devices: 79.2 us -> 86.7 us
    pallas_call x4, Pallas kernels: 61.1 us -> 48.2 us  [attend_back(): pl.pallas_call(partial(attend_back_kernel, words, gw, heads, final, count...]
    ppermute x12, waiting for transfers between devices: 31.1 us -> 23.3 us  [shift_z(): return lax.ppermute(v, 'tensor', [(i, (i + by) % n) for i in range(n)])]
    pallas_call x4, Pallas kernels: 44 us -> 37.4 us  [attend(): pl.pallas_call(partial(attend_kernel, words, gw, heads, count), in_specs=...]
    ppermute x15, waiting for transfers between devices: 3 us -> 9.27 us  [first(): lax.ppermute(v, 'dp', [(i, i ^ (4 if i % 2 else 2)) for i in range(self.d...]
    ppermute x23, waiting for transfers between devices: 25 us -> 30.2 us  [second(): lax.ppermute(v, 'dp', [(i, i ^ (2 if i % 2 else 4)) for i in range(self.d...]
    ppermute x5, waiting for transfers between devices: 10.2 us -> 6.09 us  [swap_z(): return lax.ppermute(v, 'tensor', [(i, i ^ mask) for i in range(self.ring)])]
    ppermute x23, starting transfers between devices: 26.6 us -> 30.7 us  [second(): lax.ppermute(v, 'dp', [(i, i ^ (2 if i % 2 else 4)) for i in range(self.d...]
    unnamed x175 -> x173, local copies, waits for them, and re-layouts: 7.69 us -> 6.03 us
  transfers between devices with their start and end apart: 97 -> 97, of which waited for: 28 -> 31; matrix products, arithmetic and copies ran while one was open for 3% -> 3% of each run, Pallas kernels for 36% -> 32%
where the time goes in v6:
time: 344 us; the launch traced here: 338 us
  Pallas kernels  143 us (42%)
  waiting for transfers between devices  87.2 us (25%)
  starting transfers between devices  86.7 us (25%)
  local copies, waits for them, and re-layouts  11.8 us (3%)
  other arithmetic  6.4 us (2%)
    pallas_call x4, Pallas kernels, attend_back(): pl.pallas_call(partial(attend_back_kernel, words, gw, heads, final, count...  48.2 us
    pallas_call x4, Pallas kernels, attend(): pl.pallas_call(partial(attend_kernel, words, gw, heads, count), in_specs=...  37.4 us
    ppermute x23, starting transfers between devices, second(): lax.ppermute(v, 'dp', [(i, i ^ (2 if i % 2 else 4)) for i in range(self.d...  30.7 us
    ppermute x23, waiting for transfers between devices, second(): lax.ppermute(v, 'dp', [(i, i ^ (2 if i % 2 else 4)) for i in range(self.d...  30.2 us
    ppermute x12, waiting for transfers between devices, shift_z(): return lax.ppermute(v, 'tensor', [(i, (i + by) % n) for i in range(n)])  23.3 us
    ppermute x12, starting transfers between devices, shift_z(): return lax.ppermute(v, 'tensor', [(i, (i + by) % n) for i in range(n)])  23 us
    pallas_call x1, Pallas kernels, hidden(): pl.pallas_call(partial(hidden_kernel, n), in_specs=[SMEM] + [VMEM] * (6 +...  20 us
    pallas_call x3, Pallas kernels, hidden_back(): pl.pallas_call(partial(hidden_back_kernel, pair), in_specs=[SMEM] + [VMEM...  19.9 us
  transfers between devices with their start and end apart: 97, of which 31 were waited for; matrix products, arithmetic and copies ran while one was open for 3% of the time, Pallas kernels for 32%

profile of v6, /device:TPU:0, one launch (start us, length us, event | category | flops | bytes accessed | tf_op | source)
XLA Modules:
  0.0 337.8 jit_solution(3921852466499300148)
XLA Ops:
  2.8 2.4 pack.1
  5.3 5.1 %collective-permute-start.1 = (bf16[176,768]{1,0:T(8,128)(2,1)}, bf16[176,768]{1,0:T(8,128)(2,1)S(1)}, u32[]{:S(2)}, u32[]{:S(2)}) collective-permute-start(bf16[176,768]{1,0:T(8,128)(2,1)} %get-tuple-element.275), channel_id=1, source_target_pairs={{0,3},{1,0},{2,1},{3,2},{4,7},{5,4},{6,5},{7,6},{8,11},{9,8},{10,9... | collective-permute-start | bytes 811016 | tf_op jit(solution)/shard_map/ppermute | solution.py:723
  10.6 2.2 start_rows.1
  12.9 3.9 %collective-permute-start.5 = (bf16[192,768]{1,0:T(8,128)(2,1)S(1)}, bf16[192,768]{1,0:T(8,128)(2,1)S(1)}, u32[]{:S(2)}, u32[]{:S(2)}) collective-permute-start(bf16[192,768]{1,0:T(8,128)(2,1)S(1)} %copy-done.62), channel_id=1, source_target_pairs={{0,3},{1,0},{2,1},{3,2},{4,7},{5,4},{6,5},{7,6},{8,11},{9,8},{10,9... | collective-permute-start | bytes 884744 | tf_op jit(solution)/shard_map/ppermute | solution.py:723
  16.7 9.1 %attend_own.1 = (bf16[512,768]{1,0:T(8,128)(2,1)}, bf16[128,768]{1,0:T(8,128)(2,1)}, bf16[640,192]{1,0:T(8,128)(2,1)}, f32[8,640]{1,0:T(8,128)S(1)}, bf16[16,768...) custom-call(s32[4]{0:T(128)S(1)} %pad_add_fusion.info_ref, ...), custom_call_target="tpu_custom_call", output_to_operand_aliasing={{5}: (2, {})} | custom-call | flops 8000000000 | bytes 6000000 | tf_op jit(solution)/shard_map/attend_own/pallas_call | solution.py:284
  29.6 7.2 %collective-permute-done.4 = bf16[192,768]{1,0:T(8,128)(2,1)S(1)} collective-permute-done((bf16[192,768]{1,0:T(8,128)(2,1)S(1)}, bf16[192,768]{1,0:T(8,128)(2,1)S(1)}, u32[]{:S(2)}, u32[]{:S(2)}) %collective-permute-start.4) | collective-permute-done | bytes 294944 | tf_op jit(solution)/shard_map/ppermute | solution.py:723
  39.1 2.5 collective-permute-done.10.refs_0_.refs_3_
  41.6 2.4 collective-permute-done.6.refs_3_.refs_6_
  44.0 1.7 collective-permute-start.19
  48.7 5.9 %collective-permute-done.13.refs_2_.refs_5_ = bf16[176,768]{1,0:T(8,128)(2,1)S(1)} collective-permute-done((bf16[176,768]{1,0:T(8,128)(2,1)S(1)}, bf16[176,768]{1,0:T(8,128)(2,1)S(1)}, u32[]{:S(2)}, u32[]{:S(2)}) %collective-permute-start.13) | collective-permute-done | bytes 270368 | tf_op jit(solution)/shard_map/ppermute | solution.py:738
  60.3 9.4 %attend_far.3 = (bf16[512,768]{1,0:T(8,128)(2,1)}, bf16[128,768]{1,0:T(8,128)(2,1)}, bf16[640,192]{1,0:T(8,128)(2,1)}, f32[8,640]{1,0:T(8,128)S(1)}, bf16[16,768...) custom-call(s32[4]{0:T(128)S(1)} %pad_add_fusion.info_ref, ...), custom_call_target="tpu_custom_call", output_to_operand_aliasing={{5}: (2, {})} | custom-call | flops 8000000000 | bytes 6000000 | tf_op jit(solution)/shard_map/attend_far/pallas_call | solution.py:284
  77.9 9.4 %attend_far.4 = (bf16[512,768]{1,0:T(8,128)(2,1)}, bf16[128,768]{1,0:T(8,128)(2,1)}, bf16[640,192]{1,0:T(8,128)(2,1)}, f32[8,640]{1,0:T(8,128)S(1)}, bf16[16,768...) custom-call(s32[4]{0:T(128)S(1)} %pad_add_fusion.info_ref, ...), custom_call_target="tpu_custom_call", output_to_operand_aliasing={{5}: (2, {})} | custom-call | flops 8000000000 | bytes 6000000 | tf_op jit(solution)/shard_map/attend_far/pallas_call | solution.py:284
  87.4 2.1 collective-permute-done.26.refs_7_
  94.7 9.4 %attend_far.5 = (bf16[512,768]{1,0:T(8,128)(2,1)}, bf16[128,768]{1,0:T(8,128)(2,1)}, bf16[640,192]{1,0:T(8,128)(2,1)}, f32[8,640]{1,0:T(8,128)S(1)}, bf16[16,768...) custom-call(s32[4]{0:T(128)S(1)} %pad_add_fusion.info_ref, ...), custom_call_target="tpu_custom_call", output_to_operand_aliasing={{5}: (2, {})} | custom-call | flops 8000000000 | bytes 6000000 | tf_op jit(solution)/shard_map/attend_far/pallas_call | solution.py:284
  104.2 4.9 %collective-permute-done.32.refs_9_ = bf16[384,768]{1,0:T(8,128)(2,1)} collective-permute-done((bf16[384,768]{1,0:T(8,128)(2,1)}, bf16[384,768]{1,0:T(8,128)(2,1)}, u32[]{:S(2)}, u32[]{:S(2)}) %collective-permute-start.32) | collective-permute-done | bytes 589856 | tf_op jit(solution)/shard_map/ppermute | solution.py:738
  115.7 20.0 %hidden.1 = (bf16[768,640]{1,0:T(8,128)(2,1)S(1)}, bf16[4,768,640]{2,1,0:T(8,128)(2,1)S(1)}, f32[4,640,768]{2,1,0:T(8,128)S(1)}, bf16[4,768,768]{2,1,0:T(8,128)(...) custom-call(s32[4]{0:T(128)S(1)} %pad_add_fusion.info_ref, ...), custom_call_target="tpu_custom_call" | custom-call | flops 22000001024 | bytes 20000000 | tf_op jit(solution)/shard_map/hidden/pallas_call | solution.py:393
  135.7 9.6 %hidden_back.3 = (bf16[1536,768]{1,0:T(8,128)(2,1)}, bf16[768,768]{1,0:T(8,128)(2,1)}, bf16[768,768]{1,0:T(8,128)(2,1)}, f32[640,768]{1,0:T(8,128)S(1)}, f32[16,768]{1,0:T(8,128)S(1)}) custom-call(s32[4]{0:T(128)S(1)} %pad_add_fusion.info_ref, bf16[640,768]{1,0:T(8,128)(2,1)S(1)} %get-tuple-element.353.low_ref, ...), custom_call_target="tpu_custom_call", output_to_operand_aliasing={{3}: (7, {})} | custom-call | flops 14000000000 | bytes 16000000 | tf_op jit(solution)/shard_map/hidden_back/pallas_call | solution.py:454
  145.5 5.1 %hidden_back.4 = (bf16[768,768]{1,0:T(8,128)(2,1)}, bf16[384,768]{1,0:T(8,128)(2,1)}, bf16[384,768]{1,0:T(8,128)(2,1)}, f32[640,768]{1,0:T(8,128)S(1)}, f32[8,768]{1,0:T(8,128)S(1)}) custom-call(s32[4]{0:T(128)S(1)} %pad_add_fusion.info_ref, bf16[640,768]{1,0:T(8,128)(2,1)S(1)} %get-tuple-element.353.low_ref, ...), custom_call_target="tpu_custom_call", output_to_operand_aliasing={{3}: (7, {})} | custom-call | flops 7000000000 | bytes 8000000 | tf_op jit(solution)/shard_map/hidden_back/pallas_call | solution.py:454
  151.4 5.1 %hidden_back.5 = (bf16[768,768]{1,0:T(8,128)(2,1)}, bf16[384,768]{1,0:T(8,128)(2,1)}, bf16[384,768]{1,0:T(8,128)(2,1)}, f32[640,768]{1,0:T(8,128)S(1)}, f32[8,768]{1,0:T(8,128)S(1)}) custom-call(s32[4]{0:T(128)S(1)} %pad_add_fusion.info_ref, bf16[640,768]{1,0:T(8,128)(2,1)S(1)} %get-tuple-element.353.low_ref, ...), custom_call_target="tpu_custom_call", output_to_operand_aliasing={{3}: (7, {})} | custom-call | flops 7000000000 | bytes 8000000 | tf_op jit(solution)/shard_map/hidden_back/pallas_call | solution.py:454
  156.8 1.7 collective-permute-start.45
  163.4 11.7 %attend_back.4 = (bf16[704,768]{1,0:T(8,128)(2,1)}, bf16[352,768]{1,0:T(8,128)(2,1)}, bf16[352,768]{1,0:T(8,128)(2,1)}, f32[640,768]{1,0:T(8,128)S(1)}) custom-call(s32[4]{0:T(128)S(1)} %pad_add_fusion.info_ref, bf16[640,768]{1,0:T(8,128)(2,1)S(1)} %get-tuple-element.270.rows_ref, f32[8,640]{1,0:T(8,128)S(1)} %copy-done.9, ...), custom_call_target="tpu_custom_call", output_to_operand_aliasing={{3}: (5, {})} | custom-call | flops 11000000512 | bytes 8000000 | tf_op jit(solution)/shard_map/attend_back/pallas_call | solution.py:597
  176.5 9.6 %collective-permute-done.48 = f32[8,768]{1,0:T(8,128)S(1)} collective-permute-done((f32[8,768]{1,0:T(8,128)S(1)}, f32[8,768]{1,0:T(8,128)S(1)}, u32[]{:S(2)}, u32[]{:S(2)}) %collective-permute-start.48) | collective-permute-done | bytes 24608 | tf_op jit(solution)/shard_map/ppermute | solution.py:729
  188.6 1.7 collective-permute-start.53
  191.9 11.5 %attend_back.5 = (bf16[704,768]{1,0:T(8,128)(2,1)}, bf16[352,768]{1,0:T(8,128)(2,1)}, bf16[352,768]{1,0:T(8,128)(2,1)}, f32[640,768]{1,0:T(8,128)S(1)}) custom-call(s32[4]{0:T(128)S(1)} %pad_add_fusion.info_ref, bf16[640,768]{1,0:T(8,128)(2,1)S(1)} %get-tuple-element.270.rows_ref, f32[8,640]{1,0:T(8,128)S(1)} %copy-done.7, ...), custom_call_target="tpu_custom_call", output_to_operand_aliasing={{3}: (5, {})} | custom-call | flops 11000000512 | bytes 8000000 | tf_op jit(solution)/shard_map/attend_back/pallas_call | solution.py:597
  205.6 1.8 collective-permute-done.54
  207.9 2.9 collective-permute-done.51
  210.8 3.3 collective-permute-done.52
  217.8 1.9 collective-permute-start.57
  220.3 11.3 %attend_back.6 = (bf16[704,768]{1,0:T(8,128)(2,1)}, bf16[352,768]{1,0:T(8,128)(2,1)}, bf16[352,768]{1,0:T(8,128)(2,1)}, f32[640,768]{1,0:T(8,128)S(1)}) custom-call(s32[4]{0:T(128)S(1)} %pad_add_fusion.info_ref, bf16[640,768]{1,0:T(8,128)(2,1)S(1)} %get-tuple-element.270.rows_ref, ...), custom_call_target="tpu_custom_call", output_to_operand_aliasing={{3}: (5, {})} | custom-call | flops 11000000512 | bytes 8000000 | tf_op jit(solution)/shard_map/attend_back/pallas_call | solution.py:597
  231.7 2.3 collective-permute-done.56
  234.0 3.5 %collective-permute-done.58 = bf16[192,768]{1,0:T(8,128)(2,1)S(1)} collective-permute-done((bf16[192,768]{1,0:T(8,128)(2,1)S(1)}, bf16[192,768]{1,0:T(8,128)(2,1)S(1)}, u32[]{:S(2)}, u32[]{:S(2)}) %collective-permute-start.58) | collective-permute-done | bytes 294944 | tf_op jit(solution)/shard_map/ppermute | solution.py:723
  241.2 7.3 %collective-permute-start.62 = (bf16[176,768]{1,0:T(8,128)(2,1)S(1)}, bf16[176,768]{1,0:T(8,128)(2,1)S(1)}, u32[]{:S(2)}, u32[]{:S(2)}) collective-permute-start(bf16[176,768]{1,0:T(8,128)(2,1)S(1)} %add_convert_fusion.20), channel_id=1, source_target_pairs={{0,2},{1,3},{2,0},{3,1},{4,6},{5,7},{6,4},{7,5},{8,10},{9,11},{10,... | collective-permute-start | bytes 811016 | tf_op jit(solution)/shard_map/ppermute | solution.py:723
  249.5 13.6 %attend_back.7 = (bf16[960,768]{1,0:T(8,128)(2,1)}, bf16[480,768]{1,0:T(8,128)(2,1)}, bf16[480,768]{1,0:T(8,128)(2,1)}, f32[512,768]{1,0:T(8,128)}, f32[128,768]{1,0:T(8,128)}) custom-call(s32[4]{0:T(128)S(1)} %pad_add_fusion.info_ref, bf16[640,768]{1,0:T(8,128)(2,1)S(1)} %get-tuple-element.270.rows_ref, f32[8,640]{1,0:T(8,128)S(1)} %copy-done.11, ...), custom_call_target="tpu_custom_call" | custom-call | flops 11000000512 | bytes 8000000 | tf_op jit(solution)/shard_map/attend_back/pallas_call | solution.py:597
  264.7 1.9 collective-permute-done.67
  268.0 1.7 collective-permute-start.68
  271.5 1.9 collective-permute-start.70
  273.4 6.0 %collective-permute-done.69 = bf16[176,768]{1,0:T(8,128)(2,1)S(1)} collective-permute-done((bf16[176,768]{1,0:T(8,128)(2,1)S(1)}, bf16[176,768]{1,0:T(8,128)(2,1)S(1)}, u32[]{:S(2)}, u32[]{:S(2)}) %collective-permute-start.69) | collective-permute-done | bytes 270368 | tf_op jit(solution)/shard_map/ppermute | solution.py:738
  279.5 2.9 collective-permute-done.68
  284.9 7.1 %collective-permute-done.73 = bf16[176,768]{1,0:T(8,128)(2,1)S(1)} collective-permute-done((bf16[176,768]{1,0:T(8,128)(2,1)S(1)}, bf16[176,768]{1,0:T(8,128)(2,1)S(1)}, u32[]{:S(2)}, u32[]{:S(2)}) %collective-permute-start.73) | collective-permute-done | bytes 270368 | tf_op jit(solution)/shard_map/ppermute | solution.py:723
  297.8 3.9 %collective-permute-start.78 = (bf16[64,768]{1,0:T(8,128)(2,1)S(1)}, bf16[64,768]{1,0:T(8,128)(2,1)S(1)}, u32[]{:S(2)}, u32[]{:S(2)}) collective-permute-start(bf16[64,768]{1,0:T(8,128)(2,1)S(1)} %add_convert_fusion.23), channel_id=1, source_target_pairs={{0,1},{1,0},{2,3},{3,2},{4,5},{5,4},{6,7},{7,6},{8,9},{9,8},{10,11... | collective-permute-start | bytes 294920 | tf_op jit(solution)/shard_map/ppermute | solution.py:726
  301.7 4.6 %spread_hidden.1 = (f32[768,768]{1,0:T(8,128)}, f32[768,768]{1,0:T(8,128)}) custom-call(s32[4]{0:T(128)S(1)} %pad_add_fusion.info_ref, bf16[192,768]{1,0:T(8,128)(2,1)} %copy-done.12, bf16[192,768]{1,0:T(8,128)(2,1)} %copy-done.29, bf16[192,768]{1,0:T(8,128)(2,1)} %copy-done.28, bf16[192,768]{1,0:T(8,128)(2,1)} %copy-done.30, bf16[192,768]{1,0:T(8,128)(2,1)} %copy-done.31, ...), custom_call_target="tpu_custom_call" | custom-call | flops 500000000 | bytes 7000000 | tf_op jit(solution)/shard_map/spread_hidden/pallas_call | solution.py:678
  308.4 2.9 collective-permute-done.86
  312.8 3.1 collective-permute-done.84.refs_2_
  316.3 4.2 %collective-permute-done.83.refs_1_ = bf16[64,768]{1,0:T(8,128)(2,1)S(1)} collective-permute-done((bf16[64,768]{1,0:T(8,128)(2,1)S(1)}, bf16[64,768]{1,0:T(8,128)(2,1)S(1)}, u32[]{:S(2)}, u32[]{:S(2)}) %collective-permute-start.83) | collective-permute-done | bytes 98336 | tf_op jit(solution)/shard_map/ppermute | solution.py:735
  322.8 2.7 collective-permute-done.96
  325.6 1.9 collective-permute-start.91
  328.3 4.1 %spread_query.1 = (f32[4,192,768]{2,1,0:T(8,128)}, f32[192,768]{1,0:T(8,128)}, f32[192,768]{1,0:T(8,128)}, f32[192,768]{1,0:T(8,128)}, f32[4,192]{1,0:T(4,128)}, /*index=5*/f32[1,192]{1,0:T(1,128)}, f32[1,768]{1,0:T(1,128)S(1)}) custom-call(s32[4]{0:T(128)S(1)} %pad_add_fusion.info_ref, bf16[176,768]{1,0:T(8,128)(2,1)} %copy-done.15, ...), custom_call_target="tpu_custom_call" | custom-call | flops 500000000 | bytes 7000000 | tf_op jit(solution)/shard_map/spread_query/pallas_call | solution.py:652
  334.5 3.0 spread_pos.1
  (378 shorter events, 81.6 us)
Async XLA Ops:
  5.3 20.6 %collective-permute-start.1 = (bf16[176,768]{1,0:T(8,128)(2,1)}, bf16[176,768]{1,0:T(8,128)(2,1)S(1)}, u32[]{:S(2)}, u32[]{:S(2)}) collective-permute-start(bf16[176,768]{1,0:T(8,128)(2,1)} %get-tuple-element.275), channel_id=1, source_target_pairs={{0,3},{1,0},{2,1},{3,2},{4,7},{5,4},{6,5},{7,6},{8,11},{9,8},{10,9... | collective-permute-start | bytes 811016 | tf_op jit(solution)/shard_map/ppermute | solution.py:723
  10.4 15.5 %collective-permute-start = (bf16[176,768]{1,0:T(8,128)(2,1)}, bf16[176,768]{1,0:T(8,128)(2,1)}, u32[]{:S(2)}, u32[]{:S(2)}) collective-permute-start(bf16[176,768]{1,0:T(8,128)(2,1)} %get-tuple-element.275), channel_id=1, source_target_pairs={{0,1},{1,2},{2,3},{3,0},{4,5},{5,6},{6,7},{7,4},{8,9},{9,10},{10,1... | collective-permute-start | bytes 811016 | tf_op jit(solution)/shard_map/ppermute | solution.py:723
  12.9 16.8 %collective-permute-start.5 = (bf16[192,768]{1,0:T(8,128)(2,1)S(1)}, bf16[192,768]{1,0:T(8,128)(2,1)S(1)}, u32[]{:S(2)}, u32[]{:S(2)}) collective-permute-start(bf16[192,768]{1,0:T(8,128)(2,1)S(1)} %copy-done.62), channel_id=1, source_target_pairs={{0,3},{1,0},{2,1},{3,2},{4,7},{5,4},{6,5},{7,6},{8,11},{9,8},{10,9... | collective-permute-start | bytes 884744 | tf_op jit(solution)/shard_map/ppermute | solution.py:723
  16.7 20.1 %collective-permute-start.4 = (bf16[192,768]{1,0:T(8,128)(2,1)S(1)}, bf16[192,768]{1,0:T(8,128)(2,1)S(1)}, u32[]{:S(2)}, u32[]{:S(2)}) collective-permute-start(bf16[192,768]{1,0:T(8,128)(2,1)S(1)} %copy-done.62), channel_id=1, source_target_pairs={{0,1},{1,2},{2,3},{3,0},{4,5},{5,6},{6,7},{7,4},{8,9},{9,10},{10,1... | collective-permute-start | bytes 884744 | tf_op jit(solution)/shard_map/ppermute | solution.py:723
  25.9 11.0 %collective-permute-start.3 = (bf16[176,768]{1,0:T(8,128)(2,1)}, bf16[176,768]{1,0:T(8,128)(2,1)S(1)}, u32[]{:S(2)}, u32[]{:S(2)}) collective-permute-start(bf16[176,768]{1,0:T(8,128)(2,1)} %collective-permute-done.refs_0_.refs_3_), channel_id=1, source_target_pairs={{0,16},{4,12},{8,24},{12,4},{16,0},{20,28},{24,8},{28,20},{1,17},{... | collective-permute-start | bytes 811016 | tf_op jit(solution)/shard_map/ppermute | solution.py:738
  29.0 12.5 %collective-permute-start.10 = (bf16[176,768]{1,0:T(8,128)(2,1)}, bf16[176,768]{1,0:T(8,128)(2,1)S(1)}, u32[]{:S(2)}, u32[]{:S(2)}) collective-permute-start(bf16[176,768]{1,0:T(8,128)(2,1)} %collective-permute-done.refs_0_.refs_3_), channel_id=1, source_target_pairs={{0,1},{1,2},{2,3},{3,0},{4,5},{5,6},{6,7},{7,4},{8,9},{9,10},{10,1... | collective-permute-start | bytes 811016 | tf_op jit(solution)/shard_map/ppermute | solution.py:723
  44.0 14.8 %collective-permute-start.19 = (bf16[192,768]{1,0:T(8,128)(2,1)S(1)}, bf16[192,768]{1,0:T(8,128)(2,1)S(1)}, u32[]{:S(2)}, u32[]{:S(2)}) collective-permute-start(bf16[192,768]{1,0:T(8,128)(2,1)S(1)} %collective-permute-done.4), channel_id=1, source_target_pairs={{0,1},{1,2},{2,3},{3,0},{4,5},{5,6},{6,7},{7,4},{8,9},{9,10},{10,1... | collective-permute-start | bytes 884744 | tf_op jit(solution)/shard_map/ppermute | solution.py:723
  54.6 15.1 %collective-permute-start.16 = (bf16[176,768]{1,0:T(8,128)(2,1)S(1)}, bf16[176,768]{1,0:T(8,128)(2,1)S(1)}, u32[]{:S(2)}, u32[]{:S(2)}) collective-permute-start(bf16[176,768]{1,0:T(8,128)(2,1)S(1)} %collective-permute-done.10.refs_0_.refs_3_), channel_id=1, source_target_pairs={{0,16},{4,12},{8,24},{12,4},{16,0},{20,28},{24,8},{28,20},{1,17},{... | collective-permute-start | bytes 811016 | tf_op jit(solution)/shard_map/ppermute | solution.py:738
  56.2 13.6 %collective-permute-start.15 = (bf16[176,768]{1,0:T(8,128)(2,1)S(1)}, bf16[176,768]{1,0:T(8,128)(2,1)S(1)}, u32[]{:S(2)}, u32[]{:S(2)}) collective-permute-start(bf16[176,768]{1,0:T(8,128)(2,1)S(1)} %collective-permute-done.10.refs_0_.refs_3_), channel_id=1, source_target_pairs={{0,8},{4,20},{8,0},{12,28},{16,24},{20,4},{24,16},{28,12},{1,9},{5... | collective-permute-start | bytes 811016 | tf_op jit(solution)/shard_map/ppermute | solution.py:735
  56.8 15.3 %collective-permute-start.18 = (bf16[192,768]{1,0:T(8,128)(2,1)S(1)}, bf16[192,768]{1,0:T(8,128)(2,1)S(1)}, u32[]{:S(2)}, u32[]{:S(2)}) collective-permute-start(bf16[192,768]{1,0:T(8,128)(2,1)S(1)} %collective-permute-done.5.refs_14_), channel_id=1, source_target_pairs={{0,16},{4,12},{8,24},{12,4},{16,0},{20,28},{24,8},{28,20},{1,17},{... | collective-permute-start | bytes 884744 | tf_op jit(solution)/shard_map/ppermute | solution.py:738
  57.3 14.8 %collective-permute-start.17 = (bf16[192,768]{1,0:T(8,128)(2,1)S(1)}, bf16[192,768]{1,0:T(8,128)(2,1)S(1)}, u32[]{:S(2)}, u32[]{:S(2)}) collective-permute-start(bf16[192,768]{1,0:T(8,128)(2,1)S(1)} %collective-permute-done.5.refs_14_), channel_id=1, source_target_pairs={{0,8},{4,20},{8,0},{12,28},{16,24},{20,4},{24,16},{28,12},{1,9},{5... | collective-permute-start | bytes 884744 | tf_op jit(solution)/shard_map/ppermute | solution.py:735
  58.8 13.3 %collective-permute-start.14 = (bf16[176,768]{1,0:T(8,128)(2,1)S(1)}, bf16[176,768]{1,0:T(8,128)(2,1)S(1)}, u32[]{:S(2)}, u32[]{:S(2)}) collective-permute-start(bf16[176,768]{1,0:T(8,128)(2,1)S(1)} %collective-permute-done.12.refs_1_.refs_4_), channel_id=1, source_target_pairs={{0,16},{4,12},{8,24},{12,4},{16,0},{20,28},{24,8},{28,20},{1,17},{... | collective-permute-start | bytes 811016 | tf_op jit(solution)/shard_map/ppermute | solution.py:738
  74.0 13.4 %collective-permute-start.28 = (bf16[176,768]{1,0:T(8,128)(2,1)S(1)}, bf16[176,768]{1,0:T(8,128)(2,1)S(1)}, u32[]{:S(2)}, u32[]{:S(2)}) collective-permute-start(bf16[176,768]{1,0:T(8,128)(2,1)S(1)} %collective-permute-done.15.refs_1_.refs_4_), channel_id=1, source_target_pairs={{0,4},{4,0},{8,12},{12,8},{16,20},{20,16},{24,28},{28,24},{1,5},{5... | collective-permute-start | bytes 811016 | tf_op jit(solution)/shard_map/ppermute | solution.py:729
  74.2 13.2 %collective-permute-start.24 = (bf16[176,768]{1,0:T(8,128)(2,1)S(1)}, bf16[176,768]{1,0:T(8,128)(2,1)S(1)}, u32[]{:S(2)}, u32[]{:S(2)}) collective-permute-start(bf16[176,768]{1,0:T(8,128)(2,1)S(1)} %collective-permute-done.15.refs_1_.refs_4_), channel_id=1, source_target_pairs={{0,16},{4,12},{8,24},{12,4},{16,0},{20,28},{24,8},{28,20},{1,17},{... | collective-permute-start | bytes 811016 | tf_op jit(solution)/shard_map/ppermute | solution.py:738
  75.7 11.7 %collective-permute-start.27 = (bf16[176,768]{1,0:T(8,128)(2,1)S(1)}, bf16[176,768]{1,0:T(8,128)(2,1)S(1)}, u32[]{:S(2)}, u32[]{:S(2)}) collective-permute-start(bf16[176,768]{1,0:T(8,128)(2,1)S(1)} %collective-permute-done.10.refs_0_.refs_3_), channel_id=1, source_target_pairs={{0,4},{4,0},{8,12},{12,8},{16,20},{20,16},{24,28},{28,24},{1,5},{5... | collective-permute-start | bytes 811016 | tf_op jit(solution)/shard_map/ppermute | solution.py:729
  75.9 11.6 %collective-permute-start.25 = (bf16[192,768]{1,0:T(8,128)(2,1)S(1)}, bf16[192,768]{1,0:T(8,128)(2,1)}, u32[]{:S(2)}, u32[]{:S(2)}) collective-permute-start(bf16[192,768]{1,0:T(8,128)(2,1)S(1)} %collective-permute-done.17.refs_15_), channel_id=1, source_target_pairs={{0,16},{4,12},{8,24},{12,4},{16,0},{20,28},{24,8},{28,20},{1,17},{... | collective-permute-start | bytes 884744 | tf_op jit(solution)/shard_map/ppermute | solution.py:738
  77.4 12.2 %collective-permute-start.26 = (bf16[384,768]{1,0:T(8,128)(2,1)}, bf16[384,768]{1,0:T(8,128)(2,1)}, u32[]{:S(2)}, u32[]{:S(2)}) collective-permute-start(bf16[384,768]{1,0:T(8,128)(2,1)} %pad_maximum_fusion.refs_6_), channel_id=1, source_target_pairs={{0,8},{4,20},{8,0},{12,28},{16,24},{20,4},{24,16},{28,12},{1,9},{5... | collective-permute-start | bytes 1769480 | tf_op jit(solution)/shard_map/ppermute | solution.py:735
  91.8 12.4 %collective-permute-start.33 = (bf16[192,768]{1,0:T(8,128)(2,1)S(1)}, bf16[192,768]{1,0:T(8,128)(2,1)S(1)}, u32[]{:S(2)}, u32[]{:S(2)}) collective-permute-start(bf16[192,768]{1,0:T(8,128)(2,1)S(1)} %collective-permute-done.5.refs_14_), channel_id=1, source_target_pairs={{0,4},{4,0},{8,12},{12,8},{16,20},{20,16},{24,28},{28,24},{1,5},{5... | collective-permute-start | bytes 884744 | tf_op jit(solution)/shard_map/ppermute | solution.py:729
  92.1 12.0 %collective-permute-start.34 = (bf16[192,768]{1,0:T(8,128)(2,1)S(1)}, bf16[192,768]{1,0:T(8,128)(2,1)S(1)}, u32[]{:S(2)}, u32[]{:S(2)}) collective-permute-start(bf16[192,768]{1,0:T(8,128)(2,1)S(1)} %collective-permute-done.17.refs_15_), channel_id=1, source_target_pairs={{0,4},{4,0},{8,12},{12,8},{16,20},{20,16},{24,28},{28,24},{1,5},{5... | collective-permute-start | bytes 884744 | tf_op jit(solution)/shard_map/ppermute | solution.py:729
  92.3 11.9 %collective-permute-start.35 = (bf16[192,768]{1,0:T(8,128)(2,1)S(1)}, bf16[192,768]{1,0:T(8,128)(2,1)S(1)}, u32[]{:S(2)}, u32[]{:S(2)}) collective-permute-start(bf16[192,768]{1,0:T(8,128)(2,1)S(1)} %collective-permute-done.18.refs_16_), channel_id=1, source_target_pairs={{0,4},{4,0},{8,12},{12,8},{16,20},{20,16},{24,28},{28,24},{1,5},{5... | collective-permute-start | bytes 884744 | tf_op jit(solution)/shard_map/ppermute | solution.py:729
  92.6 11.6 %collective-permute-start.31 = (bf16[384,768]{1,0:T(8,128)(2,1)}, bf16[384,768]{1,0:T(8,128)(2,1)}, u32[]{:S(2)}, u32[]{:S(2)}) collective-permute-start(bf16[384,768]{1,0:T(8,128)(2,1)} %pad_maximum_fusion.refs_6_), channel_id=1, source_target_pairs={{0,16},{4,12},{8,24},{12,4},{16,0},{20,28},{24,8},{28,20},{1,17},{... | collective-permute-start | bytes 1769480 | tf_op jit(solution)/shard_map/ppermute | solution.py:738
  94.2 15.0 %collective-permute-start.32 = (bf16[384,768]{1,0:T(8,128)(2,1)}, bf16[384,768]{1,0:T(8,128)(2,1)}, u32[]{:S(2)}, u32[]{:S(2)}) collective-permute-start(bf16[384,768]{1,0:T(8,128)(2,1)} %collective-permute-done.26.refs_7_), channel_id=1, source_target_pairs={{0,16},{4,12},{8,24},{12,4},{16,0},{20,28},{24,8},{28,20},{1,17},{... | collective-permute-start | bytes 1769480 | tf_op jit(solution)/shard_map/ppermute | solution.py:738
  156.8 19.8 %collective-permute-start.45 = (bf16[768,768]{1,0:T(8,128)(2,1)S(1)}, bf16[768,768]{1,0:T(8,128)(2,1)S(1)}, u32[]{:S(2)}, u32[]{:S(2)}) collective-permute-start(bf16[768,768]{1,0:T(8,128)(2,1)S(1)} %add_convert_fusion), channel_id=1, source_target_pairs={{0,8},{4,20},{8,0},{12,28},{16,24},{20,4},{24,16},{28,12},{1,9},{5... | collective-permute-start | bytes 3538952 | tf_op jit(solution)/shard_map/ppermute | solution.py:735
  161.3 24.8 %collective-permute-start.47 = (bf16[384,768]{1,0:T(8,128)(2,1)S(1)}, bf16[384,768]{1,0:T(8,128)(2,1)S(1)}, u32[]{:S(2)}, u32[]{:S(2)}) collective-permute-start(bf16[384,768]{1,0:T(8,128)(2,1)S(1)} %add_convert_fusion.3), channel_id=1, source_target_pairs={{0,8},{4,20},{8,0},{12,28},{16,24},{20,4},{24,16},{28,12},{1,9},{5... | collective-permute-start | bytes 1769480 | tf_op jit(solution)/shard_map/ppermute | solution.py:735
  162.6 23.5 %collective-permute-start.46 = (bf16[384,768]{1,0:T(8,128)(2,1)S(1)}, bf16[384,768]{1,0:T(8,128)(2,1)S(1)}, u32[]{:S(2)}, u32[]{:S(2)}) collective-permute-start(bf16[384,768]{1,0:T(8,128)(2,1)S(1)} %add_convert_fusion.4), channel_id=1, source_target_pairs={{0,8},{4,20},{8,0},{12,28},{16,24},{20,4},{24,16},{28,12},{1,9},{5... | collective-permute-start | bytes 1769480 | tf_op jit(solution)/shard_map/ppermute | solution.py:735
  175.1 12.5 %collective-permute-start.49 = (bf16[704,768]{1,0:T(8,128)(2,1)}, bf16[704,768]{1,0:T(8,128)(2,1)S(1)}, u32[]{:S(2)}, u32[]{:S(2)}) collective-permute-start(bf16[704,768]{1,0:T(8,128)(2,1)} %get-tuple-element.405), channel_id=1, source_target_pairs={{0,4},{4,0},{8,12},{12,8},{16,20},{20,16},{24,28},{28,24},{1,5},{5... | collective-permute-start | bytes 3244040 | tf_op jit(solution)/shard_map/ppermute | solution.py:729
  175.2 10.9 %collective-permute-start.48 = (f32[8,768]{1,0:T(8,128)S(1)}, f32[8,768]{1,0:T(8,128)S(1)}, u32[]{:S(2)}, u32[]{:S(2)}) collective-permute-start(f32[8,768]{1,0:T(8,128)S(1)} %add.212), channel_id=1, source_target_pairs={{0,8},{4,12},{8,0},{12,4},{16,24},{20,28},{24,16},{28,20},{1,9},{5... | collective-permute-start | bytes 73736 | tf_op jit(solution)/shard_map/ppermute | solution.py:729
  188.6 25.5 %collective-permute-start.53 = (bf16[352,768]{1,0:T(8,128)(2,1)S(1)}, bf16[352,768]{1,0:T(8,128)(2,1)S(1)}, u32[]{:S(2)}, u32[]{:S(2)}) collective-permute-start(bf16[352,768]{1,0:T(8,128)(2,1)S(1)} %add_convert_fusion.7), channel_id=1, source_target_pairs={{0,8},{4,20},{8,0},{12,28},{16,24},{20,4},{24,16},{28,12},{1,9},{5... | collective-permute-start | bytes 1622024 | tf_op jit(solution)/shard_map/ppermute | solution.py:735
  190.4 23.8 %collective-permute-start.50 = (bf16[384,768]{1,0:T(8,128)(2,1)S(1)}, bf16[384,768]{1,0:T(8,128)(2,1)S(1)}, u32[]{:S(2)}, u32[]{:S(2)}) collective-permute-start(bf16[384,768]{1,0:T(8,128)(2,1)S(1)} %add_convert_fusion.2), channel_id=1, source_target_pairs={{0,16},{4,12},{8,24},{12,4},{16,0},{20,28},{24,8},{28,20},{1,17},{... | collective-permute-start | bytes 1769480 | tf_op jit(solution)/shard_map/ppermute | solution.py:738
  203.4 11.3 %collective-permute-start.55 = (bf16[704,768]{1,0:T(8,128)(2,1)}, bf16[704,768]{1,0:T(8,128)(2,1)S(1)}, u32[]{:S(2)}, u32[]{:S(2)}) collective-permute-start(bf16[704,768]{1,0:T(8,128)(2,1)} %get-tuple-element.424), channel_id=1, source_target_pairs={{0,4},{4,0},{8,12},{12,8},{16,20},{20,16},{24,28},{28,24},{1,5},{5... | collective-permute-start | bytes 3244040 | tf_op jit(solution)/shard_map/ppermute | solution.py:729
  215.5 16.1 %collective-permute-start.59 = (bf16[176,768]{1,0:T(8,128)(2,1)S(1)}, bf16[176,768]{1,0:T(8,128)(2,1)S(1)}, u32[]{:S(2)}, u32[]{:S(2)}) collective-permute-start(bf16[176,768]{1,0:T(8,128)(2,1)S(1)} %add_convert_fusion.21), channel_id=1, source_target_pairs={{0,16},{4,12},{8,24},{12,4},{16,0},{20,28},{24,8},{28,20},{1,17},{... | collective-permute-start | bytes 811016 | tf_op jit(solution)/shard_map/ppermute | solution.py:738
  216.9 17.1 %collective-permute-start.56 = (bf16[192,768]{1,0:T(8,128)(2,1)S(1)}, bf16[192,768]{1,0:T(8,128)(2,1)S(1)}, u32[]{:S(2)}, u32[]{:S(2)}) collective-permute-start(bf16[192,768]{1,0:T(8,128)(2,1)S(1)} %get-tuple-element.434), channel_id=1, source_target_pairs={{0,2},{1,3},{2,0},{3,1},{4,6},{5,7},{6,4},{7,5},{8,10},{9,11},{10,... | collective-permute-start | bytes 884744 | tf_op jit(solution)/shard_map/ppermute | solution.py:723
  217.8 16.1 %collective-permute-start.57 = (bf16[192,768]{1,0:T(8,128)(2,1)S(1)}, bf16[192,768]{1,0:T(8,128)(2,1)S(1)}, u32[]{:S(2)}, u32[]{:S(2)}) collective-permute-start(bf16[192,768]{1,0:T(8,128)(2,1)S(1)} %get-tuple-element.435), channel_id=1, source_target_pairs={{0,3},{1,0},{2,1},{3,2},{4,7},{5,4},{6,5},{7,6},{8,11},{9,8},{10,9... | collective-permute-start | bytes 884744 | tf_op jit(solution)/shard_map/ppermute | solution.py:723
  219.7 17.7 %collective-permute-start.58 = (bf16[192,768]{1,0:T(8,128)(2,1)S(1)}, bf16[192,768]{1,0:T(8,128)(2,1)S(1)}, u32[]{:S(2)}, u32[]{:S(2)}) collective-permute-start(bf16[192,768]{1,0:T(8,128)(2,1)S(1)} %get-tuple-element.436), channel_id=1, source_target_pairs={{0,1},{1,2},{2,3},{3,0},{4,5},{5,6},{6,7},{7,4},{8,9},{9,10},{10,1... | collective-permute-start | bytes 884744 | tf_op jit(solution)/shard_map/ppermute | solution.py:723
  219.9 17.6 %collective-permute-start.60 = (bf16[352,768]{1,0:T(8,128)(2,1)S(1)}, bf16[352,768]{1,0:T(8,128)(2,1)S(1)}, u32[]{:S(2)}, u32[]{:S(2)}) collective-permute-start(bf16[352,768]{1,0:T(8,128)(2,1)S(1)} %add_convert_fusion.6), channel_id=1, source_target_pairs={{0,8},{4,20},{8,0},{12,28},{16,24},{20,4},{24,16},{28,12},{1,9},{5... | collective-permute-start | bytes 1622024 | tf_op jit(solution)/shard_map/ppermute | solution.py:735
  238.0 25.0 %collective-permute-start.64 = (bf16[192,768]{1,0:T(8,128)(2,1)S(1)}, bf16[192,768]{1,0:T(8,128)(2,1)S(1)}, u32[]{:S(2)}, u32[]{:S(2)}) collective-permute-start(bf16[192,768]{1,0:T(8,128)(2,1)S(1)} %add_convert_fusion.9.refs_0_), channel_id=1, source_target_pairs={{0,16},{4,12},{8,24},{12,4},{16,0},{20,28},{24,8},{28,20},{1,17},{... | collective-permute-start | bytes 884744 | tf_op jit(solution)/shard_map/ppermute | solution.py:738
  239.6 23.5 %collective-permute-start.63 = (bf16[192,768]{1,0:T(8,128)(2,1)S(1)}, bf16[192,768]{1,0:T(8,128)(2,1)S(1)}, u32[]{:S(2)}, u32[]{:S(2)}) collective-permute-start(bf16[192,768]{1,0:T(8,128)(2,1)S(1)} %add_convert_fusion.9.refs_0_), channel_id=1, source_target_pairs={{0,8},{4,20},{8,0},{12,28},{16,24},{20,4},{24,16},{28,12},{1,9},{5... | collective-permute-start | bytes 884744 | tf_op jit(solution)/shard_map/ppermute | solution.py:735
  241.2 21.8 %collective-permute-start.62 = (bf16[176,768]{1,0:T(8,128)(2,1)S(1)}, bf16[176,768]{1,0:T(8,128)(2,1)S(1)}, u32[]{:S(2)}, u32[]{:S(2)}) collective-permute-start(bf16[176,768]{1,0:T(8,128)(2,1)S(1)} %add_convert_fusion.20), channel_id=1, source_target_pairs={{0,2},{1,3},{2,0},{3,1},{4,6},{5,7},{6,4},{7,5},{8,10},{9,11},{10,... | collective-permute-start | bytes 811016 | tf_op jit(solution)/shard_map/ppermute | solution.py:723
  248.6 14.5 %collective-permute-start.65 = (bf16[176,768]{1,0:T(8,128)(2,1)S(1)}, bf16[176,768]{1,0:T(8,128)(2,1)S(1)}, u32[]{:S(2)}, u32[]{:S(2)}) collective-permute-start(bf16[176,768]{1,0:T(8,128)(2,1)S(1)} %add_convert_fusion.19), channel_id=1, source_target_pairs={{0,16},{4,12},{8,24},{12,4},{16,0},{20,28},{24,8},{28,20},{1,17},{... | collective-permute-start | bytes 811016 | tf_op jit(solution)/shard_map/ppermute | solution.py:738
  249.1 14.0 %collective-permute-start.66 = (bf16[352,768]{1,0:T(8,128)(2,1)S(1)}, bf16[352,768]{1,0:T(8,128)(2,1)S(1)}, u32[]{:S(2)}, u32[]{:S(2)}) collective-permute-start(bf16[352,768]{1,0:T(8,128)(2,1)S(1)} %add_convert_fusion.5), channel_id=1, source_target_pairs={{0,8},{4,20},{8,0},{12,28},{16,24},{20,4},{24,16},{28,12},{1,9},{5... | collective-permute-start | bytes 1622024 | tf_op jit(solution)/shard_map/ppermute | solution.py:735
  263.2 16.3 %collective-permute-start.71 = (bf16[192,768]{1,0:T(8,128)(2,1)S(1)}, bf16[192,768]{1,0:T(8,128)(2,1)S(1)}, u32[]{:S(2)}, u32[]{:S(2)}) collective-permute-start(bf16[192,768]{1,0:T(8,128)(2,1)S(1)} %collective-permute-done.63.refs_1_), channel_id=1, source_target_pairs={{0,16},{4,12},{8,24},{12,4},{16,0},{20,28},{24,8},{28,20},{1,17},{... | collective-permute-start | bytes 884744 | tf_op jit(solution)/shard_map/ppermute | solution.py:738
  268.0 14.4 %collective-permute-start.68 = (bf16[480,768]{1,0:T(8,128)(2,1)S(1)}, bf16[480,768]{1,0:T(8,128)(2,1)S(1)}, u32[]{:S(2)}, u32[]{:S(2)}) collective-permute-start(bf16[480,768]{1,0:T(8,128)(2,1)S(1)} %add_convert_fusion.1), channel_id=1, source_target_pairs={{0,8},{4,20},{8,0},{12,28},{16,24},{20,4},{24,16},{28,12},{1,9},{5... | collective-permute-start | bytes 2211848 | tf_op jit(solution)/shard_map/ppermute | solution.py:735
  293.9 12.9 %collective-permute-start.82 = (bf16[176,768]{1,0:T(8,128)(2,1)S(1)}, bf16[176,768]{1,0:T(8,128)(2,1)S(1)}, u32[]{:S(2)}, u32[]{:S(2)}) collective-permute-start(bf16[176,768]{1,0:T(8,128)(2,1)S(1)} %add_convert_fusion.15.refs_0_), channel_id=1, source_target_pairs={{0,16},{4,12},{8,24},{12,4},{16,0},{20,28},{24,8},{28,20},{1,17},{... | collective-permute-start | bytes 811016 | tf_op jit(solution)/shard_map/ppermute | solution.py:738
  295.5 11.3 %collective-permute-start.81 = (bf16[176,768]{1,0:T(8,128)(2,1)S(1)}, bf16[176,768]{1,0:T(8,128)(2,1)S(1)}, u32[]{:S(2)}, u32[]{:S(2)}) collective-permute-start(bf16[176,768]{1,0:T(8,128)(2,1)S(1)} %add_convert_fusion.15.refs_0_), channel_id=1, source_target_pairs={{0,8},{4,20},{8,0},{12,28},{16,24},{20,4},{24,16},{28,12},{1,9},{5... | collective-permute-start | bytes 811016 | tf_op jit(solution)/shard_map/ppermute | solution.py:735
  306.8 13.7 %collective-permute-start.88 = (bf16[176,768]{1,0:T(8,128)(2,1)S(1)}, bf16[176,768]{1,0:T(8,128)(2,1)S(1)}, u32[]{:S(2)}, u32[]{:S(2)}) collective-permute-start(bf16[176,768]{1,0:T(8,128)(2,1)S(1)} %collective-permute-done.81.refs_1_), channel_id=1, source_target_pairs={{0,4},{4,0},{8,12},{12,8},{16,20},{20,16},{24,28},{28,24},{1,5},{5... | collective-permute-start | bytes 811016 | tf_op jit(solution)/shard_map/ppermute | solution.py:729
  306.9 13.7 %collective-permute-start.85 = (bf16[176,768]{1,0:T(8,128)(2,1)S(1)}, bf16[176,768]{1,0:T(8,128)(2,1)S(1)}, u32[]{:S(2)}, u32[]{:S(2)}) collective-permute-start(bf16[176,768]{1,0:T(8,128)(2,1)S(1)} %collective-permute-done.81.refs_1_), channel_id=1, source_target_pairs={{0,16},{4,12},{8,24},{12,4},{16,0},{20,28},{24,8},{28,20},{1,17},{... | collective-permute-start | bytes 811016 | tf_op jit(solution)/shard_map/ppermute | solution.py:738
  307.8 12.7 %collective-permute-start.87 = (bf16[176,768]{1,0:T(8,128)(2,1)S(1)}, bf16[176,768]{1,0:T(8,128)(2,1)S(1)}, u32[]{:S(2)}, u32[]{:S(2)}) collective-permute-start(bf16[176,768]{1,0:T(8,128)(2,1)S(1)} %add_convert_fusion.15.refs_0_), channel_id=1, source_target_pairs={{0,4},{4,0},{8,12},{12,8},{16,20},{20,16},{24,28},{28,24},{1,5},{5... | collective-permute-start | bytes 811016 | tf_op jit(solution)/shard_map/ppermute | solution.py:729
  307.8 12.7 %collective-permute-start.89 = (bf16[176,768]{1,0:T(8,128)(2,1)S(1)}, bf16[176,768]{1,0:T(8,128)(2,1)S(1)}, u32[]{:S(2)}, u32[]{:S(2)}) collective-permute-start(bf16[176,768]{1,0:T(8,128)(2,1)S(1)} %collective-permute-done.82.refs_2_), channel_id=1, source_target_pairs={{0,4},{4,0},{8,12},{12,8},{16,20},{20,16},{24,28},{28,24},{1,5},{5... | collective-permute-start | bytes 811016 | tf_op jit(solution)/shard_map/ppermute | solution.py:729
  (135 other events, 1399.3 us)

commit v7 on v6

--- a/solution.py
+++ b/solution.py
@@ -499,7 +499,7 @@
     pw_ref, pe_ref, ctx_ref = refs[:3]
     pieces, refs = refs[3 : 3 + count], refs[3 + count :]
     if final:
-        spans_ref, send_ref, near_ref, pass_ref, words_ref, ents_ref, pos_s, *refs = refs
+        spans_ref, sums_ref, send_ref, near_ref, pass_ref, words_ref, ents_ref, pos_s, *refs = refs
     else:
         send_ref, near_ref, pass_ref, out_ref, *refs = refs
     (
@@ -574,8 +574,16 @@
         scaled = grad * (1.0 / (end - begin).astype(F32))
         high = scaled.astype(BF16)
         rest = (scaled - high.astype(F32)).astype(BF16)
-        pos_s[...] = (mm_tn(inside, high) + mm_tn(inside, rest)).astype(BF16)
-        sources = [(full_s, size), (pos_s, words // 8)]
+        pos = (mm_tn(inside, high) + mm_tn(inside, rest)).astype(BF16)
+        unit = words // 8
+        step = unit + TILE
+        for i in range(8):
+            pos_s[i * step : i * step + unit] = pos[i * unit : (i + 1) * unit]
+            if i:
+                pos_s[i * step + unit : (i + 1) * step] = jnp.zeros((TILE, pos.shape[1]), BF16)
+        sums = sums_ref[...]
+        pos_s[unit:step] = jnp.concatenate([sums, jnp.zeros_like(sums)], 0).astype(BF16)
+        sources = [(full_s, size), (pos_s, step)]
         writes = start(blocks_out(sources, info_ref, send_ref, near_ref, pass_ref), sem.at[3])
         words_ref[...] = acc_ref[:words] + mm(dpw, w_s[: 2 * half])
     else:
@@ -585,18 +593,19 @@
     wait(writes)
 
 
-def attend_back(info, rows_low, saved, low, up_sums, acc, pieces, words, heads, rows, spans=None):
+def attend_back(info, rows_low, saved, low, up_sums, acc, pieces, words, heads, rows, spans=None, sums=None):
     total, width = rows_low.shape
     pw, pe, ctx, lt = saved
     ents = total - words
     gw = heads * HEAD_DIM
     count = len(pieces)
     final = spans is not None
-    moved = rows + words if final else rows
+    extra = words + 8 * TILE
+    moved = rows + extra if final else rows
     grads = (shape((words, width), F32), shape((ents, width), F32)) if final else (shape((total, width), F32),)
     return pl.pallas_call(
         partial(attend_back_kernel, words, gw, heads, final, count),
-        in_specs=[SMEM] + [VMEM] * 5 + [HBM] * (3 + count) + [VMEM] * final,
+        in_specs=[SMEM] + [VMEM] * 5 + [HBM] * (3 + count) + [VMEM] * (2 * final),
         out_specs=[HBM] * 3 + [VMEM] * len(grads),
         out_shape=(
             far_shape((moved // 2, width), BF16),
@@ -604,7 +613,7 @@
             far_shape((moved // 4, width), BF16),
         )
         + grads,
-        scratch_shapes=[pltpu.VMEM((words, width), BF16)] * final
+        scratch_shapes=[pltpu.VMEM((extra, width), BF16)] * final
         + [
             pltpu.VMEM((rows, width), BF16),
             pltpu.VMEM((words, 4 * gw), BF16),
@@ -624,7 +633,7 @@
         compiler_params=params(24),
         cost_estimate=cost(11, 8),
         name="attend_back",
-    )(info, rows_low, lt, low, up_sums, acc, *far((pw, pe, ctx)), *far(pieces), *((spans,) if final else ()))
+    )(info, rows_low, lt, low, up_sums, acc, *far((pw, pe, ctx)), *far(pieces), *((spans, sums) if final else ()))
 
 
 def spread_query_kernel(info_ref, *refs):
@@ -689,9 +698,13 @@
 
 def spread_pos_kernel(info_ref, *refs):
     pieces = refs[:8]
-    pos_ref, s, sem = refs[8:]
-    wait(start(place(pieces, info_ref, s.shape[0] // 8, (s,)), sem))
-    pos_ref[...] = s[...].astype(F32)
+    pos_ref, sums_ref, s, sem = refs[8:]
+    step = s.shape[0] // 8
+    unit = step - TILE
+    wait(start(place(pieces, info_ref, step, (s,)), sem))
+    for i in range(8):
+        pos_ref[i * unit : (i + 1) * unit] = s[i * step : i * step + unit].astype(F32)
+    sums_ref[...] = s[unit:step].astype(F32)[:8]
 
 
 def spread_pos(info, pieces):
@@ -699,10 +712,10 @@
     return pl.pallas_call(
         spread_pos_kernel,
         in_specs=[SMEM] + [HBM] * 8,
-        out_specs=VMEM,
-        out_shape=shape((8 * rows, width), F32),
+        out_specs=[VMEM] * 2,
+        out_shape=(shape((8 * (rows - TILE), width), F32), shape((8, width), F32)),
         scratch_shapes=[pltpu.VMEM((8 * rows, width), BF16), DMA],
-        compiler_params=params(4),
+        compiler_params=params(5),
         cost_estimate=cost(0.5, 3),
         name="spread_pos",
     )(info, *far(pieces))
@@ -874,92 +887,76 @@
             up_sums[r] = up_sum[8 * k : 8 * k + 8]
         return Blocks(links, send, near, rest), acc
 
-    def back(r, acc, spans=None):
+    def back(r, acc, *last):
         send, near, rest, *acc = attend_back(
-            info, rows_low, saved[r], attended_low, up_sums[r], acc, query_groups[r], words, heads, rows, spans
+            info, rows_low, saved[r], attended_low, up_sums[r], acc, query_groups[r], words, heads, rows, *last
         )
         return Blocks(links, send, near, rest), *acc
 
     fa, acc = ffn_blocks((2, 1), acc)
     fa.got = core(fa.send)
-    fb, acc = ffn_blocks((3,), acc)
+    fb, acc = ffn_blocks((3, 0), acc)
     acc, fa.got = sync(acc, fa.got)
     acc, one_a = sync(acc, fa.one())
 
     fa.a, fb.got = first(one_a), core(fb.send)
-    fc, acc = ffn_blocks((0,), acc)
+    acc, attended_low, sums = norm_back(attended, acc, vec, sums)
     acc, fb.got = sync(acc, fb.got)
-    one_b = fb.one()
-    fc.got = core(fc.send)
-    acc, attended_low, sums = norm_back(attended, acc, vec, sums)
-    more = core(sums)
-    acc, one_b, sums, more, fc.got = sync(acc, one_b, sums, more, fc.got)
-    acc, one_c, sums = sync(acc, fc.one(), sums + more)
-
-    fb.a, fc.a, more = first(one_b), first(one_c), links.swap(sums, 2)
+    acc, one_b = sync(acc, fb.one())
+
+    fb.a = first(one_b)
     q1, acc = back(2, acc)
-    acc, fa.a, fb.a, fc.a, more = sync(acc, fa.a, fb.a, fc.a, more)
+    acc, q1.send, fa.a, fb.a = sync(acc, q1.send, fa.a, fb.a)
     q1.got = core(q1.send)
-    acc, two_a, two_b, two_c, sums, q1.got = sync(acc, fa.two(), fb.two(), fc.two(), sums + more, q1.got)
+    acc, two_a, two_b, q1.got = sync(acc, fa.two(), fb.two(), q1.got)
     acc, one_1 = sync(acc, q1.one())
 
-    fa.b, fb.b, fc.b, q1.a, more = second(two_a), second(two_b), second(two_c), first(one_1), links.swap(sums, 4)
+    fa.b, fb.b, q1.a = second(two_a), second(two_b), first(one_1)
     q2, acc = back(1, acc)
-    acc, fa.b, fb.b, fc.b, q1.a, more = sync(acc, fa.b, fb.b, fc.b, q1.a, more)
+    acc, q2.send, fa.b, fb.b, q1.a = sync(acc, q2.send, fa.b, fb.b, q1.a)
     q2.got = core(q2.send)
-    sums = sums + more
-    for j in range(2, links.bits):
-        sums = sums + links.swap(sums, 2 << j)
-    acc, r2, r1, r3, two_1, q2.got, sums = sync(
-        acc, fa.rest(0, size), fa.rest(size, 2 * size), fb.rest(0, size), q1.two(), q2.got, sums
-    )
+    acc, r2, r3, two_1, q2.got = sync(acc, fa.rest(0, size), fb.rest(0, size), q1.two(), q2.got)
     acc, one_2 = sync(acc, q2.one())
 
-    z2, z1, z3, q1.b, q2.a = shift(r2, -2), shift(r1, -1), shift(r3, -3), second(two_1), first(one_2)
+    z2, z3, q1.b, q2.a = shift(r2, -1), shift(r3, -3), second(two_1), first(one_2)
     q3, acc = back(3, acc)
-    acc, z2, z1, z3, q1.b, q2.a = sync(acc, z2, z1, z3, q1.b, q2.a)
+    acc, q3.send, z2, z3, q1.b, q2.a = sync(acc, q3.send, z2, z3, q1.b, q2.a)
     q3.got = core(q3.send)
-    acc, own_f, value_1, two_2, q3.got = sync(
-        acc, fc.rest(0, size, z1, z2, z3), q1.rest(0, unit), q2.two(), q3.got
-    )
+    acc, r1, value_2, two_2, q3.got = sync(acc, fa.rest(size, 2 * size, z2), q1.rest(0, unit), q2.two(), q3.got)
     acc, one_3 = sync(acc, q3.one())
 
-    y1, ga, gb, q2.b, q3.a = shift(value_1, -2), first(own_f), second(own_f), second(two_2), first(one_3)
-    q4, grad_words, grad_ents = back(0, acc, entity_spans)
-    q4.send, y1, ga, gb, q2.b, q3.a, sums = sync(q4.send, y1, ga, gb, q2.b, q3.a, sums)
+    z1, y2, q2.b, q3.a = shift(r1, -1), shift(value_2, -1), second(two_2), first(one_3)
+    q4, grad_words, grad_ents = back(0, acc, entity_spans, sums)
+    q4.send, z1, y2, q2.b, q3.a = sync(q4.send, z1, y2, q2.b, q3.a)
 
     q4.got = core(q4.send)
-    y2, q3.b, gc = shift(q2.rest(0, unit), -1), second(q3.two()), second(ga)
-    q4.a = first(q4.one())
-    q4.a, q3.b, y2, gc, own_f, ga, gb, sums = sync(q4.a, q3.b, y2, gc, own_f, ga, gb, sums)
-
-    y3, q4.b = shift(q3.rest(0, unit), -3), second(q4.two())
-    near_f = (own_f, ga, gb, gc)
-    far_f = tuple(core(v) for v in near_f)
-    q4.b, y3, sums, *far_f = sync(q4.b, y3, sums, *far_f)
-
-    pos = q4.rest(unit, unit + words // 8)
-    own_q = q4.rest(0, unit, y1, y2, y3)
+    y1, q3.b = shift(q2.rest(0, unit, y2), -1), second(q3.two())
+    own_f = fb.rest(size, 2 * size, z1, z3)
+    q4.a, ga = first(q4.one()), first(own_f)
+    q4.a, q3.b, y1, ga, own_f = sync(q4.a, q3.b, y1, ga, own_f)
+
+    q4.b, y3, gb, gc = second(q4.two()), shift(q3.rest(0, unit), -3), second(own_f), second(ga)
+    q4.b, y3, gb, gc, own_f, ga = sync(q4.b, y3, gb, gc, own_f, ga)
+
+    pos = q4.rest(unit, q4.unit)
+    own_q = q4.rest(0, unit, y1, y3)
     p1, p2, p3 = (links.swap_z(pos, mask) for mask in (1, 2, 3))
     qa, qb = first(own_q), second(own_q)
-    grad_up, grad_down = spread_hidden(info, near_f + tuple(far_f))
-    p1, p2, p3, qa, qb, own_q, pos, sums, grad_up, grad_down = sync(
-        p1, p2, p3, qa, qb, own_q, pos, sums, grad_up, grad_down
-    )
+    p1, p2, p3, qa, qb, own_q, pos, own_f, ga, gb, gc = sync(p1, p2, p3, qa, qb, own_q, pos, own_f, ga, gb, gc)
 
     pos = ((pos.astype(F32) + p1.astype(F32)) + (p2.astype(F32) + p3.astype(F32))).astype(BF16)
-    pa, pb, qc, more = first(pos), second(pos), second(qa), links.swap_z(sums, 1)
-    kv, ka, kb = core(own_q), core(qa), core(qb)
-    pa, pb, qc, more, kv, ka, kb, pos = sync(pa, pb, qc, more, kv, ka, kb, pos)
-    sums = sums + more
-    pc, more, kc = second(pa), links.swap_z(sums, 2), core(qc)
-    kp = tuple(core(v) for v in (pos, pa, pb))
+    pa, pb, qc, kf, kg = first(pos), second(pos), second(qa), core(own_f), core(ga)
+    pa, pb, qc, kf, kg, pos, own_q, qa, qb, gb, gc = sync(pa, pb, qc, kf, kg, pos, own_q, qa, qb, gb, gc)
+    pc, kh, ki, kv, ka = second(pa), core(gb), core(gc), core(own_q), core(qa)
+    pc, kh, ki, kv, ka, qb, qc, pos, pa, pb = sync(pc, kh, ki, kv, ka, qb, qc, pos, pa, pb)
+    kb, kc = core(qb), core(qc)
+    kp = tuple(core(v) for v in (pos, pa, pb, pc))
+    grad_up, grad_down = spread_hidden(info, (own_f, ga, gb, gc, kf, kg, kh, ki))
+    kb, kc, grad_up, grad_down, *kp = sync(kb, kc, grad_up, grad_down, *kp)
     grad_query_t, grad_key_t, grad_value_t, grad_out, grad_query_b, grad_value_b, grad_up_b = spread_query(
         info, (own_q, qa, qb, qc, kv, ka, kb, kc), gw
     )
-    total_sums = sums + more
-    grad_query_t, pc, *kp = sync(grad_query_t, pc, *kp)
-    pos_sum = spread_pos(info, (pos, pa, pb, pc, *kp, core(pc)))
+    pos_sum, total_sums = spread_pos(info, (pos, pa, pb, pc, *kp))
     return (
         out_words,
         out_ents,

time: 344 us -> 341 us (level)
  waiting for transfers between devices: 87.2 us -> 101 us
  starting transfers between devices: 86.7 us -> 75.8 us
    ppermute x15 -> x14, waiting for transfers between devices: 9.27 us -> 20.8 us  [first(): lax.ppermute(v, 'dp', [(i, i ^ (4 if i % 2 else 2)) for i in range(self.d...]
    ppermute x23 -> x22, starting transfers between devices: 30.7 us -> 26.3 us  [second(): lax.ppermute(v, 'dp', [(i, i ^ (2 if i % 2 else 4)) for i in range(self.d...]
    ppermute x42 -> x38, waiting for transfers between devices: 18.3 us -> 15.2 us  [swap(): return lax.ppermute(v, 'dp', [(i, i ^ code) for i in range(self.dp)])]
    ppermute x5 -> x3, waiting for transfers between devices: 6.09 us -> 8 us  [swap_z(): return lax.ppermute(v, 'tensor', [(i, i ^ mask) for i in range(self.ring)])]
    ppermute x23 -> x22, waiting for transfers between devices: 30.2 us -> 32 us  [second(): lax.ppermute(v, 'dp', [(i, i ^ (2 if i % 2 else 4)) for i in range(self.d...]
    ppermute x15 -> x14, starting transfers between devices: 17 us -> 15.5 us  [first(): lax.ppermute(v, 'dp', [(i, i ^ (4 if i % 2 else 2)) for i in range(self.d...]
    pallas_call x3 -> x2, Pallas kernels: 19.9 us -> 19 us  [hidden_back(): pl.pallas_call(partial(hidden_back_kernel, pair), in_specs=[SMEM] + [VMEM...]
    ppermute x42 -> x38, starting transfers between devices: 9.78 us -> 8.99 us  [swap(): return lax.ppermute(v, 'dp', [(i, i ^ code) for i in range(self.dp)])]
  transfers between devices with their start and end apart: 97 -> 89, of which waited for: 31 -> 31; matrix products, arithmetic and copies ran while one was open for 3% -> 2% of each run, Pallas kernels for 32% -> 31%
where the time goes in v7:
time: 341 us; the launch traced here: 336 us
  Pallas kernels  142 us (42%)
  waiting for transfers between devices  101 us (30%)
  starting transfers between devices  75.8 us (22%)
  local copies, waits for them, and re-layouts  9.29 us (3%)
  other arithmetic  5.36 us (2%)
    pallas_call x4, Pallas kernels, attend_back(): pl.pallas_call(partial(attend_back_kernel, words, gw, heads, final, count...  48.3 us
    pallas_call x4, Pallas kernels, attend(): pl.pallas_call(partial(attend_kernel, words, gw, heads, count), in_specs=...  37.3 us
    ppermute x22, waiting for transfers between devices, second(): lax.ppermute(v, 'dp', [(i, i ^ (2 if i % 2 else 4)) for i in range(self.d...  32 us
    ppermute x22, starting transfers between devices, second(): lax.ppermute(v, 'dp', [(i, i ^ (2 if i % 2 else 4)) for i in range(self.d...  26.3 us
    ppermute x12, waiting for transfers between devices, shift_z(): return lax.ppermute(v, 'tensor', [(i, (i + by) % n) for i in range(n)])  24.7 us
    ppermute x14, waiting for transfers between devices, first(): lax.ppermute(v, 'dp', [(i, i ^ (4 if i % 2 else 2)) for i in range(self.d...  20.8 us
    ppermute x12, starting transfers between devices, shift_z(): return lax.ppermute(v, 'tensor', [(i, (i + by) % n) for i in range(n)])  20.5 us
    pallas_call x1, Pallas kernels, hidden(): pl.pallas_call(partial(hidden_kernel, n), in_specs=[SMEM] + [VMEM] * (6 +...  19.7 us
  transfers between devices with their start and end apart: 89, of which 31 were waited for; matrix products, arithmetic and copies ran while one was open for 2% of the time, Pallas kernels for 31%

profile of v7, /device:TPU:0, one launch (start us, length us, event | category | flops | bytes accessed | tf_op | source)
XLA Modules:
  0.0 335.5 jit_solution(2392805080527845568)
XLA Ops:
  2.8 2.4 pack.1
  5.3 5.1 %collective-permute-start.1 = (bf16[176,768]{1,0:T(8,128)(2,1)}, bf16[176,768]{1,0:T(8,128)(2,1)S(1)}, u32[]{:S(2)}, u32[]{:S(2)}) collective-permute-start(bf16[176,768]{1,0:T(8,128)(2,1)} %get-tuple-element.271), channel_id=1, source_target_pairs={{0,3},{1,0},{2,1},{3,2},{4,7},{5,4},{6,5},{7,6},{8,11},{9,8},{10,9... | collective-permute-start | bytes 811016 | tf_op jit(solution)/shard_map/ppermute | solution.py:736
  10.6 2.2 start_rows.1
  12.9 3.9 %collective-permute-start.5 = (bf16[192,768]{1,0:T(8,128)(2,1)S(1)}, bf16[192,768]{1,0:T(8,128)(2,1)S(1)}, u32[]{:S(2)}, u32[]{:S(2)}) collective-permute-start(bf16[192,768]{1,0:T(8,128)(2,1)S(1)} %copy-done.54), channel_id=1, source_target_pairs={{0,3},{1,0},{2,1},{3,2},{4,7},{5,4},{6,5},{7,6},{8,11},{9,8},{10,9... | collective-permute-start | bytes 884744 | tf_op jit(solution)/shard_map/ppermute | solution.py:736
  16.7 9.1 %attend_own.1 = (bf16[512,768]{1,0:T(8,128)(2,1)}, bf16[128,768]{1,0:T(8,128)(2,1)}, bf16[640,192]{1,0:T(8,128)(2,1)}, f32[8,640]{1,0:T(8,128)S(1)}, bf16[16,768...) custom-call(s32[4]{0:T(128)S(1)} %pad_add_fusion.info_ref, ...), custom_call_target="tpu_custom_call", output_to_operand_aliasing={{5}: (2, {})} | custom-call | flops 8000000000 | bytes 6000000 | tf_op jit(solution)/shard_map/attend_own/pallas_call | solution.py:284
  29.6 7.2 %collective-permute-done.4 = bf16[192,768]{1,0:T(8,128)(2,1)S(1)} collective-permute-done((bf16[192,768]{1,0:T(8,128)(2,1)S(1)}, bf16[192,768]{1,0:T(8,128)(2,1)S(1)}, u32[]{:S(2)}, u32[]{:S(2)}) %collective-permute-start.4) | collective-permute-done | bytes 294944 | tf_op jit(solution)/shard_map/ppermute | solution.py:736
  39.1 2.5 collective-permute-done.10.refs_0_.refs_3_
  41.6 2.4 collective-permute-done.6.refs_3_.refs_6_
  44.0 1.7 collective-permute-start.19
  48.7 5.9 %collective-permute-done.13.refs_2_.refs_5_ = bf16[176,768]{1,0:T(8,128)(2,1)S(1)} collective-permute-done((bf16[176,768]{1,0:T(8,128)(2,1)S(1)}, bf16[176,768]{1,0:T(8,128)(2,1)S(1)}, u32[]{:S(2)}, u32[]{:S(2)}) %collective-permute-start.13) | collective-permute-done | bytes 270368 | tf_op jit(solution)/shard_map/ppermute | solution.py:751
  60.3 9.4 %attend_far.3 = (bf16[512,768]{1,0:T(8,128)(2,1)}, bf16[128,768]{1,0:T(8,128)(2,1)}, bf16[640,192]{1,0:T(8,128)(2,1)}, f32[8,640]{1,0:T(8,128)S(1)}, bf16[16,768...) custom-call(s32[4]{0:T(128)S(1)} %pad_add_fusion.info_ref, ...), custom_call_target="tpu_custom_call", output_to_operand_aliasing={{5}: (2, {})} | custom-call | flops 8000000000 | bytes 6000000 | tf_op jit(solution)/shard_map/attend_far/pallas_call | solution.py:284
  77.9 9.4 %attend_far.4 = (bf16[512,768]{1,0:T(8,128)(2,1)}, bf16[128,768]{1,0:T(8,128)(2,1)}, bf16[640,192]{1,0:T(8,128)(2,1)}, f32[8,640]{1,0:T(8,128)S(1)}, bf16[16,768...) custom-call(s32[4]{0:T(128)S(1)} %pad_add_fusion.info_ref, ...), custom_call_target="tpu_custom_call", output_to_operand_aliasing={{5}: (2, {})} | custom-call | flops 8000000000 | bytes 6000000 | tf_op jit(solution)/shard_map/attend_far/pallas_call | solution.py:284
  94.7 9.4 %attend_far.5 = (bf16[512,768]{1,0:T(8,128)(2,1)}, bf16[128,768]{1,0:T(8,128)(2,1)}, bf16[640,192]{1,0:T(8,128)(2,1)}, f32[8,640]{1,0:T(8,128)S(1)}, bf16[16,768...) custom-call(s32[4]{0:T(128)S(1)} %pad_add_fusion.info_ref, ...), custom_call_target="tpu_custom_call", output_to_operand_aliasing={{5}: (2, {})} | custom-call | flops 8000000000 | bytes 6000000 | tf_op jit(solution)/shard_map/attend_far/pallas_call | solution.py:284
  104.2 5.0 %collective-permute-done.32.refs_9_ = bf16[384,768]{1,0:T(8,128)(2,1)} collective-permute-done((bf16[384,768]{1,0:T(8,128)(2,1)}, bf16[384,768]{1,0:T(8,128)(2,1)}, u32[]{:S(2)}, u32[]{:S(2)}) %collective-permute-start.32) | collective-permute-done | bytes 589856 | tf_op jit(solution)/shard_map/ppermute | solution.py:751
  115.7 19.7 %hidden.1 = (bf16[768,640]{1,0:T(8,128)(2,1)S(1)}, bf16[4,768,640]{2,1,0:T(8,128)(2,1)S(1)}, f32[4,640,768]{2,1,0:T(8,128)S(1)}, bf16[4,768,768]{2,1,0:T(8,128)(...) custom-call(s32[4]{0:T(128)S(1)} %pad_add_fusion.info_ref, ...), custom_call_target="tpu_custom_call" | custom-call | flops 22000001024 | bytes 20000000 | tf_op jit(solution)/shard_map/hidden/pallas_call | solution.py:393
  135.4 9.6 %hidden_back.2 = (bf16[1536,768]{1,0:T(8,128)(2,1)}, bf16[768,768]{1,0:T(8,128)(2,1)}, bf16[768,768]{1,0:T(8,128)(2,1)}, f32[640,768]{1,0:T(8,128)S(1)}, f32[16,768]{1,0:T(8,128)S(1)}) custom-call(s32[4]{0:T(128)S(1)} %pad_add_fusion.info_ref, bf16[640,768]{1,0:T(8,128)(2,1)S(1)} %get-tuple-element.349.low_ref, ...), custom_call_target="tpu_custom_call", output_to_operand_aliasing={{3}: (7, {})} | custom-call | flops 14000000000 | bytes 16000000 | tf_op jit(solution)/shard_map/hidden_back/pallas_call | solution.py:454
  145.2 9.4 %hidden_back.3 = (bf16[1536,768]{1,0:T(8,128)(2,1)}, bf16[768,768]{1,0:T(8,128)(2,1)}, bf16[768,768]{1,0:T(8,128)(2,1)}, f32[640,768]{1,0:T(8,128)S(1)}, f32[16,768]{1,0:T(8,128)S(1)}) custom-call(s32[4]{0:T(128)S(1)} %pad_add_fusion.info_ref, bf16[640,768]{1,0:T(8,128)(2,1)S(1)} %get-tuple-element.349.low_ref, ...), custom_call_target="tpu_custom_call", output_to_operand_aliasing={{3}: (7, {})} | custom-call | flops 14000000000 | bytes 16000000 | tf_op jit(solution)/shard_map/hidden_back/pallas_call | solution.py:454
  156.7 2.6 collective-permute-done.42
  159.7 1.7 collective-permute-start.44
  161.8 11.9 %attend_back.4 = (bf16[704,768]{1,0:T(8,128)(2,1)}, bf16[352,768]{1,0:T(8,128)(2,1)}, bf16[352,768]{1,0:T(8,128)(2,1)}, f32[640,768]{1,0:T(8,128)S(1)}) custom-call(s32[4]{0:T(128)S(1)} %pad_add_fusion.info_ref, bf16[640,768]{1,0:T(8,128)(2,1)S(1)} %get-tuple-element.266.rows_ref, f32[8,640]{1,0:T(8,128)S(1)} %copy-done.9, ...), custom_call_target="tpu_custom_call", output_to_operand_aliasing={{3}: (5, {})} | custom-call | flops 11000000512 | bytes 8000000 | tf_op jit(solution)/shard_map/attend_back/pallas_call | solution.py:606
  173.8 2.2 collective-permute-done.44
  176.0 12.6 %collective-permute-done.43 = bf16[768,768]{1,0:T(8,128)(2,1)S(1)} collective-permute-done((bf16[768,768]{1,0:T(8,128)(2,1)S(1)}, bf16[768,768]{1,0:T(8,128)(2,1)S(1)}, u32[]{:S(2)}, u32[]{:S(2)}) %collective-permute-start.43) | collective-permute-done | bytes 1179680 | tf_op jit(solution)/shard_map/ppermute | solution.py:748
  189.1 2.4 collective-permute-done.45
  191.7 1.7 collective-permute-start.48
  195.5 11.6 %attend_back.5 = (bf16[704,768]{1,0:T(8,128)(2,1)}, bf16[352,768]{1,0:T(8,128)(2,1)}, bf16[352,768]{1,0:T(8,128)(2,1)}, f32[640,768]{1,0:T(8,128)S(1)}) custom-call(s32[4]{0:T(128)S(1)} %pad_add_fusion.info_ref, bf16[640,768]{1,0:T(8,128)(2,1)S(1)} %get-tuple-element.266.rows_ref, ...), custom_call_target="tpu_custom_call", output_to_operand_aliasing={{3}: (5, {})} | custom-call | flops 11000000512 | bytes 8000000 | tf_op jit(solution)/shard_map/attend_back/pallas_call | solution.py:606
  207.1 5.9 %collective-permute-done.47 = bf16[384,768]{1,0:T(8,128)(2,1)S(1)} collective-permute-done((bf16[384,768]{1,0:T(8,128)(2,1)S(1)}, bf16[384,768]{1,0:T(8,128)(2,1)S(1)}, u32[]{:S(2)}, u32[]{:S(2)}) %collective-permute-start.47) | collective-permute-done | bytes 589856 | tf_op jit(solution)/shard_map/ppermute | solution.py:751
  214.0 2.1 collective-permute-done.49
  217.6 2.2 collective-permute-start.50
  221.5 11.4 %attend_back.6 = (bf16[704,768]{1,0:T(8,128)(2,1)}, bf16[352,768]{1,0:T(8,128)(2,1)}, bf16[352,768]{1,0:T(8,128)(2,1)}, f32[640,768]{1,0:T(8,128)S(1)}) custom-call(s32[4]{0:T(128)S(1)} %pad_add_fusion.info_ref, bf16[640,768]{1,0:T(8,128)(2,1)S(1)} %get-tuple-element.266.rows_ref, f32[8,640]{1,0:T(8,128)S(1)} %copy-done.7, ...), custom_call_target="tpu_custom_call", output_to_operand_aliasing={{3}: (5, {})} | custom-call | flops 11000000512 | bytes 8000000 | tf_op jit(solution)/shard_map/attend_back/pallas_call | solution.py:606
  234.4 2.4 collective-permute-done.54
  236.9 3.0 collective-permute-start.56
  241.3 13.4 %attend_back.7 = (bf16[1024,768]{1,0:T(8,128)(2,1)}, bf16[512,768]{1,0:T(8,128)(2,1)}, bf16[512,768]{1,0:T(8,128)(2,1)}, f32[512,768]{1,0:T(8,128)}, f32[128,768]{1,0:T(8,128)}) custom-call(s32[4]{0:T(128)S(1)} %pad_add_fusion.info_ref, bf16[640,768]{1,0:T(8,128)(2,1)S(1)} %get-tuple-element.266.rows_ref, f32[8,640]{1,0:T(8,128)S(1)} %copy-done.11, ...), custom_call_target="tpu_custom_call" | custom-call | flops 11000000512 | bytes 8000000 | tf_op jit(solution)/shard_map/attend_back/pallas_call | solution.py:606
  256.3 2.2 collective-permute-done.59
  258.7 1.7 collective-permute-start.60
  261.3 1.9 collective-permute-start.62
  263.3 6.3 %collective-permute-done.62 = bf16[176,768]{1,0:T(8,128)(2,1)S(1)} collective-permute-done((bf16[176,768]{1,0:T(8,128)(2,1)S(1)}, bf16[176,768]{1,0:T(8,128)(2,1)S(1)}, u32[]{:S(2)}, u32[]{:S(2)}) %collective-permute-start.62) | collective-permute-done | bytes 270368 | tf_op jit(solution)/shard_map/ppermute | solution.py:736
  269.6 4.4 %collective-permute-done.63.refs_1_ = bf16[192,768]{1,0:T(8,128)(2,1)S(1)} collective-permute-done((bf16[192,768]{1,0:T(8,128)(2,1)S(1)}, bf16[192,768]{1,0:T(8,128)(2,1)S(1)}, u32[]{:S(2)}, u32[]{:S(2)}) %collective-permute-start.63) | collective-permute-done | bytes 294944 | tf_op jit(solution)/shard_map/ppermute | solution.py:748
  277.6 2.3 collective-permute-start.65
  279.8 7.1 %collective-permute-done.65 = bf16[176,768]{1,0:T(8,128)(2,1)S(1)} collective-permute-done((bf16[176,768]{1,0:T(8,128)(2,1)S(1)}, bf16[176,768]{1,0:T(8,128)(2,1)S(1)}, u32[]{:S(2)}, u32[]{:S(2)}) %collective-permute-start.65) | collective-permute-done | bytes 270368 | tf_op jit(solution)/shard_map/ppermute | solution.py:736
  291.3 1.7 collective-permute-start.70
  293.1 1.8 collective-permute-start.69
  295.8 3.3 collective-permute-done.70
  299.1 4.7 %collective-permute-done.69 = bf16[80,768]{1,0:T(8,128)(2,1)S(1)} collective-permute-done((bf16[80,768]{1,0:T(8,128)(2,1)S(1)}, bf16[80,768]{1,0:T(8,128)(2,1)S(1)}, u32[]{:S(2)}, u32[]{:S(2)}) %collective-permute-start.69) | collective-permute-done | bytes 122912 | tf_op jit(solution)/shard_map/ppermute | solution.py:739
  306.9 6.0 %collective-permute-done.74.refs_2_ = bf16[80,768]{1,0:T(8,128)(2,1)S(1)} collective-permute-done((bf16[80,768]{1,0:T(8,128)(2,1)S(1)}, bf16[80,768]{1,0:T(8,128)(2,1)S(1)}, u32[]{:S(2)}, u32[]{:S(2)}) %collective-permute-start.74) | collective-permute-done | bytes 122912 | tf_op jit(solution)/shard_map/ppermute | solution.py:751
  314.9 4.1 %collective-permute-done.78.refs_3_ = bf16[80,768]{1,0:T(8,128)(2,1)S(1)} collective-permute-done((bf16[80,768]{1,0:T(8,128)(2,1)S(1)}, bf16[80,768]{1,0:T(8,128)(2,1)S(1)}, u32[]{:S(2)}, u32[]{:S(2)}) %collective-permute-start.78) | collective-permute-done | bytes 122912 | tf_op jit(solution)/shard_map/ppermute | solution.py:751
  321.4 4.6 %spread_hidden.1 = (f32[768,768]{1,0:T(8,128)}, f32[768,768]{1,0:T(8,128)}) custom-call(s32[4]{0:T(128)S(1)} %pad_add_fusion.info_ref, bf16[192,768]{1,0:T(8,128)(2,1)} %copy-done.16, bf16[192,768]{1,0:T(8,128)(2,1)} %copy-done.26, bf16[192,768]{1,0:T(8,128)(2,1)} %copy-done.27, bf16[192,768]{1,0:T(8,128)(2,1)} %copy-done.28, bf16[192,768]{1,0:T(8,128)(2,1)} %copy-done.29, ...), custom_call_target="tpu_custom_call" | custom-call | flops 500000000 | bytes 7000000 | tf_op jit(solution)/shard_map/spread_hidden/pallas_call | solution.py:687
  326.8 3.1 spread_pos.1
  330.5 4.1 %spread_query.1 = (f32[4,192,768]{2,1,0:T(8,128)}, f32[192,768]{1,0:T(8,128)}, f32[192,768]{1,0:T(8,128)}, f32[192,768]{1,0:T(8,128)}, f32[4,192]{1,0:T(4,128)}, /*index=5*/f32[1,192]{1,0:T(1,128)}, f32[1,768]{1,0:T(1,128)S(1)}) custom-call(s32[4]{0:T(128)S(1)} %pad_add_fusion.info_ref, bf16[176,768]{1,0:T(8,128)(2,1)} %copy-done.17, ...), custom_call_target="tpu_custom_call" | custom-call | flops 500000000 | bytes 7000000 | tf_op jit(solution)/shard_map/spread_query/pallas_call | solution.py:661
  (354 shorter events, 72.3 us)
Async XLA Ops:
  5.3 20.6 %collective-permute-start.1 = (bf16[176,768]{1,0:T(8,128)(2,1)}, bf16[176,768]{1,0:T(8,128)(2,1)S(1)}, u32[]{:S(2)}, u32[]{:S(2)}) collective-permute-start(bf16[176,768]{1,0:T(8,128)(2,1)} %get-tuple-element.271), channel_id=1, source_target_pairs={{0,3},{1,0},{2,1},{3,2},{4,7},{5,4},{6,5},{7,6},{8,11},{9,8},{10,9... | collective-permute-start | bytes 811016 | tf_op jit(solution)/shard_map/ppermute | solution.py:736
  10.4 15.5 %collective-permute-start = (bf16[176,768]{1,0:T(8,128)(2,1)}, bf16[176,768]{1,0:T(8,128)(2,1)}, u32[]{:S(2)}, u32[]{:S(2)}) collective-permute-start(bf16[176,768]{1,0:T(8,128)(2,1)} %get-tuple-element.271), channel_id=1, source_target_pairs={{0,1},{1,2},{2,3},{3,0},{4,5},{5,6},{6,7},{7,4},{8,9},{9,10},{10,1... | collective-permute-start | bytes 811016 | tf_op jit(solution)/shard_map/ppermute | solution.py:736
  12.9 16.8 %collective-permute-start.5 = (bf16[192,768]{1,0:T(8,128)(2,1)S(1)}, bf16[192,768]{1,0:T(8,128)(2,1)S(1)}, u32[]{:S(2)}, u32[]{:S(2)}) collective-permute-start(bf16[192,768]{1,0:T(8,128)(2,1)S(1)} %copy-done.54), channel_id=1, source_target_pairs={{0,3},{1,0},{2,1},{3,2},{4,7},{5,4},{6,5},{7,6},{8,11},{9,8},{10,9... | collective-permute-start | bytes 884744 | tf_op jit(solution)/shard_map/ppermute | solution.py:736
  16.7 20.1 %collective-permute-start.4 = (bf16[192,768]{1,0:T(8,128)(2,1)S(1)}, bf16[192,768]{1,0:T(8,128)(2,1)S(1)}, u32[]{:S(2)}, u32[]{:S(2)}) collective-permute-start(bf16[192,768]{1,0:T(8,128)(2,1)S(1)} %copy-done.54), channel_id=1, source_target_pairs={{0,1},{1,2},{2,3},{3,0},{4,5},{5,6},{6,7},{7,4},{8,9},{9,10},{10,1... | collective-permute-start | bytes 884744 | tf_op jit(solution)/shard_map/ppermute | solution.py:736
  25.9 10.9 %collective-permute-start.3 = (bf16[176,768]{1,0:T(8,128)(2,1)}, bf16[176,768]{1,0:T(8,128)(2,1)S(1)}, u32[]{:S(2)}, u32[]{:S(2)}) collective-permute-start(bf16[176,768]{1,0:T(8,128)(2,1)} %collective-permute-done.refs_0_.refs_3_), channel_id=1, source_target_pairs={{0,16},{4,12},{8,24},{12,4},{16,0},{20,28},{24,8},{28,20},{1,17},{... | collective-permute-start | bytes 811016 | tf_op jit(solution)/shard_map/ppermute | solution.py:751
  27.5 9.4 %collective-permute-start.2 = (bf16[176,768]{1,0:T(8,128)(2,1)}, bf16[176,768]{1,0:T(8,128)(2,1)S(1)}, u32[]{:S(2)}, u32[]{:S(2)}) collective-permute-start(bf16[176,768]{1,0:T(8,128)(2,1)} %collective-permute-done.refs_0_.refs_3_), channel_id=1, source_target_pairs={{0,8},{4,20},{8,0},{12,28},{16,24},{20,4},{24,16},{28,12},{1,9},{5... | collective-permute-start | bytes 811016 | tf_op jit(solution)/shard_map/ppermute | solution.py:748
  29.0 12.5 %collective-permute-start.10 = (bf16[176,768]{1,0:T(8,128)(2,1)}, bf16[176,768]{1,0:T(8,128)(2,1)S(1)}, u32[]{:S(2)}, u32[]{:S(2)}) collective-permute-start(bf16[176,768]{1,0:T(8,128)(2,1)} %collective-permute-done.refs_0_.refs_3_), channel_id=1, source_target_pairs={{0,1},{1,2},{2,3},{3,0},{4,5},{5,6},{6,7},{7,4},{8,9},{9,10},{10,1... | collective-permute-start | bytes 811016 | tf_op jit(solution)/shard_map/ppermute | solution.py:736
  44.0 14.8 %collective-permute-start.19 = (bf16[192,768]{1,0:T(8,128)(2,1)S(1)}, bf16[192,768]{1,0:T(8,128)(2,1)S(1)}, u32[]{:S(2)}, u32[]{:S(2)}) collective-permute-start(bf16[192,768]{1,0:T(8,128)(2,1)S(1)} %collective-permute-done.4), channel_id=1, source_target_pairs={{0,1},{1,2},{2,3},{3,0},{4,5},{5,6},{6,7},{7,4},{8,9},{9,10},{10,1... | collective-permute-start | bytes 884744 | tf_op jit(solution)/shard_map/ppermute | solution.py:736
  54.6 15.1 %collective-permute-start.16 = (bf16[176,768]{1,0:T(8,128)(2,1)S(1)}, bf16[176,768]{1,0:T(8,128)(2,1)S(1)}, u32[]{:S(2)}, u32[]{:S(2)}) collective-permute-start(bf16[176,768]{1,0:T(8,128)(2,1)S(1)} %collective-permute-done.10.refs_0_.refs_3_), channel_id=1, source_target_pairs={{0,16},{4,12},{8,24},{12,4},{16,0},{20,28},{24,8},{28,20},{1,17},{... | collective-permute-start | bytes 811016 | tf_op jit(solution)/shard_map/ppermute | solution.py:751
  56.2 13.6 %collective-permute-start.15 = (bf16[176,768]{1,0:T(8,128)(2,1)S(1)}, bf16[176,768]{1,0:T(8,128)(2,1)S(1)}, u32[]{:S(2)}, u32[]{:S(2)}) collective-permute-start(bf16[176,768]{1,0:T(8,128)(2,1)S(1)} %collective-permute-done.10.refs_0_.refs_3_), channel_id=1, source_target_pairs={{0,8},{4,20},{8,0},{12,28},{16,24},{20,4},{24,16},{28,12},{1,9},{5... | collective-permute-start | bytes 811016 | tf_op jit(solution)/shard_map/ppermute | solution.py:748
  56.8 15.3 %collective-permute-start.18 = (bf16[192,768]{1,0:T(8,128)(2,1)S(1)}, bf16[192,768]{1,0:T(8,128)(2,1)S(1)}, u32[]{:S(2)}, u32[]{:S(2)}) collective-permute-start(bf16[192,768]{1,0:T(8,128)(2,1)S(1)} %collective-permute-done.5.refs_14_), channel_id=1, source_target_pairs={{0,16},{4,12},{8,24},{12,4},{16,0},{20,28},{24,8},{28,20},{1,17},{... | collective-permute-start | bytes 884744 | tf_op jit(solution)/shard_map/ppermute | solution.py:751
  57.3 14.8 %collective-permute-start.17 = (bf16[192,768]{1,0:T(8,128)(2,1)S(1)}, bf16[192,768]{1,0:T(8,128)(2,1)S(1)}, u32[]{:S(2)}, u32[]{:S(2)}) collective-permute-start(bf16[192,768]{1,0:T(8,128)(2,1)S(1)} %collective-permute-done.5.refs_14_), channel_id=1, source_target_pairs={{0,8},{4,20},{8,0},{12,28},{16,24},{20,4},{24,16},{28,12},{1,9},{5... | collective-permute-start | bytes 884744 | tf_op jit(solution)/shard_map/ppermute | solution.py:748
  58.8 13.3 %collective-permute-start.14 = (bf16[176,768]{1,0:T(8,128)(2,1)S(1)}, bf16[176,768]{1,0:T(8,128)(2,1)S(1)}, u32[]{:S(2)}, u32[]{:S(2)}) collective-permute-start(bf16[176,768]{1,0:T(8,128)(2,1)S(1)} %collective-permute-done.12.refs_1_.refs_4_), channel_id=1, source_target_pairs={{0,16},{4,12},{8,24},{12,4},{16,0},{20,28},{24,8},{28,20},{1,17},{... | collective-permute-start | bytes 811016 | tf_op jit(solution)/shard_map/ppermute | solution.py:751
  74.0 14.0 %collective-permute-start.28 = (bf16[176,768]{1,0:T(8,128)(2,1)S(1)}, bf16[176,768]{1,0:T(8,128)(2,1)S(1)}, u32[]{:S(2)}, u32[]{:S(2)}) collective-permute-start(bf16[176,768]{1,0:T(8,128)(2,1)S(1)} %collective-permute-done.15.refs_1_.refs_4_), channel_id=1, source_target_pairs={{0,4},{4,0},{8,12},{12,8},{16,20},{20,16},{24,28},{28,24},{1,5},{5... | collective-permute-start | bytes 811016 | tf_op jit(solution)/shard_map/ppermute | solution.py:742
  74.2 13.8 %collective-permute-start.24 = (bf16[176,768]{1,0:T(8,128)(2,1)S(1)}, bf16[176,768]{1,0:T(8,128)(2,1)S(1)}, u32[]{:S(2)}, u32[]{:S(2)}) collective-permute-start(bf16[176,768]{1,0:T(8,128)(2,1)S(1)} %collective-permute-done.15.refs_1_.refs_4_), channel_id=1, source_target_pairs={{0,16},{4,12},{8,24},{12,4},{16,0},{20,28},{24,8},{28,20},{1,17},{... | collective-permute-start | bytes 811016 | tf_op jit(solution)/shard_map/ppermute | solution.py:751
  75.7 12.2 %collective-permute-start.27 = (bf16[176,768]{1,0:T(8,128)(2,1)S(1)}, bf16[176,768]{1,0:T(8,128)(2,1)S(1)}, u32[]{:S(2)}, u32[]{:S(2)}) collective-permute-start(bf16[176,768]{1,0:T(8,128)(2,1)S(1)} %collective-permute-done.10.refs_0_.refs_3_), channel_id=1, source_target_pairs={{0,4},{4,0},{8,12},{12,8},{16,20},{20,16},{24,28},{28,24},{1,5},{5... | collective-permute-start | bytes 811016 | tf_op jit(solution)/shard_map/ppermute | solution.py:742
  75.9 12.1 %collective-permute-start.25 = (bf16[192,768]{1,0:T(8,128)(2,1)S(1)}, bf16[192,768]{1,0:T(8,128)(2,1)}, u32[]{:S(2)}, u32[]{:S(2)}) collective-permute-start(bf16[192,768]{1,0:T(8,128)(2,1)S(1)} %collective-permute-done.17.refs_15_), channel_id=1, source_target_pairs={{0,16},{4,12},{8,24},{12,4},{16,0},{20,28},{24,8},{28,20},{1,17},{... | collective-permute-start | bytes 884744 | tf_op jit(solution)/shard_map/ppermute | solution.py:751
  77.4 12.2 %collective-permute-start.26 = (bf16[384,768]{1,0:T(8,128)(2,1)}, bf16[384,768]{1,0:T(8,128)(2,1)}, u32[]{:S(2)}, u32[]{:S(2)}) collective-permute-start(bf16[384,768]{1,0:T(8,128)(2,1)} %pad_maximum_fusion.refs_6_), channel_id=1, source_target_pairs={{0,8},{4,20},{8,0},{12,28},{16,24},{20,4},{24,16},{28,12},{1,9},{5... | collective-permute-start | bytes 1769480 | tf_op jit(solution)/shard_map/ppermute | solution.py:748
  91.8 12.3 %collective-permute-start.33 = (bf16[192,768]{1,0:T(8,128)(2,1)S(1)}, bf16[192,768]{1,0:T(8,128)(2,1)S(1)}, u32[]{:S(2)}, u32[]{:S(2)}) collective-permute-start(bf16[192,768]{1,0:T(8,128)(2,1)S(1)} %collective-permute-done.5.refs_14_), channel_id=1, source_target_pairs={{0,4},{4,0},{8,12},{12,8},{16,20},{20,16},{24,28},{28,24},{1,5},{5... | collective-permute-start | bytes 884744 | tf_op jit(solution)/shard_map/ppermute | solution.py:742
  92.1 12.0 %collective-permute-start.34 = (bf16[192,768]{1,0:T(8,128)(2,1)S(1)}, bf16[192,768]{1,0:T(8,128)(2,1)S(1)}, u32[]{:S(2)}, u32[]{:S(2)}) collective-permute-start(bf16[192,768]{1,0:T(8,128)(2,1)S(1)} %collective-permute-done.17.refs_15_), channel_id=1, source_target_pairs={{0,4},{4,0},{8,12},{12,8},{16,20},{20,16},{24,28},{28,24},{1,5},{5... | collective-permute-start | bytes 884744 | tf_op jit(solution)/shard_map/ppermute | solution.py:742
  92.3 11.9 %collective-permute-start.35 = (bf16[192,768]{1,0:T(8,128)(2,1)S(1)}, bf16[192,768]{1,0:T(8,128)(2,1)S(1)}, u32[]{:S(2)}, u32[]{:S(2)}) collective-permute-start(bf16[192,768]{1,0:T(8,128)(2,1)S(1)} %collective-permute-done.18.refs_16_), channel_id=1, source_target_pairs={{0,4},{4,0},{8,12},{12,8},{16,20},{20,16},{24,28},{28,24},{1,5},{5... | collective-permute-start | bytes 884744 | tf_op jit(solution)/shard_map/ppermute | solution.py:742
  92.6 11.5 %collective-permute-start.31 = (bf16[384,768]{1,0:T(8,128)(2,1)}, bf16[384,768]{1,0:T(8,128)(2,1)}, u32[]{:S(2)}, u32[]{:S(2)}) collective-permute-start(bf16[384,768]{1,0:T(8,128)(2,1)} %pad_maximum_fusion.refs_6_), channel_id=1, source_target_pairs={{0,16},{4,12},{8,24},{12,4},{16,0},{20,28},{24,8},{28,20},{1,17},{... | collective-permute-start | bytes 1769480 | tf_op jit(solution)/shard_map/ppermute | solution.py:751
  94.2 15.0 %collective-permute-start.32 = (bf16[384,768]{1,0:T(8,128)(2,1)}, bf16[384,768]{1,0:T(8,128)(2,1)}, u32[]{:S(2)}, u32[]{:S(2)}) collective-permute-start(bf16[384,768]{1,0:T(8,128)(2,1)} %collective-permute-done.26.refs_7_), channel_id=1, source_target_pairs={{0,16},{4,12},{8,24},{12,4},{16,0},{20,28},{24,8},{28,20},{1,17},{... | collective-permute-start | bytes 1769480 | tf_op jit(solution)/shard_map/ppermute | solution.py:751
  145.0 10.0 %collective-permute-start.41 = (bf16[1536,768]{1,0:T(8,128)(2,1)}, bf16[1536,768]{1,0:T(8,128)(2,1)S(1)}, u32[]{:S(2)}, u32[]{:S(2)}) collective-permute-start(bf16[1536,768]{1,0:T(8,128)(2,1)} %get-tuple-element.358), channel_id=1, source_target_pairs={{0,4},{4,0},{8,12},{12,8},{16,20},{20,16},{24,28},{28,24},{1,5},{5... | collective-permute-start | bytes 7077896 | tf_op jit(solution)/shard_map/ppermute | solution.py:742
  159.7 16.3 %collective-permute-start.44 = (bf16[768,768]{1,0:T(8,128)(2,1)S(1)}, bf16[768,768]{1,0:T(8,128)(2,1)S(1)}, u32[]{:S(2)}, u32[]{:S(2)}) collective-permute-start(bf16[768,768]{1,0:T(8,128)(2,1)S(1)} %add_convert_fusion), channel_id=1, source_target_pairs={{0,8},{4,20},{8,0},{12,28},{16,24},{20,4},{24,16},{28,12},{1,9},{5... | collective-permute-start | bytes 3538952 | tf_op jit(solution)/shard_map/ppermute | solution.py:748
  161.5 27.2 %collective-permute-start.43 = (bf16[768,768]{1,0:T(8,128)(2,1)S(1)}, bf16[768,768]{1,0:T(8,128)(2,1)S(1)}, u32[]{:S(2)}, u32[]{:S(2)}) collective-permute-start(bf16[768,768]{1,0:T(8,128)(2,1)S(1)} %add_convert_fusion.1), channel_id=1, source_target_pairs={{0,8},{4,20},{8,0},{12,28},{16,24},{20,4},{24,16},{28,12},{1,9},{5... | collective-permute-start | bytes 3538952 | tf_op jit(solution)/shard_map/ppermute | solution.py:748
  191.7 15.3 %collective-permute-start.48 = (bf16[352,768]{1,0:T(8,128)(2,1)S(1)}, bf16[352,768]{1,0:T(8,128)(2,1)S(1)}, u32[]{:S(2)}, u32[]{:S(2)}) collective-permute-start(bf16[352,768]{1,0:T(8,128)(2,1)S(1)} %add_convert_fusion.7), channel_id=1, source_target_pairs={{0,8},{4,20},{8,0},{12,28},{16,24},{20,4},{24,16},{28,12},{1,9},{5... | collective-permute-start | bytes 1622024 | tf_op jit(solution)/shard_map/ppermute | solution.py:748
  193.4 13.6 %collective-permute-start.46 = (bf16[384,768]{1,0:T(8,128)(2,1)S(1)}, bf16[384,768]{1,0:T(8,128)(2,1)S(1)}, u32[]{:S(2)}, u32[]{:S(2)}) collective-permute-start(bf16[384,768]{1,0:T(8,128)(2,1)S(1)} %get-tuple-element.398), channel_id=1, source_target_pairs={{0,16},{4,12},{8,24},{12,4},{16,0},{20,28},{24,8},{28,20},{1,17},{... | collective-permute-start | bytes 1769480 | tf_op jit(solution)/shard_map/ppermute | solution.py:751
  194.9 18.0 %collective-permute-start.47 = (bf16[384,768]{1,0:T(8,128)(2,1)S(1)}, bf16[384,768]{1,0:T(8,128)(2,1)S(1)}, u32[]{:S(2)}, u32[]{:S(2)}) collective-permute-start(bf16[384,768]{1,0:T(8,128)(2,1)S(1)} %get-tuple-element.399), channel_id=1, source_target_pairs={{0,16},{4,12},{8,24},{12,4},{16,0},{20,28},{24,8},{28,20},{1,17},{... | collective-permute-start | bytes 1769480 | tf_op jit(solution)/shard_map/ppermute | solution.py:751
  216.3 16.6 %collective-permute-start.52 = (bf16[176,768]{1,0:T(8,128)(2,1)S(1)}, bf16[176,768]{1,0:T(8,128)(2,1)S(1)}, u32[]{:S(2)}, u32[]{:S(2)}) collective-permute-start(bf16[176,768]{1,0:T(8,128)(2,1)S(1)} %add_convert_fusion.19), channel_id=1, source_target_pairs={{0,16},{4,12},{8,24},{12,4},{16,0},{20,28},{24,8},{28,20},{1,17},{... | collective-permute-start | bytes 811016 | tf_op jit(solution)/shard_map/ppermute | solution.py:751
  217.6 15.3 %collective-permute-start.50 = (bf16[192,768]{1,0:T(8,128)(2,1)S(1)}, bf16[192,768]{1,0:T(8,128)(2,1)S(1)}, u32[]{:S(2)}, u32[]{:S(2)}) collective-permute-start(bf16[192,768]{1,0:T(8,128)(2,1)S(1)} %add_convert_fusion.12), channel_id=1, source_target_pairs={{0,3},{1,0},{2,1},{3,2},{4,7},{5,4},{6,5},{7,6},{8,11},{9,8},{10,9... | collective-permute-start | bytes 884744 | tf_op jit(solution)/shard_map/ppermute | solution.py:736
  219.8 14.0 %collective-permute-start.51 = (bf16[192,768]{1,0:T(8,128)(2,1)S(1)}, bf16[192,768]{1,0:T(8,128)(2,1)S(1)}, u32[]{:S(2)}, u32[]{:S(2)}) collective-permute-start(bf16[192,768]{1,0:T(8,128)(2,1)S(1)} %add_convert_fusion.11), channel_id=1, source_target_pairs={{0,1},{1,2},{2,3},{3,0},{4,5},{5,6},{6,7},{7,4},{8,9},{9,10},{10,1... | collective-permute-start | bytes 884744 | tf_op jit(solution)/shard_map/ppermute | solution.py:736
  219.8 14.0 %collective-permute-start.53 = (bf16[352,768]{1,0:T(8,128)(2,1)S(1)}, bf16[352,768]{1,0:T(8,128)(2,1)S(1)}, u32[]{:S(2)}, u32[]{:S(2)}) collective-permute-start(bf16[352,768]{1,0:T(8,128)(2,1)S(1)} %add_convert_fusion.6), channel_id=1, source_target_pairs={{0,8},{4,20},{8,0},{12,28},{16,24},{20,4},{24,16},{28,12},{1,9},{5... | collective-permute-start | bytes 1622024 | tf_op jit(solution)/shard_map/ppermute | solution.py:748
  236.9 17.9 %collective-permute-start.56 = (bf16[176,768]{1,0:T(8,128)(2,1)S(1)}, bf16[176,768]{1,0:T(8,128)(2,1)S(1)}, u32[]{:S(2)}, u32[]{:S(2)}) collective-permute-start(bf16[176,768]{1,0:T(8,128)(2,1)S(1)} %add_convert_fusion.18), channel_id=1, source_target_pairs={{0,3},{1,0},{2,1},{3,2},{4,7},{5,4},{6,5},{7,6},{8,11},{9,8},{10,9... | collective-permute-start | bytes 811016 | tf_op jit(solution)/shard_map/ppermute | solution.py:736
  239.9 14.8 %collective-permute-start.57 = (bf16[176,768]{1,0:T(8,128)(2,1)S(1)}, bf16[176,768]{1,0:T(8,128)(2,1)S(1)}, u32[]{:S(2)}, u32[]{:S(2)}) collective-permute-start(bf16[176,768]{1,0:T(8,128)(2,1)S(1)} %add_convert_fusion.17), channel_id=1, source_target_pairs={{0,16},{4,12},{8,24},{12,4},{16,0},{20,28},{24,8},{28,20},{1,17},{... | collective-permute-start | bytes 811016 | tf_op jit(solution)/shard_map/ppermute | solution.py:751
  240.7 14.1 %collective-permute-start.55 = (bf16[192,768]{1,0:T(8,128)(2,1)S(1)}, bf16[192,768]{1,0:T(8,128)(2,1)S(1)}, u32[]{:S(2)}, u32[]{:S(2)}) collective-permute-start(bf16[192,768]{1,0:T(8,128)(2,1)S(1)} %add_convert_fusion.10), channel_id=1, source_target_pairs={{0,3},{1,0},{2,1},{3,2},{4,7},{5,4},{6,5},{7,6},{8,11},{9,8},{10,9... | collective-permute-start | bytes 884744 | tf_op jit(solution)/shard_map/ppermute | solution.py:736
  241.0 13.8 %collective-permute-start.58 = (bf16[352,768]{1,0:T(8,128)(2,1)S(1)}, bf16[352,768]{1,0:T(8,128)(2,1)S(1)}, u32[]{:S(2)}, u32[]{:S(2)}) collective-permute-start(bf16[352,768]{1,0:T(8,128)(2,1)S(1)} %add_convert_fusion.5), channel_id=1, source_target_pairs={{0,8},{4,20},{8,0},{12,28},{16,24},{20,4},{24,16},{28,12},{1,9},{5... | collective-permute-start | bytes 1622024 | tf_op jit(solution)/shard_map/ppermute | solution.py:748
  258.7 15.2 %collective-permute-start.60 = (bf16[512,768]{1,0:T(8,128)(2,1)S(1)}, bf16[512,768]{1,0:T(8,128)(2,1)S(1)}, u32[]{:S(2)}, u32[]{:S(2)}) collective-permute-start(bf16[512,768]{1,0:T(8,128)(2,1)S(1)} %add_convert_fusion.2), channel_id=1, source_target_pairs={{0,8},{4,20},{8,0},{12,28},{16,24},{20,4},{24,16},{28,12},{1,9},{5... | collective-permute-start | bytes 2359304 | tf_op jit(solution)/shard_map/ppermute | solution.py:748
  260.7 13.2 %collective-permute-start.63 = (bf16[192,768]{1,0:T(8,128)(2,1)S(1)}, bf16[192,768]{1,0:T(8,128)(2,1)S(1)}, u32[]{:S(2)}, u32[]{:S(2)}) collective-permute-start(bf16[192,768]{1,0:T(8,128)(2,1)S(1)} %add_convert_fusion.9.refs_0_), channel_id=1, source_target_pairs={{0,8},{4,20},{8,0},{12,28},{16,24},{20,4},{24,16},{28,12},{1,9},{5... | collective-permute-start | bytes 884744 | tf_op jit(solution)/shard_map/ppermute | solution.py:748
  273.9 13.0 %collective-permute-start.66 = (bf16[192,768]{1,0:T(8,128)(2,1)S(1)}, bf16[192,768]{1,0:T(8,128)(2,1)S(1)}, u32[]{:S(2)}, u32[]{:S(2)}) collective-permute-start(bf16[192,768]{1,0:T(8,128)(2,1)S(1)} %add_convert_fusion.9.refs_0_), channel_id=1, source_target_pairs={{0,16},{4,12},{8,24},{12,4},{16,0},{20,28},{24,8},{28,20},{1,17},{... | collective-permute-start | bytes 884744 | tf_op jit(solution)/shard_map/ppermute | solution.py:751
  275.2 11.8 %collective-permute-start.67 = (bf16[192,768]{1,0:T(8,128)(2,1)S(1)}, bf16[192,768]{1,0:T(8,128)(2,1)S(1)}, u32[]{:S(2)}, u32[]{:S(2)}) collective-permute-start(bf16[192,768]{1,0:T(8,128)(2,1)S(1)} %collective-permute-done.63.refs_1_), channel_id=1, source_target_pairs={{0,16},{4,12},{8,24},{12,4},{16,0},{20,28},{24,8},{28,20},{1,17},{... | collective-permute-start | bytes 884744 | tf_op jit(solution)/shard_map/ppermute | solution.py:751
  276.1 11.9 %collective-permute-start.64 = (bf16[256,768]{1,0:T(8,128)(2,1)S(1)}, bf16[256,768]{1,0:T(8,128)(2,1)S(1)}, u32[]{:S(2)}, u32[]{:S(2)}) collective-permute-start(bf16[256,768]{1,0:T(8,128)(2,1)S(1)} %add_convert_fusion.8), channel_id=1, source_target_pairs={{0,16},{4,12},{8,24},{12,4},{16,0},{20,28},{24,8},{28,20},{1,17},{... | collective-permute-start | bytes 1179656 | tf_op jit(solution)/shard_map/ppermute | solution.py:751
  277.6 9.4 %collective-permute-start.65 = (bf16[176,768]{1,0:T(8,128)(2,1)S(1)}, bf16[176,768]{1,0:T(8,128)(2,1)S(1)}, u32[]{:S(2)}, u32[]{:S(2)}) collective-permute-start(bf16[176,768]{1,0:T(8,128)(2,1)S(1)} %add_convert_fusion.14), channel_id=1, source_target_pairs={{0,1},{1,2},{2,3},{3,0},{4,5},{5,6},{6,7},{7,4},{8,9},{9,10},{10,1... | collective-permute-start | bytes 811016 | tf_op jit(solution)/shard_map/ppermute | solution.py:736
  288.3 15.5 %collective-permute-start.72 = (bf16[176,768]{1,0:T(8,128)(2,1)S(1)}, bf16[176,768]{1,0:T(8,128)(2,1)S(1)}, u32[]{:S(2)}, u32[]{:S(2)}) collective-permute-start(bf16[176,768]{1,0:T(8,128)(2,1)S(1)} %add_convert_fusion.13.refs_0_), channel_id=1, source_target_pairs={{0,16},{4,12},{8,24},{12,4},{16,0},{20,28},{24,8},{28,20},{1,17},{... | collective-permute-start | bytes 811016 | tf_op jit(solution)/shard_map/ppermute | solution.py:751
  289.6 14.2 %collective-permute-start.71 = (bf16[176,768]{1,0:T(8,128)(2,1)S(1)}, bf16[176,768]{1,0:T(8,128)(2,1)S(1)}, u32[]{:S(2)}, u32[]{:S(2)}) collective-permute-start(bf16[176,768]{1,0:T(8,128)(2,1)S(1)} %add_convert_fusion.13.refs_0_), channel_id=1, source_target_pairs={{0,8},{4,20},{8,0},{12,28},{16,24},{20,4},{24,16},{28,12},{1,9},{5... | collective-permute-start | bytes 811016 | tf_op jit(solution)/shard_map/ppermute | solution.py:748
  293.1 10.7 %collective-permute-start.69 = (bf16[80,768]{1,0:T(8,128)(2,1)S(1)}, bf16[80,768]{1,0:T(8,128)(2,1)S(1)}, u32[]{:S(2)}, u32[]{:S(2)}) collective-permute-start(bf16[80,768]{1,0:T(8,128)(2,1)S(1)} %add_convert_fusion.21), channel_id=1, source_target_pairs={{0,2},{1,3},{2,0},{3,1},{4,6},{5,7},{6,4},{7,5},{8,10},{9,11},{10,... | collective-permute-start | bytes 368648 | tf_op jit(solution)/shard_map/ppermute | solution.py:739
  294.8 9.0 %collective-permute-start.68 = (bf16[80,768]{1,0:T(8,128)(2,1)S(1)}, bf16[80,768]{1,0:T(8,128)(2,1)S(1)}, u32[]{:S(2)}, u32[]{:S(2)}) collective-permute-start(bf16[80,768]{1,0:T(8,128)(2,1)S(1)} %add_convert_fusion.21), channel_id=1, source_target_pairs={{0,1},{1,0},{2,3},{3,2},{4,5},{5,4},{6,7},{7,6},{8,9},{9,8},{10,11... | collective-permute-start | bytes 368648 | tf_op jit(solution)/shard_map/ppermute | solution.py:739
  303.8 9.2 %collective-permute-start.75 = (bf16[176,768]{1,0:T(8,128)(2,1)S(1)}, bf16[176,768]{1,0:T(8,128)(2,1)S(1)}, u32[]{:S(2)}, u32[]{:S(2)}) collective-permute-start(bf16[176,768]{1,0:T(8,128)(2,1)S(1)} %collective-permute-done.71.refs_1_), channel_id=1, source_target_pairs={{0,16},{4,12},{8,24},{12,4},{16,0},{20,28},{24,8},{28,20},{1,17},{... | collective-permute-start | bytes 811016 | tf_op jit(solution)/shard_map/ppermute | solution.py:751
  (126 other events, 1421.7 us)

commit v8 on v7

--- a/solution.py
+++ b/solution.py
@@ -89,8 +89,9 @@
     pairs = []
     for piece, code in zip(pieces, (0, first, second, 3, 4, 4 + second, 4 + first, 7)):
         row = lax.bitwise_xor(part, jnp.int32(code)) * unit
+        ref, begin = piece if isinstance(piece, tuple) else (piece, skip)
         for t, target in enumerate(targets):
-            pairs.append((piece.at[pl.ds(skip + t * unit, unit)], target.at[rows_at(row, unit)]))
+            pairs.append((ref.at[pl.ds(begin + t * unit, unit)], target.at[rows_at(row, unit)]))
     return pairs
 
 
@@ -674,9 +675,10 @@
 
 
 def spread_hidden_kernel(info_ref, *refs):
-    pieces = refs[:8]
-    up_ref, down_ref, up_s, down_s, sem = refs[8:]
-    wait(start(place(pieces, info_ref, up_ref.shape[0] // 8, (up_s, down_s)), sem))
+    up_ref, down_ref, up_s, down_s, sem = refs[5:]
+    unit = up_ref.shape[0] // 8
+    pieces = refs[:4] + tuple((refs[4], 2 * unit * i) for i in range(4))
+    wait(start(place(pieces, info_ref, unit, (up_s, down_s)), sem))
     up_ref[...] = up_s[...].astype(F32)
     down_ref[...] = down_s[...].astype(F32)
 
@@ -686,7 +688,7 @@
     out = shape((4 * rows, width), F32)
     return pl.pallas_call(
         spread_hidden_kernel,
-        in_specs=[SMEM] + [HBM] * 8,
+        in_specs=[SMEM] + [HBM] * 5,
         out_specs=[VMEM] * 2,
         out_shape=(out, out),
         scratch_shapes=[pltpu.VMEM((4 * rows, width), BF16)] * 2 + [DMA],
@@ -841,7 +843,8 @@
     acc = attend_one(0, acc, own, small)
     acc, v1, v3 = sync(acc, v1, v3)
     a1, b1, v2 = first(v1), second(v1), shift(v1, 1)
-    acc, v1, a1, b1, v3, f1, f3 = sync(acc, v1, a1, b1, v3, f1, f3)
+    vec = jnp.stack([norm1_gain, norm1_bias, down_b, norm2_gain, norm2_bias] + [down_b] * 3)
+    acc, v1, a1, b1, v3, f1, f3, vec = sync(acc, v1, a1, b1, v3, f1, f3, vec)
     c1, kv, ka, kb, a3, b3 = second(a1), core(v1), core(a1), core(b1), first(v3), second(v3)
     acc, c1, kv, ka, kb, v2, f1, v3 = sync(acc, c1, kv, ka, kb, v2, f1, v3)
     kc, f2 = core(c1), shift(f1, 1)
@@ -872,7 +875,6 @@
     )
     query_groups = (own, group_1, group_2, group_3)
 
-    vec = jnp.stack([norm1_gain, norm1_bias, down_b, norm2_gain, norm2_bias] + [down_b] * 3)
     normed_t, act_t, slope, up, down, out_words, out_ents, mixed_low, acc, sums = hidden(
         info, attended, vec, word_mask, entity_mask, cot_words, cot_entities, biases, (up_w, down_w), ffn_pieces
     )
@@ -895,25 +897,29 @@
 
     fa, acc = ffn_blocks((2, 1), acc)
     fa.got = core(fa.send)
-    fb, acc = ffn_blocks((3, 0), acc)
+    fb, acc = ffn_blocks((3,), acc)
     acc, fa.got = sync(acc, fa.got)
     acc, one_a = sync(acc, fa.one())
 
     fa.a, fb.got = first(one_a), core(fb.send)
+    fc, acc = ffn_blocks((0,), acc)
+    acc, fb.got = sync(acc, fb.got)
+    one_b = fb.one()
+    fc.got = core(fc.send)
     acc, attended_low, sums = norm_back(attended, acc, vec, sums)
-    acc, fb.got = sync(acc, fb.got)
-    acc, one_b = sync(acc, fb.one())
-
-    fb.a = first(one_b)
+    acc, one_b, fc.got = sync(acc, one_b, fc.got)
+    acc, one_c = sync(acc, fc.one())
+
+    fb.a, fc.a = first(one_b), first(one_c)
     q1, acc = back(2, acc)
-    acc, q1.send, fa.a, fb.a = sync(acc, q1.send, fa.a, fb.a)
+    acc, q1.send, fa.a, fb.a, fc.a = sync(acc, q1.send, fa.a, fb.a, fc.a)
     q1.got = core(q1.send)
-    acc, two_a, two_b, q1.got = sync(acc, fa.two(), fb.two(), q1.got)
+    acc, two_a, two_b, two_c, q1.got = sync(acc, fa.two(), fb.two(), fc.two(), q1.got)
     acc, one_1 = sync(acc, q1.one())
 
-    fa.b, fb.b, q1.a = second(two_a), second(two_b), first(one_1)
+    fa.b, fb.b, fc.b, q1.a = second(two_a), second(two_b), second(two_c), first(one_1)
     q2, acc = back(1, acc)
-    acc, q2.send, fa.b, fb.b, q1.a = sync(acc, q2.send, fa.b, fb.b, q1.a)
+    acc, q2.send, fa.b, fb.b, fc.b, q1.a = sync(acc, q2.send, fa.b, fb.b, fc.b, q1.a)
     q2.got = core(q2.send)
     acc, r2, r3, two_1, q2.got = sync(acc, fa.rest(0, size), fb.rest(0, size), q1.two(), q2.got)
     acc, one_2 = sync(acc, q2.one())
@@ -931,7 +937,7 @@
 
     q4.got = core(q4.send)
     y1, q3.b = shift(q2.rest(0, unit, y2), -1), second(q3.two())
-    own_f = fb.rest(size, 2 * size, z1, z3)
+    own_f = fc.rest(0, size, z1, z3)
     q4.a, ga = first(q4.one()), first(own_f)
     q4.a, q3.b, y1, ga, own_f = sync(q4.a, q3.b, y1, ga, own_f)
 
@@ -941,21 +947,21 @@
     pos = q4.rest(unit, q4.unit)
     own_q = q4.rest(0, unit, y1, y3)
     p1, p2, p3 = (links.swap_z(pos, mask) for mask in (1, 2, 3))
-    qa, qb = first(own_q), second(own_q)
-    p1, p2, p3, qa, qb, own_q, pos, own_f, ga, gb, gc = sync(p1, p2, p3, qa, qb, own_q, pos, own_f, ga, gb, gc)
+    near_f = (own_f, ga, gb, gc)
+    qa, far_f = first(own_q), core(jnp.concatenate(near_f, 0))
+    p1, p2, p3, qa, own_q, pos, far_f = sync(p1, p2, p3, qa, own_q, pos, far_f)
 
     pos = ((pos.astype(F32) + p1.astype(F32)) + (p2.astype(F32) + p3.astype(F32))).astype(BF16)
-    pa, pb, qc, kf, kg = first(pos), second(pos), second(qa), core(own_f), core(ga)
-    pa, pb, qc, kf, kg, pos, own_q, qa, qb, gb, gc = sync(pa, pb, qc, kf, kg, pos, own_q, qa, qb, gb, gc)
-    pc, kh, ki, kv, ka = second(pa), core(gb), core(gc), core(own_q), core(qa)
-    pc, kh, ki, kv, ka, qb, qc, pos, pa, pb = sync(pc, kh, ki, kv, ka, qb, qc, pos, pa, pb)
-    kb, kc = core(qb), core(qc)
+    pa, pb, qb, qc = first(pos), second(pos), second(own_q), second(qa)
+    grad_up, grad_down = spread_hidden(info, near_f + (far_f,))
+    pa, pb, qb, qc, pos, own_q, qa, grad_up, grad_down = sync(pa, pb, qb, qc, pos, own_q, qa, grad_up, grad_down)
+    pc, kv, ka, kb, kc = second(pa), core(own_q), core(qa), core(qb), core(qc)
+    kv, ka, kb, kc, pos, pa, pb, pc = sync(kv, ka, kb, kc, pos, pa, pb, pc)
     kp = tuple(core(v) for v in (pos, pa, pb, pc))
-    grad_up, grad_down = spread_hidden(info, (own_f, ga, gb, gc, kf, kg, kh, ki))
-    kb, kc, grad_up, grad_down, *kp = sync(kb, kc, grad_up, grad_down, *kp)
     grad_query_t, grad_key_t, grad_value_t, grad_out, grad_query_b, grad_value_b, grad_up_b = spread_query(
         info, (own_q, qa, qb, qc, kv, ka, kb, kc), gw
     )
+    grad_query_t, *kp = sync(grad_query_t, *kp)
     pos_sum, total_sums = spread_pos(info, (pos, pa, pb, pc, *kp))
     return (
         out_words,

time: 341 us -> 337 us (0.988)
  waiting for transfers between devices: 101 us -> 94.2 us
    another operation x6, local copies, waits for them, and re-layouts: 3.79 us -> 0.08 us  [shards(): jnp.stack([norm1_gain, norm1_bias, down_b, norm2_gain, norm2_bias] + [dow...]
    ppermute x22 -> x23, waiting for transfers between devices: 32 us -> 28.7 us  [second(): lax.ppermute(v, 'dp', [(i, i ^ (2 if i % 2 else 4)) for i in range(self.d...]
    ppermute x14 -> x15, waiting for transfers between devices: 20.8 us -> 17.6 us  [first(): lax.ppermute(v, 'dp', [(i, i ^ (4 if i % 2 else 2)) for i in range(self.d...]
    ppermute x14 -> x15, starting transfers between devices: 15.5 us -> 18.5 us  [first(): lax.ppermute(v, 'dp', [(i, i ^ (4 if i % 2 else 2)) for i in range(self.d...]
    ppermute x38 -> x36, starting transfers between devices: 8.99 us -> 7.88 us  [swap(): return lax.ppermute(v, 'dp', [(i, i ^ code) for i in range(self.dp)])]
    ppermute x38 -> x36, waiting for transfers between devices: 15.2 us -> 14.2 us  [swap(): return lax.ppermute(v, 'dp', [(i, i ^ code) for i in range(self.dp)])]
    pallas_call x2 -> x3, Pallas kernels: 19 us -> 19.8 us  [hidden_back(): pl.pallas_call(partial(hidden_back_kernel, pair), in_specs=[SMEM] + [VMEM...]
    ppermute x22 -> x23, starting transfers between devices: 26.3 us -> 26.9 us  [second(): lax.ppermute(v, 'dp', [(i, i ^ (2 if i % 2 else 4)) for i in range(self.d...]
  transfers between devices with their start and end apart: 89 -> 89, of which waited for: 31 -> 30; matrix products, arithmetic and copies ran while one was open for 2% -> 2% of each run, Pallas kernels for 31% -> 33%
where the time goes in v8:
time: 337 us; the launch traced here: 331 us
  Pallas kernels  143 us (42%)
  waiting for transfers between devices  94.2 us (28%)
  starting transfers between devices  78.8 us (23%)
  local copies, waits for them, and re-layouts  7.27 us (2%)
  other arithmetic  5.42 us (2%)
    pallas_call x4, Pallas kernels, attend_back(): pl.pallas_call(partial(attend_back_kernel, words, gw, heads, final, count...  48.1 us
    pallas_call x4, Pallas kernels, attend(): pl.pallas_call(partial(attend_kernel, words, gw, heads, count), in_specs=...  37.3 us
    ppermute x23, waiting for transfers between devices, second(): lax.ppermute(v, 'dp', [(i, i ^ (2 if i % 2 else 4)) for i in range(self.d...  28.7 us
    ppermute x23, starting transfers between devices, second(): lax.ppermute(v, 'dp', [(i, i ^ (2 if i % 2 else 4)) for i in range(self.d...  26.9 us
    ppermute x12, waiting for transfers between devices, shift_z(): return lax.ppermute(v, 'tensor', [(i, (i + by) % n) for i in range(n)])  23.6 us
    ppermute x12, starting transfers between devices, shift_z(): return lax.ppermute(v, 'tensor', [(i, (i + by) % n) for i in range(n)])  21.1 us
    pallas_call x3, Pallas kernels, hidden_back(): pl.pallas_call(partial(hidden_back_kernel, pair), in_specs=[SMEM] + [VMEM...  19.8 us
    pallas_call x1, Pallas kernels, hidden(): pl.pallas_call(partial(hidden_kernel, n), in_specs=[SMEM] + [VMEM] * (6 +...  19.8 us
  transfers between devices with their start and end apart: 89, of which 30 were waited for; matrix products, arithmetic and copies ran while one was open for 2% of the time, Pallas kernels for 33%

profile of v8, /device:TPU:0, one launch (start us, length us, event | category | flops | bytes accessed | tf_op | source)
XLA Modules:
  0.0 330.9 jit_solution(1196060317733040200)
XLA Ops:
  2.8 2.4 pack.1
  5.3 5.1 %collective-permute-start.1 = (bf16[176,768]{1,0:T(8,128)(2,1)}, bf16[176,768]{1,0:T(8,128)(2,1)S(1)}, u32[]{:S(2)}, u32[]{:S(2)}) collective-permute-start(bf16[176,768]{1,0:T(8,128)(2,1)} %get-tuple-element.272), channel_id=1, source_target_pairs={{0,3},{1,0},{2,1},{3,2},{4,7},{5,4},{6,5},{7,6},{8,11},{9,8},{10,9... | collective-permute-start | bytes 811016 | tf_op jit(solution)/shard_map/ppermute | solution.py:738
  10.6 2.2 start_rows.1
  12.8 3.9 %collective-permute-start.5 = (bf16[192,768]{1,0:T(8,128)(2,1)}, bf16[192,768]{1,0:T(8,128)(2,1)}, u32[]{:S(2)}, u32[]{:S(2)}) collective-permute-start(bf16[192,768]{1,0:T(8,128)(2,1)} %get-tuple-element.276), channel_id=1, source_target_pairs={{0,3},{1,0},{2,1},{3,2},{4,7},{5,4},{6,5},{7,6},{8,11},{9,8},{10,9... | collective-permute-start | bytes 884744 | tf_op jit(solution)/shard_map/ppermute | solution.py:738
  16.8 9.1 %attend_own.1 = (bf16[512,768]{1,0:T(8,128)(2,1)}, bf16[128,768]{1,0:T(8,128)(2,1)}, bf16[640,192]{1,0:T(8,128)(2,1)}, f32[8,640]{1,0:T(8,128)S(1)}, bf16[16,768...) custom-call(s32[4]{0:T(128)S(1)} %pad_add_fusion.info_ref, ...), custom_call_target="tpu_custom_call", output_to_operand_aliasing={{5}: (2, {})} | custom-call | flops 8000000000 | bytes 6000000 | tf_op jit(solution)/shard_map/attend_own/pallas_call | solution.py:285
  29.7 7.2 %collective-permute-done.4 = bf16[192,768]{1,0:T(8,128)(2,1)} collective-permute-done((bf16[192,768]{1,0:T(8,128)(2,1)}, bf16[192,768]{1,0:T(8,128)(2,1)}, u32[]{:S(2)}, u32[]{:S(2)}) %collective-permute-start.4) | collective-permute-done | bytes 294944 | tf_op jit(solution)/shard_map/ppermute | solution.py:738
  39.1 2.4 collective-permute-done.10.refs_0_.refs_3_
  41.6 2.7 collective-permute-done.6.refs_3_.refs_6_
  44.2 1.7 collective-permute-start.19
  49.0 6.1 %collective-permute-done.13.refs_2_.refs_5_ = bf16[176,768]{1,0:T(8,128)(2,1)S(1)} collective-permute-done((bf16[176,768]{1,0:T(8,128)(2,1)}, bf16[176,768]{1,0:T(8,128)(2,1)S(1)}, u32[]{:S(2)}, u32[]{:S(2)}) %collective-permute-start.13) | collective-permute-done | bytes 270368 | tf_op jit(solution)/shard_map/ppermute | solution.py:753
  60.8 9.4 %attend_far.3 = (bf16[512,768]{1,0:T(8,128)(2,1)}, bf16[128,768]{1,0:T(8,128)(2,1)}, bf16[640,192]{1,0:T(8,128)(2,1)}, f32[8,640]{1,0:T(8,128)S(1)}, bf16[16,768...) custom-call(s32[4]{0:T(128)S(1)} %pad_add_fusion.info_ref, ...), custom_call_target="tpu_custom_call", output_to_operand_aliasing={{5}: (2, {})} | custom-call | flops 8000000000 | bytes 6000000 | tf_op jit(solution)/shard_map/attend_far/pallas_call | solution.py:285
  78.4 9.4 %attend_far.4 = (bf16[512,768]{1,0:T(8,128)(2,1)}, bf16[128,768]{1,0:T(8,128)(2,1)}, bf16[640,192]{1,0:T(8,128)(2,1)}, f32[8,640]{1,0:T(8,128)S(1)}, bf16[16,768...) custom-call(s32[4]{0:T(128)S(1)} %pad_add_fusion.info_ref, ...), custom_call_target="tpu_custom_call", output_to_operand_aliasing={{5}: (2, {})} | custom-call | flops 8000000000 | bytes 6000000 | tf_op jit(solution)/shard_map/attend_far/pallas_call | solution.py:285
  87.9 2.0 collective-permute-done.26.refs_7_
  95.0 9.4 %attend_far.5 = (bf16[512,768]{1,0:T(8,128)(2,1)}, bf16[128,768]{1,0:T(8,128)(2,1)}, bf16[640,192]{1,0:T(8,128)(2,1)}, f32[8,640]{1,0:T(8,128)S(1)}, bf16[16,768...) custom-call(s32[4]{0:T(128)S(1)} %pad_add_fusion.info_ref, ...), custom_call_target="tpu_custom_call", output_to_operand_aliasing={{5}: (2, {})} | custom-call | flops 8000000000 | bytes 6000000 | tf_op jit(solution)/shard_map/attend_far/pallas_call | solution.py:285
  104.5 4.7 %collective-permute-done.32.refs_9_ = bf16[384,768]{1,0:T(8,128)(2,1)S(1)} collective-permute-done((bf16[384,768]{1,0:T(8,128)(2,1)S(1)}, bf16[384,768]{1,0:T(8,128)(2,1)S(1)}, u32[]{:S(2)}, u32[]{:S(2)}) %collective-permute-start.32) | collective-permute-done | bytes 589856 | tf_op jit(solution)/shard_map/ppermute | solution.py:753
  110.3 3.9 %collective-permute-done.40.refs_21_ = bf16[192,768]{1,0:T(8,128)(2,1)S(1)} collective-permute-done((bf16[192,768]{1,0:T(8,128)(2,1)S(1)}, bf16[192,768]{1,0:T(8,128)(2,1)S(1)}, u32[]{:S(2)}, u32[]{:S(2)}) %collective-permute-start.40) | collective-permute-done | bytes 294944 | tf_op jit(solution)/shard_map/ppermute | solution.py:744
  115.7 19.8 %hidden.1 = (bf16[768,640]{1,0:T(8,128)(2,1)S(1)}, bf16[4,768,640]{2,1,0:T(8,128)(2,1)S(1)}, f32[4,640,768]{2,1,0:T(8,128)S(1)}, bf16[4,768,768]{2,1,0:T(8,128)(...) custom-call(s32[4]{0:T(128)S(1)} %pad_add_fusion.info_ref, ...), custom_call_target="tpu_custom_call" | custom-call | flops 22000001024 | bytes 20000000 | tf_op jit(solution)/shard_map/hidden/pallas_call | solution.py:394
  135.4 9.5 %hidden_back.3 = (bf16[1536,768]{1,0:T(8,128)(2,1)}, bf16[768,768]{1,0:T(8,128)(2,1)}, bf16[768,768]{1,0:T(8,128)(2,1)}, f32[640,768]{1,0:T(8,128)S(1)}, f32[16,768]{1,0:T(8,128)S(1)}) custom-call(s32[4]{0:T(128)S(1)} %pad_add_fusion.info_ref, bf16[640,768]{1,0:T(8,128)(2,1)S(1)} %get-tuple-element.351.low_ref, ...), custom_call_target="tpu_custom_call", output_to_operand_aliasing={{3}: (7, {})} | custom-call | flops 14000000000 | bytes 16000000 | tf_op jit(solution)/shard_map/hidden_back/pallas_call | solution.py:455
  145.2 5.1 %hidden_back.4 = (bf16[768,768]{1,0:T(8,128)(2,1)}, bf16[384,768]{1,0:T(8,128)(2,1)}, bf16[384,768]{1,0:T(8,128)(2,1)}, f32[640,768]{1,0:T(8,128)S(1)}, f32[8,768]{1,0:T(8,128)S(1)}) custom-call(s32[4]{0:T(128)S(1)} %pad_add_fusion.info_ref, bf16[640,768]{1,0:T(8,128)(2,1)S(1)} %get-tuple-element.351.low_ref, ...), custom_call_target="tpu_custom_call", output_to_operand_aliasing={{3}: (7, {})} | custom-call | flops 7000000000 | bytes 8000000 | tf_op jit(solution)/shard_map/hidden_back/pallas_call | solution.py:455
  151.1 5.1 %hidden_back.5 = (bf16[768,768]{1,0:T(8,128)(2,1)}, bf16[384,768]{1,0:T(8,128)(2,1)}, bf16[384,768]{1,0:T(8,128)(2,1)}, f32[640,768]{1,0:T(8,128)S(1)}, f32[8,768]{1,0:T(8,128)S(1)}) custom-call(s32[4]{0:T(128)S(1)} %pad_add_fusion.info_ref, bf16[640,768]{1,0:T(8,128)(2,1)S(1)} %get-tuple-element.351.low_ref, ...), custom_call_target="tpu_custom_call", output_to_operand_aliasing={{3}: (7, {})} | custom-call | flops 7000000000 | bytes 8000000 | tf_op jit(solution)/shard_map/hidden_back/pallas_call | solution.py:455
  156.4 1.7 collective-permute-start.44
  162.8 11.8 %attend_back.4 = (bf16[704,768]{1,0:T(8,128)(2,1)}, bf16[352,768]{1,0:T(8,128)(2,1)}, bf16[352,768]{1,0:T(8,128)(2,1)}, f32[640,768]{1,0:T(8,128)S(1)}) custom-call(s32[4]{0:T(128)S(1)} %pad_add_fusion.info_ref, bf16[640,768]{1,0:T(8,128)(2,1)S(1)} %get-tuple-element.267.rows_ref, ...), custom_call_target="tpu_custom_call", output_to_operand_aliasing={{3}: (5, {})} | custom-call | flops 11000000512 | bytes 8000000 | tf_op jit(solution)/shard_map/attend_back/pallas_call | solution.py:607
  174.6 4.3 %collective-permute-done.46 = bf16[384,768]{1,0:T(8,128)(2,1)S(1)} collective-permute-done((bf16[384,768]{1,0:T(8,128)(2,1)S(1)}, bf16[384,768]{1,0:T(8,128)(2,1)S(1)}, u32[]{:S(2)}, u32[]{:S(2)}) %collective-permute-start.46) | collective-permute-done | bytes 589856 | tf_op jit(solution)/shard_map/ppermute | solution.py:750
  178.9 6.3 %collective-permute-done.45 = bf16[384,768]{1,0:T(8,128)(2,1)S(1)} collective-permute-done((bf16[384,768]{1,0:T(8,128)(2,1)S(1)}, bf16[384,768]{1,0:T(8,128)(2,1)S(1)}, u32[]{:S(2)}, u32[]{:S(2)}) %collective-permute-start.45) | collective-permute-done | bytes 589856 | tf_op jit(solution)/shard_map/ppermute | solution.py:750
  190.4 1.7 collective-permute-start.51
  193.6 11.6 %attend_back.5 = (bf16[704,768]{1,0:T(8,128)(2,1)}, bf16[352,768]{1,0:T(8,128)(2,1)}, bf16[352,768]{1,0:T(8,128)(2,1)}, f32[640,768]{1,0:T(8,128)S(1)}) custom-call(s32[4]{0:T(128)S(1)} %pad_add_fusion.info_ref, bf16[640,768]{1,0:T(8,128)(2,1)S(1)} %get-tuple-element.267.rows_ref, ...), custom_call_target="tpu_custom_call", output_to_operand_aliasing={{3}: (5, {})} | custom-call | flops 11000000512 | bytes 8000000 | tf_op jit(solution)/shard_map/attend_back/pallas_call | solution.py:607
  205.6 4.8 %collective-permute-done.48 = bf16[384,768]{1,0:T(8,128)(2,1)S(1)} collective-permute-done((bf16[384,768]{1,0:T(8,128)(2,1)S(1)}, bf16[384,768]{1,0:T(8,128)(2,1)S(1)}, u32[]{:S(2)}, u32[]{:S(2)}) %collective-permute-start.48) | collective-permute-done | bytes 589856 | tf_op jit(solution)/shard_map/ppermute | solution.py:753
  210.8 2.5 collective-permute-done.52
  215.0 2.2 collective-permute-start.53
  218.9 11.4 %attend_back.6 = (bf16[704,768]{1,0:T(8,128)(2,1)}, bf16[352,768]{1,0:T(8,128)(2,1)}, bf16[352,768]{1,0:T(8,128)(2,1)}, f32[640,768]{1,0:T(8,128)S(1)}) custom-call(s32[4]{0:T(128)S(1)} %pad_add_fusion.info_ref, bf16[640,768]{1,0:T(8,128)(2,1)S(1)} %get-tuple-element.267.rows_ref, ...), custom_call_target="tpu_custom_call", output_to_operand_aliasing={{3}: (5, {})} | custom-call | flops 11000000512 | bytes 8000000 | tf_op jit(solution)/shard_map/attend_back/pallas_call | solution.py:607
  231.2 2.5 collective-permute-done.57
  233.8 3.5 %collective-permute-start.59 = (bf16[176,768]{1,0:T(8,128)(2,1)S(1)}, bf16[176,768]{1,0:T(8,128)(2,1)S(1)}, u32[]{:S(2)}, u32[]{:S(2)}) collective-permute-start(bf16[176,768]{1,0:T(8,128)(2,1)S(1)} %add_convert_fusion.20), channel_id=1, source_target_pairs={{0,3},{1,0},{2,1},{3,2},{4,7},{5,4},{6,5},{7,6},{8,11},{9,8},{10,9... | collective-permute-start | bytes 811016 | tf_op jit(solution)/shard_map/ppermute | solution.py:738
  238.7 13.4 %attend_back.7 = (bf16[1024,768]{1,0:T(8,128)(2,1)}, bf16[512,768]{1,0:T(8,128)(2,1)}, bf16[512,768]{1,0:T(8,128)(2,1)}, f32[512,768]{1,0:T(8,128)}, f32[128,768]{1,0:T(8,128)}) custom-call(s32[4]{0:T(128)S(1)} %pad_add_fusion.info_ref, bf16[640,768]{1,0:T(8,128)(2,1)S(1)} %get-tuple-element.267.rows_ref, f32[8,640]{1,0:T(8,128)S(1)} %get-tuple-element.350.lt_ref, ...), custom_call_target="tpu_custom_call" | custom-call | flops 11000000512 | bytes 8000000 | tf_op jit(solution)/shard_map/attend_back/pallas_call | solution.py:607
  253.8 2.1 collective-permute-done.62
  258.7 2.0 collective-permute-start.65
  260.7 6.0 %collective-permute-done.65 = bf16[176,768]{1,0:T(8,128)(2,1)S(1)} collective-permute-done((bf16[176,768]{1,0:T(8,128)(2,1)S(1)}, bf16[176,768]{1,0:T(8,128)(2,1)S(1)}, u32[]{:S(2)}, u32[]{:S(2)}) %collective-permute-start.65) | collective-permute-done | bytes 270368 | tf_op jit(solution)/shard_map/ppermute | solution.py:738
  266.7 4.6 %collective-permute-done.66.refs_1_ = bf16[192,768]{1,0:T(8,128)(2,1)S(1)} collective-permute-done((bf16[192,768]{1,0:T(8,128)(2,1)S(1)}, bf16[192,768]{1,0:T(8,128)(2,1)S(1)}, u32[]{:S(2)}, u32[]{:S(2)}) %collective-permute-start.66) | collective-permute-done | bytes 294944 | tf_op jit(solution)/shard_map/ppermute | solution.py:750
  275.0 2.3 collective-permute-start.68
  277.3 6.9 %collective-permute-done.68 = bf16[176,768]{1,0:T(8,128)(2,1)S(1)} collective-permute-done((bf16[176,768]{1,0:T(8,128)(2,1)S(1)}, bf16[176,768]{1,0:T(8,128)(2,1)S(1)}, u32[]{:S(2)}, u32[]{:S(2)}) %collective-permute-start.68) | collective-permute-done | bytes 270368 | tf_op jit(solution)/shard_map/ppermute | solution.py:738
  287.5 2.0 collective-permute-start.73
  292.0 3.7 %collective-permute-done.73 = bf16[80,768]{1,0:T(8,128)(2,1)S(1)} collective-permute-done((bf16[80,768]{1,0:T(8,128)(2,1)S(1)}, bf16[80,768]{1,0:T(8,128)(2,1)S(1)}, u32[]{:S(2)}, u32[]{:S(2)}) %collective-permute-start.73) | collective-permute-done | bytes 122912 | tf_op jit(solution)/shard_map/ppermute | solution.py:741
  295.6 6.4 %collective-permute-done.72 = bf16[80,768]{1,0:T(8,128)(2,1)S(1)} collective-permute-done((bf16[80,768]{1,0:T(8,128)(2,1)S(1)}, bf16[80,768]{1,0:T(8,128)(2,1)S(1)}, u32[]{:S(2)}, u32[]{:S(2)}) %collective-permute-start.72) | collective-permute-done | bytes 122912 | tf_op jit(solution)/shard_map/ppermute | solution.py:741
  304.8 1.7 collective-permute-start.76
  306.5 4.6 %spread_hidden.1 = (f32[768,768]{1,0:T(8,128)}, f32[768,768]{1,0:T(8,128)}) custom-call(s32[4]{0:T(128)S(1)} %pad_add_fusion.info_ref, bf16[192,768]{1,0:T(8,128)(2,1)} %copy-done.6, bf16[192,768]{1,0:T(8,128)(2,1)} %copy-done.7, bf16[192,768]{1,0:T(8,128)(2,1)} %copy-done.8, bf16[192,768]{1,0:T(8,128)(2,1)} %copy-done.9, bf16[768,768]{1,0:T(8,128)(2,1)} %copy-done.12), custom_call_target="tpu_custom_call" | custom-call | flops 500000000 | bytes 7000000 | tf_op jit(solution)/shard_map/spread_hidden/pallas_call | solution.py:689
  311.1 3.1 collective-permute-done.77.refs_2_
  315.8 4.4 %collective-permute-done.84.refs_3_ = bf16[80,768]{1,0:T(8,128)(2,1)S(1)} collective-permute-done((bf16[80,768]{1,0:T(8,128)(2,1)S(1)}, bf16[80,768]{1,0:T(8,128)(2,1)S(1)}, u32[]{:S(2)}, u32[]{:S(2)}) %collective-permute-start.84) | collective-permute-done | bytes 122912 | tf_op jit(solution)/shard_map/ppermute | solution.py:753
  321.4 4.1 %spread_query.1 = (f32[4,192,768]{2,1,0:T(8,128)}, f32[192,768]{1,0:T(8,128)}, f32[192,768]{1,0:T(8,128)}, f32[192,768]{1,0:T(8,128)}, f32[4,192]{1,0:T(4,128)}, /*index=5*/f32[1,192]{1,0:T(1,128)}, f32[1,768]{1,0:T(1,128)S(1)}) custom-call(s32[4]{0:T(128)S(1)} %pad_add_fusion.info_ref, bf16[176,768]{1,0:T(8,128)(2,1)} %copy-done.13, ...), custom_call_target="tpu_custom_call" | custom-call | flops 500000000 | bytes 7000000 | tf_op jit(solution)/shard_map/spread_query/pallas_call | solution.py:662
  326.9 3.1 spread_pos.1
  (357 shorter events, 72.7 us)
Async XLA Ops:
  5.3 20.6 %collective-permute-start.1 = (bf16[176,768]{1,0:T(8,128)(2,1)}, bf16[176,768]{1,0:T(8,128)(2,1)S(1)}, u32[]{:S(2)}, u32[]{:S(2)}) collective-permute-start(bf16[176,768]{1,0:T(8,128)(2,1)} %get-tuple-element.272), channel_id=1, source_target_pairs={{0,3},{1,0},{2,1},{3,2},{4,7},{5,4},{6,5},{7,6},{8,11},{9,8},{10,9... | collective-permute-start | bytes 811016 | tf_op jit(solution)/shard_map/ppermute | solution.py:738
  10.4 15.5 %collective-permute-start = (bf16[176,768]{1,0:T(8,128)(2,1)}, bf16[176,768]{1,0:T(8,128)(2,1)}, u32[]{:S(2)}, u32[]{:S(2)}) collective-permute-start(bf16[176,768]{1,0:T(8,128)(2,1)} %get-tuple-element.272), channel_id=1, source_target_pairs={{0,1},{1,2},{2,3},{3,0},{4,5},{5,6},{6,7},{7,4},{8,9},{9,10},{10,1... | collective-permute-start | bytes 811016 | tf_op jit(solution)/shard_map/ppermute | solution.py:738
  12.8 16.9 %collective-permute-start.5 = (bf16[192,768]{1,0:T(8,128)(2,1)}, bf16[192,768]{1,0:T(8,128)(2,1)}, u32[]{:S(2)}, u32[]{:S(2)}) collective-permute-start(bf16[192,768]{1,0:T(8,128)(2,1)} %get-tuple-element.276), channel_id=1, source_target_pairs={{0,3},{1,0},{2,1},{3,2},{4,7},{5,4},{6,5},{7,6},{8,11},{9,8},{10,9... | collective-permute-start | bytes 884744 | tf_op jit(solution)/shard_map/ppermute | solution.py:738
  16.7 20.3 %collective-permute-start.4 = (bf16[192,768]{1,0:T(8,128)(2,1)}, bf16[192,768]{1,0:T(8,128)(2,1)}, u32[]{:S(2)}, u32[]{:S(2)}) collective-permute-start(bf16[192,768]{1,0:T(8,128)(2,1)} %get-tuple-element.276), channel_id=1, source_target_pairs={{0,1},{1,2},{2,3},{3,0},{4,5},{5,6},{6,7},{7,4},{8,9},{9,10},{10,1... | collective-permute-start | bytes 884744 | tf_op jit(solution)/shard_map/ppermute | solution.py:738
  25.9 11.0 %collective-permute-start.3 = (bf16[176,768]{1,0:T(8,128)(2,1)}, bf16[176,768]{1,0:T(8,128)(2,1)}, u32[]{:S(2)}, u32[]{:S(2)}) collective-permute-start(bf16[176,768]{1,0:T(8,128)(2,1)} %collective-permute-done.refs_0_.refs_3_), channel_id=1, source_target_pairs={{0,16},{4,12},{8,24},{12,4},{16,0},{20,28},{24,8},{28,20},{1,17},{... | collective-permute-start | bytes 811016 | tf_op jit(solution)/shard_map/ppermute | solution.py:753
  29.2 12.4 %collective-permute-start.10 = (bf16[176,768]{1,0:T(8,128)(2,1)}, bf16[176,768]{1,0:T(8,128)(2,1)S(1)}, u32[]{:S(2)}, u32[]{:S(2)}) collective-permute-start(bf16[176,768]{1,0:T(8,128)(2,1)} %collective-permute-done.refs_0_.refs_3_), channel_id=1, source_target_pairs={{0,1},{1,2},{2,3},{3,0},{4,5},{5,6},{6,7},{7,4},{8,9},{9,10},{10,1... | collective-permute-start | bytes 811016 | tf_op jit(solution)/shard_map/ppermute | solution.py:738
  44.2 15.0 %collective-permute-start.19 = (bf16[192,768]{1,0:T(8,128)(2,1)}, bf16[192,768]{1,0:T(8,128)(2,1)S(1)}, u32[]{:S(2)}, u32[]{:S(2)}) collective-permute-start(bf16[192,768]{1,0:T(8,128)(2,1)} %collective-permute-done.4), channel_id=1, source_target_pairs={{0,1},{1,2},{2,3},{3,0},{4,5},{5,6},{6,7},{7,4},{8,9},{9,10},{10,1... | collective-permute-start | bytes 884744 | tf_op jit(solution)/shard_map/ppermute | solution.py:738
  55.1 15.1 %collective-permute-start.16 = (bf16[176,768]{1,0:T(8,128)(2,1)S(1)}, bf16[176,768]{1,0:T(8,128)(2,1)S(1)}, u32[]{:S(2)}, u32[]{:S(2)}) collective-permute-start(bf16[176,768]{1,0:T(8,128)(2,1)S(1)} %collective-permute-done.10.refs_0_.refs_3_), channel_id=1, source_target_pairs={{0,16},{4,12},{8,24},{12,4},{16,0},{20,28},{24,8},{28,20},{1,17},{... | collective-permute-start | bytes 811016 | tf_op jit(solution)/shard_map/ppermute | solution.py:753
  56.7 13.6 %collective-permute-start.15 = (bf16[176,768]{1,0:T(8,128)(2,1)S(1)}, bf16[176,768]{1,0:T(8,128)(2,1)S(1)}, u32[]{:S(2)}, u32[]{:S(2)}) collective-permute-start(bf16[176,768]{1,0:T(8,128)(2,1)S(1)} %collective-permute-done.10.refs_0_.refs_3_), channel_id=1, source_target_pairs={{0,8},{4,20},{8,0},{12,28},{16,24},{20,4},{24,16},{28,12},{1,9},{5... | collective-permute-start | bytes 811016 | tf_op jit(solution)/shard_map/ppermute | solution.py:750
  57.2 15.3 %collective-permute-start.18 = (bf16[192,768]{1,0:T(8,128)(2,1)}, bf16[192,768]{1,0:T(8,128)(2,1)S(1)}, u32[]{:S(2)}, u32[]{:S(2)}) collective-permute-start(bf16[192,768]{1,0:T(8,128)(2,1)} %collective-permute-done.5.refs_14_), channel_id=1, source_target_pairs={{0,16},{4,12},{8,24},{12,4},{16,0},{20,28},{24,8},{28,20},{1,17},{... | collective-permute-start | bytes 884744 | tf_op jit(solution)/shard_map/ppermute | solution.py:753
  57.7 14.8 %collective-permute-start.17 = (bf16[192,768]{1,0:T(8,128)(2,1)}, bf16[192,768]{1,0:T(8,128)(2,1)S(1)}, u32[]{:S(2)}, u32[]{:S(2)}) collective-permute-start(bf16[192,768]{1,0:T(8,128)(2,1)} %collective-permute-done.5.refs_14_), channel_id=1, source_target_pairs={{0,8},{4,20},{8,0},{12,28},{16,24},{20,4},{24,16},{28,12},{1,9},{5... | collective-permute-start | bytes 884744 | tf_op jit(solution)/shard_map/ppermute | solution.py:750
  59.2 13.3 %collective-permute-start.14 = (bf16[176,768]{1,0:T(8,128)(2,1)S(1)}, bf16[176,768]{1,0:T(8,128)(2,1)S(1)}, u32[]{:S(2)}, u32[]{:S(2)}) collective-permute-start(bf16[176,768]{1,0:T(8,128)(2,1)S(1)} %collective-permute-done.12.refs_1_.refs_4_), channel_id=1, source_target_pairs={{0,16},{4,12},{8,24},{12,4},{16,0},{20,28},{24,8},{28,20},{1,17},{... | collective-permute-start | bytes 811016 | tf_op jit(solution)/shard_map/ppermute | solution.py:753
  74.4 13.4 %collective-permute-start.28 = (bf16[176,768]{1,0:T(8,128)(2,1)S(1)}, bf16[176,768]{1,0:T(8,128)(2,1)S(1)}, u32[]{:S(2)}, u32[]{:S(2)}) collective-permute-start(bf16[176,768]{1,0:T(8,128)(2,1)S(1)} %collective-permute-done.15.refs_1_.refs_4_), channel_id=1, source_target_pairs={{0,4},{4,0},{8,12},{12,8},{16,20},{20,16},{24,28},{28,24},{1,5},{5... | collective-permute-start | bytes 811016 | tf_op jit(solution)/shard_map/ppermute | solution.py:744
  74.6 13.2 %collective-permute-start.24 = (bf16[176,768]{1,0:T(8,128)(2,1)S(1)}, bf16[176,768]{1,0:T(8,128)(2,1)S(1)}, u32[]{:S(2)}, u32[]{:S(2)}) collective-permute-start(bf16[176,768]{1,0:T(8,128)(2,1)S(1)} %collective-permute-done.15.refs_1_.refs_4_), channel_id=1, source_target_pairs={{0,16},{4,12},{8,24},{12,4},{16,0},{20,28},{24,8},{28,20},{1,17},{... | collective-permute-start | bytes 811016 | tf_op jit(solution)/shard_map/ppermute | solution.py:753
  76.2 11.6 %collective-permute-start.27 = (bf16[176,768]{1,0:T(8,128)(2,1)S(1)}, bf16[176,768]{1,0:T(8,128)(2,1)S(1)}, u32[]{:S(2)}, u32[]{:S(2)}) collective-permute-start(bf16[176,768]{1,0:T(8,128)(2,1)S(1)} %collective-permute-done.10.refs_0_.refs_3_), channel_id=1, source_target_pairs={{0,4},{4,0},{8,12},{12,8},{16,20},{20,16},{24,28},{28,24},{1,5},{5... | collective-permute-start | bytes 811016 | tf_op jit(solution)/shard_map/ppermute | solution.py:744
  76.3 11.6 %collective-permute-start.25 = (bf16[192,768]{1,0:T(8,128)(2,1)S(1)}, bf16[192,768]{1,0:T(8,128)(2,1)S(1)}, u32[]{:S(2)}, u32[]{:S(2)}) collective-permute-start(bf16[192,768]{1,0:T(8,128)(2,1)S(1)} %collective-permute-done.17.refs_15_), channel_id=1, source_target_pairs={{0,16},{4,12},{8,24},{12,4},{16,0},{20,28},{24,8},{28,20},{1,17},{... | collective-permute-start | bytes 884744 | tf_op jit(solution)/shard_map/ppermute | solution.py:753
  77.8 12.1 %collective-permute-start.26 = (bf16[384,768]{1,0:T(8,128)(2,1)S(1)}, bf16[384,768]{1,0:T(8,128)(2,1)S(1)}, u32[]{:S(2)}, u32[]{:S(2)}) collective-permute-start(bf16[384,768]{1,0:T(8,128)(2,1)S(1)} %pad_maximum_fusion.1.refs_6_), channel_id=1, source_target_pairs={{0,8},{4,20},{8,0},{12,28},{16,24},{20,4},{24,16},{28,12},{1,9},{5... | collective-permute-start | bytes 1769480 | tf_op jit(solution)/shard_map/ppermute | solution.py:750
  92.1 12.3 %collective-permute-start.33 = (bf16[192,768]{1,0:T(8,128)(2,1)}, bf16[192,768]{1,0:T(8,128)(2,1)S(1)}, u32[]{:S(2)}, u32[]{:S(2)}) collective-permute-start(bf16[192,768]{1,0:T(8,128)(2,1)} %collective-permute-done.5.refs_14_), channel_id=1, source_target_pairs={{0,4},{4,0},{8,12},{12,8},{16,20},{20,16},{24,28},{28,24},{1,5},{5... | collective-permute-start | bytes 884744 | tf_op jit(solution)/shard_map/ppermute | solution.py:744
  92.4 12.0 %collective-permute-start.34 = (bf16[192,768]{1,0:T(8,128)(2,1)S(1)}, bf16[192,768]{1,0:T(8,128)(2,1)S(1)}, u32[]{:S(2)}, u32[]{:S(2)}) collective-permute-start(bf16[192,768]{1,0:T(8,128)(2,1)S(1)} %collective-permute-done.17.refs_15_), channel_id=1, source_target_pairs={{0,4},{4,0},{8,12},{12,8},{16,20},{20,16},{24,28},{28,24},{1,5},{5... | collective-permute-start | bytes 884744 | tf_op jit(solution)/shard_map/ppermute | solution.py:744
  92.6 11.9 %collective-permute-start.35 = (bf16[192,768]{1,0:T(8,128)(2,1)S(1)}, bf16[192,768]{1,0:T(8,128)(2,1)S(1)}, u32[]{:S(2)}, u32[]{:S(2)}) collective-permute-start(bf16[192,768]{1,0:T(8,128)(2,1)S(1)} %collective-permute-done.18.refs_16_), channel_id=1, source_target_pairs={{0,4},{4,0},{8,12},{12,8},{16,20},{20,16},{24,28},{28,24},{1,5},{5... | collective-permute-start | bytes 884744 | tf_op jit(solution)/shard_map/ppermute | solution.py:744
  93.0 11.5 %collective-permute-start.31 = (bf16[384,768]{1,0:T(8,128)(2,1)S(1)}, bf16[384,768]{1,0:T(8,128)(2,1)S(1)}, u32[]{:S(2)}, u32[]{:S(2)}) collective-permute-start(bf16[384,768]{1,0:T(8,128)(2,1)S(1)} %pad_maximum_fusion.1.refs_6_), channel_id=1, source_target_pairs={{0,16},{4,12},{8,24},{12,4},{16,0},{20,28},{24,8},{28,20},{1,17},{... | collective-permute-start | bytes 1769480 | tf_op jit(solution)/shard_map/ppermute | solution.py:753
  94.5 14.7 %collective-permute-start.32 = (bf16[384,768]{1,0:T(8,128)(2,1)S(1)}, bf16[384,768]{1,0:T(8,128)(2,1)S(1)}, u32[]{:S(2)}, u32[]{:S(2)}) collective-permute-start(bf16[384,768]{1,0:T(8,128)(2,1)S(1)} %collective-permute-done.26.refs_7_), channel_id=1, source_target_pairs={{0,16},{4,12},{8,24},{12,4},{16,0},{20,28},{24,8},{28,20},{1,17},{... | collective-permute-start | bytes 1769480 | tf_op jit(solution)/shard_map/ppermute | solution.py:753
  156.4 18.2 %collective-permute-start.44 = (bf16[768,768]{1,0:T(8,128)(2,1)S(1)}, bf16[768,768]{1,0:T(8,128)(2,1)S(1)}, u32[]{:S(2)}, u32[]{:S(2)}) collective-permute-start(bf16[768,768]{1,0:T(8,128)(2,1)S(1)} %add_convert_fusion), channel_id=1, source_target_pairs={{0,8},{4,20},{8,0},{12,28},{16,24},{20,4},{24,16},{28,12},{1,9},{5... | collective-permute-start | bytes 3538952 | tf_op jit(solution)/shard_map/ppermute | solution.py:750
  160.7 18.2 %collective-permute-start.46 = (bf16[384,768]{1,0:T(8,128)(2,1)S(1)}, bf16[384,768]{1,0:T(8,128)(2,1)S(1)}, u32[]{:S(2)}, u32[]{:S(2)}) collective-permute-start(bf16[384,768]{1,0:T(8,128)(2,1)S(1)} %add_convert_fusion.3), channel_id=1, source_target_pairs={{0,8},{4,20},{8,0},{12,28},{16,24},{20,4},{24,16},{28,12},{1,9},{5... | collective-permute-start | bytes 1769480 | tf_op jit(solution)/shard_map/ppermute | solution.py:750
  161.2 24.0 %collective-permute-start.45 = (bf16[384,768]{1,0:T(8,128)(2,1)S(1)}, bf16[384,768]{1,0:T(8,128)(2,1)S(1)}, u32[]{:S(2)}, u32[]{:S(2)}) collective-permute-start(bf16[384,768]{1,0:T(8,128)(2,1)S(1)} %add_convert_fusion.4), channel_id=1, source_target_pairs={{0,8},{4,20},{8,0},{12,28},{16,24},{20,4},{24,16},{28,12},{1,9},{5... | collective-permute-start | bytes 1769480 | tf_op jit(solution)/shard_map/ppermute | solution.py:750
  188.3 16.9 %collective-permute-start.49 = (bf16[192,768]{1,0:T(8,128)(2,1)S(1)}, bf16[192,768]{1,0:T(8,128)(2,1)S(1)}, u32[]{:S(2)}, u32[]{:S(2)}) collective-permute-start(bf16[192,768]{1,0:T(8,128)(2,1)S(1)} %add_convert_fusion.14), channel_id=1, source_target_pairs={{0,16},{4,12},{8,24},{12,4},{16,0},{20,28},{24,8},{28,20},{1,17},{... | collective-permute-start | bytes 884744 | tf_op jit(solution)/shard_map/ppermute | solution.py:753
  189.9 15.3 %collective-permute-start.50 = (bf16[192,768]{1,0:T(8,128)(2,1)S(1)}, bf16[192,768]{1,0:T(8,128)(2,1)S(1)}, u32[]{:S(2)}, u32[]{:S(2)}) collective-permute-start(bf16[192,768]{1,0:T(8,128)(2,1)S(1)} %add_convert_fusion.13), channel_id=1, source_target_pairs={{0,16},{4,12},{8,24},{12,4},{16,0},{20,28},{24,8},{28,20},{1,17},{... | collective-permute-start | bytes 884744 | tf_op jit(solution)/shard_map/ppermute | solution.py:753
  190.4 15.1 %collective-permute-start.51 = (bf16[352,768]{1,0:T(8,128)(2,1)S(1)}, bf16[352,768]{1,0:T(8,128)(2,1)S(1)}, u32[]{:S(2)}, u32[]{:S(2)}) collective-permute-start(bf16[352,768]{1,0:T(8,128)(2,1)S(1)} %add_convert_fusion.7), channel_id=1, source_target_pairs={{0,8},{4,20},{8,0},{12,28},{16,24},{20,4},{24,16},{28,12},{1,9},{5... | collective-permute-start | bytes 1622024 | tf_op jit(solution)/shard_map/ppermute | solution.py:750
  192.1 18.3 %collective-permute-start.48 = (bf16[384,768]{1,0:T(8,128)(2,1)S(1)}, bf16[384,768]{1,0:T(8,128)(2,1)S(1)}, u32[]{:S(2)}, u32[]{:S(2)}) collective-permute-start(bf16[384,768]{1,0:T(8,128)(2,1)S(1)} %add_convert_fusion.2), channel_id=1, source_target_pairs={{0,16},{4,12},{8,24},{12,4},{16,0},{20,28},{24,8},{28,20},{1,17},{... | collective-permute-start | bytes 1769480 | tf_op jit(solution)/shard_map/ppermute | solution.py:753
  213.4 16.9 %collective-permute-start.55 = (bf16[176,768]{1,0:T(8,128)(2,1)S(1)}, bf16[176,768]{1,0:T(8,128)(2,1)S(1)}, u32[]{:S(2)}, u32[]{:S(2)}) collective-permute-start(bf16[176,768]{1,0:T(8,128)(2,1)S(1)} %add_convert_fusion.21), channel_id=1, source_target_pairs={{0,16},{4,12},{8,24},{12,4},{16,0},{20,28},{24,8},{28,20},{1,17},{... | collective-permute-start | bytes 811016 | tf_op jit(solution)/shard_map/ppermute | solution.py:753
  215.0 15.3 %collective-permute-start.53 = (bf16[192,768]{1,0:T(8,128)(2,1)S(1)}, bf16[192,768]{1,0:T(8,128)(2,1)S(1)}, u32[]{:S(2)}, u32[]{:S(2)}) collective-permute-start(bf16[192,768]{1,0:T(8,128)(2,1)S(1)} %get-tuple-element.428), channel_id=1, source_target_pairs={{0,3},{1,0},{2,1},{3,2},{4,7},{5,4},{6,5},{7,6},{8,11},{9,8},{10,9... | collective-permute-start | bytes 884744 | tf_op jit(solution)/shard_map/ppermute | solution.py:738
  217.3 13.5 %collective-permute-start.54 = (bf16[192,768]{1,0:T(8,128)(2,1)S(1)}, bf16[192,768]{1,0:T(8,128)(2,1)S(1)}, u32[]{:S(2)}, u32[]{:S(2)}) collective-permute-start(bf16[192,768]{1,0:T(8,128)(2,1)S(1)} %get-tuple-element.429), channel_id=1, source_target_pairs={{0,1},{1,2},{2,3},{3,0},{4,5},{5,6},{6,7},{7,4},{8,9},{9,10},{10,1... | collective-permute-start | bytes 884744 | tf_op jit(solution)/shard_map/ppermute | solution.py:738
  217.3 13.5 %collective-permute-start.56 = (bf16[352,768]{1,0:T(8,128)(2,1)S(1)}, bf16[352,768]{1,0:T(8,128)(2,1)S(1)}, u32[]{:S(2)}, u32[]{:S(2)}) collective-permute-start(bf16[352,768]{1,0:T(8,128)(2,1)S(1)} %add_convert_fusion.6), channel_id=1, source_target_pairs={{0,8},{4,20},{8,0},{12,28},{16,24},{20,4},{24,16},{28,12},{1,9},{5... | collective-permute-start | bytes 1622024 | tf_op jit(solution)/shard_map/ppermute | solution.py:750
  233.8 18.3 %collective-permute-start.59 = (bf16[176,768]{1,0:T(8,128)(2,1)S(1)}, bf16[176,768]{1,0:T(8,128)(2,1)S(1)}, u32[]{:S(2)}, u32[]{:S(2)}) collective-permute-start(bf16[176,768]{1,0:T(8,128)(2,1)S(1)} %add_convert_fusion.20), channel_id=1, source_target_pairs={{0,3},{1,0},{2,1},{3,2},{4,7},{5,4},{6,5},{7,6},{8,11},{9,8},{10,9... | collective-permute-start | bytes 811016 | tf_op jit(solution)/shard_map/ppermute | solution.py:738
  237.4 14.8 %collective-permute-start.60 = (bf16[176,768]{1,0:T(8,128)(2,1)S(1)}, bf16[176,768]{1,0:T(8,128)(2,1)S(1)}, u32[]{:S(2)}, u32[]{:S(2)}) collective-permute-start(bf16[176,768]{1,0:T(8,128)(2,1)S(1)} %add_convert_fusion.19), channel_id=1, source_target_pairs={{0,16},{4,12},{8,24},{12,4},{16,0},{20,28},{24,8},{28,20},{1,17},{... | collective-permute-start | bytes 811016 | tf_op jit(solution)/shard_map/ppermute | solution.py:753
  237.9 14.3 %collective-permute-start.58 = (bf16[192,768]{1,0:T(8,128)(2,1)S(1)}, bf16[192,768]{1,0:T(8,128)(2,1)S(1)}, u32[]{:S(2)}, u32[]{:S(2)}) collective-permute-start(bf16[192,768]{1,0:T(8,128)(2,1)S(1)} %add_convert_fusion.10), channel_id=1, source_target_pairs={{0,3},{1,0},{2,1},{3,2},{4,7},{5,4},{6,5},{7,6},{8,11},{9,8},{10,9... | collective-permute-start | bytes 884744 | tf_op jit(solution)/shard_map/ppermute | solution.py:738
  238.2 14.0 %collective-permute-start.61 = (bf16[352,768]{1,0:T(8,128)(2,1)S(1)}, bf16[352,768]{1,0:T(8,128)(2,1)S(1)}, u32[]{:S(2)}, u32[]{:S(2)}) collective-permute-start(bf16[352,768]{1,0:T(8,128)(2,1)S(1)} %add_convert_fusion.5), channel_id=1, source_target_pairs={{0,8},{4,20},{8,0},{12,28},{16,24},{20,4},{24,16},{28,12},{1,9},{5... | collective-permute-start | bytes 1622024 | tf_op jit(solution)/shard_map/ppermute | solution.py:750
  256.1 15.2 %collective-permute-start.63 = (bf16[512,768]{1,0:T(8,128)(2,1)S(1)}, bf16[512,768]{1,0:T(8,128)(2,1)S(1)}, u32[]{:S(2)}, u32[]{:S(2)}) collective-permute-start(bf16[512,768]{1,0:T(8,128)(2,1)S(1)} %add_convert_fusion.1), channel_id=1, source_target_pairs={{0,8},{4,20},{8,0},{12,28},{16,24},{20,4},{24,16},{28,12},{1,9},{5... | collective-permute-start | bytes 2359304 | tf_op jit(solution)/shard_map/ppermute | solution.py:750
  258.0 13.4 %collective-permute-start.66 = (bf16[192,768]{1,0:T(8,128)(2,1)S(1)}, bf16[192,768]{1,0:T(8,128)(2,1)S(1)}, u32[]{:S(2)}, u32[]{:S(2)}) collective-permute-start(bf16[192,768]{1,0:T(8,128)(2,1)S(1)} %add_convert_fusion.9.refs_0_), channel_id=1, source_target_pairs={{0,8},{4,20},{8,0},{12,28},{16,24},{20,4},{24,16},{28,12},{1,9},{5... | collective-permute-start | bytes 884744 | tf_op jit(solution)/shard_map/ppermute | solution.py:750
  271.3 12.8 %collective-permute-start.69 = (bf16[192,768]{1,0:T(8,128)(2,1)S(1)}, bf16[192,768]{1,0:T(8,128)(2,1)S(1)}, u32[]{:S(2)}, u32[]{:S(2)}) collective-permute-start(bf16[192,768]{1,0:T(8,128)(2,1)S(1)} %add_convert_fusion.9.refs_0_), channel_id=1, source_target_pairs={{0,16},{4,12},{8,24},{12,4},{16,0},{20,28},{24,8},{28,20},{1,17},{... | collective-permute-start | bytes 884744 | tf_op jit(solution)/shard_map/ppermute | solution.py:753
  272.6 11.6 %collective-permute-start.70 = (bf16[192,768]{1,0:T(8,128)(2,1)S(1)}, bf16[192,768]{1,0:T(8,128)(2,1)S(1)}, u32[]{:S(2)}, u32[]{:S(2)}) collective-permute-start(bf16[192,768]{1,0:T(8,128)(2,1)S(1)} %collective-permute-done.66.refs_1_), channel_id=1, source_target_pairs={{0,16},{4,12},{8,24},{12,4},{16,0},{20,28},{24,8},{28,20},{1,17},{... | collective-permute-start | bytes 884744 | tf_op jit(solution)/shard_map/ppermute | solution.py:753
  273.5 11.9 %collective-permute-start.67 = (bf16[256,768]{1,0:T(8,128)(2,1)S(1)}, bf16[256,768]{1,0:T(8,128)(2,1)S(1)}, u32[]{:S(2)}, u32[]{:S(2)}) collective-permute-start(bf16[256,768]{1,0:T(8,128)(2,1)S(1)} %add_convert_fusion.8), channel_id=1, source_target_pairs={{0,16},{4,12},{8,24},{12,4},{16,0},{20,28},{24,8},{28,20},{1,17},{... | collective-permute-start | bytes 1179656 | tf_op jit(solution)/shard_map/ppermute | solution.py:753
  285.5 16.5 %collective-permute-start.75 = (bf16[768,768]{1,0:T(8,128)(2,1)S(1)}, bf16[768,768]{1,0:T(8,128)(2,1)S(1)}, u32[]{:S(2)}, u32[]{:S(2)}) collective-permute-start(bf16[768,768]{1,0:T(8,128)(2,1)S(1)} %pad_maximum_fusion), channel_id=1, source_target_pairs={{0,4},{4,0},{8,12},{12,8},{16,20},{20,16},{24,28},{28,24},{1,5},{5... | collective-permute-start | bytes 3538952 | tf_op jit(solution)/shard_map/ppermute | solution.py:744
  285.9 16.2 %collective-permute-start.74 = (bf16[176,768]{1,0:T(8,128)(2,1)S(1)}, bf16[176,768]{1,0:T(8,128)(2,1)S(1)}, u32[]{:S(2)}, u32[]{:S(2)}) collective-permute-start(bf16[176,768]{1,0:T(8,128)(2,1)S(1)} %add_convert_fusion.15.refs_0_), channel_id=1, source_target_pairs={{0,8},{4,20},{8,0},{12,28},{16,24},{20,4},{24,16},{28,12},{1,9},{5... | collective-permute-start | bytes 811016 | tf_op jit(solution)/shard_map/ppermute | solution.py:750
  289.5 12.5 %collective-permute-start.72 = (bf16[80,768]{1,0:T(8,128)(2,1)S(1)}, bf16[80,768]{1,0:T(8,128)(2,1)S(1)}, u32[]{:S(2)}, u32[]{:S(2)}) collective-permute-start(bf16[80,768]{1,0:T(8,128)(2,1)S(1)} %add_convert_fusion.23), channel_id=1, source_target_pairs={{0,2},{1,3},{2,0},{3,1},{4,6},{5,7},{6,4},{7,5},{8,10},{9,11},{10,... | collective-permute-start | bytes 368648 | tf_op jit(solution)/shard_map/ppermute | solution.py:741
  290.9 11.2 %collective-permute-start.71 = (bf16[80,768]{1,0:T(8,128)(2,1)S(1)}, bf16[80,768]{1,0:T(8,128)(2,1)S(1)}, u32[]{:S(2)}, u32[]{:S(2)}) collective-permute-start(bf16[80,768]{1,0:T(8,128)(2,1)S(1)} %add_convert_fusion.23), channel_id=1, source_target_pairs={{0,1},{1,0},{2,3},{3,2},{4,5},{5,4},{6,7},{7,6},{8,9},{9,8},{10,11... | collective-permute-start | bytes 368648 | tf_op jit(solution)/shard_map/ppermute | solution.py:741
  302.1 12.1 %collective-permute-start.78 = (bf16[176,768]{1,0:T(8,128)(2,1)S(1)}, bf16[176,768]{1,0:T(8,128)(2,1)S(1)}, u32[]{:S(2)}, u32[]{:S(2)}) collective-permute-start(bf16[176,768]{1,0:T(8,128)(2,1)S(1)} %add_convert_fusion.15.refs_0_), channel_id=1, source_target_pairs={{0,16},{4,12},{8,24},{12,4},{16,0},{20,28},{24,8},{28,20},{1,17},{... | collective-permute-start | bytes 811016 | tf_op jit(solution)/shard_map/ppermute | solution.py:753
  302.7 11.5 %collective-permute-start.79 = (bf16[176,768]{1,0:T(8,128)(2,1)S(1)}, bf16[176,768]{1,0:T(8,128)(2,1)S(1)}, u32[]{:S(2)}, u32[]{:S(2)}) collective-permute-start(bf16[176,768]{1,0:T(8,128)(2,1)S(1)} %collective-permute-done.74.refs_1_), channel_id=1, source_target_pairs={{0,16},{4,12},{8,24},{12,4},{16,0},{20,28},{24,8},{28,20},{1,17},{... | collective-permute-start | bytes 811016 | tf_op jit(solution)/shard_map/ppermute | solution.py:753
  (126 other events, 1119.8 us)

commit v9 on v8

--- a/solution.py
+++ b/solution.py
@@ -912,21 +912,23 @@
 
     fb.a, fc.a = first(one_b), first(one_c)
     q1, acc = back(2, acc)
-    acc, q1.send, fa.a, fb.a, fc.a = sync(acc, q1.send, fa.a, fb.a, fc.a)
+    acc, q1.send, fa.a, fb.a = sync(acc, q1.send, fa.a, fb.a)
     q1.got = core(q1.send)
-    acc, two_a, two_b, two_c, q1.got = sync(acc, fa.two(), fb.two(), fc.two(), q1.got)
+    acc, two_a, two_b, q1.got = sync(acc, fa.two(), fb.two(), q1.got)
     acc, one_1 = sync(acc, q1.one())
 
-    fa.b, fb.b, fc.b, q1.a = second(two_a), second(two_b), second(two_c), first(one_1)
+    fa.b, fb.b, q1.a = second(two_a), second(two_b), first(one_1)
     q2, acc = back(1, acc)
-    acc, q2.send, fa.b, fb.b, fc.b, q1.a = sync(acc, q2.send, fa.b, fb.b, fc.b, q1.a)
+    acc, q2.send, fa.b, fb.b, fc.a, q1.a = sync(acc, q2.send, fa.b, fb.b, fc.a, q1.a)
     q2.got = core(q2.send)
-    acc, r2, r3, two_1, q2.got = sync(acc, fa.rest(0, size), fb.rest(0, size), q1.two(), q2.got)
+    acc, r2, r3, two_c, two_1, q2.got = sync(
+        acc, fa.rest(0, size), fb.rest(0, size), fc.two(), q1.two(), q2.got
+    )
     acc, one_2 = sync(acc, q2.one())
 
-    z2, z3, q1.b, q2.a = shift(r2, -1), shift(r3, -3), second(two_1), first(one_2)
+    z2, z3, q1.b, q2.a, fc.b = shift(r2, -1), shift(r3, -3), second(two_1), first(one_2), second(two_c)
     q3, acc = back(3, acc)
-    acc, q3.send, z2, z3, q1.b, q2.a = sync(acc, q3.send, z2, z3, q1.b, q2.a)
+    acc, q3.send, z2, z3, q1.b, q2.a, fc.b = sync(acc, q3.send, z2, z3, q1.b, q2.a, fc.b)
     q3.got = core(q3.send)
     acc, r1, value_2, two_2, q3.got = sync(acc, fa.rest(size, 2 * size, z2), q1.rest(0, unit), q2.two(), q3.got)
     acc, one_3 = sync(acc, q3.one())

time: 337 us -> 331 us (0.982)
  waiting for transfers between devices: 94.2 us -> 90.1 us
    ppermute x23, waiting for transfers between devices: 28.7 us -> 22.4 us  [second(): lax.ppermute(v, 'dp', [(i, i ^ (2 if i % 2 else 4)) for i in range(self.d...]
  transfers between devices with their start and end apart: 89 -> 89, of which waited for: 30 -> 27; matrix products, arithmetic and copies ran while one was open for 2% -> 2% of each run, Pallas kernels for 33% -> 33%
where the time goes in v9:
time: 331 us; the launch traced here: 325 us
  Pallas kernels  143 us (43%)
  waiting for transfers between devices  90.1 us (27%)
  starting transfers between devices  78 us (24%)
  local copies, waits for them, and re-layouts  6.27 us (2%)
  other arithmetic  5.49 us (2%)
    pallas_call x4, Pallas kernels, attend_back(): pl.pallas_call(partial(attend_back_kernel, words, gw, heads, final, count...  48.1 us
    pallas_call x4, Pallas kernels, attend(): pl.pallas_call(partial(attend_kernel, words, gw, heads, count), in_specs=...  37.3 us
    ppermute x23, starting transfers between devices, second(): lax.ppermute(v, 'dp', [(i, i ^ (2 if i % 2 else 4)) for i in range(self.d...  27.4 us
    ppermute x12, waiting for transfers between devices, shift_z(): return lax.ppermute(v, 'tensor', [(i, (i + by) % n) for i in range(n)])  25.3 us
    ppermute x23, waiting for transfers between devices, second(): lax.ppermute(v, 'dp', [(i, i ^ (2 if i % 2 else 4)) for i in range(self.d...  22.4 us
    ppermute x12, starting transfers between devices, shift_z(): return lax.ppermute(v, 'tensor', [(i, (i + by) % n) for i in range(n)])  20.4 us
    pallas_call x3, Pallas kernels, hidden_back(): pl.pallas_call(partial(hidden_back_kernel, pair), in_specs=[SMEM] + [VMEM...  19.7 us
    pallas_call x1, Pallas kernels, hidden(): pl.pallas_call(partial(hidden_kernel, n), in_specs=[SMEM] + [VMEM] * (6 +...  19.6 us
  transfers between devices with their start and end apart: 89, of which 27 were waited for; matrix products, arithmetic and copies ran while one was open for 2% of the time, Pallas kernels for 33%

profile of v9, /device:TPU:0, one launch (start us, length us, event | category | flops | bytes accessed | tf_op | source)
XLA Modules:
  0.0 324.9 jit_solution(3018023096926561851)
XLA Ops:
  2.8 2.4 pack.1
  5.3 5.1 %collective-permute-start.1 = (bf16[176,768]{1,0:T(8,128)(2,1)}, bf16[176,768]{1,0:T(8,128)(2,1)S(1)}, u32[]{:S(2)}, u32[]{:S(2)}) collective-permute-start(bf16[176,768]{1,0:T(8,128)(2,1)} %get-tuple-element.272), channel_id=1, source_target_pairs={{0,3},{1,0},{2,1},{3,2},{4,7},{5,4},{6,5},{7,6},{8,11},{9,8},{10,9... | collective-permute-start | bytes 811016 | tf_op jit(solution)/shard_map/ppermute | solution.py:738
  10.6 2.2 start_rows.1
  12.8 3.9 %collective-permute-start.5 = (bf16[192,768]{1,0:T(8,128)(2,1)}, bf16[192,768]{1,0:T(8,128)(2,1)}, u32[]{:S(2)}, u32[]{:S(2)}) collective-permute-start(bf16[192,768]{1,0:T(8,128)(2,1)} %get-tuple-element.276), channel_id=1, source_target_pairs={{0,3},{1,0},{2,1},{3,2},{4,7},{5,4},{6,5},{7,6},{8,11},{9,8},{10,9... | collective-permute-start | bytes 884744 | tf_op jit(solution)/shard_map/ppermute | solution.py:738
  16.8 9.1 %attend_own.1 = (bf16[512,768]{1,0:T(8,128)(2,1)}, bf16[128,768]{1,0:T(8,128)(2,1)}, bf16[640,192]{1,0:T(8,128)(2,1)}, f32[8,640]{1,0:T(8,128)S(1)}, bf16[16,768...) custom-call(s32[4]{0:T(128)S(1)} %pad_add_fusion.info_ref, ...), custom_call_target="tpu_custom_call", output_to_operand_aliasing={{5}: (2, {})} | custom-call | flops 8000000000 | bytes 6000000 | tf_op jit(solution)/shard_map/attend_own/pallas_call | solution.py:285
  29.7 7.2 %collective-permute-done.4 = bf16[192,768]{1,0:T(8,128)(2,1)} collective-permute-done((bf16[192,768]{1,0:T(8,128)(2,1)}, bf16[192,768]{1,0:T(8,128)(2,1)}, u32[]{:S(2)}, u32[]{:S(2)}) %collective-permute-start.4) | collective-permute-done | bytes 294944 | tf_op jit(solution)/shard_map/ppermute | solution.py:738
  39.1 2.4 collective-permute-done.10.refs_0_.refs_3_
  41.6 2.7 collective-permute-done.6.refs_3_.refs_6_
  44.2 1.7 collective-permute-start.19
  49.0 6.1 %collective-permute-done.13.refs_2_.refs_5_ = bf16[176,768]{1,0:T(8,128)(2,1)S(1)} collective-permute-done((bf16[176,768]{1,0:T(8,128)(2,1)}, bf16[176,768]{1,0:T(8,128)(2,1)S(1)}, u32[]{:S(2)}, u32[]{:S(2)}) %collective-permute-start.13) | collective-permute-done | bytes 270368 | tf_op jit(solution)/shard_map/ppermute | solution.py:753
  60.8 9.4 %attend_far.3 = (bf16[512,768]{1,0:T(8,128)(2,1)}, bf16[128,768]{1,0:T(8,128)(2,1)}, bf16[640,192]{1,0:T(8,128)(2,1)}, f32[8,640]{1,0:T(8,128)S(1)}, bf16[16,768...) custom-call(s32[4]{0:T(128)S(1)} %pad_add_fusion.info_ref, ...), custom_call_target="tpu_custom_call", output_to_operand_aliasing={{5}: (2, {})} | custom-call | flops 8000000000 | bytes 6000000 | tf_op jit(solution)/shard_map/attend_far/pallas_call | solution.py:285
  78.4 9.4 %attend_far.4 = (bf16[512,768]{1,0:T(8,128)(2,1)}, bf16[128,768]{1,0:T(8,128)(2,1)}, bf16[640,192]{1,0:T(8,128)(2,1)}, f32[8,640]{1,0:T(8,128)S(1)}, bf16[16,768...) custom-call(s32[4]{0:T(128)S(1)} %pad_add_fusion.info_ref, ...), custom_call_target="tpu_custom_call", output_to_operand_aliasing={{5}: (2, {})} | custom-call | flops 8000000000 | bytes 6000000 | tf_op jit(solution)/shard_map/attend_far/pallas_call | solution.py:285
  87.9 2.0 collective-permute-done.26.refs_7_
  95.0 9.4 %attend_far.5 = (bf16[512,768]{1,0:T(8,128)(2,1)}, bf16[128,768]{1,0:T(8,128)(2,1)}, bf16[640,192]{1,0:T(8,128)(2,1)}, f32[8,640]{1,0:T(8,128)S(1)}, bf16[16,768...) custom-call(s32[4]{0:T(128)S(1)} %pad_add_fusion.info_ref, ...), custom_call_target="tpu_custom_call", output_to_operand_aliasing={{5}: (2, {})} | custom-call | flops 8000000000 | bytes 6000000 | tf_op jit(solution)/shard_map/attend_far/pallas_call | solution.py:285
  104.5 4.7 %collective-permute-done.32.refs_9_ = bf16[384,768]{1,0:T(8,128)(2,1)S(1)} collective-permute-done((bf16[384,768]{1,0:T(8,128)(2,1)S(1)}, bf16[384,768]{1,0:T(8,128)(2,1)S(1)}, u32[]{:S(2)}, u32[]{:S(2)}) %collective-permute-start.32) | collective-permute-done | bytes 589856 | tf_op jit(solution)/shard_map/ppermute | solution.py:753
  110.3 3.9 %collective-permute-done.40.refs_21_ = bf16[192,768]{1,0:T(8,128)(2,1)S(1)} collective-permute-done((bf16[192,768]{1,0:T(8,128)(2,1)S(1)}, bf16[192,768]{1,0:T(8,128)(2,1)S(1)}, u32[]{:S(2)}, u32[]{:S(2)}) %collective-permute-start.40) | collective-permute-done | bytes 294944 | tf_op jit(solution)/shard_map/ppermute | solution.py:744
  115.7 19.6 %hidden.1 = (bf16[768,640]{1,0:T(8,128)(2,1)S(1)}, bf16[4,768,640]{2,1,0:T(8,128)(2,1)S(1)}, f32[4,640,768]{2,1,0:T(8,128)S(1)}, bf16[4,768,768]{2,1,0:T(8,128)(...) custom-call(s32[4]{0:T(128)S(1)} %pad_add_fusion.info_ref, ...), custom_call_target="tpu_custom_call" | custom-call | flops 22000001024 | bytes 20000000 | tf_op jit(solution)/shard_map/hidden/pallas_call | solution.py:394
  135.3 9.5 %hidden_back.3 = (bf16[1536,768]{1,0:T(8,128)(2,1)}, bf16[768,768]{1,0:T(8,128)(2,1)}, bf16[768,768]{1,0:T(8,128)(2,1)}, f32[640,768]{1,0:T(8,128)S(1)}, f32[16,768]{1,0:T(8,128)S(1)}) custom-call(s32[4]{0:T(128)S(1)} %pad_add_fusion.info_ref, bf16[640,768]{1,0:T(8,128)(2,1)S(1)} %get-tuple-element.351.low_ref, ...), custom_call_target="tpu_custom_call", output_to_operand_aliasing={{3}: (7, {})} | custom-call | flops 14000000000 | bytes 16000000 | tf_op jit(solution)/shard_map/hidden_back/pallas_call | solution.py:455
  145.0 5.1 %hidden_back.4 = (bf16[768,768]{1,0:T(8,128)(2,1)}, bf16[384,768]{1,0:T(8,128)(2,1)}, bf16[384,768]{1,0:T(8,128)(2,1)}, f32[640,768]{1,0:T(8,128)S(1)}, f32[8,768]{1,0:T(8,128)S(1)}) custom-call(s32[4]{0:T(128)S(1)} %pad_add_fusion.info_ref, bf16[640,768]{1,0:T(8,128)(2,1)S(1)} %get-tuple-element.351.low_ref, ...), custom_call_target="tpu_custom_call", output_to_operand_aliasing={{3}: (7, {})} | custom-call | flops 7000000000 | bytes 8000000 | tf_op jit(solution)/shard_map/hidden_back/pallas_call | solution.py:455
  150.9 5.1 %hidden_back.5 = (bf16[768,768]{1,0:T(8,128)(2,1)}, bf16[384,768]{1,0:T(8,128)(2,1)}, bf16[384,768]{1,0:T(8,128)(2,1)}, f32[640,768]{1,0:T(8,128)S(1)}, f32[8,768]{1,0:T(8,128)S(1)}) custom-call(s32[4]{0:T(128)S(1)} %pad_add_fusion.info_ref, bf16[640,768]{1,0:T(8,128)(2,1)S(1)} %get-tuple-element.351.low_ref, ...), custom_call_target="tpu_custom_call", output_to_operand_aliasing={{3}: (7, {})} | custom-call | flops 7000000000 | bytes 8000000 | tf_op jit(solution)/shard_map/hidden_back/pallas_call | solution.py:455
  156.2 1.7 collective-permute-start.44
  161.0 11.7 %attend_back.4 = (bf16[704,768]{1,0:T(8,128)(2,1)}, bf16[352,768]{1,0:T(8,128)(2,1)}, bf16[352,768]{1,0:T(8,128)(2,1)}, f32[640,768]{1,0:T(8,128)S(1)}) custom-call(s32[4]{0:T(128)S(1)} %pad_add_fusion.info_ref, bf16[640,768]{1,0:T(8,128)(2,1)S(1)} %get-tuple-element.267.rows_ref, ...), custom_call_target="tpu_custom_call", output_to_operand_aliasing={{3}: (5, {})} | custom-call | flops 11000000512 | bytes 8000000 | tf_op jit(solution)/shard_map/attend_back/pallas_call | solution.py:607
  172.8 5.9 %collective-permute-done.45 = bf16[384,768]{1,0:T(8,128)(2,1)S(1)} collective-permute-done((bf16[384,768]{1,0:T(8,128)(2,1)S(1)}, bf16[384,768]{1,0:T(8,128)(2,1)S(1)}, u32[]{:S(2)}, u32[]{:S(2)}) %collective-permute-start.45) | collective-permute-done | bytes 589856 | tf_op jit(solution)/shard_map/ppermute | solution.py:750
  178.7 1.7 collective-permute-start.49
  185.6 11.6 %attend_back.5 = (bf16[704,768]{1,0:T(8,128)(2,1)}, bf16[352,768]{1,0:T(8,128)(2,1)}, bf16[352,768]{1,0:T(8,128)(2,1)}, f32[640,768]{1,0:T(8,128)S(1)}) custom-call(s32[4]{0:T(128)S(1)} %pad_add_fusion.info_ref, bf16[640,768]{1,0:T(8,128)(2,1)S(1)} %get-tuple-element.267.rows_ref, ...), custom_call_target="tpu_custom_call", output_to_operand_aliasing={{3}: (5, {})} | custom-call | flops 11000000512 | bytes 8000000 | tf_op jit(solution)/shard_map/attend_back/pallas_call | solution.py:607
  197.2 6.7 %collective-permute-done.50 = bf16[352,768]{1,0:T(8,128)(2,1)S(1)} collective-permute-done((bf16[352,768]{1,0:T(8,128)(2,1)S(1)}, bf16[352,768]{1,0:T(8,128)(2,1)S(1)}, u32[]{:S(2)}, u32[]{:S(2)}) %collective-permute-start.50) | collective-permute-done | bytes 540704 | tf_op jit(solution)/shard_map/ppermute | solution.py:750
  204.5 2.3 collective-permute-done.51
  208.6 2.2 collective-permute-start.52
  211.3 1.7 collective-permute-start.55
  213.0 11.4 %attend_back.6 = (bf16[704,768]{1,0:T(8,128)(2,1)}, bf16[352,768]{1,0:T(8,128)(2,1)}, bf16[352,768]{1,0:T(8,128)(2,1)}, f32[640,768]{1,0:T(8,128)S(1)}) custom-call(s32[4]{0:T(128)S(1)} %pad_add_fusion.info_ref, bf16[640,768]{1,0:T(8,128)(2,1)S(1)} %get-tuple-element.267.rows_ref, ...), custom_call_target="tpu_custom_call", output_to_operand_aliasing={{3}: (5, {})} | custom-call | flops 11000000512 | bytes 8000000 | tf_op jit(solution)/shard_map/attend_back/pallas_call | solution.py:607
  225.0 2.4 collective-permute-done.57
  227.5 3.9 %collective-permute-start.59 = (bf16[176,768]{1,0:T(8,128)(2,1)S(1)}, bf16[176,768]{1,0:T(8,128)(2,1)S(1)}, u32[]{:S(2)}, u32[]{:S(2)}) collective-permute-start(bf16[176,768]{1,0:T(8,128)(2,1)S(1)} %add_convert_fusion.20), channel_id=1, source_target_pairs={{0,3},{1,0},{2,1},{3,2},{4,7},{5,4},{6,5},{7,6},{8,11},{9,8},{10,9... | collective-permute-start | bytes 811016 | tf_op jit(solution)/shard_map/ppermute | solution.py:738
  233.6 13.4 %attend_back.7 = (bf16[1024,768]{1,0:T(8,128)(2,1)}, bf16[512,768]{1,0:T(8,128)(2,1)}, bf16[512,768]{1,0:T(8,128)(2,1)}, f32[512,768]{1,0:T(8,128)}, f32[128,768]{1,0:T(8,128)}) custom-call(s32[4]{0:T(128)S(1)} %pad_add_fusion.info_ref, bf16[640,768]{1,0:T(8,128)(2,1)S(1)} %get-tuple-element.267.rows_ref, f32[8,640]{1,0:T(8,128)S(1)} %get-tuple-element.350.lt_ref, ...), custom_call_target="tpu_custom_call" | custom-call | flops 11000000512 | bytes 8000000 | tf_op jit(solution)/shard_map/attend_back/pallas_call | solution.py:607
  247.8 2.9 collective-permute-done.62
  250.9 1.7 collective-permute-start.63
  254.5 7.2 %collective-permute-done.65 = bf16[176,768]{1,0:T(8,128)(2,1)S(1)} collective-permute-done((bf16[176,768]{1,0:T(8,128)(2,1)S(1)}, bf16[176,768]{1,0:T(8,128)(2,1)S(1)}, u32[]{:S(2)}, u32[]{:S(2)}) %collective-permute-start.65) | collective-permute-done | bytes 270368 | tf_op jit(solution)/shard_map/ppermute | solution.py:738
  261.7 4.4 %collective-permute-done.66.refs_1_ = bf16[192,768]{1,0:T(8,128)(2,1)S(1)} collective-permute-done((bf16[192,768]{1,0:T(8,128)(2,1)S(1)}, bf16[192,768]{1,0:T(8,128)(2,1)S(1)}, u32[]{:S(2)}, u32[]{:S(2)}) %collective-permute-start.66) | collective-permute-done | bytes 294944 | tf_op jit(solution)/shard_map/ppermute | solution.py:750
  269.0 2.3 collective-permute-start.68
  271.3 7.9 %collective-permute-done.68 = bf16[176,768]{1,0:T(8,128)(2,1)S(1)} collective-permute-done((bf16[176,768]{1,0:T(8,128)(2,1)S(1)}, bf16[176,768]{1,0:T(8,128)(2,1)S(1)}, u32[]{:S(2)}, u32[]{:S(2)}) %collective-permute-start.68) | collective-permute-done | bytes 270368 | tf_op jit(solution)/shard_map/ppermute | solution.py:738
  280.6 1.7 collective-permute-start.74
  283.1 2.9 collective-permute-start.72
  286.9 3.6 %collective-permute-done.73 = bf16[80,768]{1,0:T(8,128)(2,1)S(1)} collective-permute-done((bf16[80,768]{1,0:T(8,128)(2,1)S(1)}, bf16[80,768]{1,0:T(8,128)(2,1)S(1)}, u32[]{:S(2)}, u32[]{:S(2)}) %collective-permute-start.73) | collective-permute-done | bytes 122912 | tf_op jit(solution)/shard_map/ppermute | solution.py:741
  290.5 5.6 %collective-permute-done.72 = bf16[80,768]{1,0:T(8,128)(2,1)S(1)} collective-permute-done((bf16[80,768]{1,0:T(8,128)(2,1)S(1)}, bf16[80,768]{1,0:T(8,128)(2,1)S(1)}, u32[]{:S(2)}, u32[]{:S(2)}) %collective-permute-start.72) | collective-permute-done | bytes 122912 | tf_op jit(solution)/shard_map/ppermute | solution.py:741
  300.7 4.6 %spread_hidden.1 = (f32[768,768]{1,0:T(8,128)}, f32[768,768]{1,0:T(8,128)}) custom-call(s32[4]{0:T(128)S(1)} %pad_add_fusion.info_ref, bf16[192,768]{1,0:T(8,128)(2,1)} %copy-done.6, bf16[192,768]{1,0:T(8,128)(2,1)} %copy-done.7, bf16[192,768]{1,0:T(8,128)(2,1)} %copy-done.8, bf16[192,768]{1,0:T(8,128)(2,1)} %copy-done.9, bf16[768,768]{1,0:T(8,128)(2,1)} %copy-done.12), custom_call_target="tpu_custom_call" | custom-call | flops 500000000 | bytes 7000000 | tf_op jit(solution)/shard_map/spread_hidden/pallas_call | solution.py:689
  305.3 2.9 collective-permute-done.77.refs_2_
  310.8 3.4 %collective-permute-done.84.refs_3_ = bf16[80,768]{1,0:T(8,128)(2,1)S(1)} collective-permute-done((bf16[80,768]{1,0:T(8,128)(2,1)S(1)}, bf16[80,768]{1,0:T(8,128)(2,1)S(1)}, u32[]{:S(2)}, u32[]{:S(2)}) %collective-permute-start.84) | collective-permute-done | bytes 122912 | tf_op jit(solution)/shard_map/ppermute | solution.py:753
  315.4 4.1 %spread_query.1 = (f32[4,192,768]{2,1,0:T(8,128)}, f32[192,768]{1,0:T(8,128)}, f32[192,768]{1,0:T(8,128)}, f32[192,768]{1,0:T(8,128)}, f32[4,192]{1,0:T(4,128)}, /*index=5*/f32[1,192]{1,0:T(1,128)}, f32[1,768]{1,0:T(1,128)S(1)}) custom-call(s32[4]{0:T(128)S(1)} %pad_add_fusion.info_ref, bf16[176,768]{1,0:T(8,128)(2,1)} %copy-done.13, ...), custom_call_target="tpu_custom_call" | custom-call | flops 500000000 | bytes 7000000 | tf_op jit(solution)/shard_map/spread_query/pallas_call | solution.py:662
  320.9 3.1 spread_pos.1
  (357 shorter events, 66.7 us)
Async XLA Ops:
  5.3 20.6 %collective-permute-start.1 = (bf16[176,768]{1,0:T(8,128)(2,1)}, bf16[176,768]{1,0:T(8,128)(2,1)S(1)}, u32[]{:S(2)}, u32[]{:S(2)}) collective-permute-start(bf16[176,768]{1,0:T(8,128)(2,1)} %get-tuple-element.272), channel_id=1, source_target_pairs={{0,3},{1,0},{2,1},{3,2},{4,7},{5,4},{6,5},{7,6},{8,11},{9,8},{10,9... | collective-permute-start | bytes 811016 | tf_op jit(solution)/shard_map/ppermute | solution.py:738
  10.4 15.5 %collective-permute-start = (bf16[176,768]{1,0:T(8,128)(2,1)}, bf16[176,768]{1,0:T(8,128)(2,1)}, u32[]{:S(2)}, u32[]{:S(2)}) collective-permute-start(bf16[176,768]{1,0:T(8,128)(2,1)} %get-tuple-element.272), channel_id=1, source_target_pairs={{0,1},{1,2},{2,3},{3,0},{4,5},{5,6},{6,7},{7,4},{8,9},{9,10},{10,1... | collective-permute-start | bytes 811016 | tf_op jit(solution)/shard_map/ppermute | solution.py:738
  12.8 16.9 %collective-permute-start.5 = (bf16[192,768]{1,0:T(8,128)(2,1)}, bf16[192,768]{1,0:T(8,128)(2,1)}, u32[]{:S(2)}, u32[]{:S(2)}) collective-permute-start(bf16[192,768]{1,0:T(8,128)(2,1)} %get-tuple-element.276), channel_id=1, source_target_pairs={{0,3},{1,0},{2,1},{3,2},{4,7},{5,4},{6,5},{7,6},{8,11},{9,8},{10,9... | collective-permute-start | bytes 884744 | tf_op jit(solution)/shard_map/ppermute | solution.py:738
  16.7 20.3 %collective-permute-start.4 = (bf16[192,768]{1,0:T(8,128)(2,1)}, bf16[192,768]{1,0:T(8,128)(2,1)}, u32[]{:S(2)}, u32[]{:S(2)}) collective-permute-start(bf16[192,768]{1,0:T(8,128)(2,1)} %get-tuple-element.276), channel_id=1, source_target_pairs={{0,1},{1,2},{2,3},{3,0},{4,5},{5,6},{6,7},{7,4},{8,9},{9,10},{10,1... | collective-permute-start | bytes 884744 | tf_op jit(solution)/shard_map/ppermute | solution.py:738
  25.9 11.0 %collective-permute-start.3 = (bf16[176,768]{1,0:T(8,128)(2,1)}, bf16[176,768]{1,0:T(8,128)(2,1)}, u32[]{:S(2)}, u32[]{:S(2)}) collective-permute-start(bf16[176,768]{1,0:T(8,128)(2,1)} %collective-permute-done.refs_0_.refs_3_), channel_id=1, source_target_pairs={{0,16},{4,12},{8,24},{12,4},{16,0},{20,28},{24,8},{28,20},{1,17},{... | collective-permute-start | bytes 811016 | tf_op jit(solution)/shard_map/ppermute | solution.py:753
  29.2 12.4 %collective-permute-start.10 = (bf16[176,768]{1,0:T(8,128)(2,1)}, bf16[176,768]{1,0:T(8,128)(2,1)S(1)}, u32[]{:S(2)}, u32[]{:S(2)}) collective-permute-start(bf16[176,768]{1,0:T(8,128)(2,1)} %collective-permute-done.refs_0_.refs_3_), channel_id=1, source_target_pairs={{0,1},{1,2},{2,3},{3,0},{4,5},{5,6},{6,7},{7,4},{8,9},{9,10},{10,1... | collective-permute-start | bytes 811016 | tf_op jit(solution)/shard_map/ppermute | solution.py:738
  44.2 15.0 %collective-permute-start.19 = (bf16[192,768]{1,0:T(8,128)(2,1)}, bf16[192,768]{1,0:T(8,128)(2,1)S(1)}, u32[]{:S(2)}, u32[]{:S(2)}) collective-permute-start(bf16[192,768]{1,0:T(8,128)(2,1)} %collective-permute-done.4), channel_id=1, source_target_pairs={{0,1},{1,2},{2,3},{3,0},{4,5},{5,6},{6,7},{7,4},{8,9},{9,10},{10,1... | collective-permute-start | bytes 884744 | tf_op jit(solution)/shard_map/ppermute | solution.py:738
  55.1 15.1 %collective-permute-start.16 = (bf16[176,768]{1,0:T(8,128)(2,1)S(1)}, bf16[176,768]{1,0:T(8,128)(2,1)S(1)}, u32[]{:S(2)}, u32[]{:S(2)}) collective-permute-start(bf16[176,768]{1,0:T(8,128)(2,1)S(1)} %collective-permute-done.10.refs_0_.refs_3_), channel_id=1, source_target_pairs={{0,16},{4,12},{8,24},{12,4},{16,0},{20,28},{24,8},{28,20},{1,17},{... | collective-permute-start | bytes 811016 | tf_op jit(solution)/shard_map/ppermute | solution.py:753
  56.7 13.6 %collective-permute-start.15 = (bf16[176,768]{1,0:T(8,128)(2,1)S(1)}, bf16[176,768]{1,0:T(8,128)(2,1)S(1)}, u32[]{:S(2)}, u32[]{:S(2)}) collective-permute-start(bf16[176,768]{1,0:T(8,128)(2,1)S(1)} %collective-permute-done.10.refs_0_.refs_3_), channel_id=1, source_target_pairs={{0,8},{4,20},{8,0},{12,28},{16,24},{20,4},{24,16},{28,12},{1,9},{5... | collective-permute-start | bytes 811016 | tf_op jit(solution)/shard_map/ppermute | solution.py:750
  57.2 15.3 %collective-permute-start.18 = (bf16[192,768]{1,0:T(8,128)(2,1)}, bf16[192,768]{1,0:T(8,128)(2,1)S(1)}, u32[]{:S(2)}, u32[]{:S(2)}) collective-permute-start(bf16[192,768]{1,0:T(8,128)(2,1)} %collective-permute-done.5.refs_14_), channel_id=1, source_target_pairs={{0,16},{4,12},{8,24},{12,4},{16,0},{20,28},{24,8},{28,20},{1,17},{... | collective-permute-start | bytes 884744 | tf_op jit(solution)/shard_map/ppermute | solution.py:753
  57.7 14.8 %collective-permute-start.17 = (bf16[192,768]{1,0:T(8,128)(2,1)}, bf16[192,768]{1,0:T(8,128)(2,1)S(1)}, u32[]{:S(2)}, u32[]{:S(2)}) collective-permute-start(bf16[192,768]{1,0:T(8,128)(2,1)} %collective-permute-done.5.refs_14_), channel_id=1, source_target_pairs={{0,8},{4,20},{8,0},{12,28},{16,24},{20,4},{24,16},{28,12},{1,9},{5... | collective-permute-start | bytes 884744 | tf_op jit(solution)/shard_map/ppermute | solution.py:750
  59.2 13.3 %collective-permute-start.14 = (bf16[176,768]{1,0:T(8,128)(2,1)S(1)}, bf16[176,768]{1,0:T(8,128)(2,1)S(1)}, u32[]{:S(2)}, u32[]{:S(2)}) collective-permute-start(bf16[176,768]{1,0:T(8,128)(2,1)S(1)} %collective-permute-done.12.refs_1_.refs_4_), channel_id=1, source_target_pairs={{0,16},{4,12},{8,24},{12,4},{16,0},{20,28},{24,8},{28,20},{1,17},{... | collective-permute-start | bytes 811016 | tf_op jit(solution)/shard_map/ppermute | solution.py:753
  74.4 13.4 %collective-permute-start.28 = (bf16[176,768]{1,0:T(8,128)(2,1)S(1)}, bf16[176,768]{1,0:T(8,128)(2,1)S(1)}, u32[]{:S(2)}, u32[]{:S(2)}) collective-permute-start(bf16[176,768]{1,0:T(8,128)(2,1)S(1)} %collective-permute-done.15.refs_1_.refs_4_), channel_id=1, source_target_pairs={{0,4},{4,0},{8,12},{12,8},{16,20},{20,16},{24,28},{28,24},{1,5},{5... | collective-permute-start | bytes 811016 | tf_op jit(solution)/shard_map/ppermute | solution.py:744
  74.6 13.2 %collective-permute-start.24 = (bf16[176,768]{1,0:T(8,128)(2,1)S(1)}, bf16[176,768]{1,0:T(8,128)(2,1)S(1)}, u32[]{:S(2)}, u32[]{:S(2)}) collective-permute-start(bf16[176,768]{1,0:T(8,128)(2,1)S(1)} %collective-permute-done.15.refs_1_.refs_4_), channel_id=1, source_target_pairs={{0,16},{4,12},{8,24},{12,4},{16,0},{20,28},{24,8},{28,20},{1,17},{... | collective-permute-start | bytes 811016 | tf_op jit(solution)/shard_map/ppermute | solution.py:753
  76.2 11.6 %collective-permute-start.27 = (bf16[176,768]{1,0:T(8,128)(2,1)S(1)}, bf16[176,768]{1,0:T(8,128)(2,1)S(1)}, u32[]{:S(2)}, u32[]{:S(2)}) collective-permute-start(bf16[176,768]{1,0:T(8,128)(2,1)S(1)} %collective-permute-done.10.refs_0_.refs_3_), channel_id=1, source_target_pairs={{0,4},{4,0},{8,12},{12,8},{16,20},{20,16},{24,28},{28,24},{1,5},{5... | collective-permute-start | bytes 811016 | tf_op jit(solution)/shard_map/ppermute | solution.py:744
  76.3 11.6 %collective-permute-start.25 = (bf16[192,768]{1,0:T(8,128)(2,1)S(1)}, bf16[192,768]{1,0:T(8,128)(2,1)S(1)}, u32[]{:S(2)}, u32[]{:S(2)}) collective-permute-start(bf16[192,768]{1,0:T(8,128)(2,1)S(1)} %collective-permute-done.17.refs_15_), channel_id=1, source_target_pairs={{0,16},{4,12},{8,24},{12,4},{16,0},{20,28},{24,8},{28,20},{1,17},{... | collective-permute-start | bytes 884744 | tf_op jit(solution)/shard_map/ppermute | solution.py:753
  77.8 12.1 %collective-permute-start.26 = (bf16[384,768]{1,0:T(8,128)(2,1)S(1)}, bf16[384,768]{1,0:T(8,128)(2,1)S(1)}, u32[]{:S(2)}, u32[]{:S(2)}) collective-permute-start(bf16[384,768]{1,0:T(8,128)(2,1)S(1)} %pad_maximum_fusion.1.refs_6_), channel_id=1, source_target_pairs={{0,8},{4,20},{8,0},{12,28},{16,24},{20,4},{24,16},{28,12},{1,9},{5... | collective-permute-start | bytes 1769480 | tf_op jit(solution)/shard_map/ppermute | solution.py:750
  92.1 12.3 %collective-permute-start.33 = (bf16[192,768]{1,0:T(8,128)(2,1)}, bf16[192,768]{1,0:T(8,128)(2,1)S(1)}, u32[]{:S(2)}, u32[]{:S(2)}) collective-permute-start(bf16[192,768]{1,0:T(8,128)(2,1)} %collective-permute-done.5.refs_14_), channel_id=1, source_target_pairs={{0,4},{4,0},{8,12},{12,8},{16,20},{20,16},{24,28},{28,24},{1,5},{5... | collective-permute-start | bytes 884744 | tf_op jit(solution)/shard_map/ppermute | solution.py:744
  92.4 12.0 %collective-permute-start.34 = (bf16[192,768]{1,0:T(8,128)(2,1)S(1)}, bf16[192,768]{1,0:T(8,128)(2,1)S(1)}, u32[]{:S(2)}, u32[]{:S(2)}) collective-permute-start(bf16[192,768]{1,0:T(8,128)(2,1)S(1)} %collective-permute-done.17.refs_15_), channel_id=1, source_target_pairs={{0,4},{4,0},{8,12},{12,8},{16,20},{20,16},{24,28},{28,24},{1,5},{5... | collective-permute-start | bytes 884744 | tf_op jit(solution)/shard_map/ppermute | solution.py:744
  92.6 11.9 %collective-permute-start.35 = (bf16[192,768]{1,0:T(8,128)(2,1)S(1)}, bf16[192,768]{1,0:T(8,128)(2,1)S(1)}, u32[]{:S(2)}, u32[]{:S(2)}) collective-permute-start(bf16[192,768]{1,0:T(8,128)(2,1)S(1)} %collective-permute-done.18.refs_16_), channel_id=1, source_target_pairs={{0,4},{4,0},{8,12},{12,8},{16,20},{20,16},{24,28},{28,24},{1,5},{5... | collective-permute-start | bytes 884744 | tf_op jit(solution)/shard_map/ppermute | solution.py:744
  93.0 11.5 %collective-permute-start.31 = (bf16[384,768]{1,0:T(8,128)(2,1)S(1)}, bf16[384,768]{1,0:T(8,128)(2,1)S(1)}, u32[]{:S(2)}, u32[]{:S(2)}) collective-permute-start(bf16[384,768]{1,0:T(8,128)(2,1)S(1)} %pad_maximum_fusion.1.refs_6_), channel_id=1, source_target_pairs={{0,16},{4,12},{8,24},{12,4},{16,0},{20,28},{24,8},{28,20},{1,17},{... | collective-permute-start | bytes 1769480 | tf_op jit(solution)/shard_map/ppermute | solution.py:753
  94.5 14.7 %collective-permute-start.32 = (bf16[384,768]{1,0:T(8,128)(2,1)S(1)}, bf16[384,768]{1,0:T(8,128)(2,1)S(1)}, u32[]{:S(2)}, u32[]{:S(2)}) collective-permute-start(bf16[384,768]{1,0:T(8,128)(2,1)S(1)} %collective-permute-done.26.refs_7_), channel_id=1, source_target_pairs={{0,16},{4,12},{8,24},{12,4},{16,0},{20,28},{24,8},{28,20},{1,17},{... | collective-permute-start | bytes 1769480 | tf_op jit(solution)/shard_map/ppermute | solution.py:753
  156.2 16.6 %collective-permute-start.44 = (bf16[768,768]{1,0:T(8,128)(2,1)S(1)}, bf16[768,768]{1,0:T(8,128)(2,1)S(1)}, u32[]{:S(2)}, u32[]{:S(2)}) collective-permute-start(bf16[768,768]{1,0:T(8,128)(2,1)S(1)} %add_convert_fusion), channel_id=1, source_target_pairs={{0,8},{4,20},{8,0},{12,28},{16,24},{20,4},{24,16},{28,12},{1,9},{5... | collective-permute-start | bytes 3538952 | tf_op jit(solution)/shard_map/ppermute | solution.py:750
  160.5 18.2 %collective-permute-start.45 = (bf16[384,768]{1,0:T(8,128)(2,1)S(1)}, bf16[384,768]{1,0:T(8,128)(2,1)S(1)}, u32[]{:S(2)}, u32[]{:S(2)}) collective-permute-start(bf16[384,768]{1,0:T(8,128)(2,1)S(1)} %add_convert_fusion.4), channel_id=1, source_target_pairs={{0,8},{4,20},{8,0},{12,28},{16,24},{20,4},{24,16},{28,12},{1,9},{5... | collective-permute-start | bytes 1769480 | tf_op jit(solution)/shard_map/ppermute | solution.py:750
  178.7 18.4 %collective-permute-start.49 = (bf16[384,768]{1,0:T(8,128)(2,1)S(1)}, bf16[384,768]{1,0:T(8,128)(2,1)S(1)}, u32[]{:S(2)}, u32[]{:S(2)}) collective-permute-start(bf16[384,768]{1,0:T(8,128)(2,1)S(1)} %add_convert_fusion.3), channel_id=1, source_target_pairs={{0,8},{4,20},{8,0},{12,28},{16,24},{20,4},{24,16},{28,12},{1,9},{5... | collective-permute-start | bytes 1769480 | tf_op jit(solution)/shard_map/ppermute | solution.py:750
  181.8 15.4 %collective-permute-start.48 = (bf16[192,768]{1,0:T(8,128)(2,1)S(1)}, bf16[192,768]{1,0:T(8,128)(2,1)S(1)}, u32[]{:S(2)}, u32[]{:S(2)}) collective-permute-start(bf16[192,768]{1,0:T(8,128)(2,1)S(1)} %add_convert_fusion.14), channel_id=1, source_target_pairs={{0,16},{4,12},{8,24},{12,4},{16,0},{20,28},{24,8},{28,20},{1,17},{... | collective-permute-start | bytes 884744 | tf_op jit(solution)/shard_map/ppermute | solution.py:753
  183.4 20.5 %collective-permute-start.50 = (bf16[352,768]{1,0:T(8,128)(2,1)S(1)}, bf16[352,768]{1,0:T(8,128)(2,1)S(1)}, u32[]{:S(2)}, u32[]{:S(2)}) collective-permute-start(bf16[352,768]{1,0:T(8,128)(2,1)S(1)} %add_convert_fusion.7), channel_id=1, source_target_pairs={{0,8},{4,20},{8,0},{12,28},{16,24},{20,4},{24,16},{28,12},{1,9},{5... | collective-permute-start | bytes 1622024 | tf_op jit(solution)/shard_map/ppermute | solution.py:750
  185.1 18.8 %collective-permute-start.47 = (bf16[384,768]{1,0:T(8,128)(2,1)S(1)}, bf16[384,768]{1,0:T(8,128)(2,1)S(1)}, u32[]{:S(2)}, u32[]{:S(2)}) collective-permute-start(bf16[384,768]{1,0:T(8,128)(2,1)S(1)} %add_convert_fusion.2), channel_id=1, source_target_pairs={{0,16},{4,12},{8,24},{12,4},{16,0},{20,28},{24,8},{28,20},{1,17},{... | collective-permute-start | bytes 1769480 | tf_op jit(solution)/shard_map/ppermute | solution.py:753
  207.0 17.4 %collective-permute-start.54 = (bf16[176,768]{1,0:T(8,128)(2,1)S(1)}, bf16[176,768]{1,0:T(8,128)(2,1)S(1)}, u32[]{:S(2)}, u32[]{:S(2)}) collective-permute-start(bf16[176,768]{1,0:T(8,128)(2,1)S(1)} %add_convert_fusion.21), channel_id=1, source_target_pairs={{0,16},{4,12},{8,24},{12,4},{16,0},{20,28},{24,8},{28,20},{1,17},{... | collective-permute-start | bytes 811016 | tf_op jit(solution)/shard_map/ppermute | solution.py:753
  208.6 15.8 %collective-permute-start.52 = (bf16[192,768]{1,0:T(8,128)(2,1)S(1)}, bf16[192,768]{1,0:T(8,128)(2,1)S(1)}, u32[]{:S(2)}, u32[]{:S(2)}) collective-permute-start(bf16[192,768]{1,0:T(8,128)(2,1)S(1)} %get-tuple-element.427), channel_id=1, source_target_pairs={{0,3},{1,0},{2,1},{3,2},{4,7},{5,4},{6,5},{7,6},{8,11},{9,8},{10,9... | collective-permute-start | bytes 884744 | tf_op jit(solution)/shard_map/ppermute | solution.py:738
  210.8 13.6 %collective-permute-start.53 = (bf16[192,768]{1,0:T(8,128)(2,1)S(1)}, bf16[192,768]{1,0:T(8,128)(2,1)S(1)}, u32[]{:S(2)}, u32[]{:S(2)}) collective-permute-start(bf16[192,768]{1,0:T(8,128)(2,1)S(1)} %get-tuple-element.428), channel_id=1, source_target_pairs={{0,1},{1,2},{2,3},{3,0},{4,5},{5,6},{6,7},{7,4},{8,9},{9,10},{10,1... | collective-permute-start | bytes 884744 | tf_op jit(solution)/shard_map/ppermute | solution.py:738
  210.8 13.6 %collective-permute-start.56 = (bf16[192,768]{1,0:T(8,128)(2,1)S(1)}, bf16[192,768]{1,0:T(8,128)(2,1)S(1)}, u32[]{:S(2)}, u32[]{:S(2)}) collective-permute-start(bf16[192,768]{1,0:T(8,128)(2,1)S(1)} %add_convert_fusion.11), channel_id=1, source_target_pairs={{0,16},{4,12},{8,24},{12,4},{16,0},{20,28},{24,8},{28,20},{1,17},{... | collective-permute-start | bytes 884744 | tf_op jit(solution)/shard_map/ppermute | solution.py:753
  211.3 13.1 %collective-permute-start.55 = (bf16[352,768]{1,0:T(8,128)(2,1)S(1)}, bf16[352,768]{1,0:T(8,128)(2,1)S(1)}, u32[]{:S(2)}, u32[]{:S(2)}) collective-permute-start(bf16[352,768]{1,0:T(8,128)(2,1)S(1)} %add_convert_fusion.6), channel_id=1, source_target_pairs={{0,8},{4,20},{8,0},{12,28},{16,24},{20,4},{24,16},{28,12},{1,9},{5... | collective-permute-start | bytes 1622024 | tf_op jit(solution)/shard_map/ppermute | solution.py:750
  227.5 19.5 %collective-permute-start.59 = (bf16[176,768]{1,0:T(8,128)(2,1)S(1)}, bf16[176,768]{1,0:T(8,128)(2,1)S(1)}, u32[]{:S(2)}, u32[]{:S(2)}) collective-permute-start(bf16[176,768]{1,0:T(8,128)(2,1)S(1)} %add_convert_fusion.20), channel_id=1, source_target_pairs={{0,3},{1,0},{2,1},{3,2},{4,7},{5,4},{6,5},{7,6},{8,11},{9,8},{10,9... | collective-permute-start | bytes 811016 | tf_op jit(solution)/shard_map/ppermute | solution.py:738
  231.4 15.6 %collective-permute-start.60 = (bf16[176,768]{1,0:T(8,128)(2,1)S(1)}, bf16[176,768]{1,0:T(8,128)(2,1)S(1)}, u32[]{:S(2)}, u32[]{:S(2)}) collective-permute-start(bf16[176,768]{1,0:T(8,128)(2,1)S(1)} %add_convert_fusion.19), channel_id=1, source_target_pairs={{0,16},{4,12},{8,24},{12,4},{16,0},{20,28},{24,8},{28,20},{1,17},{... | collective-permute-start | bytes 811016 | tf_op jit(solution)/shard_map/ppermute | solution.py:753
  232.9 14.1 %collective-permute-start.58 = (bf16[192,768]{1,0:T(8,128)(2,1)S(1)}, bf16[192,768]{1,0:T(8,128)(2,1)S(1)}, u32[]{:S(2)}, u32[]{:S(2)}) collective-permute-start(bf16[192,768]{1,0:T(8,128)(2,1)S(1)} %add_convert_fusion.10), channel_id=1, source_target_pairs={{0,3},{1,0},{2,1},{3,2},{4,7},{5,4},{6,5},{7,6},{8,11},{9,8},{10,9... | collective-permute-start | bytes 884744 | tf_op jit(solution)/shard_map/ppermute | solution.py:738
  233.2 13.8 %collective-permute-start.61 = (bf16[352,768]{1,0:T(8,128)(2,1)S(1)}, bf16[352,768]{1,0:T(8,128)(2,1)S(1)}, u32[]{:S(2)}, u32[]{:S(2)}) collective-permute-start(bf16[352,768]{1,0:T(8,128)(2,1)S(1)} %add_convert_fusion.5), channel_id=1, source_target_pairs={{0,8},{4,20},{8,0},{12,28},{16,24},{20,4},{24,16},{28,12},{1,9},{5... | collective-permute-start | bytes 1622024 | tf_op jit(solution)/shard_map/ppermute | solution.py:750
  250.9 15.2 %collective-permute-start.63 = (bf16[512,768]{1,0:T(8,128)(2,1)S(1)}, bf16[512,768]{1,0:T(8,128)(2,1)S(1)}, u32[]{:S(2)}, u32[]{:S(2)}) collective-permute-start(bf16[512,768]{1,0:T(8,128)(2,1)S(1)} %add_convert_fusion.1), channel_id=1, source_target_pairs={{0,8},{4,20},{8,0},{12,28},{16,24},{20,4},{24,16},{28,12},{1,9},{5... | collective-permute-start | bytes 2359304 | tf_op jit(solution)/shard_map/ppermute | solution.py:750
  252.9 13.2 %collective-permute-start.66 = (bf16[192,768]{1,0:T(8,128)(2,1)S(1)}, bf16[192,768]{1,0:T(8,128)(2,1)S(1)}, u32[]{:S(2)}, u32[]{:S(2)}) collective-permute-start(bf16[192,768]{1,0:T(8,128)(2,1)S(1)} %add_convert_fusion.9.refs_0_), channel_id=1, source_target_pairs={{0,8},{4,20},{8,0},{12,28},{16,24},{20,4},{24,16},{28,12},{1,9},{5... | collective-permute-start | bytes 884744 | tf_op jit(solution)/shard_map/ppermute | solution.py:750
  266.1 13.0 %collective-permute-start.69 = (bf16[192,768]{1,0:T(8,128)(2,1)S(1)}, bf16[192,768]{1,0:T(8,128)(2,1)S(1)}, u32[]{:S(2)}, u32[]{:S(2)}) collective-permute-start(bf16[192,768]{1,0:T(8,128)(2,1)S(1)} %add_convert_fusion.9.refs_0_), channel_id=1, source_target_pairs={{0,16},{4,12},{8,24},{12,4},{16,0},{20,28},{24,8},{28,20},{1,17},{... | collective-permute-start | bytes 884744 | tf_op jit(solution)/shard_map/ppermute | solution.py:753
  266.6 12.5 %collective-permute-start.70 = (bf16[192,768]{1,0:T(8,128)(2,1)S(1)}, bf16[192,768]{1,0:T(8,128)(2,1)S(1)}, u32[]{:S(2)}, u32[]{:S(2)}) collective-permute-start(bf16[192,768]{1,0:T(8,128)(2,1)S(1)} %collective-permute-done.66.refs_1_), channel_id=1, source_target_pairs={{0,16},{4,12},{8,24},{12,4},{16,0},{20,28},{24,8},{28,20},{1,17},{... | collective-permute-start | bytes 884744 | tf_op jit(solution)/shard_map/ppermute | solution.py:753
  268.3 11.9 %collective-permute-start.67 = (bf16[256,768]{1,0:T(8,128)(2,1)S(1)}, bf16[256,768]{1,0:T(8,128)(2,1)S(1)}, u32[]{:S(2)}, u32[]{:S(2)}) collective-permute-start(bf16[256,768]{1,0:T(8,128)(2,1)S(1)} %add_convert_fusion.8), channel_id=1, source_target_pairs={{0,16},{4,12},{8,24},{12,4},{16,0},{20,28},{24,8},{28,20},{1,17},{... | collective-permute-start | bytes 1179656 | tf_op jit(solution)/shard_map/ppermute | solution.py:753
  280.3 15.8 %collective-permute-start.75 = (bf16[768,768]{1,0:T(8,128)(2,1)S(1)}, bf16[768,768]{1,0:T(8,128)(2,1)S(1)}, u32[]{:S(2)}, u32[]{:S(2)}) collective-permute-start(bf16[768,768]{1,0:T(8,128)(2,1)S(1)} %pad_maximum_fusion), channel_id=1, source_target_pairs={{0,4},{4,0},{8,12},{12,8},{16,20},{20,16},{24,28},{28,24},{1,5},{5... | collective-permute-start | bytes 3538952 | tf_op jit(solution)/shard_map/ppermute | solution.py:744
  280.6 15.4 %collective-permute-start.74 = (bf16[176,768]{1,0:T(8,128)(2,1)S(1)}, bf16[176,768]{1,0:T(8,128)(2,1)S(1)}, u32[]{:S(2)}, u32[]{:S(2)}) collective-permute-start(bf16[176,768]{1,0:T(8,128)(2,1)S(1)} %add_convert_fusion.15.refs_0_), channel_id=1, source_target_pairs={{0,8},{4,20},{8,0},{12,28},{16,24},{20,4},{24,16},{28,12},{1,9},{5... | collective-permute-start | bytes 811016 | tf_op jit(solution)/shard_map/ppermute | solution.py:750
  283.1 13.0 %collective-permute-start.72 = (bf16[80,768]{1,0:T(8,128)(2,1)S(1)}, bf16[80,768]{1,0:T(8,128)(2,1)S(1)}, u32[]{:S(2)}, u32[]{:S(2)}) collective-permute-start(bf16[80,768]{1,0:T(8,128)(2,1)S(1)} %add_convert_fusion.23), channel_id=1, source_target_pairs={{0,2},{1,3},{2,0},{3,1},{4,6},{5,7},{6,4},{7,5},{8,10},{9,11},{10,... | collective-permute-start | bytes 368648 | tf_op jit(solution)/shard_map/ppermute | solution.py:741
  285.9 10.2 %collective-permute-start.71 = (bf16[80,768]{1,0:T(8,128)(2,1)S(1)}, bf16[80,768]{1,0:T(8,128)(2,1)S(1)}, u32[]{:S(2)}, u32[]{:S(2)}) collective-permute-start(bf16[80,768]{1,0:T(8,128)(2,1)S(1)} %add_convert_fusion.23), channel_id=1, source_target_pairs={{0,1},{1,0},{2,3},{3,2},{4,5},{5,4},{6,7},{7,6},{8,9},{9,8},{10,11... | collective-permute-start | bytes 368648 | tf_op jit(solution)/shard_map/ppermute | solution.py:741
  296.1 12.1 %collective-permute-start.78 = (bf16[176,768]{1,0:T(8,128)(2,1)S(1)}, bf16[176,768]{1,0:T(8,128)(2,1)S(1)}, u32[]{:S(2)}, u32[]{:S(2)}) collective-permute-start(bf16[176,768]{1,0:T(8,128)(2,1)S(1)} %add_convert_fusion.15.refs_0_), channel_id=1, source_target_pairs={{0,16},{4,12},{8,24},{12,4},{16,0},{20,28},{24,8},{28,20},{1,17},{... | collective-permute-start | bytes 811016 | tf_op jit(solution)/shard_map/ppermute | solution.py:753
  297.7 10.5 %collective-permute-start.79 = (bf16[176,768]{1,0:T(8,128)(2,1)S(1)}, bf16[176,768]{1,0:T(8,128)(2,1)S(1)}, u32[]{:S(2)}, u32[]{:S(2)}) collective-permute-start(bf16[176,768]{1,0:T(8,128)(2,1)S(1)} %collective-permute-done.74.refs_1_), channel_id=1, source_target_pairs={{0,16},{4,12},{8,24},{12,4},{16,0},{20,28},{24,8},{28,20},{1,17},{... | collective-permute-start | bytes 811016 | tf_op jit(solution)/shard_map/ppermute | solution.py:753
  (126 other events, 1117.6 us)
